TPU v7x, 32 devices: a whole 2x2x4 slice. The times are simulated.
32 devices in a mesh: dp: 4 (over z), seq: 8 (over y, x, core).
Axes of the slice: x: 2, y: 2, z: 4, core: 2. Of those that a mesh axis runs over, the one named last changes fastest.
Arguments:
- layer_input: bfloat16 [4, 2048, 1152], P('dp', 'seq'), may hold values from -6 to 6
- segment_ids: int32 [4, 2048], P('dp'), may hold values from 0 to 3, as said below
- position_ids: int32 [4, 2048], P('dp', 'seq'), may hold values from 0 to 1023, as said below
- w_query: bfloat16 [1152, 1024], P('seq'), may hold values from -0.1875 to 0.1875
- w_keyval: bfloat16 [1152, 512], P('seq'), may hold values from -0.1875 to 0.1875
- w_out: bfloat16 [1024, 1152], P('seq'), may hold values from -0.1875 to 0.1875
- w_gate: bfloat16 [1152, 6912], P(None, 'seq'), may hold values from -0.1875 to 0.1875
- w_up: bfloat16 [1152, 6912], P(None, 'seq'), may hold values from -0.1875 to 0.1875
- w_down: bfloat16 [6912, 1152], P('seq'), may hold values from -0.078125 to 0.078125
- g_input: float32 [1152], replicated, may hold values from 0.25 to 1.75
- g_post_attn: float32 [1152], replicated, may hold values from 0.25 to 1.75
- g_pre_ffn: float32 [1152], replicated, may hold values from 0.25 to 1.75
- g_post_ffn: float32 [1152], replicated, may hold values from 0.25 to 1.75
- g_query: float32 [256], replicated, may hold values from 0.25 to 1.75
- g_key: float32 [256], replicated, may hold values from 0.25 to 1.75
- out_grad: float32 [4, 2048, 1152], P('dp', 'seq'), may hold values from -6 to 6
Outputs:
- layer_output: bfloat16 [4, 2048, 1152], P('dp', 'seq')
- input_grad: float32 [4, 2048, 1152], P('dp', 'seq')
- grad_w_query: float32 [1152, 1024], P('seq')
- grad_w_keyval: float32 [1152, 512], P('seq')
- grad_w_out: float32 [1024, 1152], P('seq')
- grad_w_gate: float32 [1152, 6912], P(None, 'seq')
- grad_w_up: float32 [1152, 6912], P(None, 'seq')
- grad_w_down: float32 [6912, 1152], P('seq')
- grad_g_input: float32 [1152], P('seq')
- grad_g_post_attn: float32 [1152], P('seq')
- grad_g_pre_ffn: float32 [1152], P('seq')
- grad_g_post_ffn: float32 [1152], P('seq')
- grad_g_query: float32 [256], P('seq')
- grad_g_key: float32 [256], P('seq')
Inputs may be any that keep to these rules, and one draw needn't show every extreme that they name: `segment_ids`: in each row the ids never fall, start at 0 and rise by one at each document's first token; every row holds 4 documents, none longer than 1024 tokens, and in every row one of them is exactly that long. `position_ids`: A token's place within its document: 0 at the document's first token, rising by one along it; the documents are those of segment_ids.
All inputs are finite; a program needn't handle non-finite values.
Results may differ from a plain program's by a relative error of at most 0.023.
Values may be sent and summed in bfloat16 or wider, within the bound.
No kernel may reach another device: no remote copies, remote signals or barrier semaphores. Data moves between devices by JAX's collectives and lax.ppermute only.
A program may use at most 256 MiB of HBM per device.

v0:
```python
import jax
import jax.numpy as jnp
from jax import lax
from jax.sharding import PartitionSpec as P

HEADS = 4
HEAD = 256


norm_eps = 1e-06
rope_base = 1000000.0


def rms_forward(values):
    factor = lax.rsqrt(jnp.mean(values * values, axis=-1, keepdims=True) + norm_eps)
    return (values * factor, factor)


def rms_backward(upstream, normed, factor):
    return factor * (upstream - normed * jnp.mean(upstream * normed, axis=-1, keepdims=True))


def rope_angles(positions, width):
    half_width = width // 2
    inverse_freq = rope_base ** (-(jnp.arange(half_width).astype(jnp.float32) * 2.0 / width))
    return positions.astype(jnp.float32)[:, None] * inverse_freq[None, :]


def rotate(values, angles):
    half_width = values.shape[-1] // 2
    first_half = values[..., :half_width]
    second_half = values[..., half_width:]
    cosine = jnp.cos(angles)
    sine_part = jnp.sin(angles)
    return jnp.concatenate(
        [
            first_half * cosine - second_half * sine_part,
            second_half * cosine + first_half * sine_part,
        ],
        axis=-1,
    )


def dot_rows(left, right):
    return lax.dot_general(
        left, right, (((1,), (1,)), ((), ())), preferred_element_type=jnp.float32
    )


def dot_cols(left, right):
    return lax.dot_general(
        left, right, (((0,), (0,)), ((), ())), preferred_element_type=jnp.float32
    )


def gelu_gate(gate_proj, up_proj):
    return jax.nn.gelu(gate_proj, approximate=True) * up_proj


def on_device(
    layer_input,
    segment_ids,
    position_ids,
    w_query,
    w_keyval,
    w_out,
    w_gate,
    w_up,
    w_down,
    g_input,
    g_post_attn,
    g_pre_ffn,
    g_post_ffn,
    g_query,
    g_key,
    out_grad,
):
    local_rows = layer_input.shape[1]
    row_len = local_rows * lax.axis_size("seq")
    row_offset = lax.axis_index("seq") * local_rows
    input_f32 = layer_input[0].astype(jnp.float32)
    seg_row = segment_ids[0]
    seg_local = lax.dynamic_slice_in_dim(seg_row, row_offset, local_rows)
    angles = rope_angles(position_ids[0], HEAD)
    score_scale = HEAD ** (-0.5)
    query_full, keyval_full, out_full, gate_full, up_full, down_full = (
        lax.all_gather(w_query, "seq", axis=0, tiled=True),
        lax.all_gather(w_keyval, "seq", axis=0, tiled=True),
        lax.all_gather(w_out, "seq", axis=0, tiled=True),
        lax.all_gather(w_gate, "seq", axis=1, tiled=True),
        lax.all_gather(w_up, "seq", axis=1, tiled=True),
        lax.all_gather(w_down, "seq", axis=0, tiled=True),
    )
    a_normed, a_factor = rms_forward(input_f32)
    a_low = (a_normed * g_input).astype(jnp.bfloat16)
    q_pre = jnp.dot(a_low, query_full, preferred_element_type=jnp.float32).reshape(
        local_rows, HEADS, HEAD
    )
    kv_pre = jnp.dot(a_low, keyval_full, preferred_element_type=jnp.float32)
    q_hat, q_factor = rms_forward(q_pre)
    q_low = rotate(q_hat * g_query, angles[:, None, :]).astype(jnp.bfloat16)
    k_hat, k_factor = rms_forward(kv_pre[:, :HEAD])
    k_low = rotate(k_hat * g_key, angles).astype(jnp.bfloat16)
    kv_low = jnp.concatenate([k_low, kv_pre[:, HEAD:].astype(jnp.bfloat16)], axis=1)
    kv_row = lax.all_gather(kv_low, "seq", axis=0, tiled=True)
    key_block = min(512, row_len)
    first_block = jnp.maximum(row_offset - row_len // 2 + 1, 0) // key_block
    end_block = (row_offset + local_rows - 1) // key_block + 1
    query_rows = q_low.reshape(local_rows * HEADS, HEAD)
    query_index = jnp.broadcast_to(
        (row_offset + jnp.arange(local_rows, dtype=jnp.int32))[:, None], (local_rows, HEADS)
    ).reshape(-1)
    query_seg = jnp.broadcast_to(seg_local[:, None], (local_rows, HEADS)).reshape(-1)

    def block_at(block_num):
        key_start = (block_num * key_block).astype(jnp.int32)
        kv_piece = lax.dynamic_slice_in_dim(kv_row, key_start, key_block, 0)
        seg_piece = lax.dynamic_slice_in_dim(seg_row, key_start, key_block, 0)
        return (key_start, kv_piece, seg_piece)

    def block_scores(key_start, key_rows, key_seg):
        raw_scores = dot_rows(query_rows, key_rows) * score_scale
        key_index = key_start + jnp.arange(key_block, dtype=jnp.int32)
        visible = (key_seg[None, :] == query_seg[:, None]) & (
            key_index[None, :] <= query_index[:, None]
        )
        return (raw_scores, visible)

    def max_and_total(block_num, state_pair):
        row_max, exp_total = state_pair
        key_start, kv_piece, seg_piece = block_at(block_num)
        raw_scores, visible = block_scores(key_start, kv_piece[:, :HEAD], seg_piece)
        masked = jnp.where(visible, raw_scores, -1e30)
        new_max = jnp.maximum(row_max, jnp.max(masked, axis=1))
        shifted = jnp.where(visible, jnp.exp(masked - new_max[:, None]), 0.0)
        exp_total = exp_total * jnp.exp(row_max - new_max) + jnp.sum(shifted, axis=1)
        return (new_max, exp_total)

    start_max = jnp.full((local_rows * HEADS,), -1e30, jnp.float32)
    start_total = jnp.zeros((local_rows * HEADS,), jnp.float32)
    row_max, exp_total = lax.fori_loop(
        first_block, end_block, max_and_total, (start_max, start_total)
    )
    log_total = row_max + jnp.log(exp_total)

    def weighted_sum(block_num, accum):
        key_start, kv_piece, seg_piece = block_at(block_num)
        raw_scores, visible = block_scores(key_start, kv_piece[:, :HEAD], seg_piece)
        attn_prob = jnp.where(visible, jnp.exp(raw_scores - log_total[:, None]), 0.0).astype(
            jnp.bfloat16
        )
        return accum + jnp.dot(attn_prob, kv_piece[:, HEAD:], preferred_element_type=jnp.float32)

    attended_rows = lax.fori_loop(
        first_block, end_block, weighted_sum, jnp.zeros((local_rows * HEADS, HEAD), jnp.float32)
    )
    attended_low = attended_rows.reshape(local_rows, HEADS * HEAD).astype(jnp.bfloat16)
    attn_proj = jnp.dot(attended_low, out_full, preferred_element_type=jnp.float32)
    attn_normed, attn_factor = rms_forward(attn_proj)
    middle = input_f32 + attn_normed * g_post_attn
    b_normed, b_factor = rms_forward(middle)
    b_low = (b_normed * g_pre_ffn).astype(jnp.bfloat16)
    gate_proj = jnp.dot(b_low, gate_full, preferred_element_type=jnp.float32)
    up_proj = jnp.dot(b_low, up_full, preferred_element_type=jnp.float32)
    hidden_low = gelu_gate(gate_proj, up_proj).astype(jnp.bfloat16)
    ffn_out = jnp.dot(hidden_low, down_full, preferred_element_type=jnp.float32)
    ffn_normed, ffn_factor = rms_forward(ffn_out)
    layer_out = (middle + ffn_normed * g_post_ffn).astype(jnp.bfloat16)
    grad_top = out_grad[0]
    gain_post_ffn = jnp.sum(grad_top * ffn_normed, axis=0)
    d_ffn_low = rms_backward(grad_top * g_post_ffn, ffn_normed, ffn_factor).astype(jnp.bfloat16)
    d_hidden = dot_rows(d_ffn_low, down_full)
    grad_down = dot_cols(hidden_low, d_ffn_low)
    _, gelu_back = jax.vjp(gelu_gate, gate_proj, up_proj)
    d_gate, d_up = gelu_back(d_hidden)
    d_gate_low = d_gate.astype(jnp.bfloat16)
    d_up_low = d_up.astype(jnp.bfloat16)
    grad_gate = dot_cols(b_low, d_gate_low)
    grad_upw = dot_cols(b_low, d_up_low)
    d_b = dot_rows(d_gate_low, gate_full) + dot_rows(d_up_low, up_full)
    gain_pre_ffn = jnp.sum(d_b * b_normed, axis=0)
    d_middle = grad_top + rms_backward(d_b * g_pre_ffn, b_normed, b_factor)
    gain_post_attn = jnp.sum(d_middle * attn_normed, axis=0)
    d_attn_low = rms_backward(d_middle * g_post_attn, attn_normed, attn_factor).astype(jnp.bfloat16)
    grad_outw = dot_cols(attended_low, d_attn_low)
    d_attended = dot_rows(d_attn_low, out_full).astype(jnp.bfloat16)
    d_attended_rows = d_attended.reshape(local_rows * HEADS, HEAD)
    row_dot = jnp.sum(d_attended_rows.astype(jnp.float32) * attended_rows, axis=1)

    def attend_back(block_num, carry):
        d_query, d_kv_whole = carry
        key_start, kv_piece, seg_piece = block_at(block_num)
        raw_scores, visible = block_scores(key_start, kv_piece[:, :HEAD], seg_piece)
        attn_prob = jnp.where(visible, jnp.exp(raw_scores - log_total[:, None]), 0.0)
        prob_low = attn_prob.astype(jnp.bfloat16)
        d_prob = dot_rows(d_attended_rows, kv_piece[:, HEAD:])
        d_scores = (attn_prob * (d_prob - row_dot[:, None])).astype(jnp.bfloat16)
        d_query = (
            d_query
            + jnp.dot(d_scores, kv_piece[:, :HEAD], preferred_element_type=jnp.float32)
            * score_scale
        )
        d_keys = dot_cols(d_scores, query_rows) * score_scale
        d_values = dot_cols(prob_low, d_attended_rows)
        d_kv_whole = lax.dynamic_update_slice_in_dim(
            d_kv_whole, jnp.concatenate([d_keys, d_values], axis=1), key_start, 0
        )
        return (d_query, d_kv_whole)

    d_query, d_kv_whole = lax.fori_loop(
        first_block,
        end_block,
        attend_back,
        (
            jnp.zeros((local_rows * HEADS, HEAD), jnp.float32),
            jnp.zeros((row_len, 2 * HEAD), jnp.float32),
        ),
    )
    d_kv = lax.psum_scatter(
        d_kv_whole.astype(jnp.bfloat16), "seq", scatter_dimension=0, tiled=True
    ).astype(jnp.float32)
    d_q_normed = rotate(d_query.reshape(local_rows, HEADS, HEAD), -angles[:, None, :])
    gain_query = jnp.sum(d_q_normed * q_hat, axis=(0, 1))
    d_q_pre = (
        rms_backward(d_q_normed * g_query, q_hat, q_factor)
        .reshape(local_rows, HEADS * HEAD)
        .astype(jnp.bfloat16)
    )
    d_k_normed = rotate(d_kv[:, :HEAD], -angles)
    gain_key = jnp.sum(d_k_normed * k_hat, axis=0)
    d_k_pre = rms_backward(d_k_normed * g_key, k_hat, k_factor)
    d_kv_low = jnp.concatenate([d_k_pre, d_kv[:, HEAD:]], axis=1).astype(jnp.bfloat16)
    grad_queryw = dot_cols(a_low, d_q_pre)
    grad_keyvalw = dot_cols(a_low, d_kv_low)
    d_a = dot_rows(d_q_pre, query_full) + dot_rows(d_kv_low, keyval_full)
    gain_input = jnp.sum(d_a * a_normed, axis=0)
    d_input = d_middle + rms_backward(d_a * g_input, a_normed, a_factor)
    (
        grad_queryw,
        grad_keyvalw,
        grad_outw,
        grad_gate,
        grad_upw,
        grad_down,
        gain_input,
        gain_post_attn,
        gain_pre_ffn,
        gain_post_ffn,
        gain_query,
        gain_key,
    ) = (
        lax.psum_scatter(
            grad_queryw.astype(jnp.bfloat16), "seq", scatter_dimension=0, tiled=True
        ).astype(jnp.float32),
        lax.psum_scatter(
            grad_keyvalw.astype(jnp.bfloat16), "seq", scatter_dimension=0, tiled=True
        ).astype(jnp.float32),
        lax.psum_scatter(
            grad_outw.astype(jnp.bfloat16), "seq", scatter_dimension=0, tiled=True
        ).astype(jnp.float32),
        lax.psum_scatter(
            grad_gate.astype(jnp.bfloat16), "seq", scatter_dimension=1, tiled=True
        ).astype(jnp.float32),
        lax.psum_scatter(
            grad_upw.astype(jnp.bfloat16), "seq", scatter_dimension=1, tiled=True
        ).astype(jnp.float32),
        lax.psum_scatter(
            grad_down.astype(jnp.bfloat16), "seq", scatter_dimension=0, tiled=True
        ).astype(jnp.float32),
        lax.psum_scatter(
            gain_input.astype(jnp.bfloat16), "seq", scatter_dimension=0, tiled=True
        ).astype(jnp.float32),
        lax.psum_scatter(
            gain_post_attn.astype(jnp.bfloat16), "seq", scatter_dimension=0, tiled=True
        ).astype(jnp.float32),
        lax.psum_scatter(
            gain_pre_ffn.astype(jnp.bfloat16), "seq", scatter_dimension=0, tiled=True
        ).astype(jnp.float32),
        lax.psum_scatter(
            gain_post_ffn.astype(jnp.bfloat16), "seq", scatter_dimension=0, tiled=True
        ).astype(jnp.float32),
        lax.psum_scatter(
            gain_query.astype(jnp.bfloat16), "seq", scatter_dimension=0, tiled=True
        ).astype(jnp.float32),
        lax.psum_scatter(
            gain_key.astype(jnp.bfloat16), "seq", scatter_dimension=0, tiled=True
        ).astype(jnp.float32),
    )
    totals = (
        lax.psum(grad_queryw.astype(jnp.bfloat16), "dp").astype(jnp.float32),
        lax.psum(grad_keyvalw.astype(jnp.bfloat16), "dp").astype(jnp.float32),
        lax.psum(grad_outw.astype(jnp.bfloat16), "dp").astype(jnp.float32),
        lax.psum(grad_gate.astype(jnp.bfloat16), "dp").astype(jnp.float32),
        lax.psum(grad_upw.astype(jnp.bfloat16), "dp").astype(jnp.float32),
        lax.psum(grad_down.astype(jnp.bfloat16), "dp").astype(jnp.float32),
        lax.psum(gain_input.astype(jnp.bfloat16), "dp").astype(jnp.float32),
        lax.psum(gain_post_attn.astype(jnp.bfloat16), "dp").astype(jnp.float32),
        lax.psum(gain_pre_ffn.astype(jnp.bfloat16), "dp").astype(jnp.float32),
        lax.psum(gain_post_ffn.astype(jnp.bfloat16), "dp").astype(jnp.float32),
        lax.psum(gain_query.astype(jnp.bfloat16), "dp").astype(jnp.float32),
        lax.psum(gain_key.astype(jnp.bfloat16), "dp").astype(jnp.float32),
    )
    return (
        layer_out[None],
        d_input[None],
        totals[0],
        totals[1],
        totals[2],
        totals[3],
        totals[4],
        totals[5],
        totals[6],
        totals[7],
        totals[8],
        totals[9],
        totals[10],
        totals[11],
    )


def solution(mesh):
    in_specs = (
        P("dp", "seq", None),
        P("dp", None),
        P("dp", "seq"),
        P("seq", None),
        P("seq", None),
        P("seq", None),
        P(None, "seq"),
        P(None, "seq"),
        P("seq", None),
        P(),
        P(),
        P(),
        P(),
        P(),
        P(),
        P("dp", "seq", None),
    )
    out_specs = (
        P("dp", "seq", None),
        P("dp", "seq", None),
        P("seq", None),
        P("seq", None),
        P("seq", None),
        P(None, "seq"),
        P(None, "seq"),
        P("seq", None),
        P("seq"),
        P("seq"),
        P("seq"),
        P("seq"),
        P("seq"),
        P("seq"),
    )
    return jax.shard_map(
        on_device, mesh=mesh, in_specs=in_specs, out_specs=out_specs, check_vma=False
    )
```

profile of v0, /device:TPU:0, one launch (start us, length us, event | category | flops | bytes accessed | tf_op | source)
XLA Modules:
  0.0 1255.0 jit_solution(4688408701022514957)
XLA Ops:
  10.7 26.0 %all-gather.8.cloned.1.call-done = bf16[1152,512]{1,0:T(8,128)(2,1)} async-done(((bf16[144,512]{1,0:T(8,128)(2,1)}), bf16[1152,512]{1,0:T(8,128)(2,1)}) %all-gather.8.cloned.1.call-update) | async-done | bytes 1179664 | tf_op jit(solution)/shard_map/all_gather | solution.py:88
  44.8 22.8 %all-gather.12.cloned.1.call-done = bf16[1152,1024]{1,0:T(8,128)(2,1)} async-done(((bf16[144,1024]{1,0:T(8,128)(2,1)}), bf16[1152,1024]{1,0:T(8,128)(2,1)}) %all-gather.12.cloned.1.call-update) | async-done | bytes 2359312 | tf_op jit(solution)/shard_map/all_gather | solution.py:87
  67.6 3.1 copy.39
  73.0 25.0 %all-gather.10.cloned.1.call-done = bf16[2048,512]{1,0:T(8,128)(2,1)} async-done(((bf16[256,512]{1,0:T(8,128)(2,1)}), bf16[2048,512]{1,0:T(8,128)(2,1)}) %all-gather.10.cloned.1.call-update) | async-done | bytes 2097168 | tf_op jit(solution)/shard_map/all_gather | solution.py:105
  98.0 2.9 while.37
  101.0 2.8 while.38
  104.8 24.0 %all-gather.14.cloned.1.call-done = bf16[1024,1152]{1,0:T(8,128)(2,1)} async-done(((bf16[128,1152]{1,0:T(8,128)(2,1)}), bf16[1024,1152]{1,0:T(8,128)(2,1)}) %all-gather.14.cloned.1.call-update) | async-done | bytes 2359312 | tf_op jit(solution)/shard_map/all_gather | solution.py:89
  128.8 2.7 multiply_reduce_fusion.7
  132.4 84.5 %all-gather.16.cloned.1.call-done = bf16[1152,6912]{0,1:T(8,128)(2,1)} async-done(((bf16[1152,864]{0,1:T(8,128)(2,1)}), bf16[1152,6912]{0,1:T(8,128)(2,1)}) %all-gather.16.cloned.1.call-update) | async-done | bytes 15925264 | tf_op jit(solution)/shard_map/all_gather | solution.py:90
  216.9 16.2 %fusion.84 = f32[256,6912]{1,0:T(8,128)} fusion(bf16[256,1152]{1,0:T(8,128)(2,1)S(1)} %multiply_convert_fusion.4, bf16[1152,6912]{0,1:T(8,128)(2,1)} %all-gather.16.cloned.1.call-done), kind=kOutput, calls=%fused_computation.160 | convolution fusion | flops 4076863488 | bytes 23592960 | tf_op jit(solution)/shard_map/dot_general | solution.py:163
  233.1 71.8 %all-gather.18.cloned.1.call-done = bf16[1152,6912]{0,1:T(8,128)(2,1)} async-done(((bf16[1152,864]{0,1:T(8,128)(2,1)}), bf16[1152,6912]{0,1:T(8,128)(2,1)}) %all-gather.18.cloned.1.call-update) | async-done | bytes 15925264 | tf_op jit(solution)/shard_map/all_gather | solution.py:91
  304.9 12.7 %multiply_convert_fusion.1 = (bf16[256,6912]{1,0:T(8,128)(2,1)}, f32[256,6912]{1,0:T(8,128)}) fusion(f32[256,6912]{1,0:T(8,128)} %fusion.84, bf16[256,1152]{1,0:T(8,128)(2,1)S(1)} %multiply_convert_fusion.4, bf16[1152,6912]{0,1:T(8,128)(2,1)} %all-gather.18.cloned.1.call-done), kind=kOutput, calls=%fused_computation.61 | convolution fusion | flops 4094558208 | bytes 34209792 | tf_op jit(solution)/shard_map/dot_general | solution.py:164
  317.6 75.5 %all-gather.20.cloned.1.call-done = bf16[6912,1152]{1,0:T(8,128)(2,1)} async-done(((bf16[864,1152]{1,0:T(8,128)(2,1)}), bf16[6912,1152]{1,0:T(8,128)(2,1)}) %all-gather.20.cloned.1.call-update) | async-done | bytes 15925264 | tf_op jit(solution)/shard_map/all_gather | solution.py:92
  393.1 10.5 multiply_reduce_fusion.5
  405.2 16.0 %multiply_convert_fusion = (bf16[256,6912]{1,0:T(8,128)(2,1)}, bf16[256,6912]{1,0:T(8,128)(2,1)}) fusion(f32[256,6912]{1,0:T(8,128)} %fusion.84, f32[256,6912]{1,0:T(8,128)} %get-tuple-element.378, bf16[256,1152]{1,0:T(8,128)(2,1)S(1)} %get-tuple-element.359, bf16[6912,1152]{1,0:T(8,128)(2,1)} %all-gather.20.cloned.1.call-done), kind=kOutput, calls=%fused_computation.60 | convolution fusion | flops 4119330816 | bytes 37748736 | tf_op jit(solution)/shard_map/dot_general | solution.py:45
  421.3 10.5 fusion.85
  431.9 9.5 multiply_reduce_fusion
  448.4 7.5 while.39
  465.1 47.4 %reduce-scatter.8.cloned.1.call-done = bf16[256,512]{1,0:T(8,128)(2,1)} async-done(((bf16[2048,512]{1,0:T(8,128)(2,1)}), bf16[256,512]{1,0:T(8,128)(2,1)}) %reduce-scatter.8.cloned.1.call-update) | async-done | bytes 262160 | tf_op jit(solution)/shard_map/reduce_scatter | solution.py:219
  517.1 10.9 convolution_convert_fusion.2
  528.1 11.0 convolution_convert_fusion.1
  540.1 10.9 convolution_convert_fusion
  551.2 7.5 reduce-scatter.10.cloned.1.call-done
  558.7 45.7 %reduce-scatter.14.cloned.1.call-done = bf16[128,1152]{1,0:T(8,128)(2,1)} async-done(((bf16[1024,1152]{1,0:T(8,128)(2,1)}), bf16[128,1152]{1,0:T(8,128)(2,1)}) %reduce-scatter.14.cloned.1.call-update) | async-done | bytes 294928 | tf_op jit(solution)/shard_map/reduce_scatter | solution.py:258
  604.4 40.4 %reduce-scatter.12.cloned.1.call-done = bf16[144,512]{1,0:T(8,128)(2,1)} async-done(((bf16[1152,512]{1,0:T(8,128)(2,1)}), bf16[144,512]{1,0:T(8,128)(2,1)}) %reduce-scatter.12.cloned.1.call-update) | async-done | bytes 147472 | tf_op jit(solution)/shard_map/reduce_scatter | solution.py:255
  644.8 116.4 %reduce-scatter.16.cloned.1.call-done = bf16[1152,864]{0,1:T(8,128)(2,1)} async-done(((bf16[1152,6912]{0,1:T(8,128)(2,1)}), bf16[1152,864]{0,1:T(8,128)(2,1)}) %reduce-scatter.16.cloned.1.call-update) | async-done | bytes 1990672 | tf_op jit(solution)/shard_map/reduce_scatter | solution.py:261
  761.2 117.0 %reduce-scatter.18.cloned.1.call-done = bf16[1152,864]{0,1:T(8,128)(2,1)} async-done(((bf16[1152,6912]{0,1:T(8,128)(2,1)}), bf16[1152,864]{0,1:T(8,128)(2,1)}) %reduce-scatter.18.cloned.1.call-update) | async-done | bytes 1990672 | tf_op jit(solution)/shard_map/reduce_scatter | solution.py:264
  878.2 116.3 %reduce-scatter.20.cloned.1.call-done = bf16[864,1152]{1,0:T(8,128)(2,1)} async-done(((bf16[6912,1152]{1,0:T(8,128)(2,1)}), bf16[864,1152]{1,0:T(8,128)(2,1)}) %reduce-scatter.20.cloned.1.call-update) | async-done | bytes 1990672 | tf_op jit(solution)/shard_map/reduce_scatter | solution.py:267
  997.6 2.9 fusion.62
  1000.6 24.3 %all-reduce.6 = (bf16[1152]{0:T(1024)(128)(2,1)S(1)}, bf16[1152]{0:T(1024)(128)(2,1)S(1)}, bf16[1152]{0:T(1024)(128)(2,1)S(1)}, bf16[1152]{0:T(1024)(128)(2,1)S(...) all-reduce(bf16[1152]{0:T(1024)(128)(2,1)S(1)} %get-tuple-element.2, ...), channel_id=9, replica_groups=mesh['dp'=4,'seq'=8] {'seq'}, use_global_device_ids=true, to_apply=%region_35.36.clone | all-reduce | flops 5120 | bytes 20480
  1025.3 12.4 all-reduce.7
  1042.3 193.6 %all-reduce.11.cloned.1.call-done = (bf16[144,1024]{1,0:T(8,128)(2,1)}, bf16[144,512]{1,0:T(8,128)(2,1)}, bf16[128,1152]{1,0:T(8,128)(2,1)}, bf16[1152,864]{0,1:...) async-done(((bf16[144,1024]{1,0:T(8,128)(2,1)}, bf16[144,512]{1,0:T(8,128)(2,1)}, bf16[128,1152]{1,0:T(8,128)(2,1)}, bf16[1152,864]{0,1:T(8,128)(2,1)}, ...) | async-done | bytes 6709264 | tf_op jit(solution)/shard_map/psum | solution.py:290
  (243 shorter events, 71.2 us)
Async XLA Ops:
  7.2 32.4 %copy-start.43 = (f32[256]{0:T(256)S(1)}, f32[256]{0:T(256)}, u32[]{:S(2)}) copy-start(f32[256]{0:T(256)} %param.36) | copy-start | bytes 3076
  7.2 29.5 %all-gather.8.cloned.1.call-start = ((), (), s32[]{:S(2)}) async-start(), calls=%async_computation.7 | async-start | bytes 1327104 | tf_op jit(solution)/shard_map/all_gather | solution.py:88
  7.9 59.7 %all-gather.12.cloned.1.call-start = ((), (), s32[]{:S(2)}) async-start(), calls=%async_computation.9 | async-start | bytes 2654208 | tf_op jit(solution)/shard_map/all_gather | solution.py:87
  8.7 89.4 %all-gather.10.cloned.1.call-start = ((), (), s32[]{:S(2)}) async-start(), calls=%async_computation.8 | async-start | bytes 2359296 | tf_op jit(solution)/shard_map/all_gather | solution.py:105
  9.4 30.2 %copy-start.45 = (f32[1,256]{1,0:T(1,128)}, f32[1,256]{1,0:T(1,128)S(1)}, u32[]{:S(2)}) copy-start(f32[1,256]{1,0:T(1,128)S(1)} %convert_element_type.195) | copy-start | bytes 3076
  9.4 32.1 %copy-start.47 = (f32[128]{0:T(128)}, f32[128]{0:T(128)S(1)}, u32[]{:S(2)}) copy-start(f32[128]{0:T(128)S(1)} %negate_power_fusion) | copy-start | bytes 1540
  10.7 60.0 %copy-start.38 = (f32[256]{0:T(256)}, f32[256]{0:T(256)S(1)}, u32[]{:S(2)}) copy-start(f32[256]{0:T(256)S(1)} %add_rsqrt_fusion.5) | copy-start | bytes 3076
  42.2 86.6 %all-gather.14.cloned.1.call-start = ((), (), s32[]{:S(2)}) async-start(), calls=%async_computation.10 | async-start | bytes 2654208 | tf_op jit(solution)/shard_map/all_gather | solution.py:89
  42.8 174.1 %all-gather.16.cloned.1.call-start = ((), (), s32[]{:S(2)}) async-start(), calls=%async_computation.11 | async-start | bytes 17915904 | tf_op jit(solution)/shard_map/all_gather | solution.py:90
  43.4 261.5 %all-gather.18.cloned.1.call-start = ((), (), s32[]{:S(2)}) async-start(), calls=%async_computation.12 | async-start | bytes 17915904 | tf_op jit(solution)/shard_map/all_gather | solution.py:91
  44.0 349.1 %all-gather.20.cloned.1.call-start = ((), (), s32[]{:S(2)}) async-start(), calls=%async_computation.13 | async-start | bytes 17915904 | tf_op jit(solution)/shard_map/all_gather | solution.py:92
  44.7 467.8 %reduce-scatter.8.cloned.1.call-start = ((), (), s32[]{:S(2)}) async-start(), calls=%async_computation.14 | async-start | bytes 2359296 | tf_op jit(solution)/shard_map/reduce_scatter | solution.py:219
  104.8 26.7 %copy-start.16 = (bf16[256,1024]{1,0:T(8,128)(2,1)}, bf16[256,1024]{1,0:T(8,128)(2,1)S(1)}, u32[]{:S(2)}) copy-start(bf16[256,1024]{1,0:T(8,128)(2,1)S(1)} %convert_element_type.202) | copy-start | bytes 1572868
  104.8 26.7 %copy-start.33 = (f32[1152]{0:T(1024)S(1)}, f32[1152]{0:T(1024)}, u32[]{:S(2)}) copy-start(f32[1152]{0:T(1024)} %param.32) | copy-start | bytes 13828
  132.3 172.5 %copy-start.14 = (bf16[256,1152]{1,0:T(8,128)(2,1)}, bf16[256,1152]{1,0:T(8,128)(2,1)S(1)}, u32[]{:S(2)}) copy-start(bf16[256,1152]{1,0:T(8,128)(2,1)S(1)} %multiply_convert_fusion.4) | copy-start | bytes 1769476
  393.1 10.5 copy-start.8
  393.1 10.5 copy-start.36
  405.2 16.1 %copy-start.21 = (bf16[256,1152]{1,0:T(8,128)(2,1)}, bf16[256,1152]{1,0:T(8,128)(2,1)S(1)}, u32[]{:S(2)}) copy-start(bf16[256,1152]{1,0:T(8,128)(2,1)S(1)} %get-tuple-element.359) | copy-start | bytes 1769476
  421.3 10.6 copy-start.18
  456.0 102.7 %reduce-scatter.10.cloned.1.call-start = ((), (), s32[]{:S(2)}) async-start(), calls=%async_computation.15 | async-start | bytes 2654208 | tf_op jit(solution)/shard_map/reduce_scatter | solution.py:252
  462.6 141.8 %reduce-scatter.14.cloned.1.call-start = ((), (), s32[]{:S(2)}) async-start(), calls=%async_computation.17 | async-start | bytes 2654208 | tf_op jit(solution)/shard_map/reduce_scatter | solution.py:258
  465.0 49.4 %copy-start.46 = (f32[1,256]{1,0:T(1,128)S(1)}, f32[1,256]{1,0:T(1,128)}, u32[]{:S(2)}) copy-start(f32[1,256]{1,0:T(1,128)} %copy-done.45) | copy-start | bytes 3076
  465.0 49.4 %copy-start.48 = (f32[128]{0:T(128)S(1)}, f32[128]{0:T(128)}, u32[]{:S(2)}) copy-start(f32[128]{0:T(128)} %copy-done.47) | copy-start | bytes 1540
  465.0 50.0 %copy-start.20 = (f32[256,512]{1,0:T(8,128)S(1)}, f32[256,512]{1,0:T(8,128)}, u32[]{:S(2)}) copy-start(f32[256,512]{1,0:T(8,128)} %copy-done.19) | copy-start | bytes 1572868
  465.0 50.0 %copy-start.41 = (f32[256]{0:T(256)S(1)}, f32[256]{0:T(256)}, u32[]{:S(2)}) copy-start(f32[256]{0:T(256)} %copy-done.40) | copy-start | bytes 3076
  465.0 50.0 %copy-start.44 = (f32[256]{0:T(256)S(1)}, f32[256]{0:T(256)}, u32[]{:S(2)}) copy-start(f32[256]{0:T(256)} %param.36) | copy-start | bytes 3076
  465.0 179.8 %reduce-scatter.12.cloned.1.call-start = ((), (), s32[]{:S(2)}) async-start(), calls=%async_computation.16 | async-start | bytes 1327104 | tf_op jit(solution)/shard_map/reduce_scatter | solution.py:255
  517.0 244.2 %reduce-scatter.16.cloned.1.call-start = ((), (), s32[]{:S(2)}) async-start(), calls=%async_computation.18 | async-start | bytes 17915904 | tf_op jit(solution)/shard_map/reduce_scatter | solution.py:261
  528.0 350.1 %reduce-scatter.18.cloned.1.call-start = ((), (), s32[]{:S(2)}) async-start(), calls=%async_computation.19 | async-start | bytes 17915904 | tf_op jit(solution)/shard_map/reduce_scatter | solution.py:264
  539.1 455.4 %reduce-scatter.20.cloned.1.call-start = ((), (), s32[]{:S(2)}) async-start(), calls=%async_computation.20 | async-start | bytes 17915904 | tf_op jit(solution)/shard_map/reduce_scatter | solution.py:267
  551.0 684.9 %all-reduce.11.cloned.1.call-start = ((), (), s32[]{:S(2)}) async-start(), calls=%async_computation.21 | async-start | bytes 13418496 | tf_op jit(solution)/shard_map/psum | solution.py:290
  997.6 43.4 %copy-start.7 = (f32[256,1152]{1,0:T(8,128)S(1)}, f32[256,1152]{1,0:T(8,128)}, u32[]{:S(2)}) copy-start(f32[256,1152]{1,0:T(8,128)} %copy-done.6) | copy-start | bytes 3538948
  (33 other events, 62.8 us)
Sparse Core Ops, SparseCore 0:
  9.9 26.7 all-gather.7
  38.6 28.9 all-gather.11
  70.1 27.8 all-gather.9
  99.8 29.0 all-gather.13
  130.6 86.2 all-gather.15
  218.6 86.2 all-gather.17
  306.8 86.2 all-gather.19
  456.1 56.3 reduce-scatter.7
  516.2 42.4 reduce-scatter.9
  561.9 42.4 reduce-scatter.13
  608.0 36.7 reduce-scatter.11
  648.3 112.8 reduce-scatter.15
  765.3 112.8 reduce-scatter.17
  881.7 112.8 reduce-scatter.19
  997.5 238.4 all-reduce.10
where the time goes:
time: 1260 us; the launch traced here: 1250 us
  waiting for transfers between devices  1020 us (81%)
  matrix products  134 us (11%)
  blocking collectives  36.7 us (3%)
  other arithmetic  28.9 us (2%)
  local copies, waits for them, and re-layouts  20.1 us (2%)
  between operations  16.2 us (1%)
    psum x1, waiting for transfers between devices, on_device(): lax.psum(grad_queryw.astype(jnp.bfloat16), 'dp').astype(jnp.float32)  194 us
    reduce_scatter x1, waiting for transfers between devices, on_device(): lax.psum_scatter(grad_upw.astype(jnp.bfloat16), 'seq', scatter_dimension=...  117 us
    reduce_scatter x1, waiting for transfers between devices, on_device(): lax.psum_scatter(grad_gate.astype(jnp.bfloat16), 'seq', scatter_dimension...  116 us
    reduce_scatter x1, waiting for transfers between devices, on_device(): lax.psum_scatter(grad_down.astype(jnp.bfloat16), 'seq', scatter_dimension...  116 us
    all_gather x1, waiting for transfers between devices, on_device(): lax.all_gather(w_gate, 'seq', axis=1, tiled=True)  84.5 us
    all_gather x1, waiting for transfers between devices, on_device(): lax.all_gather(w_down, 'seq', axis=0, tiled=True)  75.5 us
    all_gather x1, waiting for transfers between devices, on_device(): lax.all_gather(w_up, 'seq', axis=1, tiled=True)  71.8 us
    reduce_scatter x1, waiting for transfers between devices, on_device(): lax.psum_scatter(d_kv_whole.astype(jnp.bfloat16), 'seq', scatter_dimensio...  47.4 us
  transfers between devices with their start and end apart: 15, of which 15 were waited for; matrix products, arithmetic and copies ran while one was open for 8% of the time, Pallas kernels for 0%

commit v1 on v0

v1 whole, which is shorter than its diff:
```python
import functools

import jax
import jax.numpy as jnp
from jax import lax
from jax.experimental import pallas as pl
from jax.experimental.pallas import tpu as pltpu
from jax.sharding import PartitionSpec as P

HEADS = 4
HEAD = 256
BLOCK = 256
LANES = 128
FEED_VMEM = 16 << 20

norm_eps = 1e-06
rope_base = 1000000.0
score_scale = HEAD**-0.5
bf16 = jnp.bfloat16
f32 = jnp.float32
BRIEF = pl.CostEstimate(flops=1, bytes_accessed=1, transcendentals=0)


def rms_forward(values):
    factor = lax.rsqrt(jnp.mean(values * values, axis=-1, keepdims=True) + norm_eps)
    return (values * factor, factor)


def rms_backward(upstream, normed, factor):
    return factor * (upstream - normed * jnp.mean(upstream * normed, axis=-1, keepdims=True))


def rope_angles(positions, width):
    half_width = width // 2
    inverse_freq = rope_base ** (-(jnp.arange(half_width).astype(f32) * 2.0 / width))
    return positions.astype(f32)[:, None] * inverse_freq[None, :]


def rotate(values, cosine, sine):
    half_width = values.shape[-1] // 2
    first = values[..., :half_width]
    second = values[..., half_width:]
    return jnp.concatenate(
        [first * cosine - second * sine, second * cosine + first * sine], axis=-1
    )


def dot(left, right):
    return jnp.dot(left, right, preferred_element_type=f32)


def dot_rows(left, right):
    return lax.dot_general(left, right, (((1,), (1,)), ((), ())), preferred_element_type=f32)


def dot_cols(left, right):
    return lax.dot_general(left, right, (((0,), (0,)), ((), ())), preferred_element_type=f32)


def visible_mask(block_id, first_row, pos_ref):
    shape = (BLOCK, BLOCK)
    query = first_row + lax.broadcasted_iota(jnp.int32, shape, 0)
    key = block_id * BLOCK + lax.broadcasted_iota(jnp.int32, shape, 1)
    return (key <= query) & (key >= query - pos_ref[...])


def attend_kernel(
    n_blocks,
    columns,
    order_ref,
    q_pre_ref,
    cos_ref,
    sin_ref,
    gain_ref,
    pos_ref,
    *refs,
):
    kv_refs, (att_ref, att_low_ref, inv_ref, q_ref, total_ref) = refs[:-5], refs[-5:]
    slot = order_ref.shape[0] - columns
    first_row = order_ref[n_blocks]
    first_key = order_ref[n_blocks + 1]
    cosine, sine = cos_ref[...], sin_ref[...]
    for h in range(HEADS):
        cols = pl.ds(h * HEAD, HEAD)
        normed, _ = rms_forward(q_pre_ref[:, cols])
        q_ref[:, cols] = rotate(normed * gain_ref[...], cosine, sine).astype(bf16)
    att_ref[...] = jnp.zeros_like(att_ref)
    total_ref[...] = jnp.zeros_like(total_ref)

    def step(kv_ref, base, k, _):
        block_id = order_ref[base + k]
        live = (block_id * BLOCK <= first_row) & ((block_id + 1) * BLOCK > first_key)

        @pl.when(live)
        def _():
            rows = pl.ds(pl.multiple_of(k * BLOCK, BLOCK), BLOCK)
            keys = kv_ref[rows, :HEAD]
            vals = kv_ref[rows, HEAD:]
            visible = visible_mask(block_id, first_row, pos_ref)
            for h in range(HEADS):
                cols = pl.ds(h * HEAD, HEAD)
                scores = dot_rows(q_ref[:, cols], keys) * score_scale
                weight = jnp.where(visible, jnp.exp(scores), 0.0)
                total_ref[:, pl.ds(h * LANES, LANES)] += weight[:, :LANES] + weight[:, LANES:]
                att_ref[:, cols] += dot(weight.astype(bf16), vals)

        return 0

    each = n_blocks // len(kv_refs)
    for i, kv_ref in enumerate(kv_refs):
        lax.fori_loop(0, each, functools.partial(step, kv_ref, i * each), 0)
    for h in range(HEADS):
        cols = pl.ds(h * HEAD, HEAD)
        lanes = pl.ds(h * LANES, LANES)
        inverse = 1.0 / jnp.sum(total_ref[:, lanes], axis=-1, keepdims=True)
        inv_ref[:, lanes] = jnp.broadcast_to(inverse, (BLOCK, LANES))
        att_ref[:, cols] = att_ref[:, cols] * inverse
    size = HEADS * HEAD // columns
    for k in range(columns):
        source = pl.ds(pl.multiple_of(order_ref[slot + k] * size, size), size)
        att_low_ref[:, pl.ds(k * size, size)] = att_ref[:, source].astype(bf16)


def attend(columns, order, q_pre, cosine, sine, gain, pos, *kv):
    rows = q_pre.shape[0]
    n_blocks = sum(v.shape[0] for v in kv) // BLOCK
    whole = pl.BlockSpec(memory_space=pltpu.VMEM)
    return pl.pallas_call(
        functools.partial(attend_kernel, n_blocks, columns),
        out_shape=(
            jax.ShapeDtypeStruct((rows, HEADS * HEAD), f32),
            jax.ShapeDtypeStruct((rows, HEADS * HEAD), bf16),
            jax.ShapeDtypeStruct((rows, HEADS * LANES), f32),
            jax.ShapeDtypeStruct((rows, HEADS * HEAD), bf16),
        ),
        in_specs=[pl.BlockSpec(memory_space=pltpu.SMEM)] + [whole] * (5 + len(kv)),
        out_specs=(whole,) * 4,
        scratch_shapes=[pltpu.VMEM((rows, HEADS * LANES), f32)],
        cost_estimate=BRIEF,
        compiler_params=pltpu.CompilerParams(vmem_limit_bytes=12 << 20),
        name="attend",
    )(order, q_pre, cosine, sine, gain, pos, *kv)


def attend_back_kernel(
    n_blocks,
    columns,
    order_ref,
    q_pre_ref,
    cos_ref,
    sin_ref,
    gain_ref,
    pos_ref,
    q_ref,
    att_ref,
    inv_ref,
    d_moved_ref,
    *refs,
):
    groups = (len(refs) - 5) // 2
    kv_refs, d_q_pre_ref, d_kv_refs = refs[:groups], refs[groups], refs[groups + 1 : -4]
    d_gain_ref, d_q_ref, row_dot_ref, d_att_ref = refs[-4:]
    slot = order_ref.shape[0] - columns
    size = HEADS * HEAD // columns
    for k in range(columns):
        target = pl.ds(pl.multiple_of(order_ref[slot + k] * size, size), size)
        d_att_ref[:, target] = d_moved_ref[:, pl.ds(k * size, size)]
    first_row = order_ref[n_blocks]
    first_key = order_ref[n_blocks + 1]
    for h in range(HEADS):
        cols = pl.ds(h * HEAD, HEAD)
        product = d_att_ref[:, cols].astype(f32) * att_ref[:, cols]
        row_dot_ref[:, pl.ds(h * LANES, LANES)] = jnp.broadcast_to(
            jnp.sum(product, axis=-1, keepdims=True), (BLOCK, LANES)
        )
    d_q_ref[...] = jnp.zeros_like(d_q_ref)

    def step(kv_ref, d_kv_ref, base, k, _):
        block_id = order_ref[base + k]
        live = (block_id * BLOCK <= first_row) & ((block_id + 1) * BLOCK > first_key)
        rows = pl.ds(pl.multiple_of(k * BLOCK, BLOCK), BLOCK)

        @pl.when(live)
        def _():
            keys = kv_ref[rows, :HEAD]
            vals = kv_ref[rows, HEAD:]
            visible = visible_mask(block_id, first_row, pos_ref)
            d_keys = jnp.zeros((BLOCK, HEAD), f32)
            d_vals = jnp.zeros((BLOCK, HEAD), f32)
            for h in range(HEADS):
                cols = pl.ds(h * HEAD, HEAD)
                query = q_ref[:, cols]
                d_att = d_att_ref[:, cols]
                inverse = inv_ref[:, pl.ds(h * LANES, 1)]
                row_dot = row_dot_ref[:, pl.ds(h * LANES, 1)]
                scores = dot_rows(query, keys) * score_scale
                prob = jnp.where(visible, jnp.exp(scores), 0.0) * inverse
                d_prob = dot_rows(d_att, vals)
                d_scores = (prob * (d_prob - row_dot)).astype(bf16)
                d_q_ref[:, cols] += dot(d_scores, keys)
                d_keys += dot_cols(d_scores, query)
                d_vals += dot_cols(prob.astype(bf16), d_att)
            d_kv_ref[rows, :HEAD] = (d_keys * score_scale).astype(bf16)
            d_kv_ref[rows, HEAD:] = d_vals.astype(bf16)

        @pl.when(jnp.logical_not(live))
        def _():
            d_kv_ref[rows, :] = jnp.zeros((BLOCK, 2 * HEAD), bf16)

        return 0

    each = n_blocks // groups
    for i in range(groups):
        walk = functools.partial(step, kv_refs[i], d_kv_refs[i], i * each)
        lax.fori_loop(0, each, walk, 0)
    cosine, sine = cos_ref[...], sin_ref[...]
    d_gain = jnp.zeros((1, HEAD), f32)
    for h in range(HEADS):
        cols = pl.ds(h * HEAD, HEAD)
        normed, factor = rms_forward(q_pre_ref[:, cols])
        d_normed = rotate(d_q_ref[:, cols] * score_scale, cosine, -sine)
        d_gain += jnp.sum(d_normed * normed, axis=0, keepdims=True)
        d_q_pre_ref[:, cols] = rms_backward(d_normed * gain_ref[...], normed, factor).astype(bf16)
    d_gain_ref[...] = d_gain


def attend_back(columns, order, q_pre, cosine, sine, gain, pos, *kv, saved, d_att):
    rows = q_pre.shape[0]
    n_blocks = sum(v.shape[0] for v in kv) // BLOCK
    whole = pl.BlockSpec(memory_space=pltpu.VMEM)
    return pl.pallas_call(
        functools.partial(attend_back_kernel, n_blocks, columns),
        out_shape=(
            jax.ShapeDtypeStruct((rows, HEADS * HEAD), bf16),
            *[jax.ShapeDtypeStruct(v.shape, bf16) for v in kv],
            jax.ShapeDtypeStruct((1, HEAD), f32),
        ),
        in_specs=[pl.BlockSpec(memory_space=pltpu.SMEM)] + [whole] * (9 + len(kv)),
        out_specs=(whole,) * (2 + len(kv)),
        scratch_shapes=[
            pltpu.VMEM((rows, HEADS * HEAD), f32),
            pltpu.VMEM((rows, HEADS * LANES), f32),
            pltpu.VMEM((rows, HEADS * HEAD), bf16),
        ],
        cost_estimate=BRIEF,
        compiler_params=pltpu.CompilerParams(vmem_limit_bytes=16 << 20),
        name="attend_back",
    )(order, q_pre, cosine, sine, gain, pos, *saved, d_att, *kv)


def gelu_parts(gate):
    c = (2.0 / jnp.pi) ** 0.5
    square = gate * gate
    t = jnp.tanh(gate * (c + (c * 0.044715) * square))
    half = 0.5 + 0.5 * t
    act = gate * half
    slope = half + act * (1.0 - t) * (c + (3 * c * 0.044715) * square)
    return act, slope


def feed_kernel(groups, b_ref, *refs):
    weights, (part_ref, hidden_ref, act_ref, slope_ref) = refs[:-4], refs[-4:]
    part = 0.0
    for i in range(groups):
        gate_ref, up_ref, down_ref = weights[3 * i : 3 * i + 3]
        gate = dot_rows(b_ref[...], gate_ref[...])
        up = dot_rows(b_ref[...], up_ref[...])
        act, slope = gelu_parts(gate)
        hidden_ref[i] = (act * up).astype(bf16)
        act_ref[i] = act.astype(bf16)
        slope_ref[i] = (up * slope).astype(bf16)
        part = part + dot(hidden_ref[i], down_ref[...])
    part_ref[...] = part.astype(part_ref.dtype)


def feed(b, weights, dtype):
    rows, width = b.shape
    groups, ff = len(weights) // 3, weights[0].shape[0]
    whole = pl.BlockSpec(memory_space=pltpu.VMEM)
    return pl.pallas_call(
        functools.partial(feed_kernel, groups),
        out_shape=(
            jax.ShapeDtypeStruct((rows, width), dtype),
            *[jax.ShapeDtypeStruct((groups, rows, ff), bf16)] * 3,
        ),
        in_specs=[whole] * (1 + len(weights)),
        out_specs=(whole,) * 4,
        cost_estimate=BRIEF,
        compiler_params=pltpu.CompilerParams(vmem_limit_bytes=FEED_VMEM),
        name="feed",
    )(b, *weights)


def feed_back_kernel(groups, d_ref, act_ref, slope_ref, *refs):
    weights, (part_ref, d_gate_ref, d_up_ref) = refs[:-3], refs[-3:]
    part = 0.0
    for i in range(groups):
        gate_ref, up_ref, down_ref = weights[3 * i : 3 * i + 3]
        d_hidden = dot_rows(d_ref[...], down_ref[...])
        d_gate_ref[i] = (d_hidden * slope_ref[i].astype(f32)).astype(bf16)
        d_up_ref[i] = (d_hidden * act_ref[i].astype(f32)).astype(bf16)
        part = part + dot(d_gate_ref[i], gate_ref[...]) + dot(d_up_ref[i], up_ref[...])
    part_ref[...] = part.astype(part_ref.dtype)


def feed_back(d, act, slope, weights, dtype):
    rows, width = d.shape
    groups, ff = len(weights) // 3, weights[0].shape[0]
    whole = pl.BlockSpec(memory_space=pltpu.VMEM)
    return pl.pallas_call(
        functools.partial(feed_back_kernel, groups),
        out_shape=(
            jax.ShapeDtypeStruct((rows, width), dtype),
            *[jax.ShapeDtypeStruct((groups, rows, ff), bf16)] * 2,
        ),
        in_specs=[whole] * (3 + len(weights)),
        out_specs=(whole,) * 3,
        cost_estimate=BRIEF,
        compiler_params=pltpu.CompilerParams(vmem_limit_bytes=FEED_VMEM),
        name="feed_back",
    )(d, act, slope, *weights)


def weight_grad_kernel(index, sizes, count, *refs):
    lefts, rights, rest = refs[:count], refs[count : 2 * count], refs[2 * count :]
    extra, outs = rest[: -len(sizes)], rest[-len(sizes) :]
    left = jnp.concatenate([v[index] for v in lefts], axis=0)
    right = jnp.concatenate([v[...] for v in rights], axis=0)
    total = dot_cols(left, right)
    if extra:
        total = total + extra[0][...].astype(f32)
    begin = 0
    for size, out in zip(sizes, outs):
        out[...] = total[begin : begin + size].astype(bf16)
        begin += size


def weight_grad(index, sizes, lefts, rights, *extra):
    rows, width = rights[0].shape
    whole = pl.BlockSpec(memory_space=pltpu.VMEM)
    return pl.pallas_call(
        functools.partial(weight_grad_kernel, index, sizes, len(lefts)),
        out_shape=tuple(jax.ShapeDtypeStruct((size, width), bf16) for size in sizes),
        in_specs=[whole] * (2 * len(lefts) + len(extra)),
        out_specs=(whole,) * len(sizes),
        cost_estimate=BRIEF,
        compiler_params=pltpu.CompilerParams(vmem_limit_bytes=FEED_VMEM),
        name="weight_grad",
    )(*lefts, *rights, *extra)


def add(*terms):
    return functools.reduce(jnp.add, [t.astype(f32) for t in terms])


fence = lax.optimization_barrier


class Plain:
    def __init__(self, n):
        self.n = n
        self.rank = lax.axis_index("seq")

    def order(self):
        return jnp.arange(self.n, dtype=jnp.int32)

    def slots(self):
        return jnp.zeros(1, jnp.int32)

    def send(self, shard):
        return [shard]

    def paired(self, shards):
        return [lax.all_gather(shards[0], "seq", axis=0, tiled=True)]

    def columns(self, value):
        return [value]

    def restored(self, parts):
        return parts[0]

    def pair(self, shard):
        return [shard]

    def tokens(self, shard):
        whole = lax.all_gather(shard, "seq", axis=0, tiled=True)
        return jnp.split(whole, self.n, axis=0)

    def part_send(self, parts, at):
        return ()

    def parts_sum(self, parts, moved):
        return self.scatter(all_of([p.astype(bf16) for p in parts]))

    def across(self, value):
        return ()

    def group_send(self, partial, moved):
        return (partial[0],)

    def group_sum(self, sent):
        return self.scatter(sent[0])

    def scatter(self, partial):
        return lax.psum_scatter(
            partial.astype(bf16), "seq", scatter_dimension=0, tiled=True
        ).astype(f32)

    def projection(self, left, right, gains):
        grad = dot_cols(left, right).reshape(self.n, -1, right.shape[1])
        gains = jnp.pad(gains, ((0, 0), (0, right.shape[1] - gains.shape[1])))
        packed = [grad, jnp.pad(gains[:, None], ((0, 0), (0, 15), (0, 0)))]
        return [jnp.concatenate(packed, axis=1).reshape(-1, right.shape[1])]

    def line(self):
        return PlainLine()


class Cube(Plain):
    chips = (0, 2, 4, 6)
    ranks = (0, 2, 4, 6, 1, 3, 5, 7)

    def hop(self, value, bit):
        return lax.ppermute(value, "seq", [(i, i ^ bit) for i in range(8)])

    def order(self):
        return self.rank ^ jnp.array(self.ranks, dtype=jnp.int32)

    def slots(self):
        return self.order()

    def send(self, shard):
        return [shard] + [self.hop(shard, bit) for bit in self.chips[1:]]

    def paired(self, shards):
        group = all_of(shards)
        return [group, self.hop(group, 1)]

    def tokens(self, shard):
        return self.send(shard)

    def part_send(self, parts, at):
        return (self.hop(parts[at].astype(bf16), self.chips[at]),)

    def parts_sum(self, parts, moved):
        return add(parts[0], *moved)

    def across(self, value):
        return (self.hop(value, 1),)

    def group_send(self, partial, moved):
        mine = add(partial[0], *moved)
        parts = jnp.split(mine, 4, axis=0)
        return (parts[0], *[self.part_send(parts, at)[0] for at in (1, 2, 3)])

    def group_sum(self, sent):
        return add(*sent)

    def select(self, size, stride):
        shape = (self.n * size, self.n * stride)
        col = lax.broadcasted_iota(jnp.int32, shape, 1)
        block, at = col // stride, col % stride
        source = self.rank ^ ((2 * block) % 8 + block // 4)
        row = lax.broadcasted_iota(jnp.int32, shape, 0)
        return ((row == source * size + at) & (at < size)).astype(bf16)

    def columns(self, value):
        moved = dot(value, self.select(value.shape[1] // self.n, value.shape[1] // self.n))
        return jnp.split(moved.astype(value.dtype), 2, axis=1)

    def restored(self, parts):
        value = jnp.concatenate(parts, axis=1)
        pick = self.select(value.shape[1] // self.n, value.shape[1] // self.n).astype(f32)
        return lax.dot_general(
            value, pick, (((1,), (1,)), ((), ())), precision=lax.Precision.HIGHEST
        )

    def pair(self, shard):
        return [shard, self.hop(shard, 1)]

    def projection(self, left, right, gains):
        size = left.shape[1] // self.n
        stride = size + 16
        moved = dot(left, self.select(size, stride)).astype(bf16)
        shape = (16, self.n * stride)
        col = lax.broadcasted_iota(jnp.int32, shape, 1)
        block, at = col // stride, col % stride
        target = self.rank ^ ((2 * block) % 8 + block // 4)
        row = lax.broadcasted_iota(jnp.int32, shape, 0)
        pick = ((row == target) & (at == size)).astype(bf16)
        left = jnp.concatenate([moved, pick], axis=0)
        gains = jnp.pad(gains, ((0, 8), (0, right.shape[1] - gains.shape[1]))).astype(bf16)
        right = jnp.concatenate([right, gains], axis=0)
        half = self.n * stride // 2
        return [dot_cols(left[:, :half], right), dot_cols(left[:, half:], right)]

    def line(self):
        return CubeLine()


class PlainLine:
    def __init__(self):
        self.chunks = []

    def send(self):
        return ()

    def settle(self, got):
        pass

    def finish(self):
        return [lax.psum(c, "dp").astype(f32) for c in self.chunks]


class CubeLine(PlainLine):
    def __init__(self):
        super().__init__()
        place = lax.axis_index("dp")
        self.inner = (place == 1) | (place == 2)
        self.halves, self.totals, self.out = {}, {}, {}
        self.at = 0

    def send(self):
        tick = self.at
        mine = self.chunks[tick] if tick < len(self.chunks) else None
        back, half = self.totals.get(tick - 2), self.halves.get(tick - 1)
        got = {}
        if mine is not None and back is not None and mine.shape == back.shape:
            both = jnp.where(self.inner, back, mine)
            got["in"] = lax.ppermute(both, "dp", [(0, 1), (1, 0), (2, 3), (3, 2)])
        else:
            if back is not None:
                got["out"] = lax.ppermute(back, "dp", [(1, 0), (2, 3)])
            if mine is not None:
                got["in"] = lax.ppermute(mine, "dp", [(0, 1), (3, 2)])
        if half is not None:
            got["middle"] = lax.ppermute(half, "dp", [(1, 2), (2, 1)])
        return got

    def settle(self, got):
        tick = self.at
        self.at += 1
        if tick < len(self.chunks):
            self.halves[tick] = add(self.chunks[tick], got["in"]).astype(bf16)
        if "middle" in got:
            self.totals[tick - 1] = add(self.halves[tick - 1], got["middle"]).astype(bf16)
        if tick >= 2:
            back = got["out"] if "out" in got else got["in"]
            self.out[tick - 2] = jnp.where(self.inner, self.totals[tick - 2], back)

    def finish(self):
        while self.at < len(self.chunks) + 2:
            self.settle(fence(self.send()))
        return [self.out[i].astype(f32) for i in range(len(self.chunks))]


def all_of(values):
    return jnp.concatenate(values, axis=0)


def on_device(
    kind,
    layer_input,
    segment_ids,
    position_ids,
    w_query,
    w_keyval,
    w_out,
    w_gate,
    w_up,
    w_down,
    g_input,
    g_post_attn,
    g_pre_ffn,
    g_post_ffn,
    g_query,
    g_key,
    out_grad,
):
    n = lax.axis_size("seq")
    comm = kind(n)
    rows = layer_input.shape[1]
    width = layer_input.shape[2]
    ff = w_gate.shape[1]
    row_offset = comm.rank * rows

    x = layer_input[0].astype(f32)
    positions = position_ids[0]
    keyval_sent = comm.send(w_keyval)
    a_normed, a_factor = rms_forward(x)
    a_low = (a_normed * g_input).astype(bf16)
    a_columns = comm.columns(a_low)
    angles = rope_angles(positions, HEAD)
    cosine, sine = jnp.cos(angles), jnp.sin(angles)
    keyval_sent, a_columns, w_query = fence((keyval_sent, a_columns, w_query))
    query_sent = comm.send(w_query)
    keyval_blocks = comm.paired(keyval_sent)
    kv_pre = add(*[dot(a, w) for a, w in zip(a_columns, keyval_blocks)])
    k_hat, k_factor = rms_forward(kv_pre[:, :HEAD])
    k_low = rotate(k_hat * g_key, cosine, sine).astype(bf16)
    kv_low = jnp.concatenate([k_low, kv_pre[:, HEAD:].astype(bf16)], axis=1)
    kv_low, query_sent, w_gate, w_up, w_down = fence((kv_low, query_sent, w_gate, w_up, w_down))
    kv_sent = comm.send(kv_low)
    query_blocks = comm.paired(query_sent)
    q_pre = add(*[dot(a, w) for a, w in zip(a_columns, query_blocks)])
    kv_sent, q_pre, w_out = fence((kv_sent, q_pre, w_out))
    out_sent = comm.send(w_out)
    kv_blocks = comm.paired(kv_sent)
    weights = [comm.pair(w) for w in (w_gate.T, w_up.T, w_down)]
    weights = [w[i] for i in range(len(weights[0])) for w in weights]
    groups = len(weights) // 3
    order = jnp.concatenate(
        [comm.order(), row_offset[None], (row_offset - positions[0])[None], comm.slots()]
    ).astype(jnp.int32)
    head_args = (
        comm.slots().shape[0],
        order,
        q_pre,
        cosine,
        sine,
        g_query[None],
        positions[:, None],
        *kv_blocks,
    )
    att, att_low, inverse, q_low = attend(*head_args)
    out_sent, att_low = fence((out_sent, att_low))
    out_blocks = comm.paired(out_sent)
    att_columns = jnp.split(att_low, len(out_blocks), axis=1)
    attn = add(*[dot(v, w) for v, w in zip(att_columns, out_blocks)])
    attn_normed, attn_factor = rms_forward(attn)
    middle = x + attn_normed * g_post_attn
    b_normed, b_factor = rms_forward(middle)
    b_low = (b_normed * g_pre_ffn).astype(bf16)
    b_low, weights = fence((b_low, weights))

    b_list = comm.tokens(b_low)
    hidden, acts, slopes, parts, moved = [], [], [], [], []
    for i, b_part in enumerate(b_list):
        sent = comm.part_send(parts, i - 1) if i > 1 else ()
        kept = feed(b_part, weights, bf16 if i else f32)
        ahead = b_list[i + 1 : i + 2]
        kept, sent, ahead = fence((kept, sent, ahead))
        b_list[i + 1 : i + 2] = ahead
        moved += sent
        for values, value in zip((parts, hidden, acts, slopes), kept):
            values.append(value)
    moved += comm.part_send(parts, len(parts) - 1)
    ffn = comm.parts_sum(parts, moved)
    ffn_normed, ffn_factor = rms_forward(ffn)
    layer_out = (middle + ffn_normed * g_post_ffn).astype(bf16)

    g = out_grad[0]
    d_ffn = rms_backward(g * g_post_ffn, ffn_normed, ffn_factor).astype(bf16)
    d_ffn, ffn_normed = fence((d_ffn, ffn_normed))
    d_list = comm.tokens(d_ffn)
    gain_post_ffn = jnp.sum(g * ffn_normed, axis=0)
    d_gate, d_up, parts, moved = [], [], [], []
    line = comm.line()
    thirds = [ff // 3] * 3

    def keep(kept):
        for values, value in zip((parts, d_gate, d_up), kept):
            values.append(value)

    for i, d_part in enumerate(d_list[:-1]):
        sent = comm.part_send(parts, i - 1) if i > 1 else ()
        kept = feed_back(d_part, acts[i], slopes[i], weights, bf16 if i else f32)
        ahead = d_list[i + 1 : i + 2]
        kept, sent, ahead = fence((kept, sent, ahead))
        d_list[i + 1 : i + 2] = ahead
        moved += sent
        keep(kept)

    def grad_pair(lefts, rights):
        if groups == 1:
            return ()
        return comm.across(weight_grad(1, [ff], lefts, rights)[0])

    sent = comm.part_send(parts, len(parts) - 1)
    other = grad_pair(hidden, d_list)
    last = len(d_list) - 1
    keep(feed_back(d_list[last], acts[last], slopes[last], weights, bf16))
    other, sent, part = fence((other, sent, parts[last]))
    parts[last] = part
    moved += sent
    line.chunks += weight_grad(0, thirds, hidden, d_list, *other)

    line.chunks, parts, d_gate, d_up = fence((line.chunks, parts, d_gate, d_up))
    got = line.send()
    sent = comm.part_send(parts, last)
    other = grad_pair(d_gate, b_list)
    other_up = grad_pair(d_up, b_list)
    grads = weight_grad(0, thirds, d_gate, b_list, *other)
    got, sent, grads, other_up, d_up = fence((got, sent, list(grads), other_up, d_up))
    line.settle(got)
    line.chunks += grads
    moved += sent

    got = line.send()
    d_b = comm.parts_sum(parts, moved)
    gain_pre_ffn = jnp.sum(d_b * b_normed, axis=0)
    d_middle = g + rms_backward(d_b * g_pre_ffn, b_normed, b_factor)
    gain_post_attn = jnp.sum(d_middle * attn_normed, axis=0)
    d_attn = rms_backward(d_middle * g_post_attn, attn_normed, attn_factor).astype(bf16)
    d_att = jnp.concatenate([dot_rows(d_attn, w).astype(bf16) for w in out_blocks], axis=1)
    d_heads = attend_back(*head_args, saved=(q_low, att, inverse), d_att=d_att)
    got, d_heads, d_attn, d_up = fence((got, d_heads, d_attn, d_up))
    d_q_pre, *d_kv_blocks, gain_query = d_heads
    line.settle(got)

    got = line.send()
    d_kv_moved = comm.across(d_kv_blocks[-1])
    grads = weight_grad(0, thirds, d_up, b_list, *other_up)
    grad_out = [dot_cols(v, d_attn) for v in att_columns]
    d_kv_sent = comm.group_send(d_kv_blocks, d_kv_moved)
    out_moved = comm.across(grad_out[-1].astype(bf16))
    got, grads, d_kv_sent, grad_out, out_moved = fence(
        (got, list(grads), d_kv_sent, grad_out, out_moved)
    )
    line.settle(got)
    line.chunks += grads

    got = line.send()
    d_kv = comm.group_sum(d_kv_sent)
    out_sent = comm.group_send(grad_out, out_moved)
    d_k_normed = rotate(d_kv[:, :HEAD], cosine, -sine)
    gain_key = jnp.sum(d_k_normed * k_hat, axis=0)
    d_k_pre = rms_backward(d_k_normed * g_key, k_hat, k_factor)
    d_kv_pre = jnp.concatenate([d_k_pre, d_kv[:, HEAD:]], axis=1).astype(bf16)
    d_a = comm.restored(
        [
            dot_rows(d_q_pre, query) + dot_rows(d_kv_pre, keyval)
            for query, keyval in zip(query_blocks, keyval_blocks)
        ]
    )
    gain_input = jnp.sum(d_a * a_normed, axis=0)
    gains = [gain_input, gain_post_attn, gain_pre_ffn, gain_post_ffn, gain_query[0], gain_key]
    got, out_sent, d_a, gains, d_kv_pre = fence((got, out_sent, d_a, gains, d_kv_pre))
    line.settle(got)

    got = line.send()
    packed = jnp.concatenate([v.reshape(n, -1) for v in gains], axis=1)
    d_qkv = jnp.concatenate([d_q_pre, d_kv_pre], axis=1)
    grad_qkv = comm.projection(a_low, d_qkv, packed)
    qkv_moved = comm.across(grad_qkv[-1].astype(bf16))
    d_input = d_middle + rms_backward(d_a * g_input, a_normed, a_factor)
    got, grad_qkv, qkv_moved, d_input = fence((got, grad_qkv, qkv_moved, d_input))
    line.settle(got)

    got = line.send()
    qkv_sent = comm.group_send(grad_qkv, qkv_moved)
    got, qkv_sent = fence((got, qkv_sent))
    line.settle(got)
    line.chunks += [comm.group_sum(out_sent).astype(bf16), comm.group_sum(qkv_sent).astype(bf16)]
    *done, total_out, tail = line.finish()
    down, gate, up = [all_of(done[i : i + 3]) for i in (0, 3, 6)]
    shard = width // n
    row = tail[shard]
    names, at = [], 0
    for v in gains:
        size = v.shape[0] // n
        names.append(row[at : at + size])
        at += size
    return (
        layer_out[None],
        d_input[None],
        tail[:shard, : HEADS * HEAD],
        tail[:shard, HEADS * HEAD :],
        total_out,
        gate.T,
        up.T,
        down,
        *names,
    )


def solution(mesh):
    cube = mesh.shape["seq"] == 8 and mesh.shape["dp"] == 4
    in_specs = (
        P("dp", "seq", None),
        P("dp", None),
        P("dp", "seq"),
        P("seq", None),
        P("seq", None),
        P("seq", None),
        P(None, "seq"),
        P(None, "seq"),
        P("seq", None),
        P(),
        P(),
        P(),
        P(),
        P(),
        P(),
        P("dp", "seq", None),
    )
    out_specs = (
        P("dp", "seq", None),
        P("dp", "seq", None),
        P("seq", None),
        P("seq", None),
        P("seq", None),
        P(None, "seq"),
        P(None, "seq"),
        P("seq", None),
        P("seq"),
        P("seq"),
        P("seq"),
        P("seq"),
        P("seq"),
        P("seq"),
    )
    return jax.shard_map(
        functools.partial(on_device, Cube if cube else Plain),
        mesh=mesh,
        in_specs=in_specs,
        out_specs=out_specs,
        check_vma=False,
    )
```

time: 1260 us -> 485 us (0.38)
  waiting for transfers between devices: 1020 us -> 227 us
  matrix products: 134 us -> 19.4 us
  starting transfers between devices: 1.18 us -> 101 us
  Pallas kernels: 0 us -> 66.9 us
  blocking collectives: 36.7 us -> 0 us
    reduce_scatter x7 -> x0, waiting for transfers between devices: 491 us -> none  [the longest x1 117 us: on_device(): lax.psum_scatter(grad_upw.astype(jnp.bfloat16), 'seq', scatter_dimension=...]
    all_gather x7 -> x0, waiting for transfers between devices: 330 us -> none  [the longest x1 84.5 us: on_device(): lax.all_gather(w_gate, 'seq', axis=1, tiled=True)]
    ppermute x0 -> x72, waiting for transfers between devices: none -> 227 us  [the longest x46 135 us: hop(): return lax.ppermute(value, 'seq', [(i, i ^ bit) for i in range(8)])]
    psum x1 -> x0, waiting for transfers between devices: 194 us -> none  [on_device(): lax.psum(grad_queryw.astype(jnp.bfloat16), 'dp').astype(jnp.float32)]
    ppermute x0 -> x72, starting transfers between devices: none -> 101 us  [the longest x46 43.2 us: hop(): return lax.ppermute(value, 'seq', [(i, i ^ bit) for i in range(8)])]
    pallas_call x0 -> x16, Pallas kernels: none -> 66.9 us  [the longest x6 22.3 us: weight_grad(): pl.pallas_call(functools.partial(weight_grad_kernel, index, sizes, len(le...]
    dot_general x9 -> x6, matrix products: 45.2 us -> 3.11 us  [dot_rows(): lax.dot_general(left, right, (((1,), (1,)), ((), ())), preferred_element_...]
    dot_general x8 -> x9, matrix products: 48.9 us -> 12 us  [the longest x8 7.84 us: dot(): return jnp.dot(left, right, preferred_element_type=f32)]
  transfers between devices with their start and end apart: 15 -> 72, of which waited for: 15 -> 35; matrix products, arithmetic and copies ran while one was open for 8% -> 9% of each run, Pallas kernels for 0% -> 12%
where the time goes in v1:
time: 485 us; the launch traced here: 478 us
  waiting for transfers between devices  227 us (47%)
  starting transfers between devices  101 us (21%)
  Pallas kernels  66.9 us (14%)
  other arithmetic  30.4 us (6%)
  local copies, waits for them, and re-layouts  29.3 us (6%)
  matrix products  19.4 us (4%)
    ppermute x46, waiting for transfers between devices, hop(): return lax.ppermute(value, 'seq', [(i, i ^ bit) for i in range(8)])  135 us
    ppermute x7, waiting for transfers between devices, send(): got['in'] = lax.ppermute(both, 'dp', [(0, 1), (1, 0), (2, 3), (3, 2)])  52.7 us
    ppermute x46, starting transfers between devices, hop(): return lax.ppermute(value, 'seq', [(i, i ^ bit) for i in range(8)])  43.2 us
    ppermute x4, waiting for transfers between devices, send(): got['out'] = lax.ppermute(back, 'dp', [(1, 0), (2, 3)])  39.2 us
    ppermute x7, starting transfers between devices, send(): got['in'] = lax.ppermute(both, 'dp', [(0, 1), (1, 0), (2, 3), (3, 2)])  34.3 us
    unnamed x268, local copies, waits for them, and re-layouts  23.1 us
    pallas_call x6, Pallas kernels, weight_grad(): pl.pallas_call(functools.partial(weight_grad_kernel, index, sizes, len(le...  22.3 us
    pallas_call x4, Pallas kernels, feed(): pl.pallas_call(functools.partial(feed_kernel, groups), out_shape=(jax.Sha...  18.2 us
  transfers between devices with their start and end apart: 72, of which 35 were waited for; matrix products, arithmetic and copies ran while one was open for 9% of the time, Pallas kernels for 12%

profile of v1, /device:TPU:0, one launch (start us, length us, event | category | flops | bytes accessed | tf_op | source)
XLA Modules:
  0.0 477.7 jit_solution(3673366887639625341)
XLA Ops:
  17.9 4.5 collective-permute-done.4
  22.4 5.2 %collective-permute-done.5 = bf16[144,1024]{1,0:T(8,128)(2,1)S(1)} collective-permute-done((bf16[144,1024]{1,0:T(8,128)(2,1)S(1)}, bf16[144,1024]{1,0:T(8,128)(2,1)S(1)}, u32[]{:S(2)}, u32[]{:S(2)}) %collective-permute-start.5) | collective-permute-done | bytes 294944 | tf_op jit(solution)/shard_map/ppermute | solution.py:424
  38.7 5.7 %collective-permute-done.8 = bf16[256,512]{1,0:T(8,128)(2,1)S(1)} collective-permute-done((bf16[256,512]{1,0:T(8,128)(2,1)S(1)}, bf16[256,512]{1,0:T(8,128)(2,1)S(1)}, u32[]{:S(2)}, u32[]{:S(2)}) %collective-permute-start.8) | collective-permute-done | bytes 262176 | tf_op jit(solution)/shard_map/ppermute | solution.py:424
  58.6 5.4 %collective-permute-done.12 = bf16[128,1152]{1,0:T(8,128)(2,1)S(1)} collective-permute-done((bf16[128,1152]{1,0:T(8,128)(2,1)}, bf16[128,1152]{1,0:T(8,128)(2,1)S(1)}, u32[]{:S(2)}, u32[]{:S(2)}) %collective-permute-start.12) | collective-permute-done | bytes 294944 | tf_op jit(solution)/shard_map/ppermute | solution.py:424
  80.6 4.5 feed.4
  85.2 8.1 %collective-permute-done.19.b_ref.refs_5_ = bf16[256,1152]{1,0:T(8,128)(2,1)S(1)} collective-permute-done((bf16[256,1152]{1,0:T(8,128)(2,1)S(1)}, bf16[256,1152]{1,0:T(8,128)(2,1)S(1)}, u32[]{:S(2)}, u32[]{:S(2)}) %collective-permute-start.19) | collective-permute-done | bytes 589856 | tf_op jit(solution)/shard_map/ppermute | solution.py:424
  93.3 4.5 feed.5
  97.8 7.2 %collective-permute-done.20.b_ref.refs_6_ = bf16[256,1152]{1,0:T(8,128)(2,1)S(1)} collective-permute-done((bf16[256,1152]{1,0:T(8,128)(2,1)S(1)}, bf16[256,1152]{1,0:T(8,128)(2,1)S(1)}, u32[]{:S(2)}, u32[]{:S(2)}) %collective-permute-start.20) | collective-permute-done | bytes 589856 | tf_op jit(solution)/shard_map/ppermute | solution.py:424
  105.1 4.7 feed.6
  109.8 8.1 %collective-permute-done.21 = bf16[256,1152]{1,0:T(8,128)(2,1)S(1)} collective-permute-done((bf16[256,1152]{1,0:T(8,128)(2,1)S(1)}, bf16[256,1152]{1,0:T(8,128)(2,1)S(1)}, u32[]{:S(2)}, u32[]{:S(2)}) %collective-permute-start.21) | collective-permute-done | bytes 589856 | tf_op jit(solution)/shard_map/ppermute | solution.py:424
  118.6 4.5 feed.7
  123.1 12.8 %collective-permute-done.23 = bf16[256,1152]{1,0:T(8,128)(2,1)S(1)} collective-permute-done((bf16[256,1152]{1,0:T(8,128)(2,1)S(1)}, bf16[256,1152]{1,0:T(8,128)(2,1)S(1)}, u32[]{:S(2)}, u32[]{:S(2)}) %collective-permute-start.23) | collective-permute-done | bytes 589856 | tf_op jit(solution)/shard_map/ppermute | solution.py:424
  137.8 15.3 %collective-permute-done.24 = bf16[256,1152]{1,0:T(8,128)(2,1)S(1)} collective-permute-done((bf16[256,1152]{1,0:T(8,128)(2,1)S(1)}, bf16[256,1152]{1,0:T(8,128)(2,1)S(1)}, u32[]{:S(2)}, u32[]{:S(2)}) %collective-permute-start.24) | collective-permute-done | bytes 589856 | tf_op jit(solution)/shard_map/ppermute | solution.py:424
  158.8 9.1 %collective-permute-done.25.d_ref.refs_5_ = bf16[256,1152]{1,0:T(8,128)(2,1)S(1)} collective-permute-done((bf16[256,1152]{1,0:T(8,128)(2,1)S(1)}, bf16[256,1152]{1,0:T(8,128)(2,1)S(1)}, u32[]{:S(2)}, u32[]{:S(2)}) %collective-permute-start.25) | collective-permute-done | bytes 589856 | tf_op jit(solution)/shard_map/ppermute | solution.py:424
  174.7 4.5 feed_back.4
  188.8 5.1 %feed_back.7 = (bf16[256,1152]{1,0:T(8,128)(2,1)}, bf16[2,256,864]{2,1,0:T(8,128)(2,1)S(1)}, bf16[2,256,864]{2,1,0:T(8,128)(2,1)S(1)}) custom-call(bf16[256,1152]{1,0:T(8,128)(2,1)S(1)} %collective-permute-done.28.refs_7_.d_ref, bf16[2,256,864]{2,1,0:T(8,128)(2,1)S(1)} %get-tuple-element.299.act_ref, bf16[2,256,864]{2,1,0:T(8,128)(2,1)S(1)} %get-tuple-element.300.slope_ref, ...), custom_call_target="tpu_custom_call" | custom-call | flops 1 | bytes 1 | tf_op jit(solution)/shard_map/feed_back/pallas_call | solution.py:310
  193.9 9.4 %collective-permute-done.30 = bf16[256,1152]{1,0:T(8,128)(2,1)S(1)} collective-permute-done((bf16[256,1152]{1,0:T(8,128)(2,1)S(1)}, bf16[256,1152]{1,0:T(8,128)(2,1)S(1)}, u32[]{:S(2)}, u32[]{:S(2)}) %collective-permute-start.30) | collective-permute-done | bytes 589856 | tf_op jit(solution)/shard_map/ppermute | solution.py:424
  245.9 4.6 attend_back.1
  254.4 11.0 %collective-permute-start.37 = (bf16[288,1152]{1,0:T(8,128)(2,1)S(1)}, bf16[288,1152]{1,0:T(8,128)(2,1)S(1)}, u32[]{:S(2)}, u32[]{:S(2)}) collective-permute-start(bf16[288,1152]{1,0:T(8,128)(2,1)S(1)} %broadcast_select_fusion.15), channel_id=1, source_target_pairs={{0,8},{8,0},{16,24},{24,16},{1,9},{9,1},{17,25},{25,17},{2,10},{10... | collective-permute-start | bytes 1990664 | tf_op jit(solution)/shard_map/ppermute | solution.py:530
  281.8 5.3 %collective-permute-done.41 = bf16[256,512]{1,0:T(8,128)(2,1)S(1)} collective-permute-done((bf16[256,512]{1,0:T(8,128)(2,1)S(1)}, bf16[256,512]{1,0:T(8,128)(2,1)S(1)}, u32[]{:S(2)}, u32[]{:S(2)}) %collective-permute-start.41) | collective-permute-done | bytes 262176 | tf_op jit(solution)/shard_map/ppermute | solution.py:424
  323.3 11.1 %collective-permute-done.49 = bf16[288,1152]{1,0:T(8,128)(2,1)S(1)} collective-permute-done((bf16[288,1152]{1,0:T(8,128)(2,1)S(1)}, bf16[288,1152]{1,0:T(8,128)(2,1)S(1)}, u32[]{:S(2)}, u32[]{:S(2)}) %collective-permute-start.49) | collective-permute-done | bytes 663584 | tf_op jit(solution)/shard_map/ppermute | solution.py:530
  335.6 4.5 collective-permute-start.52
  344.7 10.4 %collective-permute-done.54 = bf16[160,1536]{1,0:T(8,128)(2,1)S(1)} collective-permute-done((bf16[160,1536]{1,0:T(8,128)(2,1)S(1)}, bf16[160,1536]{1,0:T(8,128)(2,1)S(1)}, u32[]{:S(2)}, u32[]{:S(2)}) %collective-permute-start.54) | collective-permute-done | bytes 491552 | tf_op jit(solution)/shard_map/ppermute | solution.py:424
  357.1 7.6 %collective-permute-done.55 = bf16[160,1536]{1,0:T(8,128)(2,1)S(1)} collective-permute-done((bf16[160,1536]{1,0:T(8,128)(2,1)S(1)}, bf16[160,1536]{1,0:T(8,128)(2,1)S(1)}, u32[]{:S(2)}, u32[]{:S(2)}) %collective-permute-start.55) | collective-permute-done | bytes 491552 | tf_op jit(solution)/shard_map/ppermute | solution.py:424
  370.7 9.9 %collective-permute-done.59 = bf16[288,1152]{1,0:T(8,128)(2,1)S(1)} collective-permute-done((bf16[288,1152]{1,0:T(8,128)(2,1)S(1)}, bf16[288,1152]{1,0:T(8,128)(2,1)S(1)}, u32[]{:S(2)}, u32[]{:S(2)}) %collective-permute-start.59) | collective-permute-done | bytes 663584 | tf_op jit(solution)/shard_map/ppermute | solution.py:530
  381.8 4.5 collective-permute-start.61
  388.7 12.9 %collective-permute-done.61 = bf16[288,1152]{1,0:T(8,128)(2,1)S(1)} collective-permute-done((bf16[288,1152]{1,0:T(8,128)(2,1)S(1)}, bf16[288,1152]{1,0:T(8,128)(2,1)S(1)}, u32[]{:S(2)}, u32[]{:S(2)}) %collective-permute-start.61) | collective-permute-done | bytes 663584 | tf_op jit(solution)/shard_map/ppermute | solution.py:530
  407.6 13.8 %collective-permute-done.63 = bf16[288,1152]{1,0:T(8,128)(2,1)S(1)} collective-permute-done((bf16[288,1152]{1,0:T(8,128)(2,1)S(1)}, bf16[288,1152]{1,0:T(8,128)(2,1)S(1)}, u32[]{:S(2)}, u32[]{:S(2)}) %collective-permute-start.63) | collective-permute-done | bytes 663584 | tf_op jit(solution)/shard_map/ppermute | solution.py:530
  426.3 9.3 %collective-permute-done.66 = bf16[288,1152]{1,0:T(8,128)(2,1)S(1)} collective-permute-done((bf16[288,1152]{1,0:T(8,128)(2,1)S(1)}, bf16[288,1152]{1,0:T(8,128)(2,1)S(1)}, u32[]{:S(2)}, u32[]{:S(2)}) %collective-permute-start.66) | collective-permute-done | bytes 663584 | tf_op jit(solution)/shard_map/ppermute | solution.py:533
  438.0 13.1 %collective-permute-done.68 = bf16[288,1152]{1,0:T(8,128)(2,1)S(1)} collective-permute-done((bf16[288,1152]{1,0:T(8,128)(2,1)S(1)}, bf16[288,1152]{1,0:T(8,128)(2,1)S(1)}, u32[]{:S(2)}, u32[]{:S(2)}) %collective-permute-start.68) | collective-permute-done | bytes 663584 | tf_op jit(solution)/shard_map/ppermute | solution.py:533
  455.6 8.1 %collective-permute-done.70 = bf16[128,1152]{1,0:T(8,128)(2,1)S(1)} collective-permute-done((bf16[128,1152]{1,0:T(8,128)(2,1)S(1)}, bf16[128,1152]{1,0:T(8,128)(2,1)S(1)}, u32[]{:S(2)}, u32[]{:S(2)}) %collective-permute-start.70) | collective-permute-done | bytes 294944 | tf_op jit(solution)/shard_map/ppermute | solution.py:533
  466.0 8.6 %collective-permute-done.71 = bf16[160,1536]{1,0:T(8,128)(2,1)S(1)} collective-permute-done((bf16[160,1536]{1,0:T(8,128)(2,1)S(1)}, bf16[160,1536]{1,0:T(8,128)(2,1)S(1)}, u32[]{:S(2)}, u32[]{:S(2)}) %collective-permute-start.71) | collective-permute-done | bytes 491552 | tf_op jit(solution)/shard_map/ppermute | solution.py:533
  (525 shorter events, 220.5 us)
Async XLA Ops:
  77.1 16.2 %collective-permute-start.19 = (bf16[256,1152]{1,0:T(8,128)(2,1)S(1)}, bf16[256,1152]{1,0:T(8,128)(2,1)S(1)}, u32[]{:S(2)}, u32[]{:S(2)}) collective-permute-start(bf16[256,1152]{1,0:T(8,128)(2,1)S(1)} %multiply_convert_fusion.2.b_ref.refs_4_), channel_id=1, source_target_pairs={{0,2},{1,3},{2,0},{3,1},{4,6},{5,7},{6,4},{7,5},{8,10},{9,11},{10,... | collective-permute-start | bytes 1769480 | tf_op jit(solution)/shard_map/ppermute | solution.py:424
  77.9 27.1 %collective-permute-start.20 = (bf16[256,1152]{1,0:T(8,128)(2,1)S(1)}, bf16[256,1152]{1,0:T(8,128)(2,1)S(1)}, u32[]{:S(2)}, u32[]{:S(2)}) collective-permute-start(bf16[256,1152]{1,0:T(8,128)(2,1)S(1)} %multiply_convert_fusion.2.b_ref.refs_4_), channel_id=1, source_target_pairs={{0,4},{1,5},{2,6},{3,7},{4,0},{5,1},{6,2},{7,3},{8,12},{9,13},{10,... | collective-permute-start | bytes 1769480 | tf_op jit(solution)/shard_map/ppermute | solution.py:424
  79.4 30.3 %collective-permute-start.22 = (bf16[256,1152]{1,0:T(8,128)(2,1)S(1)}, bf16[256,1152]{1,0:T(8,128)(2,1)S(1)}, u32[]{:S(2)}, u32[]{:S(2)}) collective-permute-start(bf16[256,1152]{1,0:T(8,128)(2,1)S(1)} %multiply_convert_fusion.2.b_ref.refs_4_), channel_id=1, source_target_pairs={{0,6},{1,7},{2,4},{3,5},{4,2},{5,3},{6,0},{7,1},{8,14},{9,15},{10,... | collective-permute-start | bytes 1769480 | tf_op jit(solution)/shard_map/ppermute | solution.py:424
  117.8 18.2 %collective-permute-start.23 = (bf16[256,1152]{1,0:T(8,128)(2,1)S(1)}, bf16[256,1152]{1,0:T(8,128)(2,1)S(1)}, u32[]{:S(2)}, u32[]{:S(2)}) collective-permute-start(bf16[256,1152]{1,0:T(8,128)(2,1)S(1)} %get-tuple-element.271), channel_id=1, source_target_pairs={{0,4},{1,5},{2,6},{3,7},{4,0},{5,1},{6,2},{7,3},{8,12},{9,13},{10,... | collective-permute-start | bytes 1769480 | tf_op jit(solution)/shard_map/ppermute | solution.py:424
  136.0 17.2 %collective-permute-start.24 = (bf16[256,1152]{1,0:T(8,128)(2,1)S(1)}, bf16[256,1152]{1,0:T(8,128)(2,1)S(1)}, u32[]{:S(2)}, u32[]{:S(2)}) collective-permute-start(bf16[256,1152]{1,0:T(8,128)(2,1)S(1)} %get-tuple-element.273), channel_id=1, source_target_pairs={{0,6},{1,7},{2,4},{3,5},{4,2},{5,3},{6,0},{7,1},{8,14},{9,15},{10,... | collective-permute-start | bytes 1769480 | tf_op jit(solution)/shard_map/ppermute | solution.py:424
  155.3 16.8 %collective-permute-start.26 = (bf16[256,1152]{1,0:T(8,128)(2,1)S(1)}, bf16[256,1152]{1,0:T(8,128)(2,1)S(1)}, u32[]{:S(2)}, u32[]{:S(2)}) collective-permute-start(bf16[256,1152]{1,0:T(8,128)(2,1)S(1)} %get-tuple-element.278.d_ref.refs_4_), channel_id=1, source_target_pairs={{0,4},{1,5},{2,6},{3,7},{4,0},{5,1},{6,2},{7,3},{8,12},{9,13},{10,... | collective-permute-start | bytes 1769480 | tf_op jit(solution)/shard_map/ppermute | solution.py:424
  157.0 26.5 %collective-permute-start.28 = (bf16[256,1152]{1,0:T(8,128)(2,1)S(1)}, bf16[256,1152]{1,0:T(8,128)(2,1)S(1)}, u32[]{:S(2)}, u32[]{:S(2)}) collective-permute-start(bf16[256,1152]{1,0:T(8,128)(2,1)S(1)} %get-tuple-element.278.d_ref.refs_4_), channel_id=1, source_target_pairs={{0,6},{1,7},{2,4},{3,5},{4,2},{5,3},{6,0},{7,1},{8,14},{9,15},{10,... | collective-permute-start | bytes 1769480 | tf_op jit(solution)/shard_map/ppermute | solution.py:424
  187.5 15.8 %collective-permute-start.29 = (bf16[864,1152]{1,0:T(8,128)(2,1)S(1)}, bf16[864,1152]{1,0:T(8,128)(2,1)S(1)}, u32[]{:S(2)}, u32[]{:S(2)}) collective-permute-start(bf16[864,1152]{1,0:T(8,128)(2,1)S(1)} %weight_grad.6), channel_id=1, source_target_pairs={{0,1},{1,0},{2,3},{3,2},{4,5},{5,4},{6,7},{7,6},{8,9},{9,8},{10,11... | collective-permute-start | bytes 5971976 | tf_op jit(solution)/shard_map/ppermute | solution.py:424
  187.6 15.7 %collective-permute-start.30 = (bf16[256,1152]{1,0:T(8,128)(2,1)S(1)}, bf16[256,1152]{1,0:T(8,128)(2,1)S(1)}, u32[]{:S(2)}, u32[]{:S(2)}) collective-permute-start(bf16[256,1152]{1,0:T(8,128)(2,1)S(1)} %get-tuple-element.298), channel_id=1, source_target_pairs={{0,4},{1,5},{2,6},{3,7},{4,0},{5,1},{6,2},{7,3},{8,12},{9,13},{10,... | collective-permute-start | bytes 1769480 | tf_op jit(solution)/shard_map/ppermute | solution.py:424
  211.1 24.9 %collective-permute-start.34 = (bf16[864,1152]{1,0:T(8,128)(2,1)}, bf16[864,1152]{1,0:T(8,128)(2,1)}, u32[]{:S(2)}, u32[]{:S(2)}) collective-permute-start(bf16[864,1152]{1,0:T(8,128)(2,1)} %weight_grad.10), channel_id=1, source_target_pairs={{0,1},{1,0},{2,3},{3,2},{4,5},{5,4},{6,7},{7,6},{8,9},{9,8},{10,11... | collective-permute-start | bytes 5971976 | tf_op jit(solution)/shard_map/ppermute | solution.py:424
  215.4 20.5 %collective-permute-start.31 = (bf16[288,1152]{1,0:T(8,128)(2,1)}, bf16[288,1152]{1,0:T(8,128)(2,1)}, u32[]{:S(2)}, u32[]{:S(2)}) collective-permute-start(bf16[288,1152]{1,0:T(8,128)(2,1)} %get-tuple-element.317), channel_id=1, source_target_pairs={{0,8},{24,16},{1,9},{25,17},{2,10},{26,18},{3,11},{27,19},{4,12},{... | collective-permute-start | bytes 1990664 | tf_op jit(solution)/shard_map/ppermute | solution.py:535
  219.7 16.2 %collective-permute-start.32 = (bf16[256,1152]{1,0:T(8,128)(2,1)}, bf16[256,1152]{1,0:T(8,128)(2,1)}, u32[]{:S(2)}, u32[]{:S(2)}) collective-permute-start(bf16[256,1152]{1,0:T(8,128)(2,1)} %get-tuple-element.318), channel_id=1, source_target_pairs={{0,6},{1,7},{2,4},{3,5},{4,2},{5,3},{6,0},{7,1},{8,14},{9,15},{10,... | collective-permute-start | bytes 1769480 | tf_op jit(solution)/shard_map/ppermute | solution.py:424
  224.2 26.3 %collective-permute-start.35 = (bf16[288,1152]{1,0:T(8,128)(2,1)}, bf16[288,1152]{1,0:T(8,128)(2,1)S(1)}, u32[]{:S(2)}, u32[]{:S(2)}) collective-permute-start(bf16[288,1152]{1,0:T(8,128)(2,1)} %get-tuple-element.331), channel_id=1, source_target_pairs={{0,8},{24,16},{1,9},{25,17},{2,10},{26,18},{3,11},{27,19},{4,12},{... | collective-permute-start | bytes 1990664 | tf_op jit(solution)/shard_map/ppermute | solution.py:535
  251.1 29.2 %collective-permute-start.43 = (bf16[512,1152]{1,0:T(8,128)(2,1)S(1)}, bf16[512,1152]{1,0:T(8,128)(2,1)S(1)}, u32[]{:S(2)}, u32[]{:S(2)}) collective-permute-start(bf16[512,1152]{1,0:T(8,128)(2,1)S(1)} %fusion.72), channel_id=1, source_target_pairs={{0,1},{1,0},{2,3},{3,2},{4,5},{5,4},{6,7},{7,6},{8,9},{9,8},{10,11... | collective-permute-start | bytes 3538952 | tf_op jit(solution)/shard_map/ppermute | solution.py:424
  251.8 20.3 %collective-permute-start.39 = (bf16[1024,512]{1,0:T(8,128)(2,1)S(1)}, bf16[1024,512]{1,0:T(8,128)(2,1)S(1)}, u32[]{:S(2)}, u32[]{:S(2)}) collective-permute-start(bf16[1024,512]{1,0:T(8,128)(2,1)S(1)} %get-tuple-element.358), channel_id=1, source_target_pairs={{0,1},{1,0},{2,3},{3,2},{4,5},{5,4},{6,7},{7,6},{8,9},{9,8},{10,11... | collective-permute-start | bytes 3145736 | tf_op jit(solution)/shard_map/ppermute | solution.py:424
  253.3 21.2 %collective-permute-start.38 = (bf16[288,1152]{1,0:T(8,128)(2,1)S(1)}, bf16[288,1152]{1,0:T(8,128)(2,1)S(1)}, u32[]{:S(2)}, u32[]{:S(2)}) collective-permute-start(bf16[288,1152]{1,0:T(8,128)(2,1)S(1)} %add_convert_fusion.15), channel_id=1, source_target_pairs={{8,16},{16,8},{9,17},{17,9},{10,18},{18,10},{11,19},{19,11},{12,20... | collective-permute-start | bytes 1990664 | tf_op jit(solution)/shard_map/ppermute | solution.py:537
  254.4 25.9 %collective-permute-start.37 = (bf16[288,1152]{1,0:T(8,128)(2,1)S(1)}, bf16[288,1152]{1,0:T(8,128)(2,1)S(1)}, u32[]{:S(2)}, u32[]{:S(2)}) collective-permute-start(bf16[288,1152]{1,0:T(8,128)(2,1)S(1)} %broadcast_select_fusion.15), channel_id=1, source_target_pairs={{0,8},{8,0},{16,24},{24,16},{1,9},{9,1},{17,25},{25,17},{2,10},{10... | collective-permute-start | bytes 1990664 | tf_op jit(solution)/shard_map/ppermute | solution.py:530
  288.6 19.4 %collective-permute-start.46 = (bf16[128,1152]{1,0:T(8,128)(2,1)S(1)}, bf16[128,1152]{1,0:T(8,128)(2,1)S(1)}, u32[]{:S(2)}, u32[]{:S(2)}) collective-permute-start(bf16[128,1152]{1,0:T(8,128)(2,1)S(1)} %get-tuple-element.442), channel_id=1, source_target_pairs={{0,2},{1,3},{2,0},{3,1},{4,6},{5,7},{6,4},{7,5},{8,10},{9,11},{10,... | collective-permute-start | bytes 884744 | tf_op jit(solution)/shard_map/ppermute | solution.py:424
  289.3 18.8 %collective-permute-start.47 = (bf16[128,1152]{1,0:T(8,128)(2,1)S(1)}, bf16[128,1152]{1,0:T(8,128)(2,1)S(1)}, u32[]{:S(2)}, u32[]{:S(2)}) collective-permute-start(bf16[128,1152]{1,0:T(8,128)(2,1)S(1)} %get-tuple-element.441), channel_id=1, source_target_pairs={{0,4},{1,5},{2,6},{3,7},{4,0},{5,1},{6,2},{7,3},{8,12},{9,13},{10,... | collective-permute-start | bytes 884744 | tf_op jit(solution)/shard_map/ppermute | solution.py:424
  290.4 17.6 %collective-permute-start.48 = (bf16[128,1152]{1,0:T(8,128)(2,1)S(1)}, bf16[128,1152]{1,0:T(8,128)(2,1)S(1)}, u32[]{:S(2)}, u32[]{:S(2)}) collective-permute-start(bf16[128,1152]{1,0:T(8,128)(2,1)S(1)} %get-tuple-element.440), channel_id=1, source_target_pairs={{0,6},{1,7},{2,4},{3,5},{4,2},{5,3},{6,0},{7,1},{8,14},{9,15},{10,... | collective-permute-start | bytes 884744 | tf_op jit(solution)/shard_map/ppermute | solution.py:424
  292.4 15.7 %collective-permute-start.45 = (bf16[288,1152]{1,0:T(8,128)(2,1)S(1)}, bf16[288,1152]{1,0:T(8,128)(2,1)S(1)}, u32[]{:S(2)}, u32[]{:S(2)}) collective-permute-start(bf16[288,1152]{1,0:T(8,128)(2,1)S(1)} %add_convert_fusion.14), channel_id=1, source_target_pairs={{8,16},{16,8},{9,17},{17,9},{10,18},{18,10},{11,19},{19,11},{12,20... | collective-permute-start | bytes 1990664 | tf_op jit(solution)/shard_map/ppermute | solution.py:537
  293.7 16.7 %collective-permute-start.44 = (bf16[288,1152]{1,0:T(8,128)(2,1)S(1)}, bf16[288,1152]{1,0:T(8,128)(2,1)S(1)}, u32[]{:S(2)}, u32[]{:S(2)}) collective-permute-start(bf16[288,1152]{1,0:T(8,128)(2,1)S(1)} %broadcast_select_fusion.14), channel_id=1, source_target_pairs={{0,8},{8,0},{16,24},{24,16},{1,9},{9,1},{17,25},{25,17},{2,10},{10... | collective-permute-start | bytes 1990664 | tf_op jit(solution)/shard_map/ppermute | solution.py:530
  314.2 20.3 %collective-permute-start.51 = (bf16[640,1536]{1,0:T(8,128)(2,1)S(1)}, bf16[640,1536]{1,0:T(8,128)(2,1)S(1)}, u32[]{:S(2)}, u32[]{:S(2)}) collective-permute-start(bf16[640,1536]{1,0:T(8,128)(2,1)S(1)} %fusion.70), channel_id=1, source_target_pairs={{0,1},{1,0},{2,3},{3,2},{4,5},{5,4},{6,7},{7,6},{8,9},{9,8},{10,11... | collective-permute-start | bytes 5898248 | tf_op jit(solution)/shard_map/ppermute | solution.py:424
  315.7 18.7 %collective-permute-start.49 = (bf16[288,1152]{1,0:T(8,128)(2,1)S(1)}, bf16[288,1152]{1,0:T(8,128)(2,1)S(1)}, u32[]{:S(2)}, u32[]{:S(2)}) collective-permute-start(bf16[288,1152]{1,0:T(8,128)(2,1)S(1)} %broadcast_select_fusion.13), channel_id=1, source_target_pairs={{0,8},{8,0},{16,24},{24,16},{1,9},{9,1},{17,25},{25,17},{2,10},{10... | collective-permute-start | bytes 1990664 | tf_op jit(solution)/shard_map/ppermute | solution.py:530
  334.6 30.1 %collective-permute-start.53 = (bf16[288,1152]{1,0:T(8,128)(2,1)S(1)}, bf16[288,1152]{1,0:T(8,128)(2,1)S(1)}, u32[]{:S(2)}, u32[]{:S(2)}) collective-permute-start(bf16[288,1152]{1,0:T(8,128)(2,1)S(1)} %add_convert_fusion.9), channel_id=1, source_target_pairs={{8,16},{16,8},{9,17},{17,9},{10,18},{18,10},{11,19},{19,11},{12,20... | collective-permute-start | bytes 1990664 | tf_op jit(solution)/shard_map/ppermute | solution.py:537
  335.6 29.1 %collective-permute-start.52 = (bf16[288,1152]{1,0:T(8,128)(2,1)S(1)}, bf16[288,1152]{1,0:T(8,128)(2,1)S(1)}, u32[]{:S(2)}, u32[]{:S(2)}) collective-permute-start(bf16[288,1152]{1,0:T(8,128)(2,1)S(1)} %broadcast_select_fusion.12), channel_id=1, source_target_pairs={{0,8},{8,0},{16,24},{24,16},{1,9},{9,1},{17,25},{25,17},{2,10},{10... | collective-permute-start | bytes 1990664 | tf_op jit(solution)/shard_map/ppermute | solution.py:530
  342.5 22.2 %collective-permute-start.55 = (bf16[160,1536]{1,0:T(8,128)(2,1)S(1)}, bf16[160,1536]{1,0:T(8,128)(2,1)S(1)}, u32[]{:S(2)}, u32[]{:S(2)}) collective-permute-start(bf16[160,1536]{1,0:T(8,128)(2,1)S(1)} %get-tuple-element.435), channel_id=1, source_target_pairs={{0,4},{1,5},{2,6},{3,7},{4,0},{5,1},{6,2},{7,3},{8,12},{9,13},{10,... | collective-permute-start | bytes 1474568 | tf_op jit(solution)/shard_map/ppermute | solution.py:424
  342.9 21.7 %collective-permute-start.56 = (bf16[160,1536]{1,0:T(8,128)(2,1)S(1)}, bf16[160,1536]{1,0:T(8,128)(2,1)S(1)}, u32[]{:S(2)}, u32[]{:S(2)}) collective-permute-start(bf16[160,1536]{1,0:T(8,128)(2,1)S(1)} %get-tuple-element.434), channel_id=1, source_target_pairs={{0,6},{1,7},{2,4},{3,5},{4,2},{5,3},{6,0},{7,1},{8,14},{9,15},{10,... | collective-permute-start | bytes 1474568 | tf_op jit(solution)/shard_map/ppermute | solution.py:424
  355.2 71.1 %collective-permute-start.58 = (bf16[128,1152]{1,0:T(8,128)(2,1)S(1)}, bf16[128,1152]{1,0:T(8,128)(2,1)S(1)}, u32[]{:S(2)}, u32[]{:S(2)}) collective-permute-start(bf16[128,1152]{1,0:T(8,128)(2,1)S(1)} %add_convert_fusion.24), channel_id=1, source_target_pairs={{0,8},{24,16},{1,9},{25,17},{2,10},{26,18},{3,11},{27,19},{4,12},{... | collective-permute-start | bytes 884744 | tf_op jit(solution)/shard_map/ppermute | solution.py:535
  381.8 19.9 %collective-permute-start.61 = (bf16[288,1152]{1,0:T(8,128)(2,1)S(1)}, bf16[288,1152]{1,0:T(8,128)(2,1)S(1)}, u32[]{:S(2)}, u32[]{:S(2)}) collective-permute-start(bf16[288,1152]{1,0:T(8,128)(2,1)S(1)} %broadcast_select_fusion.10), channel_id=1, source_target_pairs={{0,8},{8,0},{16,24},{24,16},{1,9},{9,1},{17,25},{25,17},{2,10},{10... | collective-permute-start | bytes 1990664 | tf_op jit(solution)/shard_map/ppermute | solution.py:530
  386.5 51.5 %collective-permute-start.57 = (bf16[160,1536]{1,0:T(8,128)(2,1)S(1)}, bf16[160,1536]{1,0:T(8,128)(2,1)S(1)}, u32[]{:S(2)}, u32[]{:S(2)}) collective-permute-start(bf16[160,1536]{1,0:T(8,128)(2,1)S(1)} %add_convert_fusion.21), channel_id=1, source_target_pairs={{0,8},{24,16},{1,9},{25,17},{2,10},{26,18},{3,11},{27,19},{4,12},{... | collective-permute-start | bytes 1474568 | tf_op jit(solution)/shard_map/ppermute | solution.py:535
  402.8 18.6 %collective-permute-start.63 = (bf16[288,1152]{1,0:T(8,128)(2,1)S(1)}, bf16[288,1152]{1,0:T(8,128)(2,1)S(1)}, u32[]{:S(2)}, u32[]{:S(2)}) collective-permute-start(bf16[288,1152]{1,0:T(8,128)(2,1)S(1)} %broadcast_select_fusion.9), channel_id=1, source_target_pairs={{0,8},{8,0},{16,24},{24,16},{1,9},{9,1},{17,25},{25,17},{2,10},{10... | collective-permute-start | bytes 1990664 | tf_op jit(solution)/shard_map/ppermute | solution.py:530
  (168 other events, 1944.5 us)

commit v2 on v1

v2 whole, which is shorter than its diff:
```python
import functools

import jax
import jax.numpy as jnp
from jax import lax
from jax.experimental import pallas as pl
from jax.experimental.pallas import tpu as pltpu
from jax.sharding import PartitionSpec as P

HEADS = 4
HEAD = 256
BLOCK = 256
LANES = 128
FEED_VMEM = 12 << 20

norm_eps = 1e-06
rope_base = 1000000.0
score_scale = HEAD**-0.5
bf16 = jnp.bfloat16
f32 = jnp.float32
BRIEF = pl.CostEstimate(flops=1, bytes_accessed=1, transcendentals=0)


def rms_forward(values):
    factor = lax.rsqrt(jnp.mean(values * values, axis=-1, keepdims=True) + norm_eps)
    return (values * factor, factor)


def rms_backward(upstream, normed, factor):
    return factor * (upstream - normed * jnp.mean(upstream * normed, axis=-1, keepdims=True))


def rope_angles(positions, width):
    half_width = width // 2
    inverse_freq = rope_base ** (-(jnp.arange(half_width).astype(f32) * 2.0 / width))
    return positions.astype(f32)[:, None] * inverse_freq[None, :]


def rotate(values, cosine, sine):
    half_width = values.shape[-1] // 2
    first = values[..., :half_width]
    second = values[..., half_width:]
    return jnp.concatenate(
        [first * cosine - second * sine, second * cosine + first * sine], axis=-1
    )


def dot(left, right):
    return jnp.dot(left, right, preferred_element_type=f32)


def dot_rows(left, right):
    return lax.dot_general(left, right, (((1,), (1,)), ((), ())), preferred_element_type=f32)


def dot_cols(left, right):
    return lax.dot_general(left, right, (((0,), (0,)), ((), ())), preferred_element_type=f32)


def visible_mask(block_id, first_row, pos_ref):
    shape = (BLOCK, BLOCK)
    query = first_row + lax.broadcasted_iota(jnp.int32, shape, 0)
    key = block_id * BLOCK + lax.broadcasted_iota(jnp.int32, shape, 1)
    return (key <= query) & (key >= query - pos_ref[...])


def put_queries(q_ref, q_pre_ref, gain_ref, cosine, sine):
    for h in range(HEADS):
        cols = pl.ds(h * HEAD, HEAD)
        normed, _ = rms_forward(q_pre_ref[:, cols])
        q_ref[:, cols] = rotate(normed * gain_ref[...], cosine, sine).astype(bf16)


def attend_kernel(
    n_blocks,
    columns,
    order_ref,
    q_pre_ref,
    cos_ref,
    sin_ref,
    gain_ref,
    pos_ref,
    *refs,
):
    kv_refs, (att_low_ref, inv_ref, q_ref, att_ref, total_ref) = refs[:-5], refs[-5:]
    slot = order_ref.shape[0] - columns
    first_row = order_ref[n_blocks]
    first_key = order_ref[n_blocks + 1]
    cosine, sine = cos_ref[...], sin_ref[...]
    put_queries(q_ref, q_pre_ref, gain_ref, cosine, sine)
    att_ref[...] = jnp.zeros_like(att_ref)
    total_ref[...] = jnp.zeros_like(total_ref)

    def step(kv_ref, base, k, _):
        block_id = order_ref[base + k]
        live = (block_id * BLOCK <= first_row) & ((block_id + 1) * BLOCK > first_key)

        @pl.when(live)
        def _():
            rows = pl.ds(pl.multiple_of(k * BLOCK, BLOCK), BLOCK)
            keys = kv_ref[rows, :HEAD]
            vals = kv_ref[rows, HEAD:]
            visible = visible_mask(block_id, first_row, pos_ref)
            for h in range(HEADS):
                cols = pl.ds(h * HEAD, HEAD)
                scores = dot_rows(q_ref[:, cols], keys) * score_scale
                weight = jnp.where(visible, jnp.exp(scores), 0.0)
                total_ref[:, pl.ds(h * LANES, LANES)] += weight[:, :LANES] + weight[:, LANES:]
                att_ref[:, cols] += dot(weight.astype(bf16), vals)

        return 0

    each = n_blocks // len(kv_refs)
    for i, kv_ref in enumerate(kv_refs):
        lax.fori_loop(0, each, functools.partial(step, kv_ref, i * each), 0)
    for h in range(HEADS):
        cols = pl.ds(h * HEAD, HEAD)
        lanes = pl.ds(h * LANES, LANES)
        inverse = 1.0 / jnp.sum(total_ref[:, lanes], axis=-1, keepdims=True)
        inv_ref[:, pl.ds(h, 1)] = inverse
        att_ref[:, cols] = att_ref[:, cols] * inverse
    size = HEADS * HEAD // columns
    for k in range(columns):
        source = pl.ds(pl.multiple_of(order_ref[slot + k] * size, size), size)
        att_low_ref[:, pl.ds(k * size, size)] = att_ref[:, source].astype(bf16)


def attend(columns, order, q_pre, cosine, sine, gain, pos, *kv):
    rows = q_pre.shape[0]
    n_blocks = sum(v.shape[0] for v in kv) // BLOCK
    whole = pl.BlockSpec(memory_space=pltpu.VMEM)
    return pl.pallas_call(
        functools.partial(attend_kernel, n_blocks, columns),
        out_shape=(
            jax.ShapeDtypeStruct((rows, HEADS * HEAD), bf16),
            jax.ShapeDtypeStruct((rows, LANES), f32),
        ),
        in_specs=[pl.BlockSpec(memory_space=pltpu.SMEM)] + [whole] * (5 + len(kv)),
        out_specs=(whole,) * 2,
        scratch_shapes=[
            pltpu.VMEM((rows, HEADS * HEAD), bf16),
            pltpu.VMEM((rows, HEADS * HEAD), f32),
            pltpu.VMEM((rows, HEADS * LANES), f32),
        ],
        cost_estimate=BRIEF,
        compiler_params=pltpu.CompilerParams(vmem_limit_bytes=8 << 20),
        name="attend",
    )(order, q_pre, cosine, sine, gain, pos, *kv)


def attend_back_kernel(
    n_blocks,
    columns,
    order_ref,
    q_pre_ref,
    cos_ref,
    sin_ref,
    gain_ref,
    pos_ref,
    att_ref,
    inv_ref,
    d_moved_ref,
    *refs,
):
    groups = (len(refs) - 7) // 2
    kv_refs, d_q_pre_ref, d_kv_refs = refs[:groups], refs[groups], refs[groups + 1 : -6]
    d_gain_ref, d_q_ref, row_dot_ref, d_att_ref, q_ref, dot_ref = refs[-6:]
    cosine, sine = cos_ref[...], sin_ref[...]
    put_queries(q_ref, q_pre_ref, gain_ref, cosine, sine)
    slot = order_ref.shape[0] - columns
    size = HEADS * HEAD // columns
    for k in range(columns):
        target = pl.ds(pl.multiple_of(order_ref[slot + k] * size, size), size)
        moved = d_moved_ref[:, pl.ds(k * size, size)]
        d_att_ref[:, target] = moved
        dot_ref[:, target] = moved.astype(f32) * att_ref[:, pl.ds(k * size, size)].astype(f32)
    first_row = order_ref[n_blocks]
    first_key = order_ref[n_blocks + 1]
    for h in range(HEADS):
        cols = pl.ds(h * HEAD, HEAD)
        row_dot_ref[:, pl.ds(h, 1)] = jnp.sum(dot_ref[:, cols], axis=-1, keepdims=True)
    d_q_ref[...] = jnp.zeros_like(d_q_ref)

    def step(kv_ref, d_kv_ref, base, k, _):
        block_id = order_ref[base + k]
        live = (block_id * BLOCK <= first_row) & ((block_id + 1) * BLOCK > first_key)
        rows = pl.ds(pl.multiple_of(k * BLOCK, BLOCK), BLOCK)

        @pl.when(live)
        def _():
            keys = kv_ref[rows, :HEAD]
            vals = kv_ref[rows, HEAD:]
            visible = visible_mask(block_id, first_row, pos_ref)
            d_keys = jnp.zeros((BLOCK, HEAD), f32)
            d_vals = jnp.zeros((BLOCK, HEAD), f32)
            for h in range(HEADS):
                cols = pl.ds(h * HEAD, HEAD)
                query = q_ref[:, cols]
                d_att = d_att_ref[:, cols]
                inverse = inv_ref[:, pl.ds(h, 1)]
                row_dot = row_dot_ref[:, pl.ds(h, 1)]
                scores = dot_rows(query, keys) * score_scale
                prob = jnp.where(visible, jnp.exp(scores), 0.0) * inverse
                d_prob = dot_rows(d_att, vals)
                d_scores = (prob * (d_prob - row_dot)).astype(bf16)
                d_q_ref[:, cols] += dot(d_scores, keys)
                d_keys += dot_cols(d_scores, query)
                d_vals += dot_cols(prob.astype(bf16), d_att)
            d_kv_ref[rows, :HEAD] = (d_keys * score_scale).astype(bf16)
            d_kv_ref[rows, HEAD:] = d_vals.astype(bf16)

        @pl.when(jnp.logical_not(live))
        def _():
            d_kv_ref[rows, :] = jnp.zeros((BLOCK, 2 * HEAD), bf16)

        return 0

    each = n_blocks // groups
    for i in range(groups):
        walk = functools.partial(step, kv_refs[i], d_kv_refs[i], i * each)
        lax.fori_loop(0, each, walk, 0)
    d_gain = jnp.zeros((1, HEAD), f32)
    for h in range(HEADS):
        cols = pl.ds(h * HEAD, HEAD)
        normed, factor = rms_forward(q_pre_ref[:, cols])
        d_normed = rotate(d_q_ref[:, cols] * score_scale, cosine, -sine)
        d_gain += jnp.sum(d_normed * normed, axis=0, keepdims=True)
        d_q_pre_ref[:, cols] = rms_backward(d_normed * gain_ref[...], normed, factor).astype(bf16)
    d_gain_ref[...] = d_gain


def attend_back(columns, order, q_pre, cosine, sine, gain, pos, *kv, saved, d_att):
    rows = q_pre.shape[0]
    n_blocks = sum(v.shape[0] for v in kv) // BLOCK
    whole = pl.BlockSpec(memory_space=pltpu.VMEM)
    return pl.pallas_call(
        functools.partial(attend_back_kernel, n_blocks, columns),
        out_shape=(
            jax.ShapeDtypeStruct((rows, HEADS * HEAD), bf16),
            *[jax.ShapeDtypeStruct(v.shape, bf16) for v in kv],
            jax.ShapeDtypeStruct((1, HEAD), f32),
        ),
        in_specs=[pl.BlockSpec(memory_space=pltpu.SMEM)] + [whole] * (8 + len(kv)),
        out_specs=(whole,) * (2 + len(kv)),
        scratch_shapes=[
            pltpu.VMEM((rows, HEADS * HEAD), f32),
            pltpu.VMEM((rows, LANES), f32),
            pltpu.VMEM((rows, HEADS * HEAD), bf16),
            pltpu.VMEM((rows, HEADS * HEAD), bf16),
            pltpu.VMEM((rows, HEADS * HEAD), f32),
        ],
        cost_estimate=BRIEF,
        compiler_params=pltpu.CompilerParams(vmem_limit_bytes=10 << 20),
        name="attend_back",
    )(order, q_pre, cosine, sine, gain, pos, *saved, d_att, *kv)


def gelu_parts(gate):
    c = (2.0 / jnp.pi) ** 0.5
    square = gate * gate
    t = jnp.tanh(gate * (c + (c * 0.044715) * square))
    half = 0.5 + 0.5 * t
    act = gate * half
    slope = half + act * (1.0 - t) * (c + (3 * c * 0.044715) * square)
    return act, slope


def put_halves(part, refs):
    half = part.shape[0] // 2
    refs[0][...] = part[:half].astype(refs[0].dtype)
    refs[1][...] = part[half:].astype(refs[1].dtype)


def feed_kernel(groups, pieces, *refs):
    weights, halves, (hidden_ref, act_ref, slope_ref) = refs[pieces:-5], refs[-5:-3], refs[-3:]
    b = jnp.concatenate([r[...] for r in refs[:pieces]], axis=0)
    part = 0.0
    for i in range(groups):
        gate_ref, up_ref, down_ref = weights[3 * i : 3 * i + 3]
        gate = dot_rows(b, gate_ref[...])
        up = dot_rows(b, up_ref[...])
        act, slope = gelu_parts(gate)
        hidden_ref[i] = (act * up).astype(bf16)
        act_ref[i] = act.astype(bf16)
        slope_ref[i] = (up * slope).astype(bf16)
        part = part + dot(hidden_ref[i], down_ref[...])
    put_halves(part, halves)


def feed(b, weights, dtype):
    rows, width = sum(v.shape[0] for v in b), b[0].shape[1]
    groups, ff = len(weights) // 3, weights[0].shape[0]
    whole = pl.BlockSpec(memory_space=pltpu.VMEM)
    return pl.pallas_call(
        functools.partial(feed_kernel, groups, len(b)),
        out_shape=(
            *[jax.ShapeDtypeStruct((rows // 2, width), dtype)] * 2,
            *[jax.ShapeDtypeStruct((groups, rows, ff), bf16)] * 3,
        ),
        in_specs=[whole] * (len(b) + len(weights)),
        out_specs=(whole,) * 5,
        cost_estimate=BRIEF,
        compiler_params=pltpu.CompilerParams(vmem_limit_bytes=FEED_VMEM),
        name="feed",
    )(*b, *weights)


def feed_back_kernel(groups, pieces, act_ref, slope_ref, *refs):
    weights, halves, (d_gate_ref, d_up_ref) = refs[pieces:-4], refs[-4:-2], refs[-2:]
    d = jnp.concatenate([r[...] for r in refs[:pieces]], axis=0)
    part = 0.0
    for i in range(groups):
        gate_ref, up_ref, down_ref = weights[3 * i : 3 * i + 3]
        d_hidden = dot_rows(d, down_ref[...])
        d_gate_ref[i] = (d_hidden * slope_ref[i].astype(f32)).astype(bf16)
        d_up_ref[i] = (d_hidden * act_ref[i].astype(f32)).astype(bf16)
        part = part + dot(d_gate_ref[i], gate_ref[...]) + dot(d_up_ref[i], up_ref[...])
    put_halves(part, halves)


def feed_back(d, act, slope, weights, dtype):
    rows, width = sum(v.shape[0] for v in d), d[0].shape[1]
    groups, ff = len(weights) // 3, weights[0].shape[0]
    whole = pl.BlockSpec(memory_space=pltpu.VMEM)
    return pl.pallas_call(
        functools.partial(feed_back_kernel, groups, len(d)),
        out_shape=(
            *[jax.ShapeDtypeStruct((rows // 2, width), dtype)] * 2,
            *[jax.ShapeDtypeStruct((groups, rows, ff), bf16)] * 2,
        ),
        in_specs=[whole] * (2 + len(d) + len(weights)),
        out_specs=(whole,) * 4,
        cost_estimate=BRIEF,
        compiler_params=pltpu.CompilerParams(vmem_limit_bytes=FEED_VMEM),
        name="feed_back",
    )(act, slope, *d, *weights)


def weight_grad_kernel(index, sizes, count, pieces, *refs):
    lefts, rights, rest = refs[:count], refs[count : count + pieces], refs[count + pieces :]
    extra, outs = rest[: -len(sizes)], rest[-len(sizes) :]
    left = jnp.concatenate([v[index] for v in lefts], axis=0)
    right = jnp.concatenate([v[...] for v in rights], axis=0)
    total = dot_cols(left, right)
    if extra:
        total = total + extra[0][...].astype(f32)
    begin = 0
    for size, out in zip(sizes, outs):
        out[...] = total[begin : begin + size].astype(bf16)
        begin += size


def weight_grad(index, sizes, lefts, rights, *extra):
    rights = [piece for part in rights for piece in part]
    width = rights[0].shape[1]
    whole = pl.BlockSpec(memory_space=pltpu.VMEM)
    return pl.pallas_call(
        functools.partial(weight_grad_kernel, index, sizes, len(lefts), len(rights)),
        out_shape=tuple(jax.ShapeDtypeStruct((size, width), bf16) for size in sizes),
        in_specs=[whole] * (len(lefts) + len(rights) + len(extra)),
        out_specs=(whole,) * len(sizes),
        cost_estimate=BRIEF,
        compiler_params=pltpu.CompilerParams(vmem_limit_bytes=FEED_VMEM),
        name="weight_grad",
    )(*lefts, *rights, *extra)


def add(*terms):
    return functools.reduce(jnp.add, [t.astype(f32) for t in terms])


fence = lax.optimization_barrier


class Plain:
    def __init__(self, n):
        self.n = n
        self.rank = lax.axis_index("seq")

    def order(self):
        return jnp.arange(self.n, dtype=jnp.int32)

    def slots(self):
        return jnp.zeros(1, jnp.int32)

    def send(self, shard):
        return [shard]

    def paired(self, shards):
        return [lax.all_gather(shards[0], "seq", axis=0, tiled=True)]

    def joined(self, shard, near, far):
        return self.paired([shard])

    def columns(self, value):
        return [value]

    def restored(self, parts):
        return parts[0]

    def pair(self, shard):
        return [shard]

    def near(self, shard):
        return ()

    def far(self, near):
        return ()

    def tokens(self, shard, near, far):
        whole = lax.all_gather(shard, "seq", axis=0, tiled=True)
        return [(part,) for part in jnp.split(whole, self.n, axis=0)]

    def early(self, x, y):
        return ()

    def relay(self, far):
        return ()

    def late(self, x, y, relay):
        return ()

    def parts_sum(self, parts, early, late):
        return self.scatter(all_of([half.astype(bf16) for part in parts for half in part]))

    def across(self, value):
        return ()

    def group(self, partial, moved):
        return (partial[0],)

    def group_near(self, group):
        return ()

    def group_far(self, group):
        return ()

    def group_sum(self, group, near, far):
        return self.scatter(group[0])

    def scatter(self, partial):
        return lax.psum_scatter(
            partial.astype(bf16), "seq", scatter_dimension=0, tiled=True
        ).astype(f32)

    def projection(self, left, right, gains):
        grad = dot_cols(left, right).reshape(self.n, -1, right.shape[1])
        gains = jnp.broadcast_to(gains[None], (self.n, *gains.shape))
        return [jnp.concatenate([grad, gains], axis=1).reshape(-1, right.shape[1])]

    def line(self):
        return PlainLine()


class Cube(Plain):
    chips = (0, 2, 4, 6)
    ranks = (0, 2, 4, 6, 1, 3, 5, 7)

    def hop(self, value, bit):
        return lax.ppermute(value, "seq", [(i, i ^ bit) for i in range(8)])

    def order(self):
        return self.rank ^ jnp.array(self.ranks, dtype=jnp.int32)

    def slots(self):
        return self.order()

    def send(self, shard):
        return [shard] + [self.hop(shard, bit) for bit in self.chips[1:]]

    def joined(self, shard, near, far):
        return self.paired([shard, *near, *far])

    def paired(self, shards):
        group = all_of(shards)
        return [group, self.hop(group, 1)]

    def near(self, shard):
        return (self.hop(shard, 2), self.hop(shard, 4))

    def far(self, near):
        half = near[0].shape[0] // 2
        return (self.hop(near[1][:half], 2), self.hop(near[0][half:], 4))

    def tokens(self, shard, near, far):
        return [(shard,), *[(v,) for v in near], tuple(far)]

    def early(self, x, y):
        return (self.hop(x[0], 2), self.hop(y[1], 4))

    def relay(self, far):
        return (self.hop(far[0], 2), self.hop(far[1], 4))

    def late(self, x, y, relay):
        return (
            self.hop(add(x[1], relay[1]).astype(bf16), 2),
            self.hop(add(y[0], relay[0]).astype(bf16), 4),
        )

    def parts_sum(self, parts, early, late):
        own = parts[0]
        return all_of([add(own[0], early[0], late[1]), add(own[1], early[1], late[0])])

    def across(self, value):
        return (self.hop(value, 1),)

    def group(self, partial, moved):
        parts = jnp.split(add(partial[0], *moved), 4, axis=0)
        return (parts[0], *[p.astype(bf16) for p in parts[1:]])

    def group_near(self, group):
        return (self.hop(group[1], 2), self.hop(group[2], 4))

    def group_far(self, group):
        return (self.hop(group[3], 6),)

    def group_sum(self, group, near, far):
        return add(group[0], *near, *far)

    def select(self, size, stride):
        shape = (self.n * size, self.n * stride)
        col = lax.broadcasted_iota(jnp.int32, shape, 1)
        block, at = col // stride, col % stride
        source = self.rank ^ ((2 * block) % 8 + block // 4)
        row = lax.broadcasted_iota(jnp.int32, shape, 0)
        return ((row == source * size + at) & (at < size)).astype(bf16)

    def columns(self, value):
        moved = dot(value, self.select(value.shape[1] // self.n, value.shape[1] // self.n))
        return jnp.split(moved.astype(value.dtype), 2, axis=1)

    def restored(self, parts):
        value = jnp.concatenate(parts, axis=1)
        pick = self.select(value.shape[1] // self.n, value.shape[1] // self.n).astype(f32)
        return lax.dot_general(
            value, pick, (((1,), (1,)), ((), ())), precision=lax.Precision.HIGHEST
        )

    def pair(self, shard):
        return [shard, self.hop(shard, 1)]

    def projection(self, left, right, gains):
        size, extra = left.shape[1] // self.n, gains.shape[0]
        stride = size + extra
        moved = dot(left, self.select(size, stride)).astype(bf16)
        shape = (extra, self.n * stride)
        at = lax.broadcasted_iota(jnp.int32, shape, 1) % stride
        pick = (at == size + lax.broadcasted_iota(jnp.int32, shape, 0)).astype(bf16)
        left = jnp.concatenate([moved, pick], axis=0)
        right = jnp.concatenate([right, gains.astype(bf16)], axis=0)
        half = self.n * stride // 2
        return [dot_cols(left[:, :half], right), dot_cols(left[:, half:], right)]

    def line(self):
        return CubeLine()


class PlainLine:
    def __init__(self):
        self.chunks = []

    def step(self, beside):
        return fence(beside(()))

    def finish(self):
        return [lax.psum(c, "dp").astype(f32) for c in self.chunks]


class CubeLine(PlainLine):
    def __init__(self):
        super().__init__()
        place = lax.axis_index("dp")
        self.inner = (place == 1) | (place == 2)
        self.halves, self.totals, self.out = {}, {}, {}
        self.at = 0

    def step(self, beside):
        tick = self.at
        self.at += 1
        mine = self.chunks[tick] if tick < len(self.chunks) else None
        back, half = self.totals.get(tick - 2), self.halves.get(tick - 1)
        got = {}
        if mine is not None and back is not None and mine.shape == back.shape:
            both = jnp.where(self.inner, back, mine)
            got["in"] = lax.ppermute(both, "dp", [(0, 1), (1, 0), (2, 3), (3, 2)])
        else:
            if back is not None:
                got["out"] = lax.ppermute(back, "dp", [(1, 0), (2, 3)])
            if mine is not None:
                got["in"] = lax.ppermute(mine, "dp", [(0, 1), (3, 2)])
        if half is not None:
            got["middle"] = lax.ppermute(half, "dp", [(1, 2), (2, 1)])
        values = beside(())
        got, values, self.chunks[tick + 1 :] = fence((got, values, self.chunks[tick + 1 :]))
        if mine is not None:
            self.halves[tick] = add(mine, got["in"]).astype(bf16)
        if half is not None:
            self.totals[tick - 1] = add(half, got["middle"]).astype(bf16)
        if back is not None:
            self.out[tick - 2] = jnp.where(self.inner, back, got["out"] if "out" in got else got["in"])
        return values

    def finish(self):
        while self.at < len(self.chunks) + 2:
            self.step(lambda values: values)
        return [self.out[i].astype(f32) for i in range(len(self.chunks))]


def all_of(values):
    return jnp.concatenate(values, axis=0)


def on_device(
    kind,
    layer_input,
    segment_ids,
    position_ids,
    w_query,
    w_keyval,
    w_out,
    w_gate,
    w_up,
    w_down,
    g_input,
    g_post_attn,
    g_pre_ffn,
    g_post_ffn,
    g_query,
    g_key,
    out_grad,
):
    n = lax.axis_size("seq")
    comm = kind(n)
    rows = layer_input.shape[1]
    width = layer_input.shape[2]
    ff = w_gate.shape[1]
    row_offset = comm.rank * rows

    x = layer_input[0].astype(f32)
    positions = position_ids[0]
    keyval_sent = comm.send(w_keyval)
    a_normed, a_factor = rms_forward(x)
    a_low = (a_normed * g_input).astype(bf16)
    a_columns = comm.columns(a_low)
    angles = rope_angles(positions, HEAD)
    cosine, sine = jnp.cos(angles), jnp.sin(angles)
    keyval_sent, a_columns, w_query = fence((keyval_sent, a_columns, w_query))
    query_near = comm.near(w_query)
    keyval_blocks = comm.paired(keyval_sent)
    kv_pre = add(*[dot(a, w) for a, w in zip(a_columns, keyval_blocks)])
    k_hat, k_factor = rms_forward(kv_pre[:, :HEAD])
    k_low = rotate(k_hat * g_key, cosine, sine).astype(bf16)
    kv_low = jnp.concatenate([k_low, kv_pre[:, HEAD:].astype(bf16)], axis=1)
    kv_low, query_near = fence((kv_low, query_near))
    kv_near = comm.near(kv_low)
    query_far = comm.far(query_near)
    kv_near, query_near, query_far, w_out = fence((kv_near, query_near, query_far, w_out))
    kv_far = comm.far(kv_near)
    query_blocks = comm.joined(w_query, query_near, query_far)
    q_pre = add(*[dot(a, w) for a, w in zip(a_columns, query_blocks)])
    kv_far, q_pre, w_out = fence((kv_far, q_pre, w_out))
    out_near = comm.near(w_out)
    kv_blocks = comm.joined(kv_low, kv_near, kv_far)
    kv_blocks, out_near = fence((kv_blocks, out_near))
    out_far = comm.far(out_near)
    order = jnp.concatenate(
        [comm.order(), row_offset[None], (row_offset - positions[0])[None], comm.slots()]
    ).astype(jnp.int32)
    head_args = (
        comm.slots().shape[0],
        order,
        q_pre,
        cosine,
        sine,
        g_query[None],
        positions[:, None],
        *kv_blocks,
    )
    att_low, inverse = attend(*head_args)
    out_far, att_low, w_gate, w_up, w_down = fence((out_far, att_low, w_gate, w_up, w_down))
    weights = [comm.pair(w) for w in (w_gate.T, w_up.T, w_down)]
    weights = [w[i] for i in range(len(weights[0])) for w in weights]
    groups = len(weights) // 3
    out_blocks = comm.joined(w_out, out_near, out_far)
    att_columns = jnp.split(att_low, len(out_blocks), axis=1)
    attn = add(*[dot(v, w) for v, w in zip(att_columns, out_blocks)])
    attn_normed, attn_factor = rms_forward(attn)
    middle = x + attn_normed * g_post_attn
    b_normed, b_factor = rms_forward(middle)
    b_low = (b_normed * g_pre_ffn).astype(bf16)
    b_low, weights = fence((b_low, weights))

    near = comm.near(b_low)
    kept = [feed((b_low,), weights, f32)]
    kept, near = fence((kept, near))
    far = comm.far(near)
    b_list = comm.tokens(b_low, near, far)
    kept += [feed(part, weights, bf16) for part in b_list[1:-1]]
    kept, far, tail = fence((kept, far, b_list[-1]))
    b_list[-1] = tail
    early = comm.early(kept[1][:2], kept[2][:2])
    kept.append(feed(tail, weights, bf16))
    kept, early = fence((kept, early))
    parts = [v[:2] for v in kept]
    hidden, acts, slopes = [[v[i] for v in kept] for i in (2, 3, 4)]
    relay = comm.relay(parts[-1])
    late = comm.late(parts[1], parts[2], relay)
    ffn = comm.parts_sum(parts, early, late)
    ffn_normed, ffn_factor = rms_forward(ffn)
    layer_out = (middle + ffn_normed * g_post_ffn).astype(bf16)

    g = out_grad[0]
    d_ffn = rms_backward(g * g_post_ffn, ffn_normed, ffn_factor).astype(bf16)
    d_ffn, ffn_normed = fence((d_ffn, ffn_normed))
    line = comm.line()
    thirds = [ff // 3] * 3

    def back(part, i):
        return feed_back(part, acts[i], slopes[i], weights, bf16 if i else f32)

    def other_half(lefts, rights):
        return weight_grad(1, [ff], lefts, rights) if groups > 1 else ()

    near = comm.near(d_ffn)
    gain_post_ffn = jnp.sum(g * ffn_normed, axis=0)
    kept = [back((d_ffn,), 0)]
    kept, near, gain_post_ffn = fence((kept, near, gain_post_ffn))
    far = comm.far(near)
    d_list = comm.tokens(d_ffn, near, far)
    last = len(d_list) - 1
    kept += [back(d_list[i], i) for i in range(1, last)]
    kept, far, tail = fence((kept, far, d_list[-1]))
    d_list[-1] = tail

    early = comm.early(kept[1][:2], kept[2][:2])
    other = [comm.hop(v, 1) for v in other_half(hidden, d_list)]
    kept.append(back(tail, last))
    kept, early, other = fence((kept, early, other))
    parts = [v[:2] for v in kept]
    d_gate, d_up = [[v[i] for v in kept] for i in (2, 3)]
    line.chunks += weight_grad(0, thirds, hidden, d_list, *other)

    line.chunks, parts, d_gate, d_up, a_late = fence((line.chunks, parts, d_gate, d_up, a_low))

    def beside(_):
        relay = comm.relay(parts[-1])
        late = comm.late(parts[1], parts[2], relay)
        others = other_half(d_gate, b_list), other_half(d_up, b_list)
        return late, others, d_gate, d_up, parts, early

    late, others, d_gate, d_up, parts, early = line.step(beside)

    def beside(_):
        other, other_up = [[comm.hop(v, 1) for v in values] for values in others]
        d_b = comm.parts_sum(parts, early, late)
        gain_pre_ffn = jnp.sum(d_b * b_normed, axis=0)
        d_middle = g + rms_backward(d_b * g_pre_ffn, b_normed, b_factor)
        gain_post_attn = jnp.sum(d_middle * attn_normed, axis=0)
        d_attn = rms_backward(d_middle * g_post_attn, attn_normed, attn_factor).astype(bf16)
        d_att = jnp.concatenate([dot_rows(d_attn, w).astype(bf16) for w in out_blocks], axis=1)
        grads = weight_grad(0, thirds, d_gate, b_list, *other)
        return list(grads), d_up, other_up, d_middle, d_attn, d_att, (gain_post_attn, gain_pre_ffn)

    grads, d_up, other_up, d_middle, d_attn, d_att, gains = line.step(beside)
    gain_post_attn, gain_pre_ffn = gains
    line.chunks += grads

    def beside(_):
        heads = attend_back(*head_args, saved=(att_low, inverse), d_att=d_att)
        return heads, d_up, d_attn

    (d_q_pre, *d_kv_blocks, gain_query), d_up, d_attn = line.step(beside)

    def beside(_):
        group = comm.group(d_kv_blocks, comm.across(d_kv_blocks[-1]))
        near = comm.group_near(group)
        grads = weight_grad(0, thirds, d_up, b_list, *other_up)
        return group, near, list(grads), d_attn, a_late

    group, near, grads, d_attn, a_late = line.step(beside)
    line.chunks += grads

    def beside(_):
        d_kv = comm.group_sum(group, near, comm.group_far(group))
        d_k_normed = rotate(d_kv[:, :HEAD], cosine, -sine)
        gain_key = jnp.sum(d_k_normed * k_hat, axis=0)
        d_k_pre = rms_backward(d_k_normed * g_key, k_hat, k_factor)
        d_kv_pre = jnp.concatenate([d_k_pre, d_kv[:, HEAD:]], axis=1).astype(bf16)
        d_a = comm.restored(
            [
                dot_rows(d_q_pre, query) + dot_rows(d_kv_pre, keyval)
                for query, keyval in zip(query_blocks, keyval_blocks)
            ]
        )
        gain_input = jnp.sum(d_a * a_normed, axis=0)
        grad_out = [dot_cols(v, d_attn) for v in att_columns]
        return d_kv_pre, d_a, (gain_input, gain_key), grad_out, a_late

    d_kv_pre, d_a, (gain_input, gain_key), grad_out, a_late = line.step(beside)

    def beside(_):
        out_moved = comm.across(grad_out[-1].astype(bf16))
        d_qkv = jnp.concatenate([d_q_pre, d_kv_pre], axis=1)
        gains = [gain_input, gain_post_attn, gain_pre_ffn, gain_post_ffn]
        gains.append(jnp.concatenate([gain_query[0], gain_key]))
        gains = [jnp.pad(v, (0, d_qkv.shape[1] - v.shape[0])) for v in gains]
        gains = jnp.pad(jnp.stack(gains), ((0, 16 - len(gains)), (0, 0)))
        grad_qkv = comm.projection(a_late, d_qkv, gains)
        return comm.group(grad_out, out_moved), grad_qkv, d_a

    out_group, grad_qkv, d_a = line.step(beside)

    def beside(_):
        qkv_moved = comm.across(grad_qkv[-1].astype(bf16))
        out_near = comm.group_near(out_group)
        d_input = d_middle + rms_backward(d_a * g_input, a_normed, a_factor)
        return comm.group(grad_qkv, qkv_moved), out_group, out_near, d_input

    group, out_group, out_near, d_input = line.step(beside)

    def beside(_):
        return group, comm.group_near(group), comm.group_far(out_group)

    group, near, out_far = line.step(beside)
    total_out = comm.group_sum(out_group, out_near, out_far).astype(bf16)

    def beside(_):
        return comm.group_far(group), near, total_out

    far, near, total_out = line.step(beside)
    line.chunks += [comm.group_sum(group, near, far).astype(bf16), total_out]
    *done, tail, total_out = line.finish()
    down, gate, up = all_of(done[:3]), all_of(done[3:6]), all_of(done[6:])
    shard = width // n

    def mine(row, at, size):
        return lax.dynamic_slice_in_dim(tail[shard + row], at + comm.rank * size, size)

    names = [mine(i, 0, shard) for i in range(4)]
    names += [mine(4, i * HEAD, HEAD // n) for i in range(2)]
    return (
        layer_out[None],
        d_input[None],
        tail[:shard, : HEADS * HEAD],
        tail[:shard, HEADS * HEAD :],
        total_out,
        gate.T,
        up.T,
        down,
        *names,
    )


def solution(mesh):
    cube = mesh.shape["seq"] == 8 and mesh.shape["dp"] == 4
    in_specs = (
        P("dp", "seq", None),
        P("dp", None),
        P("dp", "seq"),
        P("seq", None),
        P("seq", None),
        P("seq", None),
        P(None, "seq"),
        P(None, "seq"),
        P("seq", None),
        P(),
        P(),
        P(),
        P(),
        P(),
        P(),
        P("dp", "seq", None),
    )
    out_specs = (
        P("dp", "seq", None),
        P("dp", "seq", None),
        P("seq", None),
        P("seq", None),
        P("seq", None),
        P(None, "seq"),
        P(None, "seq"),
        P("seq", None),
        P("seq"),
        P("seq"),
        P("seq"),
        P("seq"),
        P("seq"),
        P("seq"),
    )
    return jax.shard_map(
        functools.partial(on_device, Cube if cube else Plain),
        mesh=mesh,
        in_specs=in_specs,
        out_specs=out_specs,
        check_vma=False,
    )
```

time: 485 us -> 428 us (0.88)
  waiting for transfers between devices: 227 us -> 158 us
  other arithmetic: 30.4 us -> 41.7 us
  starting transfers between devices: 101 us -> 109 us
  Pallas kernels: 66.9 us -> 59.7 us
    ppermute x26, waiting for transfers between devices: 92 us -> 57 us  [the longest x4 28.5 us: step(): got['out'] = lax.ppermute(back, 'dp', [(1, 0), (2, 3)])]
    ppermute x46 -> x57, waiting for transfers between devices: 135 us -> 101 us  [hop(): return lax.ppermute(value, 'seq', [(i, i ^ bit) for i in range(8)])]
    ppermute x46 -> x57, starting transfers between devices: 43.2 us -> 58.9 us  [hop(): return lax.ppermute(value, 'seq', [(i, i ^ bit) for i in range(8)])]
    ppermute x26, starting transfers between devices: 57.6 us -> 50.4 us  [the longest x7 21.1 us: step(): got['in'] = lax.ppermute(both, 'dp', [(0, 1), (1, 0), (2, 3), (3, 2)])]
    select_n x16, other arithmetic: 3.7 us -> 10.1 us  [the longest x9 6.04 us: step(): jnp.where(self.inner, back, got['out'] if 'out' in got else got['in'])]
    pallas_call x6, Pallas kernels: 22.3 us -> 16.3 us  [weight_grad(): pl.pallas_call(functools.partial(weight_grad_kernel, index, sizes, len(le...]
    convert_element_type x19 -> x24, other arithmetic: 6.54 us -> 9.89 us  [the longest x11 5 us: step(): self.halves[tick] = add(mine, got['in']).astype(bf16)]
    unnamed x268 -> x275, local copies, waits for them, and re-layouts: 23.1 us -> 20.8 us
  transfers between devices with their start and end apart: 72 -> 83, of which waited for: 35 -> 44; matrix products, arithmetic and copies ran while one was open for 9% -> 15% of each run, Pallas kernels for 12% -> 13%
where the time goes in v2:
time: 428 us; the launch traced here: 422 us
  waiting for transfers between devices  158 us (37%)
  starting transfers between devices  109 us (25%)
  Pallas kernels  59.7 us (14%)
  other arithmetic  41.7 us (10%)
  local copies, waits for them, and re-layouts  27.2 us (6%)
  matrix products  21.4 us (5%)
    ppermute x57, waiting for transfers between devices, hop(): return lax.ppermute(value, 'seq', [(i, i ^ bit) for i in range(8)])  101 us
    ppermute x57, starting transfers between devices, hop(): return lax.ppermute(value, 'seq', [(i, i ^ bit) for i in range(8)])  58.9 us
    ppermute x4, waiting for transfers between devices, step(): got['out'] = lax.ppermute(back, 'dp', [(1, 0), (2, 3)])  28.5 us
    ppermute x7, starting transfers between devices, step(): got['in'] = lax.ppermute(both, 'dp', [(0, 1), (1, 0), (2, 3), (3, 2)])  21.1 us
    unnamed x275, local copies, waits for them, and re-layouts  20.8 us
    ppermute x7, waiting for transfers between devices, step(): got['in'] = lax.ppermute(both, 'dp', [(0, 1), (1, 0), (2, 3), (3, 2)])  19.9 us
    pallas_call x4, Pallas kernels, feed(): pl.pallas_call(functools.partial(feed_kernel, groups, len(b)), out_shape=...  18.1 us
    pallas_call x4, Pallas kernels, feed_back(): pl.pallas_call(functools.partial(feed_back_kernel, groups, len(d)), out_s...  17.3 us
  transfers between devices with their start and end apart: 83, of which 44 were waited for; matrix products, arithmetic and copies ran while one was open for 15% of the time, Pallas kernels for 13%

profile of v2, /device:TPU:0, one launch (start us, length us, event | category | flops | bytes accessed | tf_op | source)
XLA Modules:
  0.0 421.8 jit_solution(2091217488152297713)
XLA Ops:
  17.0 5.1 %collective-permute-done.4 = bf16[144,1024]{1,0:T(8,128)(2,1)S(1)} collective-permute-done((bf16[144,1024]{1,0:T(8,128)(2,1)S(1)}, bf16[144,1024]{1,0:T(8,128)(2,1)S(1)}, u32[]{:S(2)}, u32[]{:S(2)}) %collective-permute-start.4) | collective-permute-done | bytes 294944 | tf_op jit(solution)/shard_map/ppermute | solution.py:460
  27.2 6.5 %collective-permute-done.8 = bf16[72,1024]{1,0:T(8,128)(2,1)S(1)} collective-permute-done((bf16[72,1024]{1,0:T(8,128)(2,1)S(1)}, bf16[72,1024]{1,0:T(8,128)(2,1)S(1)}, u32[]{:S(2)}, u32[]{:S(2)}) %collective-permute-start.8) | collective-permute-done | bytes 147488 | tf_op jit(solution)/shard_map/ppermute | solution.py:460
  46.6 6.0 %collective-permute-done.14 = bf16[128,1152]{1,0:T(8,128)(2,1)S(1)} collective-permute-done((bf16[128,1152]{1,0:T(8,128)(2,1)}, bf16[128,1152]{1,0:T(8,128)(2,1)S(1)}, u32[]{:S(2)}, u32[]{:S(2)}) %collective-permute-start.14) | collective-permute-done | bytes 294944 | tf_op jit(solution)/shard_map/ppermute | solution.py:460
  55.4 3.5 attend.1
  74.5 4.5 %feed.4 = (f32[128,1152]{1,0:T(8,128)S(1)}, f32[128,1152]{1,0:T(8,128)S(1)}, bf16[2,256,864]{2,1,0:T(8,128)(2,1)S(1)}, bf16[2,256,864]{2,1,0:T(8,128)(2,1)S(1)}, bf16[2,256,864]{2,1,0:T(8,128)(2,1)S(1)}) custom-call(bf16[256,1152]{1,0:T(8,128)(2,1)S(1)} %multiply_convert_fusion.2.refs_0_.refs_4_, bf16[864,1152]{1,0:T(8,128)(2,1)S(1)} %bitcast.68, ...), custom_call_target="tpu_custom_call" | custom-call | flops 1 | bytes 1 | tf_op jit(solution)/shard_map/feed/pallas_call | solution.py:294
  79.0 8.0 %collective-permute-done.22.refs_0_.refs_5_ = bf16[256,1152]{1,0:T(8,128)(2,1)S(1)} collective-permute-done((bf16[256,1152]{1,0:T(8,128)(2,1)S(1)}, bf16[256,1152]{1,0:T(8,128)(2,1)S(1)}, u32[]{:S(2)}, u32[]{:S(2)}) %collective-permute-start.22) | collective-permute-done | bytes 589856 | tf_op jit(solution)/shard_map/ppermute | solution.py:460
  91.8 4.5 %feed.5 = (bf16[128,1152]{1,0:T(8,128)(2,1)S(1)}, bf16[128,1152]{1,0:T(8,128)(2,1)S(1)}, bf16[2,256,864]{2,1,0:T(8,128)(2,1)S(1)}, bf16[2,256,864]{2,1,0:T(8,128)(2,1)S(1)}, bf16[2,256,864]{2,1,0:T(8,128)(2,1)S(1)}) custom-call(bf16[256,1152]{1,0:T(8,128)(2,1)S(1)} %collective-permute-done.22.refs_0_.refs_5_, bf16[864,1152]{1,0:T(8,128)(2,1)S(1)} %bitcast.69, ...), custom_call_target="tpu_custom_call" | custom-call | flops 1 | bytes 1 | tf_op jit(solution)/shard_map/feed/pallas_call | solution.py:294
  96.3 4.7 %feed.6 = (bf16[128,1152]{1,0:T(8,128)(2,1)S(1)}, bf16[128,1152]{1,0:T(8,128)(2,1)S(1)}, bf16[2,256,864]{2,1,0:T(8,128)(2,1)S(1)}, bf16[2,256,864]{2,1,0:T(8,128)(2,1)S(1)}, bf16[2,256,864]{2,1,0:T(8,128)(2,1)S(1)}) custom-call(bf16[256,1152]{1,0:T(8,128)(2,1)S(1)} %collective-permute-done.23.refs_0_.refs_6_, bf16[864,1152]{1,0:T(8,128)(2,1)S(1)} %bitcast.70, ...), custom_call_target="tpu_custom_call" | custom-call | flops 1 | bytes 1 | tf_op jit(solution)/shard_map/feed/pallas_call | solution.py:294
  101.9 4.5 %feed.7 = (bf16[128,1152]{1,0:T(8,128)(2,1)S(1)}, bf16[128,1152]{1,0:T(8,128)(2,1)S(1)}, bf16[2,256,864]{2,1,0:T(8,128)(2,1)S(1)}, bf16[2,256,864]{2,1,0:T(8,128)(2,1)S(1)}, bf16[2,256,864]{2,1,0:T(8,128)(2,1)S(1)}) custom-call(bf16[128,1152]{1,0:T(8,128)(2,1)S(1)} %collective-permute-done.24.refs_0_.refs_7_, ...), custom_call_target="tpu_custom_call" | custom-call | flops 1 | bytes 1 | tf_op jit(solution)/shard_map/feed/pallas_call | solution.py:294
  110.8 4.7 %collective-permute-done.30 = bf16[128,1152]{1,0:T(8,128)(2,1)S(1)} collective-permute-done((bf16[128,1152]{1,0:T(8,128)(2,1)S(1)}, bf16[128,1152]{1,0:T(8,128)(2,1)S(1)}, u32[]{:S(2)}, u32[]{:S(2)}) %collective-permute-start.30) | collective-permute-done | bytes 294944 | tf_op jit(solution)/shard_map/ppermute | solution.py:460
  130.1 4.3 %feed_back.4 = (f32[128,1152]{1,0:T(8,128)S(1)}, f32[128,1152]{1,0:T(8,128)S(1)}, bf16[2,256,864]{2,1,0:T(8,128)(2,1)S(1)}, bf16[2,256,864]{2,1,0:T(8,128)(2,1)S(1)}) custom-call(bf16[2,256,864]{2,1,0:T(8,128)(2,1)S(1)} %get-tuple-element.424.act_ref, bf16[2,256,864]{2,1,0:T(8,128)(2,1)S(1)} %get-tuple-element.425.slope_ref, ...), custom_call_target="tpu_custom_call" | custom-call | flops 1 | bytes 1 | tf_op jit(solution)/shard_map/feed_back/pallas_call | solution.py:325
  137.1 3.7 collective-permute-done.33.refs_0_.refs_6_
  143.5 4.5 %feed_back.5 = (bf16[128,1152]{1,0:T(8,128)(2,1)S(1)}, bf16[128,1152]{1,0:T(8,128)(2,1)S(1)}, bf16[2,256,864]{2,1,0:T(8,128)(2,1)S(1)}, bf16[2,256,864]{2,1,0:T(8,128)(2,1)S(1)}) custom-call(bf16[2,256,864]{2,1,0:T(8,128)(2,1)S(1)} %get-tuple-element.437.act_ref, bf16[2,256,864]{2,1,0:T(8,128)(2,1)S(1)} %get-tuple-element.438.slope_ref, ...), custom_call_target="tpu_custom_call" | custom-call | flops 1 | bytes 1 | tf_op jit(solution)/shard_map/feed_back/pallas_call | solution.py:325
  149.0 4.3 %feed_back.6 = (bf16[128,1152]{1,0:T(8,128)(2,1)S(1)}, bf16[128,1152]{1,0:T(8,128)(2,1)S(1)}, bf16[2,256,864]{2,1,0:T(8,128)(2,1)S(1)}, bf16[2,256,864]{2,1,0:T(8,128)(2,1)S(1)}) custom-call(bf16[2,256,864]{2,1,0:T(8,128)(2,1)S(1)} %get-tuple-element.443.act_ref, bf16[2,256,864]{2,1,0:T(8,128)(2,1)S(1)} %get-tuple-element.444.slope_ref, ...), custom_call_target="tpu_custom_call" | custom-call | flops 1 | bytes 1 | tf_op jit(solution)/shard_map/feed_back/pallas_call | solution.py:325
  157.6 4.3 %feed_back.7 = (bf16[128,1152]{1,0:T(8,128)(2,1)S(1)}, bf16[128,1152]{1,0:T(8,128)(2,1)S(1)}, bf16[2,256,864]{2,1,0:T(8,128)(2,1)S(1)}, bf16[2,256,864]{2,1,0:T(8,128)(2,1)S(1)}) custom-call(bf16[2,256,864]{2,1,0:T(8,128)(2,1)S(1)} %get-tuple-element.463.act_ref, bf16[2,256,864]{2,1,0:T(8,128)(2,1)S(1)} %get-tuple-element.464.slope_ref, ...), custom_call_target="tpu_custom_call" | custom-call | flops 1 | bytes 1 | tf_op jit(solution)/shard_map/feed_back/pallas_call | solution.py:325
  166.7 3.8 weight_grad.7
  176.8 3.7 collective-permute-done.40
  216.4 4.6 %attend_back.1 = (bf16[256,1024]{1,0:T(8,128)(2,1)S(1)}, bf16[1024,512]{1,0:T(8,128)(2,1)S(1)}, bf16[1024,512]{1,0:T(8,128)(2,1)S(1)}, f32[1,256]{1,0:T(1,128)S(1)}) custom-call(s32[18]{0:T(128)S(1)} %pad_add_fusion.order_ref, f32[256,1024]{1,0:T(8,128)S(1)} %convolution_add_fusion.1.q_pre_ref, f32[256,128]{1,0:T(8,128)S(1)} %copy-done.40, ...), custom_call_target="tpu_custom_call" | custom-call | flops 1 | bytes 1 | tf_op jit(solution)/shard_map/attend_back/pallas_call | solution.py:236
  221.1 8.9 %collective-permute-done.48 = bf16[288,1152]{1,0:T(8,128)(2,1)S(1)} collective-permute-done((bf16[288,1152]{1,0:T(8,128)(2,1)S(1)}, bf16[288,1152]{1,0:T(8,128)(2,1)S(1)}, u32[]{:S(2)}, u32[]{:S(2)}) %collective-permute-start.48) | collective-permute-done | bytes 663584 | tf_op jit(solution)/shard_map/ppermute | solution.py:585
  230.2 3.9 collective-permute-start.50
  241.6 8.1 %collective-permute-done.50 = bf16[288,1152]{1,0:T(8,128)(2,1)S(1)} collective-permute-done((bf16[288,1152]{1,0:T(8,128)(2,1)S(1)}, bf16[288,1152]{1,0:T(8,128)(2,1)S(1)}, u32[]{:S(2)}, u32[]{:S(2)}) %collective-permute-start.50) | collective-permute-done | bytes 663584 | tf_op jit(solution)/shard_map/ppermute | solution.py:585
  251.3 3.9 collective-permute-start.55
  270.0 4.2 fusion.54
  305.0 4.5 %collective-permute-done.64 = bf16[128,1152]{1,0:T(8,128)(2,1)S(1)} collective-permute-done((bf16[128,1152]{1,0:T(8,128)(2,1)S(1)}, bf16[128,1152]{1,0:T(8,128)(2,1)S(1)}, u32[]{:S(2)}, u32[]{:S(2)}) %collective-permute-start.64) | collective-permute-done | bytes 294944 | tf_op jit(solution)/shard_map/ppermute | solution.py:460
  313.5 5.2 %collective-permute-start.66 = (bf16[288,1152]{1,0:T(8,128)(2,1)S(1)}, bf16[288,1152]{1,0:T(8,128)(2,1)S(1)}, u32[]{:S(2)}, u32[]{:S(2)}) collective-permute-start(bf16[288,1152]{1,0:T(8,128)(2,1)S(1)} %broadcast_select_fusion.10), channel_id=1, source_target_pairs={{0,8},{8,0},{16,24},{24,16},{1,9},{9,1},{17,25},{25,17},{2,10},{10... | collective-permute-start | bytes 1990664 | tf_op jit(solution)/shard_map/ppermute | solution.py:585
  326.3 14.4 %collective-permute-done.70 = bf16[128,1152]{1,0:T(8,128)(2,1)S(1)} collective-permute-done((bf16[128,1152]{1,0:T(8,128)(2,1)S(1)}, bf16[128,1152]{1,0:T(8,128)(2,1)S(1)}, u32[]{:S(2)}, u32[]{:S(2)}) %collective-permute-start.70) | collective-permute-done | bytes 294944 | tf_op jit(solution)/shard_map/ppermute | solution.py:460
  348.5 7.6 %collective-permute-done.73 = bf16[160,1536]{1,0:T(8,128)(2,1)S(1)} collective-permute-done((bf16[160,1536]{1,0:T(8,128)(2,1)S(1)}, bf16[160,1536]{1,0:T(8,128)(2,1)S(1)}, u32[]{:S(2)}, u32[]{:S(2)}) %collective-permute-start.73) | collective-permute-done | bytes 491552 | tf_op jit(solution)/shard_map/ppermute | solution.py:460
  359.3 8.3 %collective-permute-start.74 = (bf16[160,1536]{1,0:T(8,128)(2,1)S(1)}, bf16[160,1536]{1,0:T(8,128)(2,1)S(1)}, u32[]{:S(2)}, u32[]{:S(2)}) collective-permute-start(bf16[160,1536]{1,0:T(8,128)(2,1)S(1)} %add_convert_fusion.21), channel_id=1, source_target_pairs={{0,8},{24,16},{1,9},{25,17},{2,10},{26,18},{3,11},{27,19},{4,12},{... | collective-permute-start | bytes 1474568 | tf_op jit(solution)/shard_map/ppermute | solution.py:590
  367.9 6.7 %collective-permute-done.74 = bf16[160,1536]{1,0:T(8,128)(2,1)S(1)} collective-permute-done((bf16[160,1536]{1,0:T(8,128)(2,1)S(1)}, bf16[160,1536]{1,0:T(8,128)(2,1)S(1)}, u32[]{:S(2)}, u32[]{:S(2)}) %collective-permute-start.74) | collective-permute-done | bytes 491552 | tf_op jit(solution)/shard_map/ppermute | solution.py:590
  383.2 9.6 %collective-permute-done.79 = bf16[288,1152]{1,0:T(8,128)(2,1)S(1)} collective-permute-done((bf16[288,1152]{1,0:T(8,128)(2,1)S(1)}, bf16[288,1152]{1,0:T(8,128)(2,1)S(1)}, u32[]{:S(2)}, u32[]{:S(2)}) %collective-permute-start.79) | collective-permute-done | bytes 663584 | tf_op jit(solution)/shard_map/ppermute | solution.py:588
  397.3 13.0 %collective-permute-done.81 = bf16[160,1536]{1,0:T(8,128)(2,1)S(1)} collective-permute-done((bf16[160,1536]{1,0:T(8,128)(2,1)S(1)}, bf16[160,1536]{1,0:T(8,128)(2,1)S(1)}, u32[]{:S(2)}, u32[]{:S(2)}) %collective-permute-start.81) | collective-permute-done | bytes 491552 | tf_op jit(solution)/shard_map/ppermute | solution.py:588
  416.5 4.2 collective-permute-done.82
  (583 shorter events, 230.5 us)
Async XLA Ops:
  71.2 15.9 %collective-permute-start.22 = (bf16[256,1152]{1,0:T(8,128)(2,1)S(1)}, bf16[256,1152]{1,0:T(8,128)(2,1)S(1)}, u32[]{:S(2)}, u32[]{:S(2)}) collective-permute-start(bf16[256,1152]{1,0:T(8,128)(2,1)S(1)} %multiply_convert_fusion.2.refs_0_.refs_4_), channel_id=1, source_target_pairs={{0,2},{1,3},{2,0},{3,1},{4,6},{5,7},{6,4},{7,5},{8,10},{9,11},{10,... | collective-permute-start | bytes 1769480 | tf_op jit(solution)/shard_map/ppermute | solution.py:460
  73.4 15.1 %collective-permute-start.23 = (bf16[256,1152]{1,0:T(8,128)(2,1)S(1)}, bf16[256,1152]{1,0:T(8,128)(2,1)S(1)}, u32[]{:S(2)}, u32[]{:S(2)}) collective-permute-start(bf16[256,1152]{1,0:T(8,128)(2,1)S(1)} %multiply_convert_fusion.2.refs_0_.refs_4_), channel_id=1, source_target_pairs={{0,4},{1,5},{2,6},{3,7},{4,0},{5,1},{6,2},{7,3},{8,12},{9,13},{10,... | collective-permute-start | bytes 1769480 | tf_op jit(solution)/shard_map/ppermute | solution.py:460
  88.5 12.5 %collective-permute-start.24 = (bf16[128,1152]{1,0:T(8,128)(2,1)S(1)}, bf16[128,1152]{1,0:T(8,128)(2,1)S(1)}, u32[]{:S(2)}, u32[]{:S(2)}) collective-permute-start(bf16[128,1152]{1,0:T(8,128)(2,1)S(1)} %slice.99), channel_id=1, source_target_pairs={{0,2},{1,3},{2,0},{3,1},{4,6},{5,7},{6,4},{7,5},{8,10},{9,11},{10,... | collective-permute-start | bytes 884744 | tf_op jit(solution)/shard_map/ppermute | solution.py:460
  128.1 12.8 %collective-permute-start.33 = (bf16[256,1152]{1,0:T(8,128)(2,1)S(1)}, bf16[256,1152]{1,0:T(8,128)(2,1)S(1)}, u32[]{:S(2)}, u32[]{:S(2)}) collective-permute-start(bf16[256,1152]{1,0:T(8,128)(2,1)S(1)} %get-tuple-element.423.refs_0_.refs_4_), channel_id=1, source_target_pairs={{0,4},{1,5},{2,6},{3,7},{4,0},{5,1},{6,2},{7,3},{8,12},{9,13},{10,... | collective-permute-start | bytes 1769480 | tf_op jit(solution)/shard_map/ppermute | solution.py:460
  140.9 12.4 %collective-permute-start.34 = (bf16[128,1152]{1,0:T(8,128)(2,1)S(1)}, bf16[128,1152]{1,0:T(8,128)(2,1)S(1)}, u32[]{:S(2)}, u32[]{:S(2)}) collective-permute-start(bf16[128,1152]{1,0:T(8,128)(2,1)S(1)} %slice.101), channel_id=1, source_target_pairs={{0,2},{1,3},{2,0},{3,1},{4,6},{5,7},{6,4},{7,5},{8,10},{9,11},{10,... | collective-permute-start | bytes 884744 | tf_op jit(solution)/shard_map/ppermute | solution.py:460
  172.5 24.3 %collective-permute-start.39 = (bf16[288,1152]{1,0:T(8,128)(2,1)}, bf16[288,1152]{1,0:T(8,128)(2,1)}, u32[]{:S(2)}, u32[]{:S(2)}) collective-permute-start(bf16[288,1152]{1,0:T(8,128)(2,1)} %get-tuple-element.487), channel_id=1, source_target_pairs={{0,8},{24,16},{1,9},{25,17},{2,10},{26,18},{3,11},{27,19},{4,12},{... | collective-permute-start | bytes 1990664 | tf_op jit(solution)/shard_map/ppermute | solution.py:590
  181.3 15.6 %collective-permute-start.41 = (bf16[128,1152]{1,0:T(8,128)(2,1)}, bf16[128,1152]{1,0:T(8,128)(2,1)}, u32[]{:S(2)}, u32[]{:S(2)}) collective-permute-start(bf16[128,1152]{1,0:T(8,128)(2,1)} %add_convert_fusion.26), channel_id=1, source_target_pairs={{0,2},{1,3},{2,0},{3,1},{4,6},{5,7},{6,4},{7,5},{8,10},{9,11},{10,... | collective-permute-start | bytes 884744 | tf_op jit(solution)/shard_map/ppermute | solution.py:460
  196.9 15.8 %collective-permute-start.44 = (bf16[288,1152]{1,0:T(8,128)(2,1)S(1)}, bf16[288,1152]{1,0:T(8,128)(2,1)S(1)}, u32[]{:S(2)}, u32[]{:S(2)}) collective-permute-start(bf16[288,1152]{1,0:T(8,128)(2,1)S(1)} %copy-done.42), channel_id=1, source_target_pairs={{0,8},{24,16},{1,9},{25,17},{2,10},{26,18},{3,11},{27,19},{4,12},{... | collective-permute-start | bytes 1990664 | tf_op jit(solution)/shard_map/ppermute | solution.py:590
  199.8 12.9 %collective-permute-start.45 = (bf16[288,1152]{1,0:T(8,128)(2,1)S(1)}, bf16[288,1152]{1,0:T(8,128)(2,1)S(1)}, u32[]{:S(2)}, u32[]{:S(2)}) collective-permute-start(bf16[288,1152]{1,0:T(8,128)(2,1)S(1)} %add_convert_fusion.17), channel_id=1, source_target_pairs={{8,16},{16,8},{9,17},{17,9},{10,18},{18,10},{11,19},{19,11},{12,20... | collective-permute-start | bytes 1990664 | tf_op jit(solution)/shard_map/ppermute | solution.py:592
  213.0 17.0 %collective-permute-start.48 = (bf16[288,1152]{1,0:T(8,128)(2,1)S(1)}, bf16[288,1152]{1,0:T(8,128)(2,1)S(1)}, u32[]{:S(2)}, u32[]{:S(2)}) collective-permute-start(bf16[288,1152]{1,0:T(8,128)(2,1)S(1)} %broadcast_select_fusion.15), channel_id=1, source_target_pairs={{0,8},{8,0},{16,24},{24,16},{1,9},{9,1},{17,25},{25,17},{2,10},{10... | collective-permute-start | bytes 1990664 | tf_op jit(solution)/shard_map/ppermute | solution.py:585
  214.9 15.1 %collective-permute-start.49 = (bf16[288,1152]{1,0:T(8,128)(2,1)S(1)}, bf16[288,1152]{1,0:T(8,128)(2,1)S(1)}, u32[]{:S(2)}, u32[]{:S(2)}) collective-permute-start(bf16[288,1152]{1,0:T(8,128)(2,1)S(1)} %add_convert_fusion.16), channel_id=1, source_target_pairs={{8,16},{16,8},{9,17},{17,9},{10,18},{18,10},{11,19},{19,11},{12,20... | collective-permute-start | bytes 1990664 | tf_op jit(solution)/shard_map/ppermute | solution.py:592
  230.2 19.5 %collective-permute-start.50 = (bf16[288,1152]{1,0:T(8,128)(2,1)S(1)}, bf16[288,1152]{1,0:T(8,128)(2,1)S(1)}, u32[]{:S(2)}, u32[]{:S(2)}) collective-permute-start(bf16[288,1152]{1,0:T(8,128)(2,1)S(1)} %broadcast_select_fusion.14), channel_id=1, source_target_pairs={{0,8},{8,0},{16,24},{24,16},{1,9},{9,1},{17,25},{25,17},{2,10},{10... | collective-permute-start | bytes 1990664 | tf_op jit(solution)/shard_map/ppermute | solution.py:585
  234.3 15.4 %collective-permute-start.51 = (bf16[288,1152]{1,0:T(8,128)(2,1)S(1)}, bf16[288,1152]{1,0:T(8,128)(2,1)S(1)}, u32[]{:S(2)}, u32[]{:S(2)}) collective-permute-start(bf16[288,1152]{1,0:T(8,128)(2,1)S(1)} %add_convert_fusion.13), channel_id=1, source_target_pairs={{8,16},{16,8},{9,17},{17,9},{10,18},{18,10},{11,19},{19,11},{12,20... | collective-permute-start | bytes 1990664 | tf_op jit(solution)/shard_map/ppermute | solution.py:592
  235.5 14.2 %collective-permute-start.53 = (bf16[256,512]{1,0:T(8,128)(2,1)S(1)}, bf16[256,512]{1,0:T(8,128)(2,1)S(1)}, u32[]{:S(2)}, u32[]{:S(2)}) collective-permute-start(bf16[256,512]{1,0:T(8,128)(2,1)S(1)} %get-tuple-element.669), channel_id=1, source_target_pairs={{0,2},{1,3},{2,0},{3,1},{4,6},{5,7},{6,4},{7,5},{8,10},{9,11},{10,... | collective-permute-start | bytes 786440 | tf_op jit(solution)/shard_map/ppermute | solution.py:460
  251.3 23.0 %collective-permute-start.55 = (bf16[288,1152]{1,0:T(8,128)(2,1)S(1)}, bf16[288,1152]{1,0:T(8,128)(2,1)S(1)}, u32[]{:S(2)}, u32[]{:S(2)}) collective-permute-start(bf16[288,1152]{1,0:T(8,128)(2,1)S(1)} %broadcast_select_fusion.13), channel_id=1, source_target_pairs={{0,8},{8,0},{16,24},{24,16},{1,9},{9,1},{17,25},{25,17},{2,10},{10... | collective-permute-start | bytes 1990664 | tf_op jit(solution)/shard_map/ppermute | solution.py:585
  255.2 19.1 %collective-permute-start.56 = (bf16[288,1152]{1,0:T(8,128)(2,1)S(1)}, bf16[288,1152]{1,0:T(8,128)(2,1)S(1)}, u32[]{:S(2)}, u32[]{:S(2)}) collective-permute-start(bf16[288,1152]{1,0:T(8,128)(2,1)S(1)} %add_convert_fusion.11), channel_id=1, source_target_pairs={{8,16},{16,8},{9,17},{17,9},{10,18},{18,10},{11,19},{19,11},{12,20... | collective-permute-start | bytes 1990664 | tf_op jit(solution)/shard_map/ppermute | solution.py:592
  275.5 16.8 %collective-permute-start.58 = (bf16[288,1152]{1,0:T(8,128)(2,1)}, bf16[288,1152]{1,0:T(8,128)(2,1)}, u32[]{:S(2)}, u32[]{:S(2)}) collective-permute-start(bf16[288,1152]{1,0:T(8,128)(2,1)} %broadcast_select_fusion.12), channel_id=1, source_target_pairs={{0,8},{8,0},{16,24},{24,16},{1,9},{9,1},{17,25},{25,17},{2,10},{10... | collective-permute-start | bytes 1990664 | tf_op jit(solution)/shard_map/ppermute | solution.py:585
  278.5 13.9 %collective-permute-start.59 = (bf16[288,1152]{1,0:T(8,128)(2,1)}, bf16[288,1152]{1,0:T(8,128)(2,1)}, u32[]{:S(2)}, u32[]{:S(2)}) collective-permute-start(bf16[288,1152]{1,0:T(8,128)(2,1)} %add_convert_fusion.10), channel_id=1, source_target_pairs={{8,16},{16,8},{9,17},{17,9},{10,18},{18,10},{11,19},{19,11},{12,20... | collective-permute-start | bytes 1990664 | tf_op jit(solution)/shard_map/ppermute | solution.py:592
  294.9 18.3 %collective-permute-start.61 = (bf16[288,1152]{1,0:T(8,128)(2,1)S(1)}, bf16[288,1152]{1,0:T(8,128)(2,1)S(1)}, u32[]{:S(2)}, u32[]{:S(2)}) collective-permute-start(bf16[288,1152]{1,0:T(8,128)(2,1)S(1)} %broadcast_select_fusion.11), channel_id=1, source_target_pairs={{0,8},{8,0},{16,24},{24,16},{1,9},{9,1},{17,25},{25,17},{2,10},{10... | collective-permute-start | bytes 1990664 | tf_op jit(solution)/shard_map/ppermute | solution.py:585
  299.0 14.2 %collective-permute-start.62 = (bf16[288,1152]{1,0:T(8,128)(2,1)S(1)}, bf16[288,1152]{1,0:T(8,128)(2,1)S(1)}, u32[]{:S(2)}, u32[]{:S(2)}) collective-permute-start(bf16[288,1152]{1,0:T(8,128)(2,1)S(1)} %add_convert_fusion.7), channel_id=1, source_target_pairs={{8,16},{16,8},{9,17},{17,9},{10,18},{18,10},{11,19},{19,11},{12,20... | collective-permute-start | bytes 1990664 | tf_op jit(solution)/shard_map/ppermute | solution.py:592
  313.5 28.3 %collective-permute-start.66 = (bf16[288,1152]{1,0:T(8,128)(2,1)S(1)}, bf16[288,1152]{1,0:T(8,128)(2,1)S(1)}, u32[]{:S(2)}, u32[]{:S(2)}) collective-permute-start(bf16[288,1152]{1,0:T(8,128)(2,1)S(1)} %broadcast_select_fusion.10), channel_id=1, source_target_pairs={{0,8},{8,0},{16,24},{24,16},{1,9},{9,1},{17,25},{25,17},{2,10},{10... | collective-permute-start | bytes 1990664 | tf_op jit(solution)/shard_map/ppermute | solution.py:585
  318.9 22.9 %collective-permute-start.67 = (bf16[288,1152]{1,0:T(8,128)(2,1)S(1)}, bf16[288,1152]{1,0:T(8,128)(2,1)S(1)}, u32[]{:S(2)}, u32[]{:S(2)}) collective-permute-start(bf16[288,1152]{1,0:T(8,128)(2,1)S(1)} %add_convert_fusion.5), channel_id=1, source_target_pairs={{8,16},{16,8},{9,17},{17,9},{10,18},{18,10},{11,19},{19,11},{12,20... | collective-permute-start | bytes 1990664 | tf_op jit(solution)/shard_map/ppermute | solution.py:592
  321.0 19.8 %collective-permute-start.68 = (bf16[160,1536]{1,0:T(8,128)(2,1)S(1)}, bf16[160,1536]{1,0:T(8,128)(2,1)S(1)}, u32[]{:S(2)}, u32[]{:S(2)}) collective-permute-start(bf16[160,1536]{1,0:T(8,128)(2,1)S(1)} %get-tuple-element.611), channel_id=1, source_target_pairs={{0,2},{1,3},{2,0},{3,1},{4,6},{5,7},{6,4},{7,5},{8,10},{9,11},{10,... | collective-permute-start | bytes 1474568 | tf_op jit(solution)/shard_map/ppermute | solution.py:460
  323.2 18.5 %collective-permute-start.69 = (bf16[160,1536]{1,0:T(8,128)(2,1)S(1)}, bf16[160,1536]{1,0:T(8,128)(2,1)S(1)}, u32[]{:S(2)}, u32[]{:S(2)}) collective-permute-start(bf16[160,1536]{1,0:T(8,128)(2,1)S(1)} %get-tuple-element.612), channel_id=1, source_target_pairs={{0,4},{1,5},{2,6},{3,7},{4,0},{5,1},{6,2},{7,3},{8,12},{9,13},{10,... | collective-permute-start | bytes 1474568 | tf_op jit(solution)/shard_map/ppermute | solution.py:460
  323.5 17.3 %collective-permute-start.70 = (bf16[128,1152]{1,0:T(8,128)(2,1)S(1)}, bf16[128,1152]{1,0:T(8,128)(2,1)S(1)}, u32[]{:S(2)}, u32[]{:S(2)}) collective-permute-start(bf16[128,1152]{1,0:T(8,128)(2,1)S(1)} %get-tuple-element.614), channel_id=1, source_target_pairs={{0,6},{1,7},{2,4},{3,5},{4,2},{5,3},{6,0},{7,1},{8,14},{9,15},{10,... | collective-permute-start | bytes 884744 | tf_op jit(solution)/shard_map/ppermute | solution.py:460
  342.5 14.2 %collective-permute-start.71 = (bf16[288,1152]{1,0:T(8,128)(2,1)S(1)}, bf16[288,1152]{1,0:T(8,128)(2,1)S(1)}, u32[]{:S(2)}, u32[]{:S(2)}) collective-permute-start(bf16[288,1152]{1,0:T(8,128)(2,1)S(1)} %broadcast_select_fusion.9), channel_id=1, source_target_pairs={{0,8},{8,0},{16,24},{24,16},{1,9},{9,1},{17,25},{25,17},{2,10},{10... | collective-permute-start | bytes 1990664 | tf_op jit(solution)/shard_map/ppermute | solution.py:585
  344.2 12.5 %collective-permute-start.72 = (bf16[288,1152]{1,0:T(8,128)(2,1)S(1)}, bf16[288,1152]{1,0:T(8,128)(2,1)S(1)}, u32[]{:S(2)}, u32[]{:S(2)}) collective-permute-start(bf16[288,1152]{1,0:T(8,128)(2,1)S(1)} %add_convert_fusion.3), channel_id=1, source_target_pairs={{8,16},{16,8},{9,17},{17,9},{10,18},{18,10},{11,19},{19,11},{12,20... | collective-permute-start | bytes 1990664 | tf_op jit(solution)/shard_map/ppermute | solution.py:592
  356.9 17.8 %collective-permute-start.75 = (bf16[288,1152]{1,0:T(8,128)(2,1)S(1)}, bf16[288,1152]{1,0:T(8,128)(2,1)S(1)}, u32[]{:S(2)}, u32[]{:S(2)}) collective-permute-start(bf16[288,1152]{1,0:T(8,128)(2,1)S(1)} %add_convert_fusion.2), channel_id=1, source_target_pairs={{8,16},{16,8},{9,17},{17,9},{10,18},{18,10},{11,19},{19,11},{12,20... | collective-permute-start | bytes 1990664 | tf_op jit(solution)/shard_map/ppermute | solution.py:592
  357.8 18.6 %collective-permute-start.76 = (bf16[288,1152]{1,0:T(8,128)(2,1)S(1)}, bf16[288,1152]{1,0:T(8,128)(2,1)S(1)}, u32[]{:S(2)}, u32[]{:S(2)}) collective-permute-start(bf16[288,1152]{1,0:T(8,128)(2,1)S(1)} %add_convert_fusion.1), channel_id=1, source_target_pairs={{8,0},{16,24},{9,1},{17,25},{10,2},{18,26},{11,3},{19,27},{12,4},{... | collective-permute-start | bytes 1990664 | tf_op jit(solution)/shard_map/ppermute | solution.py:588
  359.3 15.3 %collective-permute-start.74 = (bf16[160,1536]{1,0:T(8,128)(2,1)S(1)}, bf16[160,1536]{1,0:T(8,128)(2,1)S(1)}, u32[]{:S(2)}, u32[]{:S(2)}) collective-permute-start(bf16[160,1536]{1,0:T(8,128)(2,1)S(1)} %add_convert_fusion.21), channel_id=1, source_target_pairs={{0,8},{24,16},{1,9},{25,17},{2,10},{26,18},{3,11},{27,19},{4,12},{... | collective-permute-start | bytes 1474568 | tf_op jit(solution)/shard_map/ppermute | solution.py:590
  379.2 13.6 %collective-permute-start.79 = (bf16[288,1152]{1,0:T(8,128)(2,1)S(1)}, bf16[288,1152]{1,0:T(8,128)(2,1)S(1)}, u32[]{:S(2)}, u32[]{:S(2)}) collective-permute-start(bf16[288,1152]{1,0:T(8,128)(2,1)S(1)} %add_convert_fusion), channel_id=1, source_target_pairs={{8,0},{16,24},{9,1},{17,25},{10,2},{18,26},{11,3},{19,27},{12,4},{... | collective-permute-start | bytes 1990664 | tf_op jit(solution)/shard_map/ppermute | solution.py:588
  393.7 16.6 %collective-permute-start.81 = (bf16[160,1536]{1,0:T(8,128)(2,1)S(1)}, bf16[160,1536]{1,0:T(8,128)(2,1)S(1)}, u32[]{:S(2)}, u32[]{:S(2)}) collective-permute-start(bf16[160,1536]{1,0:T(8,128)(2,1)S(1)} %add_convert_fusion.19), channel_id=1, source_target_pairs={{8,0},{16,24},{9,1},{17,25},{10,2},{18,26},{11,3},{19,27},{12,4},{... | collective-permute-start | bytes 1474568 | tf_op jit(solution)/shard_map/ppermute | solution.py:588
  (181 other events, 1100.3 us)

commit v3 on v2

--- a/solution.py
+++ b/solution.py
@@ -365,6 +365,51 @@
     )(*lefts, *rights, *extra)
 
 
+def middle_back_kernel(counts, out_count, *refs):
+    terms, refs = refs[: sum(counts)], refs[sum(counts) :]
+    g_ref, middle_ref, attn_ref, pre_ref, post_ref = refs[:5]
+    outs, (d_middle_ref, d_attn_ref, d_att_ref, gain_ref) = refs[5 : 5 + out_count], refs[-4:]
+    pre, post = 0.0, 0.0
+    half = g_ref.shape[0] // 2
+    for i in range(2):
+        own = terms[: counts[0]] if i == 0 else terms[counts[0] :]
+        rows = pl.ds(i * half, half)
+        d_b = functools.reduce(jnp.add, [t[...].astype(f32) for t in own])
+        normed, factor = rms_forward(middle_ref[rows, :])
+        pre = pre + jnp.sum(d_b * normed, axis=0, keepdims=True)
+        d_middle = g_ref[rows, :] + rms_backward(d_b * pre_ref[...], normed, factor)
+        d_middle_ref[rows, :] = d_middle
+        normed, factor = rms_forward(attn_ref[rows, :])
+        post = post + jnp.sum(d_middle * normed, axis=0, keepdims=True)
+        d_attn = rms_backward(d_middle * post_ref[...], normed, factor).astype(bf16)
+        d_attn_ref[rows, :] = d_attn
+    at = 0
+    for out in outs:
+        d_att_ref[:, at : at + out.shape[0]] = dot_rows(d_attn_ref[...], out[...]).astype(bf16)
+        at += out.shape[0]
+    gain_ref[0:1, :] = pre
+    gain_ref[1:2, :] = post
+
+
+def middle_back(halves, g, middle, attn, g_pre, g_post, outs):
+    rows, width = g.shape
+    whole = pl.BlockSpec(memory_space=pltpu.VMEM)
+    return pl.pallas_call(
+        functools.partial(middle_back_kernel, [len(h) for h in halves], len(outs)),
+        out_shape=(
+            jax.ShapeDtypeStruct((rows, width), f32),
+            jax.ShapeDtypeStruct((rows, width), bf16),
+            jax.ShapeDtypeStruct((rows, HEADS * HEAD), bf16),
+            jax.ShapeDtypeStruct((2, width), f32),
+        ),
+        in_specs=[whole] * (sum(len(h) for h in halves) + 5 + len(outs)),
+        out_specs=(whole,) * 4,
+        cost_estimate=BRIEF,
+        compiler_params=pltpu.CompilerParams(vmem_limit_bytes=FEED_VMEM),
+        name="middle_back",
+    )(*halves[0], *halves[1], g, middle, attn, g_pre[None], g_post[None], *outs)
+
+
 def add(*terms):
     return functools.reduce(jnp.add, [t.astype(f32) for t in terms])
 
@@ -373,9 +418,8 @@
 
 
 class Plain:
-    def __init__(self, n):
-        self.n = n
-        self.rank = lax.axis_index("seq")
+    def __init__(self, n, rank, place):
+        self.n, self.rank, self.place = n, rank, place
 
     def order(self):
         return jnp.arange(self.n, dtype=jnp.int32)
@@ -395,8 +439,8 @@
     def columns(self, value):
         return [value]
 
-    def restored(self, parts):
-        return parts[0]
+    def ordered(self, blocks):
+        return blocks[0]
 
     def pair(self, shard):
         return [shard]
@@ -420,8 +464,9 @@
     def late(self, x, y, relay):
         return ()
 
-    def parts_sum(self, parts, early, late):
-        return self.scatter(all_of([half.astype(bf16) for part in parts for half in part]))
+    def halves(self, parts, early, late):
+        whole = self.scatter(all_of([half.astype(bf16) for part in parts for half in part]))
+        return [[half] for half in jnp.split(whole, 2, axis=0)]
 
     def across(self, value):
         return ()
@@ -449,7 +494,7 @@
         return [jnp.concatenate([grad, gains], axis=1).reshape(-1, right.shape[1])]
 
     def line(self):
-        return PlainLine()
+        return PlainLine(None)
 
 
 class Cube(Plain):
@@ -497,9 +542,9 @@
             self.hop(add(y[0], relay[0]).astype(bf16), 4),
         )
 
-    def parts_sum(self, parts, early, late):
+    def halves(self, parts, early, late):
         own = parts[0]
-        return all_of([add(own[0], early[0], late[1]), add(own[1], early[1], late[0])])
+        return [[own[0], early[0], late[1]], [own[1], early[1], late[0]]]
 
     def across(self, value):
         return (self.hop(value, 1),)
@@ -529,12 +574,10 @@
         moved = dot(value, self.select(value.shape[1] // self.n, value.shape[1] // self.n))
         return jnp.split(moved.astype(value.dtype), 2, axis=1)
 
-    def restored(self, parts):
-        value = jnp.concatenate(parts, axis=1)
-        pick = self.select(value.shape[1] // self.n, value.shape[1] // self.n).astype(f32)
-        return lax.dot_general(
-            value, pick, (((1,), (1,)), ((), ())), precision=lax.Precision.HIGHEST
-        )
+    def ordered(self, blocks):
+        whole = all_of(blocks)
+        size = whole.shape[0] // self.n
+        return dot(self.select(size, size), whole).astype(whole.dtype)
 
     def pair(self, shard):
         return [shard, self.hop(shard, 1)]
@@ -552,32 +595,44 @@
         return [dot_cols(left[:, :half], right), dot_cols(left[:, half:], right)]
 
     def line(self):
-        return CubeLine()
+        return CubeLine((self.place == 1) | (self.place == 2))
 
 
 class PlainLine:
-    def __init__(self):
-        self.chunks = []
+    def __init__(self, inner):
+        self.inner = inner
+        self.chunks, self.wholes = [], []
+
+    def add_rows(self, whole, parts):
+        size = whole.shape[0] // parts
+        self.wholes.append(whole)
+        self.chunks += [(len(self.wholes) - 1, i * size, size) for i in range(parts)]
+
+    def chunk(self, at):
+        if len(self.chunks[at]) == 1:
+            return self.chunks[at][0]
+        source, start, size = self.chunks[at]
+        return self.wholes[source][start : start + size]
 
     def step(self, beside):
         return fence(beside(()))
 
-    def finish(self):
-        return [lax.psum(c, "dp").astype(f32) for c in self.chunks]
+    def finish(self, early):
+        chunks = [self.chunk(i) for i in range(len(self.chunks))]
+        done = [lax.psum(c, "dp").astype(f32) for c in chunks]
+        return done, early(done[-2])
 
 
 class CubeLine(PlainLine):
-    def __init__(self):
-        super().__init__()
-        place = lax.axis_index("dp")
-        self.inner = (place == 1) | (place == 2)
+    def __init__(self, inner):
+        super().__init__(inner)
         self.halves, self.totals, self.out = {}, {}, {}
         self.at = 0
 
     def step(self, beside):
         tick = self.at
         self.at += 1
-        mine = self.chunks[tick] if tick < len(self.chunks) else None
+        mine = self.chunk(tick) if tick < len(self.chunks) else None
         back, half = self.totals.get(tick - 2), self.halves.get(tick - 1)
         got = {}
         if mine is not None and back is not None and mine.shape == back.shape:
@@ -591,7 +646,11 @@
         if half is not None:
             got["middle"] = lax.ppermute(half, "dp", [(1, 2), (2, 1)])
         values = beside(())
-        got, values, self.chunks[tick + 1 :] = fence((got, values, self.chunks[tick + 1 :]))
+        later = [c for c in self.chunks[tick + 1 :] if len(c) == 1]
+        got, values, later, self.wholes = fence((got, values, later, self.wholes))
+        for at in range(tick + 1, len(self.chunks)):
+            if len(self.chunks[at]) == 1:
+                self.chunks[at] = later.pop(0)
         if mine is not None:
             self.halves[tick] = add(mine, got["in"]).astype(bf16)
         if half is not None:
@@ -600,10 +659,12 @@
             self.out[tick - 2] = jnp.where(self.inner, back, got["out"] if "out" in got else got["in"])
         return values
 
-    def finish(self):
-        while self.at < len(self.chunks) + 2:
+    def finish(self, early):
+        count = len(self.chunks)
+        while self.at < count + 1:
             self.step(lambda values: values)
-        return [self.out[i].astype(f32) for i in range(len(self.chunks))]
+        made = self.step(lambda _: early(self.out[count - 2].astype(f32)))
+        return [self.out[i].astype(f32) for i in range(count)], made
 
 
 def all_of(values):
@@ -630,21 +691,30 @@
     out_grad,
 ):
     n = lax.axis_size("seq")
-    comm = kind(n)
+    comm = kind(n, lax.axis_index("seq"), lax.axis_index("dp"))
     rows = layer_input.shape[1]
     width = layer_input.shape[2]
     ff = w_gate.shape[1]
+    positions = position_ids[0]
     row_offset = comm.rank * rows
+    order = jnp.concatenate(
+        [comm.order(), row_offset[None], (row_offset - positions[0])[None], comm.slots()]
+    ).astype(jnp.int32)
+    shard = width // n
+    starts = (comm.rank * shard, comm.rank * (HEAD // n), HEAD + comm.rank * (HEAD // n))
+    line = comm.line()
+    position_column = positions[:, None]
 
     x = layer_input[0].astype(f32)
-    positions = position_ids[0]
     keyval_sent = comm.send(w_keyval)
     a_normed, a_factor = rms_forward(x)
     a_low = (a_normed * g_input).astype(bf16)
     a_columns = comm.columns(a_low)
     angles = rope_angles(positions, HEAD)
     cosine, sine = jnp.cos(angles), jnp.sin(angles)
-    keyval_sent, a_columns, w_query = fence((keyval_sent, a_columns, w_query))
+    keyval_sent, a_columns, w_query, order, starts, position_column, line.inner, comm.rank = fence(
+        (keyval_sent, a_columns, w_query, order, starts, position_column, line.inner, comm.rank)
+    )
     query_near = comm.near(w_query)
     keyval_blocks = comm.paired(keyval_sent)
     kv_pre = add(*[dot(a, w) for a, w in zip(a_columns, keyval_blocks)])
@@ -658,14 +728,13 @@
     kv_far = comm.far(kv_near)
     query_blocks = comm.joined(w_query, query_near, query_far)
     q_pre = add(*[dot(a, w) for a, w in zip(a_columns, query_blocks)])
-    kv_far, q_pre, w_out = fence((kv_far, q_pre, w_out))
+    kv_far, q_pre, w_out, query_blocks, keyval_blocks = fence(
+        (kv_far, q_pre, w_out, query_blocks, keyval_blocks)
+    )
     out_near = comm.near(w_out)
     kv_blocks = comm.joined(kv_low, kv_near, kv_far)
-    kv_blocks, out_near = fence((kv_blocks, out_near))
+    kv_blocks, out_near, w_gate, w_up, w_down = fence((kv_blocks, out_near, w_gate, w_up, w_down))
     out_far = comm.far(out_near)
-    order = jnp.concatenate(
-        [comm.order(), row_offset[None], (row_offset - positions[0])[None], comm.slots()]
-    ).astype(jnp.int32)
     head_args = (
         comm.slots().shape[0],
         order,
@@ -673,26 +742,27 @@
         cosine,
         sine,
         g_query[None],
-        positions[:, None],
+        position_column,
         *kv_blocks,
     )
     att_low, inverse = attend(*head_args)
     out_far, att_low, w_gate, w_up, w_down = fence((out_far, att_low, w_gate, w_up, w_down))
-    weights = [comm.pair(w) for w in (w_gate.T, w_up.T, w_down)]
-    weights = [w[i] for i in range(len(weights[0])) for w in weights]
-    groups = len(weights) // 3
     out_blocks = comm.joined(w_out, out_near, out_far)
+    gate_w, up_w, down_w = [comm.pair(w) for w in (w_gate.T, w_up.T, w_down)]
+    groups = len(gate_w)
     att_columns = jnp.split(att_low, len(out_blocks), axis=1)
     attn = add(*[dot(v, w) for v, w in zip(att_columns, out_blocks)])
     attn_normed, attn_factor = rms_forward(attn)
     middle = x + attn_normed * g_post_attn
     b_normed, b_factor = rms_forward(middle)
     b_low = (b_normed * g_pre_ffn).astype(bf16)
-    b_low, weights = fence((b_low, weights))
+    b_low, query_blocks, keyval_blocks = fence((b_low, query_blocks, keyval_blocks))
+    weights = [w[i] for i in range(groups) for w in (gate_w, up_w, down_w)]
 
     near = comm.near(b_low)
     kept = [feed((b_low,), weights, f32)]
-    kept, near = fence((kept, near))
+    query_whole = comm.ordered(query_blocks)
+    kept, near, query_whole, keyval_blocks = fence((kept, near, query_whole, keyval_blocks))
     far = comm.far(near)
     b_list = comm.tokens(b_low, near, far)
     kept += [feed(part, weights, bf16) for part in b_list[1:-1]]
@@ -705,15 +775,13 @@
     hidden, acts, slopes = [[v[i] for v in kept] for i in (2, 3, 4)]
     relay = comm.relay(parts[-1])
     late = comm.late(parts[1], parts[2], relay)
-    ffn = comm.parts_sum(parts, early, late)
+    ffn = all_of([add(*terms) for terms in comm.halves(parts, early, late)])
     ffn_normed, ffn_factor = rms_forward(ffn)
     layer_out = (middle + ffn_normed * g_post_ffn).astype(bf16)
 
     g = out_grad[0]
     d_ffn = rms_backward(g * g_post_ffn, ffn_normed, ffn_factor).astype(bf16)
-    d_ffn, ffn_normed = fence((d_ffn, ffn_normed))
-    line = comm.line()
-    thirds = [ff // 3] * 3
+    d_ffn, ffn_normed, keyval_blocks = fence((d_ffn, ffn_normed, keyval_blocks))
 
     def back(part, i):
         return feed_back(part, acts[i], slopes[i], weights, bf16 if i else f32)
@@ -724,7 +792,8 @@
     near = comm.near(d_ffn)
     gain_post_ffn = jnp.sum(g * ffn_normed, axis=0)
     kept = [back((d_ffn,), 0)]
-    kept, near, gain_post_ffn = fence((kept, near, gain_post_ffn))
+    keyval_whole = comm.ordered(keyval_blocks)
+    kept, near, gain_post_ffn, keyval_whole = fence((kept, near, gain_post_ffn, keyval_whole))
     far = comm.far(near)
     d_list = comm.tokens(d_ffn, near, far)
     last = len(d_list) - 1
@@ -732,53 +801,52 @@
     kept, far, tail = fence((kept, far, d_list[-1]))
     d_list[-1] = tail
 
-    early = comm.early(kept[1][:2], kept[2][:2])
     other = [comm.hop(v, 1) for v in other_half(hidden, d_list)]
     kept.append(back(tail, last))
-    kept, early, other = fence((kept, early, other))
+    kept, other = fence((kept, other))
     parts = [v[:2] for v in kept]
     d_gate, d_up = [[v[i] for v in kept] for i in (2, 3)]
-    line.chunks += weight_grad(0, thirds, hidden, d_list, *other)
+    thirds = [ff // 3] * 3
+    line.chunks += [(v,) for v in weight_grad(0, thirds, hidden, d_list, *other)]
 
     line.chunks, parts, d_gate, d_up, a_late = fence((line.chunks, parts, d_gate, d_up, a_low))
 
     def beside(_):
+        early = comm.early(parts[1], parts[2])
         relay = comm.relay(parts[-1])
+        others = other_half(d_gate, b_list), other_half(d_up, b_list)
+        return early, relay, others, d_gate, d_up, parts
+
+    early, relay, others, d_gate, d_up, parts = line.step(beside)
+
+    def beside(_):
         late = comm.late(parts[1], parts[2], relay)
-        others = other_half(d_gate, b_list), other_half(d_up, b_list)
-        return late, others, d_gate, d_up, parts, early
-
-    late, others, d_gate, d_up, parts, early = line.step(beside)
-
-    def beside(_):
-        other, other_up = [[comm.hop(v, 1) for v in values] for values in others]
-        d_b = comm.parts_sum(parts, early, late)
-        gain_pre_ffn = jnp.sum(d_b * b_normed, axis=0)
-        d_middle = g + rms_backward(d_b * g_pre_ffn, b_normed, b_factor)
-        gain_post_attn = jnp.sum(d_middle * attn_normed, axis=0)
-        d_attn = rms_backward(d_middle * g_post_attn, attn_normed, attn_factor).astype(bf16)
-        d_att = jnp.concatenate([dot_rows(d_attn, w).astype(bf16) for w in out_blocks], axis=1)
-        grads = weight_grad(0, thirds, d_gate, b_list, *other)
-        return list(grads), d_up, other_up, d_middle, d_attn, d_att, (gain_post_attn, gain_pre_ffn)
-
-    grads, d_up, other_up, d_middle, d_attn, d_att, gains = line.step(beside)
-    gain_post_attn, gain_pre_ffn = gains
-    line.chunks += grads
+        (grads,) = weight_grad(0, [ff], d_gate, b_list, *[comm.hop(v, 1) for v in others[0]])
+        late, grads = fence((late, grads))
+        middles = middle_back(
+            comm.halves(parts, early, late), g, middle, attn, g_pre_ffn, g_post_attn, out_blocks
+        )
+        return grads, d_up, others[1], middles
+
+    grads, d_up, other_up, (d_middle, d_attn, d_att, gain_pair) = line.step(beside)
+    line.add_rows(grads, 3)
 
     def beside(_):
         heads = attend_back(*head_args, saved=(att_low, inverse), d_att=d_att)
-        return heads, d_up, d_attn
-
-    (d_q_pre, *d_kv_blocks, gain_query), d_up, d_attn = line.step(beside)
+        grad_out = [dot_cols(v, d_attn) for v in att_columns]
+        return heads, d_up, grad_out, [comm.hop(v, 1) for v in other_up]
+
+    heads, d_up, grad_out, other_up = line.step(beside)
+    d_q_pre, *d_kv_blocks, gain_query = heads
 
     def beside(_):
         group = comm.group(d_kv_blocks, comm.across(d_kv_blocks[-1]))
         near = comm.group_near(group)
-        grads = weight_grad(0, thirds, d_up, b_list, *other_up)
-        return group, near, list(grads), d_attn, a_late
-
-    group, near, grads, d_attn, a_late = line.step(beside)
-    line.chunks += grads
+        (grads,) = weight_grad(0, [ff], d_up, b_list, *other_up)
+        return group, near, grads, grad_out, a_late, (gain_post_ffn, gain_pair, gain_query)
+
+    group, near, grads, grad_out, a_late, early_gains = line.step(beside)
+    line.add_rows(grads, 3)
 
     def beside(_):
         d_kv = comm.group_sum(group, near, comm.group_far(group))
@@ -786,63 +854,63 @@
         gain_key = jnp.sum(d_k_normed * k_hat, axis=0)
         d_k_pre = rms_backward(d_k_normed * g_key, k_hat, k_factor)
         d_kv_pre = jnp.concatenate([d_k_pre, d_kv[:, HEAD:]], axis=1).astype(bf16)
-        d_a = comm.restored(
-            [
-                dot_rows(d_q_pre, query) + dot_rows(d_kv_pre, keyval)
-                for query, keyval in zip(query_blocks, keyval_blocks)
-            ]
-        )
+        d_a = dot_rows(d_q_pre, query_whole) + dot_rows(d_kv_pre, keyval_whole)
         gain_input = jnp.sum(d_a * a_normed, axis=0)
-        grad_out = [dot_cols(v, d_attn) for v in att_columns]
-        return d_kv_pre, d_a, (gain_input, gain_key), grad_out, a_late
-
-    d_kv_pre, d_a, (gain_input, gain_key), grad_out, a_late = line.step(beside)
+        out_group = comm.group(grad_out, comm.across(grad_out[-1].astype(bf16)))
+        return d_kv_pre, d_a, (gain_input, gain_key), out_group, a_late, early_gains
+
+    d_kv_pre, d_a, (gain_input, gain_key), out_group, a_late, early_gains = line.step(beside)
+    gain_post_ffn, gain_pair, gain_query = early_gains
 
     def beside(_):
-        out_moved = comm.across(grad_out[-1].astype(bf16))
+        out_near = comm.group_near(out_group)
         d_qkv = jnp.concatenate([d_q_pre, d_kv_pre], axis=1)
-        gains = [gain_input, gain_post_attn, gain_pre_ffn, gain_post_ffn]
+        gains = [gain_input, gain_pair[1], gain_pair[0], gain_post_ffn]
         gains.append(jnp.concatenate([gain_query[0], gain_key]))
         gains = [jnp.pad(v, (0, d_qkv.shape[1] - v.shape[0])) for v in gains]
-        gains = jnp.pad(jnp.stack(gains), ((0, 16 - len(gains)), (0, 0)))
+        row = lax.broadcasted_iota(jnp.int32, (16, d_qkv.shape[1]), 0)
+        gains = add(*[jnp.where(row == i, v[None], 0.0) for i, v in enumerate(gains)])
         grad_qkv = comm.projection(a_late, d_qkv, gains)
-        return comm.group(grad_out, out_moved), grad_qkv, d_a
-
-    out_group, grad_qkv, d_a = line.step(beside)
+        return out_group, out_near, grad_qkv, d_a
+
+    out_group, out_near, grad_qkv, d_a = line.step(beside)
 
     def beside(_):
         qkv_moved = comm.across(grad_qkv[-1].astype(bf16))
-        out_near = comm.group_near(out_group)
+        out_far = comm.group_far(out_group)
         d_input = d_middle + rms_backward(d_a * g_input, a_normed, a_factor)
-        return comm.group(grad_qkv, qkv_moved), out_group, out_near, d_input
-
-    group, out_group, out_near, d_input = line.step(beside)
+        total_out = comm.group_sum(out_group, out_near, out_far).astype(bf16)
+        return comm.group(grad_qkv, qkv_moved), total_out, d_input
+
+    group, total_out, d_input = line.step(beside)
 
     def beside(_):
-        return group, comm.group_near(group), comm.group_far(out_group)
-
-    group, near, out_far = line.step(beside)
-    total_out = comm.group_sum(out_group, out_near, out_far).astype(bf16)
+        return group, comm.group_near(group), total_out
+
+    group, near, total_out = line.step(beside)
 
     def beside(_):
         return comm.group_far(group), near, total_out
 
     far, near, total_out = line.step(beside)
-    line.chunks += [comm.group_sum(group, near, far).astype(bf16), total_out]
-    *done, tail, total_out = line.finish()
+    line.chunks += [(comm.group_sum(group, near, far).astype(bf16),), (total_out,)]
+    def owned(tail):
+        def mine(row, start, size):
+            return lax.dynamic_slice(
+                tail[shard + row], (start,), (size,), allow_negative_indices=False
+            )
+
+        grads = [tail[:shard, : HEADS * HEAD], tail[:shard, HEADS * HEAD :]]
+        names = [mine(i, starts[0], shard) for i in range(4)]
+        return grads, names + [mine(4, start, HEAD // n) for start in starts[1:]]
+
+    (*done, _, total_out), ((grad_query, grad_keyval), names) = line.finish(owned)
     down, gate, up = all_of(done[:3]), all_of(done[3:6]), all_of(done[6:])
-    shard = width // n
-
-    def mine(row, at, size):
-        return lax.dynamic_slice_in_dim(tail[shard + row], at + comm.rank * size, size)
-
-    names = [mine(i, 0, shard) for i in range(4)]
-    names += [mine(4, i * HEAD, HEAD // n) for i in range(2)]
     return (
         layer_out[None],
         d_input[None],
-        tail[:shard, : HEADS * HEAD],
-        tail[:shard, HEADS * HEAD :],
+        grad_query,
+        grad_keyval,
         total_out,
         gate.T,
         up.T,

time: 428 us -> 397 us (0.928)
  other arithmetic: 41.7 us -> 24.6 us
  local copies, waits for them, and re-layouts: 27.2 us -> 15.5 us
  starting transfers between devices: 109 us -> 116 us
    unnamed x275 -> x121, local copies, waits for them, and re-layouts: 20.8 us -> 6.74 us
    ppermute x57, waiting for transfers between devices: 101 us -> 88.5 us  [hop(): return lax.ppermute(value, 'seq', [(i, i ^ bit) for i in range(8)])]
    ppermute x7, waiting for transfers between devices: 19.9 us -> 30.1 us  [step(): got['in'] = lax.ppermute(both, 'dp', [(0, 1), (1, 0), (2, 3), (3, 2)])]
    ppermute x7, starting transfers between devices: 21.1 us -> 30.4 us  [step(): got['in'] = lax.ppermute(both, 'dp', [(0, 1), (1, 0), (2, 3), (3, 2)])]
    dot_general x8 -> x10, matrix products: 7.15 us -> 13.8 us  [dot(): return jnp.dot(left, right, preferred_element_type=f32)]
  transfers between devices with their start and end apart: 83 -> 83, of which waited for: 44 -> 46; matrix products, arithmetic and copies ran while one was open for 15% -> 12% of each run, Pallas kernels for 13% -> 14%
where the time goes in v3:
time: 397 us; the launch traced here: 392 us
  waiting for transfers between devices  154 us (39%)
  starting transfers between devices  116 us (29%)
  Pallas kernels  60 us (15%)
  other arithmetic  24.6 us (6%)
  matrix products  18.8 us (5%)
  local copies, waits for them, and re-layouts  15.5 us (4%)
    ppermute x57, waiting for transfers between devices, hop(): return lax.ppermute(value, 'seq', [(i, i ^ bit) for i in range(8)])  88.5 us
    ppermute x57, starting transfers between devices, hop(): return lax.ppermute(value, 'seq', [(i, i ^ bit) for i in range(8)])  55.3 us
    ppermute x7, starting transfers between devices, step(): got['in'] = lax.ppermute(both, 'dp', [(0, 1), (1, 0), (2, 3), (3, 2)])  30.4 us
    ppermute x7, waiting for transfers between devices, step(): got['in'] = lax.ppermute(both, 'dp', [(0, 1), (1, 0), (2, 3), (3, 2)])  30.1 us
    ppermute x4, waiting for transfers between devices, step(): got['out'] = lax.ppermute(back, 'dp', [(1, 0), (2, 3)])  24.6 us
    pallas_call x4, Pallas kernels, feed(): pl.pallas_call(functools.partial(feed_kernel, groups, len(b)), out_shape=...  18.4 us
    pallas_call x4, Pallas kernels, feed_back(): pl.pallas_call(functools.partial(feed_back_kernel, groups, len(d)), out_s...  17.9 us
    ppermute x4, starting transfers between devices, step(): got['in'] = lax.ppermute(mine, 'dp', [(0, 1), (3, 2)])  16.6 us
  transfers between devices with their start and end apart: 83, of which 46 were waited for; matrix products, arithmetic and copies ran while one was open for 12% of the time, Pallas kernels for 14%

profile of v3, /device:TPU:0, one launch (start us, length us, event | category | flops | bytes accessed | tf_op | source)
XLA Modules:
  0.0 391.8 jit_solution(5247343819677362127)
XLA Ops:
  16.8 5.2 %collective-permute-done.4 = bf16[144,1024]{1,0:T(8,128)(2,1)S(1)} collective-permute-done((bf16[144,1024]{1,0:T(8,128)(2,1)S(1)}, bf16[144,1024]{1,0:T(8,128)(2,1)S(1)}, u32[]{:S(2)}, u32[]{:S(2)}) %collective-permute-start.4) | collective-permute-done | bytes 294944 | tf_op jit(solution)/shard_map/ppermute | solution.py:505
  27.2 6.5 %collective-permute-done.8 = bf16[72,1024]{1,0:T(8,128)(2,1)S(1)} collective-permute-done((bf16[72,1024]{1,0:T(8,128)(2,1)S(1)}, bf16[72,1024]{1,0:T(8,128)(2,1)S(1)}, u32[]{:S(2)}, u32[]{:S(2)}) %collective-permute-start.8) | collective-permute-done | bytes 147488 | tf_op jit(solution)/shard_map/ppermute | solution.py:505
  45.9 5.4 %collective-permute-done.14 = bf16[128,1152]{1,0:T(8,128)(2,1)} collective-permute-done((bf16[128,1152]{1,0:T(8,128)(2,1)}, bf16[128,1152]{1,0:T(8,128)(2,1)}, u32[]{:S(2)}, u32[]{:S(2)}) %collective-permute-start.14) | collective-permute-done | bytes 294944 | tf_op jit(solution)/shard_map/ppermute | solution.py:505
  70.3 4.7 %convolution_convert_fusion = bf16[1152,1024]{1,0:T(8,128)(2,1)} fusion(bf16[576,1024]{1,0:T(8,128)(2,1)S(1)} %copy-done.19, bf16[576,1024]{1,0:T(8,128)(2,1)S(1)} %copy-done.17, s32[]{:T(128)S(6)} %axis_index.22, s32[1152]{0:T(1024)S(1)} %copy-done.40, s32[1152]{0:T(1024)S(1)} %copy-done.42, pred[1152]{0:T(1024)(128)(4,1)S(1)} %copy-done.47, ...), kind=kOutput, calls=%fused_computation.58 | convolution fusion | flops 2771582976 | bytes 4739332 | tf_op jit(solution)/shard_map/dot_general | solution.py:49
  74.9 4.6 %feed.4 = (f32[128,1152]{1,0:T(8,128)S(1)}, f32[128,1152]{1,0:T(8,128)S(1)}, bf16[2,256,864]{2,1,0:T(8,128)(2,1)S(1)}, bf16[2,256,864]{2,1,0:T(8,128)(2,1)S(1)}, bf16[2,256,864]{2,1,0:T(8,128)(2,1)S(1)}) custom-call(bf16[256,1152]{1,0:T(8,128)(2,1)S(1)} %multiply_convert_fusion.1.refs_0_.refs_4_, bf16[864,1152]{1,0:T(8,128)(2,1)S(1)} %bitcast.55, ...), custom_call_target="tpu_custom_call" | custom-call | flops 1 | bytes 1 | tf_op jit(solution)/shard_map/feed/pallas_call | solution.py:294
  85.8 4.7 %feed.5 = (bf16[128,1152]{1,0:T(8,128)(2,1)S(1)}, bf16[128,1152]{1,0:T(8,128)(2,1)S(1)}, bf16[2,256,864]{2,1,0:T(8,128)(2,1)S(1)}, bf16[2,256,864]{2,1,0:T(8,128)(2,1)S(1)}, bf16[2,256,864]{2,1,0:T(8,128)(2,1)S(1)}) custom-call(bf16[256,1152]{1,0:T(8,128)(2,1)S(1)} %collective-permute-done.22.refs_0_.refs_5_, bf16[864,1152]{1,0:T(8,128)(2,1)S(1)} %bitcast.56, ...), custom_call_target="tpu_custom_call" | custom-call | flops 1 | bytes 1 | tf_op jit(solution)/shard_map/feed/pallas_call | solution.py:294
  90.6 4.6 %feed.6 = (bf16[128,1152]{1,0:T(8,128)(2,1)S(1)}, bf16[128,1152]{1,0:T(8,128)(2,1)S(1)}, bf16[2,256,864]{2,1,0:T(8,128)(2,1)S(1)}, bf16[2,256,864]{2,1,0:T(8,128)(2,1)S(1)}, bf16[2,256,864]{2,1,0:T(8,128)(2,1)S(1)}) custom-call(bf16[256,1152]{1,0:T(8,128)(2,1)S(1)} %collective-permute-done.23.refs_0_.refs_6_, bf16[864,1152]{1,0:T(8,128)(2,1)S(1)} %bitcast.57, ...), custom_call_target="tpu_custom_call" | custom-call | flops 1 | bytes 1 | tf_op jit(solution)/shard_map/feed/pallas_call | solution.py:294
  97.7 4.6 %feed.7 = (bf16[128,1152]{1,0:T(8,128)(2,1)S(1)}, bf16[128,1152]{1,0:T(8,128)(2,1)S(1)}, bf16[2,256,864]{2,1,0:T(8,128)(2,1)S(1)}, bf16[2,256,864]{2,1,0:T(8,128)(2,1)S(1)}, bf16[2,256,864]{2,1,0:T(8,128)(2,1)S(1)}) custom-call(bf16[128,1152]{1,0:T(8,128)(2,1)S(1)} %collective-permute-done.24.refs_0_.refs_7_, ...), custom_call_target="tpu_custom_call" | custom-call | flops 1 | bytes 1 | tf_op jit(solution)/shard_map/feed/pallas_call | solution.py:294
  105.4 5.8 %collective-permute-done.30 = bf16[128,1152]{1,0:T(8,128)(2,1)S(1)} collective-permute-done((bf16[128,1152]{1,0:T(8,128)(2,1)S(1)}, bf16[128,1152]{1,0:T(8,128)(2,1)S(1)}, u32[]{:S(2)}, u32[]{:S(2)}) %collective-permute-start.30) | collective-permute-done | bytes 294944 | tf_op jit(solution)/shard_map/ppermute | solution.py:505
  126.9 4.5 %feed_back.4 = (f32[128,1152]{1,0:T(8,128)S(1)}, f32[128,1152]{1,0:T(8,128)S(1)}, bf16[2,256,864]{2,1,0:T(8,128)(2,1)S(1)}, bf16[2,256,864]{2,1,0:T(8,128)(2,1)S(1)}) custom-call(bf16[2,256,864]{2,1,0:T(8,128)(2,1)S(1)} %get-tuple-element.462.act_ref, bf16[2,256,864]{2,1,0:T(8,128)(2,1)S(1)} %get-tuple-element.463.slope_ref, ...), custom_call_target="tpu_custom_call" | custom-call | flops 1 | bytes 1 | tf_op jit(solution)/shard_map/feed_back/pallas_call | solution.py:325
  138.8 4.3 %feed_back.5 = (bf16[128,1152]{1,0:T(8,128)(2,1)S(1)}, bf16[128,1152]{1,0:T(8,128)(2,1)S(1)}, bf16[2,256,864]{2,1,0:T(8,128)(2,1)S(1)}, bf16[2,256,864]{2,1,0:T(8,128)(2,1)S(1)}) custom-call(bf16[2,256,864]{2,1,0:T(8,128)(2,1)S(1)} %get-tuple-element.477.act_ref, bf16[2,256,864]{2,1,0:T(8,128)(2,1)S(1)} %get-tuple-element.478.slope_ref, ...), custom_call_target="tpu_custom_call" | custom-call | flops 1 | bytes 1 | tf_op jit(solution)/shard_map/feed_back/pallas_call | solution.py:325
  143.2 4.3 %feed_back.6 = (bf16[128,1152]{1,0:T(8,128)(2,1)S(1)}, bf16[128,1152]{1,0:T(8,128)(2,1)S(1)}, bf16[2,256,864]{2,1,0:T(8,128)(2,1)S(1)}, bf16[2,256,864]{2,1,0:T(8,128)(2,1)S(1)}) custom-call(bf16[2,256,864]{2,1,0:T(8,128)(2,1)S(1)} %get-tuple-element.483.act_ref, bf16[2,256,864]{2,1,0:T(8,128)(2,1)S(1)} %get-tuple-element.484.slope_ref, ...), custom_call_target="tpu_custom_call" | custom-call | flops 1 | bytes 1 | tf_op jit(solution)/shard_map/feed_back/pallas_call | solution.py:325
  150.1 4.7 %feed_back.7 = (bf16[128,1152]{1,0:T(8,128)(2,1)S(1)}, bf16[128,1152]{1,0:T(8,128)(2,1)S(1)}, bf16[2,256,864]{2,1,0:T(8,128)(2,1)S(1)}, bf16[2,256,864]{2,1,0:T(8,128)(2,1)S(1)}) custom-call(bf16[2,256,864]{2,1,0:T(8,128)(2,1)S(1)} %get-tuple-element.503.act_ref, bf16[2,256,864]{2,1,0:T(8,128)(2,1)S(1)} %copy-done.5, ...), custom_call_target="tpu_custom_call" | custom-call | flops 1 | bytes 1 | tf_op jit(solution)/shard_map/feed_back/pallas_call | solution.py:325
  172.4 3.9 collective-permute-done.40
  185.7 4.7 %collective-permute-done.44.refs_5_ = bf16[128,1152]{1,0:T(8,128)(2,1)S(1)} collective-permute-done((bf16[128,1152]{1,0:T(8,128)(2,1)S(1)}, bf16[128,1152]{1,0:T(8,128)(2,1)S(1)}, u32[]{:S(2)}, u32[]{:S(2)}) %collective-permute-start.44) | collective-permute-done | bytes 294944 | tf_op jit(solution)/shard_map/ppermute | solution.py:505
  195.1 4.4 %collective-permute-start.47 = (bf16[288,1152]{1,0:T(8,128)(2,1)S(1)}, bf16[288,1152]{1,0:T(8,128)(2,1)S(1)}, u32[]{:S(2)}, u32[]{:S(2)}) collective-permute-start(bf16[288,1152]{1,0:T(8,128)(2,1)S(1)} %broadcast_select_fusion.15), channel_id=1, source_target_pairs={{0,8},{8,0},{16,24},{24,16},{1,9},{9,1},{17,25},{25,17},{2,10},{10... | collective-permute-start | bytes 1990664 | tf_op jit(solution)/shard_map/ppermute | solution.py:640
  205.3 9.8 %collective-permute-done.47 = bf16[288,1152]{1,0:T(8,128)(2,1)S(1)} collective-permute-done((bf16[288,1152]{1,0:T(8,128)(2,1)S(1)}, bf16[288,1152]{1,0:T(8,128)(2,1)S(1)}, u32[]{:S(2)}, u32[]{:S(2)}) %collective-permute-start.47) | collective-permute-done | bytes 663584 | tf_op jit(solution)/shard_map/ppermute | solution.py:640
  215.3 3.9 collective-permute-start.50
  224.9 9.8 %collective-permute-done.50 = bf16[288,1152]{1,0:T(8,128)(2,1)S(1)} collective-permute-done((bf16[288,1152]{1,0:T(8,128)(2,1)S(1)}, bf16[288,1152]{1,0:T(8,128)(2,1)S(1)}, u32[]{:S(2)}, u32[]{:S(2)}) %collective-permute-start.50) | collective-permute-done | bytes 663584 | tf_op jit(solution)/shard_map/ppermute | solution.py:640
  236.3 3.8 collective-permute-start.55
  248.3 6.3 %collective-permute-done.55 = bf16[288,1152]{1,0:T(8,128)(2,1)S(1)} collective-permute-done((bf16[288,1152]{1,0:T(8,128)(2,1)S(1)}, bf16[288,1152]{1,0:T(8,128)(2,1)S(1)}, u32[]{:S(2)}, u32[]{:S(2)}) %collective-permute-start.55) | collective-permute-done | bytes 663584 | tf_op jit(solution)/shard_map/ppermute | solution.py:640
  255.3 3.8 collective-permute-start.59
  281.9 6.4 %collective-permute-done.66 = bf16[128,1152]{1,0:T(8,128)(2,1)S(1)} collective-permute-done((bf16[128,1152]{1,0:T(8,128)(2,1)S(1)}, bf16[128,1152]{1,0:T(8,128)(2,1)S(1)}, u32[]{:S(2)}, u32[]{:S(2)}) %collective-permute-start.66) | collective-permute-done | bytes 294944 | tf_op jit(solution)/shard_map/ppermute | solution.py:505
  289.7 6.9 %collective-permute-start.67 = (bf16[288,1152]{1,0:T(8,128)(2,1)S(1)}, bf16[288,1152]{1,0:T(8,128)(2,1)S(1)}, u32[]{:S(2)}, u32[]{:S(2)}) collective-permute-start(bf16[288,1152]{1,0:T(8,128)(2,1)S(1)} %broadcast_select_fusion.10), channel_id=1, source_target_pairs={{0,8},{8,0},{16,24},{24,16},{1,9},{9,1},{17,25},{25,17},{2,10},{10... | collective-permute-start | bytes 1990664 | tf_op jit(solution)/shard_map/ppermute | solution.py:640
  300.8 9.5 %collective-permute-done.69 = bf16[160,1536]{1,0:T(8,128)(2,1)S(1)} collective-permute-done((bf16[160,1536]{1,0:T(8,128)(2,1)S(1)}, bf16[160,1536]{1,0:T(8,128)(2,1)S(1)}, u32[]{:S(2)}, u32[]{:S(2)}) %collective-permute-start.69) | collective-permute-done | bytes 491552 | tf_op jit(solution)/shard_map/ppermute | solution.py:505
  311.6 3.9 collective-permute-start.71
  321.1 7.9 %collective-permute-done.73 = bf16[160,1536]{1,0:T(8,128)(2,1)S(1)} collective-permute-done((bf16[160,1536]{1,0:T(8,128)(2,1)S(1)}, bf16[160,1536]{1,0:T(8,128)(2,1)S(1)}, u32[]{:S(2)}, u32[]{:S(2)}) %collective-permute-start.73) | collective-permute-done | bytes 491552 | tf_op jit(solution)/shard_map/ppermute | solution.py:505
  332.0 8.6 %collective-permute-start.74 = (bf16[160,1536]{1,0:T(8,128)(2,1)S(1)}, bf16[160,1536]{1,0:T(8,128)(2,1)S(1)}, u32[]{:S(2)}, u32[]{:S(2)}) collective-permute-start(bf16[160,1536]{1,0:T(8,128)(2,1)S(1)} %add_convert_fusion.21), channel_id=1, source_target_pairs={{0,8},{24,16},{1,9},{25,17},{2,10},{26,18},{3,11},{27,19},{4,12},{... | collective-permute-start | bytes 1474568 | tf_op jit(solution)/shard_map/ppermute | solution.py:645
  340.9 8.0 %collective-permute-done.74 = bf16[160,1536]{1,0:T(8,128)(2,1)S(1)} collective-permute-done((bf16[160,1536]{1,0:T(8,128)(2,1)S(1)}, bf16[160,1536]{1,0:T(8,128)(2,1)S(1)}, u32[]{:S(2)}, u32[]{:S(2)}) %collective-permute-start.74) | collective-permute-done | bytes 491552 | tf_op jit(solution)/shard_map/ppermute | solution.py:645
  357.5 11.1 %collective-permute-done.79 = bf16[288,1152]{1,0:T(8,128)(2,1)S(1)} collective-permute-done((bf16[288,1152]{1,0:T(8,128)(2,1)S(1)}, bf16[288,1152]{1,0:T(8,128)(2,1)S(1)}, u32[]{:S(2)}, u32[]{:S(2)}) %collective-permute-start.79) | collective-permute-done | bytes 663584 | tf_op jit(solution)/shard_map/ppermute | solution.py:643
  373.1 7.1 %collective-permute-done.81 = bf16[160,1536]{1,0:T(8,128)(2,1)S(1)} collective-permute-done((bf16[160,1536]{1,0:T(8,128)(2,1)S(1)}, bf16[160,1536]{1,0:T(8,128)(2,1)S(1)}, u32[]{:S(2)}, u32[]{:S(2)}) %collective-permute-start.81) | collective-permute-done | bytes 491552 | tf_op jit(solution)/shard_map/ppermute | solution.py:643
  386.4 4.2 %collective-permute-done.82 = bf16[128,1152]{1,0:T(8,128)(2,1)S(1)} collective-permute-done((bf16[128,1152]{1,0:T(8,128)(2,1)S(1)}, bf16[128,1152]{1,0:T(8,128)(2,1)S(1)}, u32[]{:S(2)}, u32[]{:S(2)}) %collective-permute-start.82) | collective-permute-done | bytes 294944 | tf_op jit(solution)/shard_map/ppermute | solution.py:643
  (419 shorter events, 200.3 us)
Async XLA Ops:
  61.2 13.7 %collective-permute-start.19 = (bf16[864,1152]{1,0:T(8,128)(2,1)S(1)}, bf16[864,1152]{1,0:T(8,128)(2,1)S(1)}, u32[]{:S(2)}, u32[]{:S(2)}) collective-permute-start(bf16[864,1152]{1,0:T(8,128)(2,1)S(1)} %bitcast.54), channel_id=1, source_target_pairs={{0,1},{1,0},{2,3},{3,2},{4,5},{5,4},{6,7},{7,6},{8,9},{9,8},{10,11... | collective-permute-start | bytes 5971976 | tf_op jit(solution)/shard_map/ppermute | solution.py:505
  61.7 13.2 %collective-permute-start.20 = (bf16[864,1152]{1,0:T(8,128)(2,1)S(1)}, bf16[864,1152]{1,0:T(8,128)(2,1)S(1)}, u32[]{:S(2)}, u32[]{:S(2)}) collective-permute-start(bf16[864,1152]{1,0:T(8,128)(2,1)S(1)} %bitcast.63), channel_id=1, source_target_pairs={{0,1},{1,0},{2,3},{3,2},{4,5},{5,4},{6,7},{7,6},{8,9},{9,8},{10,11... | collective-permute-start | bytes 5971976 | tf_op jit(solution)/shard_map/ppermute | solution.py:505
  61.8 13.1 %collective-permute-start.21 = (bf16[864,1152]{1,0:T(8,128)(2,1)S(1)}, bf16[864,1152]{1,0:T(8,128)(2,1)S(1)}, u32[]{:S(2)}, u32[]{:S(2)}) collective-permute-start(bf16[864,1152]{1,0:T(8,128)(2,1)S(1)} %copy-done.2), channel_id=1, source_target_pairs={{0,1},{1,0},{2,3},{3,2},{4,5},{5,4},{6,7},{7,6},{8,9},{9,8},{10,11... | collective-permute-start | bytes 5971976 | tf_op jit(solution)/shard_map/ppermute | solution.py:505
  66.5 16.1 %collective-permute-start.22 = (bf16[256,1152]{1,0:T(8,128)(2,1)S(1)}, bf16[256,1152]{1,0:T(8,128)(2,1)S(1)}, u32[]{:S(2)}, u32[]{:S(2)}) collective-permute-start(bf16[256,1152]{1,0:T(8,128)(2,1)S(1)} %multiply_convert_fusion.1.refs_0_.refs_4_), channel_id=1, source_target_pairs={{0,2},{1,3},{2,0},{3,1},{4,6},{5,7},{6,4},{7,5},{8,10},{9,11},{10,... | collective-permute-start | bytes 1769480 | tf_op jit(solution)/shard_map/ppermute | solution.py:505
  69.0 15.1 %collective-permute-start.23 = (bf16[256,1152]{1,0:T(8,128)(2,1)S(1)}, bf16[256,1152]{1,0:T(8,128)(2,1)S(1)}, u32[]{:S(2)}, u32[]{:S(2)}) collective-permute-start(bf16[256,1152]{1,0:T(8,128)(2,1)S(1)} %multiply_convert_fusion.1.refs_0_.refs_4_), channel_id=1, source_target_pairs={{0,4},{1,5},{2,6},{3,7},{4,0},{5,1},{6,2},{7,3},{8,12},{9,13},{10,... | collective-permute-start | bytes 1769480 | tf_op jit(solution)/shard_map/ppermute | solution.py:505
  157.4 20.3 %collective-permute-start.37 = (bf16[288,1152]{1,0:T(8,128)(2,1)S(1)}, bf16[288,1152]{1,0:T(8,128)(2,1)S(1)}, u32[]{:S(2)}, u32[]{:S(2)}) collective-permute-start(bf16[288,1152]{1,0:T(8,128)(2,1)S(1)} %get-tuple-element.529), channel_id=1, source_target_pairs={{0,8},{24,16},{1,9},{25,17},{2,10},{26,18},{3,11},{27,19},{4,12},{... | collective-permute-start | bytes 1990664 | tf_op jit(solution)/shard_map/ppermute | solution.py:645
  162.5 13.8 %collective-permute-start.40 = (bf16[128,1152]{1,0:T(8,128)(2,1)S(1)}, bf16[128,1152]{1,0:T(8,128)(2,1)S(1)}, u32[]{:S(2)}, u32[]{:S(2)}) collective-permute-start(bf16[128,1152]{1,0:T(8,128)(2,1)S(1)} %get-tuple-element.532), channel_id=1, source_target_pairs={{0,2},{1,3},{2,0},{3,1},{4,6},{5,7},{6,4},{7,5},{8,10},{9,11},{10,... | collective-permute-start | bytes 884744 | tf_op jit(solution)/shard_map/ppermute | solution.py:505
  162.9 14.8 %collective-permute-start.41 = (bf16[128,1152]{1,0:T(8,128)(2,1)S(1)}, bf16[128,1152]{1,0:T(8,128)(2,1)S(1)}, u32[]{:S(2)}, u32[]{:S(2)}) collective-permute-start(bf16[128,1152]{1,0:T(8,128)(2,1)S(1)} %get-tuple-element.533), channel_id=1, source_target_pairs={{0,4},{1,5},{2,6},{3,7},{4,0},{5,1},{6,2},{7,3},{8,12},{9,13},{10,... | collective-permute-start | bytes 884744 | tf_op jit(solution)/shard_map/ppermute | solution.py:505
  177.7 17.1 %collective-permute-start.42 = (bf16[288,1152]{1,0:T(8,128)(2,1)S(1)}, bf16[288,1152]{1,0:T(8,128)(2,1)S(1)}, u32[]{:S(2)}, u32[]{:S(2)}) collective-permute-start(bf16[288,1152]{1,0:T(8,128)(2,1)S(1)} %get-tuple-element.548), channel_id=1, source_target_pairs={{0,8},{24,16},{1,9},{25,17},{2,10},{26,18},{3,11},{27,19},{4,12},{... | collective-permute-start | bytes 1990664 | tf_op jit(solution)/shard_map/ppermute | solution.py:645
  180.2 14.6 %collective-permute-start.43 = (bf16[288,1152]{1,0:T(8,128)(2,1)S(1)}, bf16[288,1152]{1,0:T(8,128)(2,1)S(1)}, u32[]{:S(2)}, u32[]{:S(2)}) collective-permute-start(bf16[288,1152]{1,0:T(8,128)(2,1)S(1)} %add_convert_fusion.17), channel_id=1, source_target_pairs={{8,16},{16,8},{9,17},{17,9},{10,18},{18,10},{11,19},{19,11},{12,20... | collective-permute-start | bytes 1990664 | tf_op jit(solution)/shard_map/ppermute | solution.py:647
  194.8 20.3 %collective-permute-start.49 = (bf16[864,1152]{1,0:T(8,128)(2,1)S(1)}, bf16[864,1152]{1,0:T(8,128)(2,1)S(1)}, u32[]{:S(2)}, u32[]{:S(2)}) collective-permute-start(bf16[864,1152]{1,0:T(8,128)(2,1)S(1)} %weight_grad.9), channel_id=1, source_target_pairs={{0,1},{1,0},{2,3},{3,2},{4,5},{5,4},{6,7},{7,6},{8,9},{9,8},{10,11... | collective-permute-start | bytes 5971976 | tf_op jit(solution)/shard_map/ppermute | solution.py:505
  195.1 20.0 %collective-permute-start.47 = (bf16[288,1152]{1,0:T(8,128)(2,1)S(1)}, bf16[288,1152]{1,0:T(8,128)(2,1)S(1)}, u32[]{:S(2)}, u32[]{:S(2)}) collective-permute-start(bf16[288,1152]{1,0:T(8,128)(2,1)S(1)} %broadcast_select_fusion.15), channel_id=1, source_target_pairs={{0,8},{8,0},{16,24},{24,16},{1,9},{9,1},{17,25},{25,17},{2,10},{10... | collective-permute-start | bytes 1990664 | tf_op jit(solution)/shard_map/ppermute | solution.py:640
  199.6 15.4 %collective-permute-start.48 = (bf16[288,1152]{1,0:T(8,128)(2,1)S(1)}, bf16[288,1152]{1,0:T(8,128)(2,1)S(1)}, u32[]{:S(2)}, u32[]{:S(2)}) collective-permute-start(bf16[288,1152]{1,0:T(8,128)(2,1)S(1)} %add_convert_fusion.16), channel_id=1, source_target_pairs={{8,16},{16,8},{9,17},{17,9},{10,18},{18,10},{11,19},{19,11},{12,20... | collective-permute-start | bytes 1990664 | tf_op jit(solution)/shard_map/ppermute | solution.py:647
  215.3 19.4 %collective-permute-start.50 = (bf16[288,1152]{1,0:T(8,128)(2,1)S(1)}, bf16[288,1152]{1,0:T(8,128)(2,1)S(1)}, u32[]{:S(2)}, u32[]{:S(2)}) collective-permute-start(bf16[288,1152]{1,0:T(8,128)(2,1)S(1)} %broadcast_select_fusion.14), channel_id=1, source_target_pairs={{0,8},{8,0},{16,24},{24,16},{1,9},{9,1},{17,25},{25,17},{2,10},{10... | collective-permute-start | bytes 1990664 | tf_op jit(solution)/shard_map/ppermute | solution.py:640
  219.4 15.4 %collective-permute-start.51 = (bf16[288,1152]{1,0:T(8,128)(2,1)S(1)}, bf16[288,1152]{1,0:T(8,128)(2,1)S(1)}, u32[]{:S(2)}, u32[]{:S(2)}) collective-permute-start(bf16[288,1152]{1,0:T(8,128)(2,1)S(1)} %add_convert_fusion.13), channel_id=1, source_target_pairs={{8,16},{16,8},{9,17},{17,9},{10,18},{18,10},{11,19},{19,11},{12,20... | collective-permute-start | bytes 1990664 | tf_op jit(solution)/shard_map/ppermute | solution.py:647
  220.8 14.0 %collective-permute-start.53 = (bf16[256,512]{1,0:T(8,128)(2,1)S(1)}, bf16[256,512]{1,0:T(8,128)(2,1)S(1)}, u32[]{:S(2)}, u32[]{:S(2)}) collective-permute-start(bf16[256,512]{1,0:T(8,128)(2,1)S(1)} %get-tuple-element.720), channel_id=1, source_target_pairs={{0,2},{1,3},{2,0},{3,1},{4,6},{5,7},{6,4},{7,5},{8,10},{9,11},{10,... | collective-permute-start | bytes 786440 | tf_op jit(solution)/shard_map/ppermute | solution.py:505
  222.1 12.7 %collective-permute-start.54 = (bf16[256,512]{1,0:T(8,128)(2,1)S(1)}, bf16[256,512]{1,0:T(8,128)(2,1)S(1)}, u32[]{:S(2)}, u32[]{:S(2)}) collective-permute-start(bf16[256,512]{1,0:T(8,128)(2,1)S(1)} %get-tuple-element.719), channel_id=1, source_target_pairs={{0,4},{1,5},{2,6},{3,7},{4,0},{5,1},{6,2},{7,3},{8,12},{9,13},{10,... | collective-permute-start | bytes 786440 | tf_op jit(solution)/shard_map/ppermute | solution.py:505
  236.3 18.3 %collective-permute-start.55 = (bf16[288,1152]{1,0:T(8,128)(2,1)S(1)}, bf16[288,1152]{1,0:T(8,128)(2,1)S(1)}, u32[]{:S(2)}, u32[]{:S(2)}) collective-permute-start(bf16[288,1152]{1,0:T(8,128)(2,1)S(1)} %broadcast_select_fusion.13), channel_id=1, source_target_pairs={{0,8},{8,0},{16,24},{24,16},{1,9},{9,1},{17,25},{25,17},{2,10},{10... | collective-permute-start | bytes 1990664 | tf_op jit(solution)/shard_map/ppermute | solution.py:640
  240.1 14.5 %collective-permute-start.56 = (bf16[288,1152]{1,0:T(8,128)(2,1)S(1)}, bf16[288,1152]{1,0:T(8,128)(2,1)S(1)}, u32[]{:S(2)}, u32[]{:S(2)}) collective-permute-start(bf16[288,1152]{1,0:T(8,128)(2,1)S(1)} %add_convert_fusion.11), channel_id=1, source_target_pairs={{8,16},{16,8},{9,17},{17,9},{10,18},{18,10},{11,19},{19,11},{12,20... | collective-permute-start | bytes 1990664 | tf_op jit(solution)/shard_map/ppermute | solution.py:647
  255.3 17.4 %collective-permute-start.59 = (bf16[288,1152]{1,0:T(8,128)(2,1)S(1)}, bf16[288,1152]{1,0:T(8,128)(2,1)S(1)}, u32[]{:S(2)}, u32[]{:S(2)}) collective-permute-start(bf16[288,1152]{1,0:T(8,128)(2,1)S(1)} %broadcast_select_fusion.12), channel_id=1, source_target_pairs={{0,8},{8,0},{16,24},{24,16},{1,9},{9,1},{17,25},{25,17},{2,10},{10... | collective-permute-start | bytes 1990664 | tf_op jit(solution)/shard_map/ppermute | solution.py:640
  259.2 13.6 %collective-permute-start.60 = (bf16[288,1152]{1,0:T(8,128)(2,1)S(1)}, bf16[288,1152]{1,0:T(8,128)(2,1)S(1)}, u32[]{:S(2)}, u32[]{:S(2)}) collective-permute-start(bf16[288,1152]{1,0:T(8,128)(2,1)S(1)} %add_convert_fusion.10), channel_id=1, source_target_pairs={{8,16},{16,8},{9,17},{17,9},{10,18},{18,10},{11,19},{19,11},{12,20... | collective-permute-start | bytes 1990664 | tf_op jit(solution)/shard_map/ppermute | solution.py:647
  273.0 16.4 %collective-permute-start.63 = (bf16[288,1152]{1,0:T(8,128)(2,1)S(1)}, bf16[288,1152]{1,0:T(8,128)(2,1)S(1)}, u32[]{:S(2)}, u32[]{:S(2)}) collective-permute-start(bf16[288,1152]{1,0:T(8,128)(2,1)S(1)} %broadcast_select_fusion.11), channel_id=1, source_target_pairs={{0,8},{8,0},{16,24},{24,16},{1,9},{9,1},{17,25},{25,17},{2,10},{10... | collective-permute-start | bytes 1990664 | tf_op jit(solution)/shard_map/ppermute | solution.py:640
  289.7 21.6 %collective-permute-start.67 = (bf16[288,1152]{1,0:T(8,128)(2,1)S(1)}, bf16[288,1152]{1,0:T(8,128)(2,1)S(1)}, u32[]{:S(2)}, u32[]{:S(2)}) collective-permute-start(bf16[288,1152]{1,0:T(8,128)(2,1)S(1)} %broadcast_select_fusion.10), channel_id=1, source_target_pairs={{0,8},{8,0},{16,24},{24,16},{1,9},{9,1},{17,25},{25,17},{2,10},{10... | collective-permute-start | bytes 1990664 | tf_op jit(solution)/shard_map/ppermute | solution.py:640
  296.7 14.6 %collective-permute-start.68 = (bf16[288,1152]{1,0:T(8,128)(2,1)S(1)}, bf16[288,1152]{1,0:T(8,128)(2,1)S(1)}, u32[]{:S(2)}, u32[]{:S(2)}) collective-permute-start(bf16[288,1152]{1,0:T(8,128)(2,1)S(1)} %add_convert_fusion.5), channel_id=1, source_target_pairs={{8,16},{16,8},{9,17},{17,9},{10,18},{18,10},{11,19},{19,11},{12,20... | collective-permute-start | bytes 1990664 | tf_op jit(solution)/shard_map/ppermute | solution.py:647
  297.7 12.6 %collective-permute-start.69 = (bf16[160,1536]{1,0:T(8,128)(2,1)S(1)}, bf16[160,1536]{1,0:T(8,128)(2,1)S(1)}, u32[]{:S(2)}, u32[]{:S(2)}) collective-permute-start(bf16[160,1536]{1,0:T(8,128)(2,1)S(1)} %get-tuple-element.657), channel_id=1, source_target_pairs={{0,2},{1,3},{2,0},{3,1},{4,6},{5,7},{6,4},{7,5},{8,10},{9,11},{10,... | collective-permute-start | bytes 1474568 | tf_op jit(solution)/shard_map/ppermute | solution.py:505
  311.6 17.8 %collective-permute-start.71 = (bf16[288,1152]{1,0:T(8,128)(2,1)S(1)}, bf16[288,1152]{1,0:T(8,128)(2,1)S(1)}, u32[]{:S(2)}, u32[]{:S(2)}) collective-permute-start(bf16[288,1152]{1,0:T(8,128)(2,1)S(1)} %broadcast_select_fusion.9), channel_id=1, source_target_pairs={{0,8},{8,0},{16,24},{24,16},{1,9},{9,1},{17,25},{25,17},{2,10},{10... | collective-permute-start | bytes 1990664 | tf_op jit(solution)/shard_map/ppermute | solution.py:640
  315.7 13.7 %collective-permute-start.72 = (bf16[288,1152]{1,0:T(8,128)(2,1)S(1)}, bf16[288,1152]{1,0:T(8,128)(2,1)S(1)}, u32[]{:S(2)}, u32[]{:S(2)}) collective-permute-start(bf16[288,1152]{1,0:T(8,128)(2,1)S(1)} %add_convert_fusion.3), channel_id=1, source_target_pairs={{8,16},{16,8},{9,17},{17,9},{10,18},{18,10},{11,19},{19,11},{12,20... | collective-permute-start | bytes 1990664 | tf_op jit(solution)/shard_map/ppermute | solution.py:647
  316.4 12.6 %collective-permute-start.73 = (bf16[160,1536]{1,0:T(8,128)(2,1)S(1)}, bf16[160,1536]{1,0:T(8,128)(2,1)S(1)}, u32[]{:S(2)}, u32[]{:S(2)}) collective-permute-start(bf16[160,1536]{1,0:T(8,128)(2,1)S(1)} %get-tuple-element.665), channel_id=1, source_target_pairs={{0,6},{1,7},{2,4},{3,5},{4,2},{5,3},{6,0},{7,1},{8,14},{9,15},{10,... | collective-permute-start | bytes 1474568 | tf_op jit(solution)/shard_map/ppermute | solution.py:505
  329.6 19.4 %collective-permute-start.75 = (bf16[288,1152]{1,0:T(8,128)(2,1)S(1)}, bf16[288,1152]{1,0:T(8,128)(2,1)S(1)}, u32[]{:S(2)}, u32[]{:S(2)}) collective-permute-start(bf16[288,1152]{1,0:T(8,128)(2,1)S(1)} %add_convert_fusion.2), channel_id=1, source_target_pairs={{8,16},{16,8},{9,17},{17,9},{10,18},{18,10},{11,19},{19,11},{12,20... | collective-permute-start | bytes 1990664 | tf_op jit(solution)/shard_map/ppermute | solution.py:647
  330.5 20.6 %collective-permute-start.76 = (bf16[288,1152]{1,0:T(8,128)(2,1)S(1)}, bf16[288,1152]{1,0:T(8,128)(2,1)S(1)}, u32[]{:S(2)}, u32[]{:S(2)}) collective-permute-start(bf16[288,1152]{1,0:T(8,128)(2,1)S(1)} %add_convert_fusion.1), channel_id=1, source_target_pairs={{8,0},{16,24},{9,1},{17,25},{10,2},{18,26},{11,3},{19,27},{12,4},{... | collective-permute-start | bytes 1990664 | tf_op jit(solution)/shard_map/ppermute | solution.py:643
  332.0 16.9 %collective-permute-start.74 = (bf16[160,1536]{1,0:T(8,128)(2,1)S(1)}, bf16[160,1536]{1,0:T(8,128)(2,1)S(1)}, u32[]{:S(2)}, u32[]{:S(2)}) collective-permute-start(bf16[160,1536]{1,0:T(8,128)(2,1)S(1)} %add_convert_fusion.21), channel_id=1, source_target_pairs={{0,8},{24,16},{1,9},{25,17},{2,10},{26,18},{3,11},{27,19},{4,12},{... | collective-permute-start | bytes 1474568 | tf_op jit(solution)/shard_map/ppermute | solution.py:645
  353.5 15.1 %collective-permute-start.79 = (bf16[288,1152]{1,0:T(8,128)(2,1)S(1)}, bf16[288,1152]{1,0:T(8,128)(2,1)S(1)}, u32[]{:S(2)}, u32[]{:S(2)}) collective-permute-start(bf16[288,1152]{1,0:T(8,128)(2,1)S(1)} %add_convert_fusion), channel_id=1, source_target_pairs={{8,0},{16,24},{9,1},{17,25},{10,2},{18,26},{11,3},{19,27},{12,4},{... | collective-permute-start | bytes 1990664 | tf_op jit(solution)/shard_map/ppermute | solution.py:643
  (104 other events, 662.2 us)

commit v4 on v3

--- a/solution.py
+++ b/solution.py
@@ -61,14 +61,29 @@
     shape = (BLOCK, BLOCK)
     query = first_row + lax.broadcasted_iota(jnp.int32, shape, 0)
     key = block_id * BLOCK + lax.broadcasted_iota(jnp.int32, shape, 1)
-    return (key <= query) & (key >= query - pos_ref[...])
+    return (key <= query) & (key >= query - pos_ref[:, :1])
+
+
+def head_rows(h):
+    return pl.ds(h * BLOCK, BLOCK)
 
 
 def put_queries(q_ref, q_pre_ref, gain_ref, cosine, sine):
     for h in range(HEADS):
-        cols = pl.ds(h * HEAD, HEAD)
-        normed, _ = rms_forward(q_pre_ref[:, cols])
-        q_ref[:, cols] = rotate(normed * gain_ref[...], cosine, sine).astype(bf16)
+        normed, _ = rms_forward(q_pre_ref[:, pl.ds(h * HEAD, HEAD)])
+        q_ref[head_rows(h), :] = rotate(normed * gain_ref[...], cosine, sine).astype(bf16)
+
+
+def column_blocks(columns, order_ref):
+    if columns == 1:
+        for h in range(HEADS):
+            yield pl.ds(h * HEAD, HEAD), head_rows(h), pl.ds(0, HEAD)
+        return
+    slot, size = order_ref.shape[0] - columns, HEADS * HEAD // columns
+    for k in range(columns):
+        at = order_ref[slot + k] * size
+        rows = pl.ds(pl.multiple_of(at // HEAD * BLOCK, BLOCK), BLOCK)
+        yield pl.ds(k * size, size), rows, pl.ds(pl.multiple_of(at % HEAD, size), size)
 
 
 def attend_kernel(
@@ -82,12 +97,11 @@
     pos_ref,
     *refs,
 ):
-    kv_refs, (att_low_ref, inv_ref, q_ref, att_ref, total_ref) = refs[:-5], refs[-5:]
-    slot = order_ref.shape[0] - columns
+    kv_refs = refs[:-7]
+    att_low_ref, inv_ref, q_ref, att_ref, total_ref, score_ref, weight_ref = refs[-7:]
     first_row = order_ref[n_blocks]
     first_key = order_ref[n_blocks + 1]
-    cosine, sine = cos_ref[...], sin_ref[...]
-    put_queries(q_ref, q_pre_ref, gain_ref, cosine, sine)
+    put_queries(q_ref, q_pre_ref, gain_ref, cos_ref[...], sin_ref[...])
     att_ref[...] = jnp.zeros_like(att_ref)
     total_ref[...] = jnp.zeros_like(total_ref)
 
@@ -98,15 +112,14 @@
         @pl.when(live)
         def _():
             rows = pl.ds(pl.multiple_of(k * BLOCK, BLOCK), BLOCK)
-            keys = kv_ref[rows, :HEAD]
-            vals = kv_ref[rows, HEAD:]
             visible = visible_mask(block_id, first_row, pos_ref)
+            score_ref[...] = dot_rows(q_ref[...], kv_ref[rows, :HEAD])
             for h in range(HEADS):
-                cols = pl.ds(h * HEAD, HEAD)
-                scores = dot_rows(q_ref[:, cols], keys) * score_scale
-                weight = jnp.where(visible, jnp.exp(scores), 0.0)
-                total_ref[:, pl.ds(h * LANES, LANES)] += weight[:, :LANES] + weight[:, LANES:]
-                att_ref[:, cols] += dot(weight.astype(bf16), vals)
+                at = head_rows(h)
+                weight = jnp.where(visible, jnp.exp(score_ref[at, :] * score_scale), 0.0)
+                total_ref[at, :] += weight[:, :LANES] + weight[:, LANES:]
+                weight_ref[at, :] = weight.astype(bf16)
+            att_ref[...] += dot(weight_ref[...], kv_ref[rows, HEAD:])
 
         return 0
 
@@ -114,15 +127,12 @@
     for i, kv_ref in enumerate(kv_refs):
         lax.fori_loop(0, each, functools.partial(step, kv_ref, i * each), 0)
     for h in range(HEADS):
-        cols = pl.ds(h * HEAD, HEAD)
-        lanes = pl.ds(h * LANES, LANES)
-        inverse = 1.0 / jnp.sum(total_ref[:, lanes], axis=-1, keepdims=True)
+        at = head_rows(h)
+        inverse = 1.0 / jnp.sum(total_ref[at, :], axis=-1, keepdims=True)
         inv_ref[:, pl.ds(h, 1)] = inverse
-        att_ref[:, cols] = att_ref[:, cols] * inverse
-    size = HEADS * HEAD // columns
-    for k in range(columns):
-        source = pl.ds(pl.multiple_of(order_ref[slot + k] * size, size), size)
-        att_low_ref[:, pl.ds(k * size, size)] = att_ref[:, source].astype(bf16)
+        att_ref[at, :] = att_ref[at, :] * inverse
+    for stored, rows, lanes in column_blocks(columns, order_ref):
+        att_low_ref[:, stored] = att_ref[rows, lanes].astype(bf16)
 
 
 def attend(columns, order, q_pre, cosine, sine, gain, pos, *kv):
@@ -138,12 +148,14 @@
         in_specs=[pl.BlockSpec(memory_space=pltpu.SMEM)] + [whole] * (5 + len(kv)),
         out_specs=(whole,) * 2,
         scratch_shapes=[
-            pltpu.VMEM((rows, HEADS * HEAD), bf16),
-            pltpu.VMEM((rows, HEADS * HEAD), f32),
-            pltpu.VMEM((rows, HEADS * LANES), f32),
+            pltpu.VMEM((HEADS * rows, HEAD), bf16),
+            pltpu.VMEM((HEADS * rows, HEAD), f32),
+            pltpu.VMEM((HEADS * rows, LANES), f32),
+            pltpu.VMEM((HEADS * rows, HEAD), f32),
+            pltpu.VMEM((HEADS * rows, HEAD), bf16),
         ],
         cost_estimate=BRIEF,
-        compiler_params=pltpu.CompilerParams(vmem_limit_bytes=8 << 20),
+        compiler_params=pltpu.CompilerParams(vmem_limit_bytes=10 << 20),
         name="attend",
     )(order, q_pre, cosine, sine, gain, pos, *kv)
 
@@ -162,23 +174,25 @@
     d_moved_ref,
     *refs,
 ):
-    groups = (len(refs) - 7) // 2
-    kv_refs, d_q_pre_ref, d_kv_refs = refs[:groups], refs[groups], refs[groups + 1 : -6]
-    d_gain_ref, d_q_ref, row_dot_ref, d_att_ref, q_ref, dot_ref = refs[-6:]
+    groups = (len(refs) - 10) // 2
+    kv_refs, d_q_pre_ref, d_kv_refs = refs[:groups], refs[groups], refs[groups + 1 : -9]
+    d_gain_ref, d_q_ref, row_dot_ref, d_att_ref, q_ref = refs[-9:-4]
+    score_ref, d_prob_ref, prob_ref, d_score_ref = refs[-4:]
     cosine, sine = cos_ref[...], sin_ref[...]
     put_queries(q_ref, q_pre_ref, gain_ref, cosine, sine)
-    slot = order_ref.shape[0] - columns
-    size = HEADS * HEAD // columns
-    for k in range(columns):
-        target = pl.ds(pl.multiple_of(order_ref[slot + k] * size, size), size)
-        moved = d_moved_ref[:, pl.ds(k * size, size)]
-        d_att_ref[:, target] = moved
-        dot_ref[:, target] = moved.astype(f32) * att_ref[:, pl.ds(k * size, size)].astype(f32)
+    row_dot_ref[...] = jnp.zeros_like(row_dot_ref)
+    for stored, rows, lanes in column_blocks(columns, order_ref):
+        moved = d_moved_ref[:, stored]
+        d_att_ref[rows, lanes] = moved
+        product = moved.astype(f32) * att_ref[:, stored].astype(f32)
+        for i in range(product.shape[1] // LANES):
+            row_dot_ref[rows, :] += product[:, i * LANES : (i + 1) * LANES]
+    for h in range(HEADS):
+        at = head_rows(h)
+        total = jnp.sum(row_dot_ref[at, :], axis=-1, keepdims=True)
+        row_dot_ref[at, pl.ds(0, 1)] = total
     first_row = order_ref[n_blocks]
     first_key = order_ref[n_blocks + 1]
-    for h in range(HEADS):
-        cols = pl.ds(h * HEAD, HEAD)
-        row_dot_ref[:, pl.ds(h, 1)] = jnp.sum(dot_ref[:, cols], axis=-1, keepdims=True)
     d_q_ref[...] = jnp.zeros_like(d_q_ref)
 
     def step(kv_ref, d_kv_ref, base, k, _):
@@ -189,25 +203,20 @@
         @pl.when(live)
         def _():
             keys = kv_ref[rows, :HEAD]
-            vals = kv_ref[rows, HEAD:]
             visible = visible_mask(block_id, first_row, pos_ref)
-            d_keys = jnp.zeros((BLOCK, HEAD), f32)
-            d_vals = jnp.zeros((BLOCK, HEAD), f32)
+            score_ref[...] = dot_rows(q_ref[...], keys)
+            d_prob_ref[...] = dot_rows(d_att_ref[...], kv_ref[rows, HEAD:])
             for h in range(HEADS):
-                cols = pl.ds(h * HEAD, HEAD)
-                query = q_ref[:, cols]
-                d_att = d_att_ref[:, cols]
-                inverse = inv_ref[:, pl.ds(h, 1)]
-                row_dot = row_dot_ref[:, pl.ds(h, 1)]
-                scores = dot_rows(query, keys) * score_scale
-                prob = jnp.where(visible, jnp.exp(scores), 0.0) * inverse
-                d_prob = dot_rows(d_att, vals)
-                d_scores = (prob * (d_prob - row_dot)).astype(bf16)
-                d_q_ref[:, cols] += dot(d_scores, keys)
-                d_keys += dot_cols(d_scores, query)
-                d_vals += dot_cols(prob.astype(bf16), d_att)
+                at = head_rows(h)
+                weight = jnp.where(visible, jnp.exp(score_ref[at, :] * score_scale), 0.0)
+                prob = weight * inv_ref[:, pl.ds(h, 1)]
+                prob_ref[at, :] = prob.astype(bf16)
+                d_score = prob * (d_prob_ref[at, :] - row_dot_ref[at, pl.ds(0, 1)])
+                d_score_ref[at, :] = d_score.astype(bf16)
+            d_q_ref[...] += dot(d_score_ref[...], keys)
+            d_keys = dot_cols(d_score_ref[...], q_ref[...])
             d_kv_ref[rows, :HEAD] = (d_keys * score_scale).astype(bf16)
-            d_kv_ref[rows, HEAD:] = d_vals.astype(bf16)
+            d_kv_ref[rows, HEAD:] = dot_cols(prob_ref[...], d_att_ref[...]).astype(bf16)
 
         @pl.when(jnp.logical_not(live))
         def _():
@@ -223,7 +232,7 @@
     for h in range(HEADS):
         cols = pl.ds(h * HEAD, HEAD)
         normed, factor = rms_forward(q_pre_ref[:, cols])
-        d_normed = rotate(d_q_ref[:, cols] * score_scale, cosine, -sine)
+        d_normed = rotate(d_q_ref[head_rows(h), :] * score_scale, cosine, -sine)
         d_gain += jnp.sum(d_normed * normed, axis=0, keepdims=True)
         d_q_pre_ref[:, cols] = rms_backward(d_normed * gain_ref[...], normed, factor).astype(bf16)
     d_gain_ref[...] = d_gain
@@ -243,14 +252,17 @@
         in_specs=[pl.BlockSpec(memory_space=pltpu.SMEM)] + [whole] * (8 + len(kv)),
         out_specs=(whole,) * (2 + len(kv)),
         scratch_shapes=[
-            pltpu.VMEM((rows, HEADS * HEAD), f32),
-            pltpu.VMEM((rows, LANES), f32),
-            pltpu.VMEM((rows, HEADS * HEAD), bf16),
-            pltpu.VMEM((rows, HEADS * HEAD), bf16),
-            pltpu.VMEM((rows, HEADS * HEAD), f32),
+            pltpu.VMEM((HEADS * rows, HEAD), f32),
+            pltpu.VMEM((HEADS * rows, LANES), f32),
+            pltpu.VMEM((HEADS * rows, HEAD), bf16),
+            pltpu.VMEM((HEADS * rows, HEAD), bf16),
+            pltpu.VMEM((HEADS * rows, HEAD), f32),
+            pltpu.VMEM((HEADS * rows, HEAD), f32),
+            pltpu.VMEM((HEADS * rows, HEAD), bf16),
+            pltpu.VMEM((HEADS * rows, HEAD), bf16),
         ],
         cost_estimate=BRIEF,
-        compiler_params=pltpu.CompilerParams(vmem_limit_bytes=10 << 20),
+        compiler_params=pltpu.CompilerParams(vmem_limit_bytes=16 << 20),
         name="attend_back",
     )(order, q_pre, cosine, sine, gain, pos, *saved, d_att, *kv)
 
@@ -703,38 +715,39 @@
     shard = width // n
     starts = (comm.rank * shard, comm.rank * (HEAD // n), HEAD + comm.rank * (HEAD // n))
     line = comm.line()
-    position_column = positions[:, None]
+    position_column = positions[:, None] + jnp.zeros((1, LANES), jnp.int32)
 
     x = layer_input[0].astype(f32)
-    keyval_sent = comm.send(w_keyval)
+    near = comm.near(w_keyval), comm.near(w_query)
     a_normed, a_factor = rms_forward(x)
     a_low = (a_normed * g_input).astype(bf16)
     a_columns = comm.columns(a_low)
     angles = rope_angles(positions, HEAD)
     cosine, sine = jnp.cos(angles), jnp.sin(angles)
-    keyval_sent, a_columns, w_query, order, starts, position_column, line.inner, comm.rank = fence(
-        (keyval_sent, a_columns, w_query, order, starts, position_column, line.inner, comm.rank)
+    near, a_columns, order, starts, position_column, line.inner, comm.rank = fence(
+        (near, a_columns, order, starts, position_column, line.inner, comm.rank)
     )
-    query_near = comm.near(w_query)
-    keyval_blocks = comm.paired(keyval_sent)
+    far = [comm.far(v) for v in near]
+    far, w_out = fence((far, w_out))
+    out_near = comm.near(w_out)
+    keyval_blocks = comm.joined(w_keyval, near[0], far[0])
+    query_blocks = comm.joined(w_query, near[1], far[1])
     kv_pre = add(*[dot(a, w) for a, w in zip(a_columns, keyval_blocks)])
     k_hat, k_factor = rms_forward(kv_pre[:, :HEAD])
     k_low = rotate(k_hat * g_key, cosine, sine).astype(bf16)
     kv_low = jnp.concatenate([k_low, kv_pre[:, HEAD:].astype(bf16)], axis=1)
-    kv_low, query_near = fence((kv_low, query_near))
+    kv_low, keyval_blocks, query_blocks = fence((kv_low, keyval_blocks, query_blocks))
     kv_near = comm.near(kv_low)
-    query_far = comm.far(query_near)
-    kv_near, query_near, query_far, w_out = fence((kv_near, query_near, query_far, w_out))
+    q_pre = add(*[dot(a, w) for a, w in zip(a_columns, query_blocks)])
+    kv_near, out_near, q_pre = fence((kv_near, out_near, q_pre))
     kv_far = comm.far(kv_near)
-    query_blocks = comm.joined(w_query, query_near, query_far)
-    q_pre = add(*[dot(a, w) for a, w in zip(a_columns, query_blocks)])
-    kv_far, q_pre, w_out, query_blocks, keyval_blocks = fence(
-        (kv_far, q_pre, w_out, query_blocks, keyval_blocks)
+    kv_far, out_near = fence((kv_far, out_near))
+    kv_blocks = comm.joined(kv_low, kv_near, kv_far)
+    out_far = comm.far(out_near)
+    kv_blocks, out_far, w_gate, w_up, w_down, query_blocks, keyval_blocks = fence(
+        (kv_blocks, out_far, w_gate, w_up, w_down, query_blocks, keyval_blocks)
     )
-    out_near = comm.near(w_out)
-    kv_blocks = comm.joined(kv_low, kv_near, kv_far)
-    kv_blocks, out_near, w_gate, w_up, w_down = fence((kv_blocks, out_near, w_gate, w_up, w_down))
-    out_far = comm.far(out_near)
+    out_blocks = comm.joined(w_out, out_near, out_far)
     head_args = (
         comm.slots().shape[0],
         order,
@@ -746,8 +759,7 @@
         *kv_blocks,
     )
     att_low, inverse = attend(*head_args)
-    out_far, att_low, w_gate, w_up, w_down = fence((out_far, att_low, w_gate, w_up, w_down))
-    out_blocks = comm.joined(w_out, out_near, out_far)
+    out_blocks, att_low, w_gate, w_up, w_down = fence((out_blocks, att_low, w_gate, w_up, w_down))
     gate_w, up_w, down_w = [comm.pair(w) for w in (w_gate.T, w_up.T, w_down)]
     groups = len(gate_w)
     att_columns = jnp.split(att_low, len(out_blocks), axis=1)

time: 397 us -> 392 us (0.987)
  waiting for transfers between devices: 154 us -> 165 us
  starting transfers between devices: 116 us -> 106 us
  local copies, waits for them, and re-layouts: 15.5 us -> 9.94 us
    ppermute x57 -> x58, starting transfers between devices: 55.3 us -> 45.9 us  [hop(): return lax.ppermute(value, 'seq', [(i, i ^ bit) for i in range(8)])]
    ppermute x57 -> x58, waiting for transfers between devices: 88.5 us -> 96.9 us  [hop(): return lax.ppermute(value, 'seq', [(i, i ^ bit) for i in range(8)])]
  transfers between devices with their start and end apart: 83 -> 84, of which waited for: 46 -> 51; matrix products, arithmetic and copies ran while one was open for 12% -> 11% of each run, Pallas kernels for 14% -> 14%
where the time goes in v4:
time: 392 us; the launch traced here: 386 us
  waiting for transfers between devices  165 us (42%)
  starting transfers between devices  106 us (27%)
  Pallas kernels  58.7 us (15%)
  other arithmetic  24.7 us (6%)
  matrix products  18.7 us (5%)
  local copies, waits for them, and re-layouts  9.94 us (3%)
    ppermute x58, waiting for transfers between devices, hop(): return lax.ppermute(value, 'seq', [(i, i ^ bit) for i in range(8)])  96.9 us
    ppermute x58, starting transfers between devices, hop(): return lax.ppermute(value, 'seq', [(i, i ^ bit) for i in range(8)])  45.9 us
    ppermute x7, waiting for transfers between devices, step(): got['in'] = lax.ppermute(both, 'dp', [(0, 1), (1, 0), (2, 3), (3, 2)])  31.9 us
    ppermute x7, starting transfers between devices, step(): got['in'] = lax.ppermute(both, 'dp', [(0, 1), (1, 0), (2, 3), (3, 2)])  30.2 us
    ppermute x4, waiting for transfers between devices, step(): got['out'] = lax.ppermute(back, 'dp', [(1, 0), (2, 3)])  24.6 us
    pallas_call x4, Pallas kernels, feed(): pl.pallas_call(functools.partial(feed_kernel, groups, len(b)), out_shape=...  18.1 us
    pallas_call x4, Pallas kernels, feed_back(): pl.pallas_call(functools.partial(feed_back_kernel, groups, len(d)), out_s...  17.7 us
    ppermute x4, starting transfers between devices, step(): got['in'] = lax.ppermute(mine, 'dp', [(0, 1), (3, 2)])  17 us
  transfers between devices with their start and end apart: 84, of which 51 were waited for; matrix products, arithmetic and copies ran while one was open for 11% of the time, Pallas kernels for 14%

profile of v4, /device:TPU:0, one launch (start us, length us, event | category | flops | bytes accessed | tf_op | source)
XLA Modules:
  0.0 386.1 jit_solution(11706405688024526928)
XLA Ops:
  35.2 4.6 %collective-permute-done.10 = bf16[256,512]{1,0:T(8,128)(2,1)S(1)} collective-permute-done((bf16[256,512]{1,0:T(8,128)(2,1)S(1)}, bf16[256,512]{1,0:T(8,128)(2,1)S(1)}, u32[]{:S(2)}, u32[]{:S(2)}) %collective-permute-start.10) | collective-permute-done | bytes 262176 | tf_op jit(solution)/shard_map/ppermute | solution.py:517
  48.0 5.2 %collective-permute-done.17 = bf16[64,1152]{1,0:T(8,128)(2,1)S(1)} collective-permute-done((bf16[64,1152]{1,0:T(8,128)(2,1)S(1)}, bf16[64,1152]{1,0:T(8,128)(2,1)S(1)}, u32[]{:S(2)}, u32[]{:S(2)}) %collective-permute-start.17) | collective-permute-done | bytes 147488 | tf_op jit(solution)/shard_map/ppermute | solution.py:517
  64.2 4.6 %convolution_convert_fusion = bf16[1152,1024]{1,0:T(8,128)(2,1)} fusion(bf16[576,1024]{1,0:T(8,128)(2,1)S(1)} %collective-permute-done.9, bf16[576,1024]{1,0:T(8,128)(2,1)S(1)} %constant_dynamic-update-slice_fusion.5, s32[]{:T(128)S(6)} %axis_index.22, s32[1152]{0:T(1024)S(1)} %get-tuple-element.749, s32[1152]{0:T(1024)S(1)} %get-tuple-element.750, ...), kind=kOutput, calls=%fused_computation.58 | convolution fusion | flops 2771582976 | bytes 4739332 | tf_op jit(solution)/shard_map/dot_general | solution.py:49
  69.6 4.5 %feed.4 = (f32[128,1152]{1,0:T(8,128)S(1)}, f32[128,1152]{1,0:T(8,128)S(1)}, bf16[2,256,864]{2,1,0:T(8,128)(2,1)S(1)}, bf16[2,256,864]{2,1,0:T(8,128)(2,1)S(1)}, bf16[2,256,864]{2,1,0:T(8,128)(2,1)S(1)}) custom-call(bf16[256,1152]{1,0:T(8,128)(2,1)S(1)} %multiply_convert_fusion.1.refs_0_.refs_4_, bf16[864,1152]{1,0:T(8,128)(2,1)S(1)} %bitcast.54, ...), custom_call_target="tpu_custom_call" | custom-call | flops 1 | bytes 1 | tf_op jit(solution)/shard_map/feed/pallas_call | solution.py:306
  79.8 4.7 %feed.5 = (bf16[128,1152]{1,0:T(8,128)(2,1)S(1)}, bf16[128,1152]{1,0:T(8,128)(2,1)S(1)}, bf16[2,256,864]{2,1,0:T(8,128)(2,1)S(1)}, bf16[2,256,864]{2,1,0:T(8,128)(2,1)S(1)}, bf16[2,256,864]{2,1,0:T(8,128)(2,1)S(1)}) custom-call(bf16[256,1152]{1,0:T(8,128)(2,1)S(1)} %collective-permute-done.23.refs_0_.refs_5_, bf16[864,1152]{1,0:T(8,128)(2,1)S(1)} %bitcast.55, ...), custom_call_target="tpu_custom_call" | custom-call | flops 1 | bytes 1 | tf_op jit(solution)/shard_map/feed/pallas_call | solution.py:306
  84.5 4.5 %feed.6 = (bf16[128,1152]{1,0:T(8,128)(2,1)S(1)}, bf16[128,1152]{1,0:T(8,128)(2,1)S(1)}, bf16[2,256,864]{2,1,0:T(8,128)(2,1)S(1)}, bf16[2,256,864]{2,1,0:T(8,128)(2,1)S(1)}, bf16[2,256,864]{2,1,0:T(8,128)(2,1)S(1)}) custom-call(bf16[256,1152]{1,0:T(8,128)(2,1)S(1)} %collective-permute-done.24.refs_0_.refs_6_, bf16[864,1152]{1,0:T(8,128)(2,1)S(1)} %bitcast.56, ...), custom_call_target="tpu_custom_call" | custom-call | flops 1 | bytes 1 | tf_op jit(solution)/shard_map/feed/pallas_call | solution.py:306
  92.2 4.5 %feed.7 = (bf16[128,1152]{1,0:T(8,128)(2,1)S(1)}, bf16[128,1152]{1,0:T(8,128)(2,1)S(1)}, bf16[2,256,864]{2,1,0:T(8,128)(2,1)S(1)}, bf16[2,256,864]{2,1,0:T(8,128)(2,1)S(1)}, bf16[2,256,864]{2,1,0:T(8,128)(2,1)S(1)}) custom-call(bf16[128,1152]{1,0:T(8,128)(2,1)S(1)} %collective-permute-done.25.refs_0_.refs_7_, ...), custom_call_target="tpu_custom_call" | custom-call | flops 1 | bytes 1 | tf_op jit(solution)/shard_map/feed/pallas_call | solution.py:306
  99.9 4.7 %collective-permute-done.31 = bf16[128,1152]{1,0:T(8,128)(2,1)S(1)} collective-permute-done((bf16[128,1152]{1,0:T(8,128)(2,1)S(1)}, bf16[128,1152]{1,0:T(8,128)(2,1)S(1)}, u32[]{:S(2)}, u32[]{:S(2)}) %collective-permute-start.31) | collective-permute-done | bytes 294944 | tf_op jit(solution)/shard_map/ppermute | solution.py:517
  120.5 4.5 %feed_back.4 = (f32[128,1152]{1,0:T(8,128)S(1)}, f32[128,1152]{1,0:T(8,128)S(1)}, bf16[2,256,864]{2,1,0:T(8,128)(2,1)S(1)}, bf16[2,256,864]{2,1,0:T(8,128)(2,1)S(1)}) custom-call(bf16[2,256,864]{2,1,0:T(8,128)(2,1)S(1)} %get-tuple-element.470.act_ref, bf16[2,256,864]{2,1,0:T(8,128)(2,1)S(1)} %get-tuple-element.471.slope_ref, ...), custom_call_target="tpu_custom_call" | custom-call | flops 1 | bytes 1 | tf_op jit(solution)/shard_map/feed_back/pallas_call | solution.py:337
  125.2 5.0 %collective-permute-done.33.refs_0_.refs_5_ = bf16[256,1152]{1,0:T(8,128)(2,1)S(1)} collective-permute-done((bf16[256,1152]{1,0:T(8,128)(2,1)S(1)}, bf16[256,1152]{1,0:T(8,128)(2,1)S(1)}, u32[]{:S(2)}, u32[]{:S(2)}) %collective-permute-start.33) | collective-permute-done | bytes 589856 | tf_op jit(solution)/shard_map/ppermute | solution.py:517
  132.1 4.3 %feed_back.5 = (bf16[128,1152]{1,0:T(8,128)(2,1)S(1)}, bf16[128,1152]{1,0:T(8,128)(2,1)S(1)}, bf16[2,256,864]{2,1,0:T(8,128)(2,1)S(1)}, bf16[2,256,864]{2,1,0:T(8,128)(2,1)S(1)}) custom-call(bf16[2,256,864]{2,1,0:T(8,128)(2,1)S(1)} %get-tuple-element.485.act_ref, bf16[2,256,864]{2,1,0:T(8,128)(2,1)S(1)} %get-tuple-element.486.slope_ref, ...), custom_call_target="tpu_custom_call" | custom-call | flops 1 | bytes 1 | tf_op jit(solution)/shard_map/feed_back/pallas_call | solution.py:337
  136.3 4.3 %feed_back.6 = (bf16[128,1152]{1,0:T(8,128)(2,1)S(1)}, bf16[128,1152]{1,0:T(8,128)(2,1)S(1)}, bf16[2,256,864]{2,1,0:T(8,128)(2,1)S(1)}, bf16[2,256,864]{2,1,0:T(8,128)(2,1)S(1)}) custom-call(bf16[2,256,864]{2,1,0:T(8,128)(2,1)S(1)} %get-tuple-element.491.act_ref, bf16[2,256,864]{2,1,0:T(8,128)(2,1)S(1)} %get-tuple-element.492.slope_ref, ...), custom_call_target="tpu_custom_call" | custom-call | flops 1 | bytes 1 | tf_op jit(solution)/shard_map/feed_back/pallas_call | solution.py:337
  143.2 4.7 %feed_back.7 = (bf16[128,1152]{1,0:T(8,128)(2,1)S(1)}, bf16[128,1152]{1,0:T(8,128)(2,1)S(1)}, bf16[2,256,864]{2,1,0:T(8,128)(2,1)S(1)}, bf16[2,256,864]{2,1,0:T(8,128)(2,1)S(1)}) custom-call(bf16[2,256,864]{2,1,0:T(8,128)(2,1)S(1)} %get-tuple-element.511.act_ref, bf16[2,256,864]{2,1,0:T(8,128)(2,1)S(1)} %get-tuple-element.512.slope_ref, ...), custom_call_target="tpu_custom_call" | custom-call | flops 1 | bytes 1 | tf_op jit(solution)/shard_map/feed_back/pallas_call | solution.py:337
  164.5 4.6 %collective-permute-done.41 = bf16[128,1152]{1,0:T(8,128)(2,1)S(1)} collective-permute-done((bf16[128,1152]{1,0:T(8,128)(2,1)S(1)}, bf16[128,1152]{1,0:T(8,128)(2,1)S(1)}, u32[]{:S(2)}, u32[]{:S(2)}) %collective-permute-start.41) | collective-permute-done | bytes 294944 | tf_op jit(solution)/shard_map/ppermute | solution.py:517
  187.9 4.2 %collective-permute-start.48 = (bf16[288,1152]{1,0:T(8,128)(2,1)S(1)}, bf16[288,1152]{1,0:T(8,128)(2,1)S(1)}, u32[]{:S(2)}, u32[]{:S(2)}) collective-permute-start(bf16[288,1152]{1,0:T(8,128)(2,1)S(1)} %broadcast_select_fusion.15), channel_id=1, source_target_pairs={{0,8},{8,0},{16,24},{24,16},{1,9},{9,1},{17,25},{25,17},{2,10},{10... | collective-permute-start | bytes 1990664 | tf_op jit(solution)/shard_map/ppermute | solution.py:652
  197.4 10.2 %collective-permute-done.48 = bf16[288,1152]{1,0:T(8,128)(2,1)S(1)} collective-permute-done((bf16[288,1152]{1,0:T(8,128)(2,1)S(1)}, bf16[288,1152]{1,0:T(8,128)(2,1)S(1)}, u32[]{:S(2)}, u32[]{:S(2)}) %collective-permute-start.48) | collective-permute-done | bytes 663584 | tf_op jit(solution)/shard_map/ppermute | solution.py:652
  207.9 3.9 %collective-permute-start.51 = (bf16[288,1152]{1,0:T(8,128)(2,1)S(1)}, bf16[288,1152]{1,0:T(8,128)(2,1)S(1)}, u32[]{:S(2)}, u32[]{:S(2)}) collective-permute-start(bf16[288,1152]{1,0:T(8,128)(2,1)S(1)} %broadcast_select_fusion.14), channel_id=1, source_target_pairs={{0,8},{8,0},{16,24},{24,16},{1,9},{9,1},{17,25},{25,17},{2,10},{10... | collective-permute-start | bytes 1990664 | tf_op jit(solution)/shard_map/ppermute | solution.py:652
  219.2 8.2 %collective-permute-done.51 = bf16[288,1152]{1,0:T(8,128)(2,1)S(1)} collective-permute-done((bf16[288,1152]{1,0:T(8,128)(2,1)S(1)}, bf16[288,1152]{1,0:T(8,128)(2,1)S(1)}, u32[]{:S(2)}, u32[]{:S(2)}) %collective-permute-start.51) | collective-permute-done | bytes 663584 | tf_op jit(solution)/shard_map/ppermute | solution.py:652
  230.6 3.8 collective-permute-start.56
  240.8 8.1 %collective-permute-done.56 = bf16[288,1152]{1,0:T(8,128)(2,1)S(1)} collective-permute-done((bf16[288,1152]{1,0:T(8,128)(2,1)S(1)}, bf16[288,1152]{1,0:T(8,128)(2,1)S(1)}, u32[]{:S(2)}, u32[]{:S(2)}) %collective-permute-start.56) | collective-permute-done | bytes 663584 | tf_op jit(solution)/shard_map/ppermute | solution.py:652
  249.6 3.8 collective-permute-start.60
  262.2 4.8 %collective-permute-done.60 = bf16[288,1152]{1,0:T(8,128)(2,1)S(1)} collective-permute-done((bf16[288,1152]{1,0:T(8,128)(2,1)S(1)}, bf16[288,1152]{1,0:T(8,128)(2,1)S(1)}, u32[]{:S(2)}, u32[]{:S(2)}) %collective-permute-start.60) | collective-permute-done | bytes 663584 | tf_op jit(solution)/shard_map/ppermute | solution.py:652
  274.4 8.1 %collective-permute-done.67 = bf16[128,1152]{1,0:T(8,128)(2,1)S(1)} collective-permute-done((bf16[128,1152]{1,0:T(8,128)(2,1)S(1)}, bf16[128,1152]{1,0:T(8,128)(2,1)S(1)}, u32[]{:S(2)}, u32[]{:S(2)}) %collective-permute-start.67) | collective-permute-done | bytes 294944 | tf_op jit(solution)/shard_map/ppermute | solution.py:517
  283.9 6.9 %collective-permute-start.68 = (bf16[288,1152]{1,0:T(8,128)(2,1)S(1)}, bf16[288,1152]{1,0:T(8,128)(2,1)S(1)}, u32[]{:S(2)}, u32[]{:S(2)}) collective-permute-start(bf16[288,1152]{1,0:T(8,128)(2,1)S(1)} %broadcast_select_fusion.10), channel_id=1, source_target_pairs={{0,8},{8,0},{16,24},{24,16},{1,9},{9,1},{17,25},{25,17},{2,10},{10... | collective-permute-start | bytes 1990664 | tf_op jit(solution)/shard_map/ppermute | solution.py:652
  293.4 11.1 %collective-permute-done.70 = bf16[160,1536]{1,0:T(8,128)(2,1)S(1)} collective-permute-done((bf16[160,1536]{1,0:T(8,128)(2,1)S(1)}, bf16[160,1536]{1,0:T(8,128)(2,1)S(1)}, u32[]{:S(2)}, u32[]{:S(2)}) %collective-permute-start.70) | collective-permute-done | bytes 491552 | tf_op jit(solution)/shard_map/ppermute | solution.py:517
  305.8 3.9 %collective-permute-start.72 = (bf16[288,1152]{1,0:T(8,128)(2,1)S(1)}, bf16[288,1152]{1,0:T(8,128)(2,1)S(1)}, u32[]{:S(2)}, u32[]{:S(2)}) collective-permute-start(bf16[288,1152]{1,0:T(8,128)(2,1)S(1)} %broadcast_select_fusion.9), channel_id=1, source_target_pairs={{0,8},{8,0},{16,24},{24,16},{1,9},{9,1},{17,25},{25,17},{2,10},{10... | collective-permute-start | bytes 1990664 | tf_op jit(solution)/shard_map/ppermute | solution.py:652
  313.7 9.6 %collective-permute-done.74 = bf16[160,1536]{1,0:T(8,128)(2,1)S(1)} collective-permute-done((bf16[160,1536]{1,0:T(8,128)(2,1)S(1)}, bf16[160,1536]{1,0:T(8,128)(2,1)S(1)}, u32[]{:S(2)}, u32[]{:S(2)}) %collective-permute-start.74) | collective-permute-done | bytes 491552 | tf_op jit(solution)/shard_map/ppermute | solution.py:517
  326.3 8.8 %collective-permute-start.75 = (bf16[160,1536]{1,0:T(8,128)(2,1)S(1)}, bf16[160,1536]{1,0:T(8,128)(2,1)S(1)}, u32[]{:S(2)}, u32[]{:S(2)}) collective-permute-start(bf16[160,1536]{1,0:T(8,128)(2,1)S(1)} %add_convert_fusion.21), channel_id=1, source_target_pairs={{0,8},{24,16},{1,9},{25,17},{2,10},{26,18},{3,11},{27,19},{4,12},{... | collective-permute-start | bytes 1474568 | tf_op jit(solution)/shard_map/ppermute | solution.py:657
  335.3 8.0 %collective-permute-done.75 = bf16[160,1536]{1,0:T(8,128)(2,1)S(1)} collective-permute-done((bf16[160,1536]{1,0:T(8,128)(2,1)S(1)}, bf16[160,1536]{1,0:T(8,128)(2,1)S(1)}, u32[]{:S(2)}, u32[]{:S(2)}) %collective-permute-start.75) | collective-permute-done | bytes 491552 | tf_op jit(solution)/shard_map/ppermute | solution.py:657
  351.9 11.1 %collective-permute-done.80 = bf16[288,1152]{1,0:T(8,128)(2,1)S(1)} collective-permute-done((bf16[288,1152]{1,0:T(8,128)(2,1)S(1)}, bf16[288,1152]{1,0:T(8,128)(2,1)S(1)}, u32[]{:S(2)}, u32[]{:S(2)}) %collective-permute-start.80) | collective-permute-done | bytes 663584 | tf_op jit(solution)/shard_map/ppermute | solution.py:655
  367.4 7.1 %collective-permute-done.82 = bf16[160,1536]{1,0:T(8,128)(2,1)S(1)} collective-permute-done((bf16[160,1536]{1,0:T(8,128)(2,1)S(1)}, bf16[160,1536]{1,0:T(8,128)(2,1)S(1)}, u32[]{:S(2)}, u32[]{:S(2)}) %collective-permute-start.82) | collective-permute-done | bytes 491552 | tf_op jit(solution)/shard_map/ppermute | solution.py:655
  380.8 4.2 %collective-permute-done.83 = bf16[128,1152]{1,0:T(8,128)(2,1)S(1)} collective-permute-done((bf16[128,1152]{1,0:T(8,128)(2,1)S(1)}, bf16[128,1152]{1,0:T(8,128)(2,1)S(1)}, u32[]{:S(2)}, u32[]{:S(2)}) %collective-permute-start.83) | collective-permute-done | bytes 294944 | tf_op jit(solution)/shard_map/ppermute | solution.py:655
  (370 shorter events, 192.7 us)
Async XLA Ops:
  61.0 16.3 %collective-permute-start.23 = (bf16[256,1152]{1,0:T(8,128)(2,1)S(1)}, bf16[256,1152]{1,0:T(8,128)(2,1)S(1)}, u32[]{:S(2)}, u32[]{:S(2)}) collective-permute-start(bf16[256,1152]{1,0:T(8,128)(2,1)S(1)} %multiply_convert_fusion.1.refs_0_.refs_4_), channel_id=1, source_target_pairs={{0,2},{1,3},{2,0},{3,1},{4,6},{5,7},{6,4},{7,5},{8,10},{9,11},{10,... | collective-permute-start | bytes 1769480 | tf_op jit(solution)/shard_map/ppermute | solution.py:517
  63.7 15.0 %collective-permute-start.24 = (bf16[256,1152]{1,0:T(8,128)(2,1)S(1)}, bf16[256,1152]{1,0:T(8,128)(2,1)S(1)}, u32[]{:S(2)}, u32[]{:S(2)}) collective-permute-start(bf16[256,1152]{1,0:T(8,128)(2,1)S(1)} %multiply_convert_fusion.1.refs_0_.refs_4_), channel_id=1, source_target_pairs={{0,4},{1,5},{2,6},{3,7},{4,0},{5,1},{6,2},{7,3},{8,12},{9,13},{10,... | collective-permute-start | bytes 1769480 | tf_op jit(solution)/shard_map/ppermute | solution.py:517
  117.6 12.6 %collective-permute-start.33 = (bf16[256,1152]{1,0:T(8,128)(2,1)S(1)}, bf16[256,1152]{1,0:T(8,128)(2,1)S(1)}, u32[]{:S(2)}, u32[]{:S(2)}) collective-permute-start(bf16[256,1152]{1,0:T(8,128)(2,1)S(1)} %get-tuple-element.469.refs_0_.refs_4_), channel_id=1, source_target_pairs={{0,2},{1,3},{2,0},{3,1},{4,6},{5,7},{6,4},{7,5},{8,10},{9,11},{10,... | collective-permute-start | bytes 1769480 | tf_op jit(solution)/shard_map/ppermute | solution.py:517
  117.8 12.9 %collective-permute-start.34 = (bf16[256,1152]{1,0:T(8,128)(2,1)S(1)}, bf16[256,1152]{1,0:T(8,128)(2,1)S(1)}, u32[]{:S(2)}, u32[]{:S(2)}) collective-permute-start(bf16[256,1152]{1,0:T(8,128)(2,1)S(1)} %get-tuple-element.469.refs_0_.refs_4_), channel_id=1, source_target_pairs={{0,4},{1,5},{2,6},{3,7},{4,0},{5,1},{6,2},{7,3},{8,12},{9,13},{10,... | collective-permute-start | bytes 1769480 | tf_op jit(solution)/shard_map/ppermute | solution.py:517
  150.4 19.6 %collective-permute-start.38 = (bf16[288,1152]{1,0:T(8,128)(2,1)S(1)}, bf16[288,1152]{1,0:T(8,128)(2,1)S(1)}, u32[]{:S(2)}, u32[]{:S(2)}) collective-permute-start(bf16[288,1152]{1,0:T(8,128)(2,1)S(1)} %get-tuple-element.537), channel_id=1, source_target_pairs={{0,8},{24,16},{1,9},{25,17},{2,10},{26,18},{3,11},{27,19},{4,12},{... | collective-permute-start | bytes 1990664 | tf_op jit(solution)/shard_map/ppermute | solution.py:657
  156.6 12.5 %collective-permute-start.41 = (bf16[128,1152]{1,0:T(8,128)(2,1)S(1)}, bf16[128,1152]{1,0:T(8,128)(2,1)S(1)}, u32[]{:S(2)}, u32[]{:S(2)}) collective-permute-start(bf16[128,1152]{1,0:T(8,128)(2,1)S(1)} %get-tuple-element.540), channel_id=1, source_target_pairs={{0,2},{1,3},{2,0},{3,1},{4,6},{5,7},{6,4},{7,5},{8,10},{9,11},{10,... | collective-permute-start | bytes 884744 | tf_op jit(solution)/shard_map/ppermute | solution.py:517
  157.7 12.4 %collective-permute-start.42 = (bf16[128,1152]{1,0:T(8,128)(2,1)S(1)}, bf16[128,1152]{1,0:T(8,128)(2,1)S(1)}, u32[]{:S(2)}, u32[]{:S(2)}) collective-permute-start(bf16[128,1152]{1,0:T(8,128)(2,1)S(1)} %get-tuple-element.541), channel_id=1, source_target_pairs={{0,4},{1,5},{2,6},{3,7},{4,0},{5,1},{6,2},{7,3},{8,12},{9,13},{10,... | collective-permute-start | bytes 884744 | tf_op jit(solution)/shard_map/ppermute | solution.py:517
  170.1 17.5 %collective-permute-start.43 = (bf16[288,1152]{1,0:T(8,128)(2,1)S(1)}, bf16[288,1152]{1,0:T(8,128)(2,1)S(1)}, u32[]{:S(2)}, u32[]{:S(2)}) collective-permute-start(bf16[288,1152]{1,0:T(8,128)(2,1)S(1)} %get-tuple-element.556), channel_id=1, source_target_pairs={{0,8},{24,16},{1,9},{25,17},{2,10},{26,18},{3,11},{27,19},{4,12},{... | collective-permute-start | bytes 1990664 | tf_op jit(solution)/shard_map/ppermute | solution.py:657
  173.1 14.6 %collective-permute-start.44 = (bf16[288,1152]{1,0:T(8,128)(2,1)S(1)}, bf16[288,1152]{1,0:T(8,128)(2,1)S(1)}, u32[]{:S(2)}, u32[]{:S(2)}) collective-permute-start(bf16[288,1152]{1,0:T(8,128)(2,1)S(1)} %add_convert_fusion.17), channel_id=1, source_target_pairs={{8,16},{16,8},{9,17},{17,9},{10,18},{18,10},{11,19},{19,11},{12,20... | collective-permute-start | bytes 1990664 | tf_op jit(solution)/shard_map/ppermute | solution.py:659
  187.7 20.0 %collective-permute-start.50 = (bf16[864,1152]{1,0:T(8,128)(2,1)S(1)}, bf16[864,1152]{1,0:T(8,128)(2,1)S(1)}, u32[]{:S(2)}, u32[]{:S(2)}) collective-permute-start(bf16[864,1152]{1,0:T(8,128)(2,1)S(1)} %weight_grad.9), channel_id=1, source_target_pairs={{0,1},{1,0},{2,3},{3,2},{4,5},{5,4},{6,7},{7,6},{8,9},{9,8},{10,11... | collective-permute-start | bytes 5971976 | tf_op jit(solution)/shard_map/ppermute | solution.py:517
  187.9 19.7 %collective-permute-start.48 = (bf16[288,1152]{1,0:T(8,128)(2,1)S(1)}, bf16[288,1152]{1,0:T(8,128)(2,1)S(1)}, u32[]{:S(2)}, u32[]{:S(2)}) collective-permute-start(bf16[288,1152]{1,0:T(8,128)(2,1)S(1)} %broadcast_select_fusion.15), channel_id=1, source_target_pairs={{0,8},{8,0},{16,24},{24,16},{1,9},{9,1},{17,25},{25,17},{2,10},{10... | collective-permute-start | bytes 1990664 | tf_op jit(solution)/shard_map/ppermute | solution.py:652
  192.3 15.4 %collective-permute-start.49 = (bf16[288,1152]{1,0:T(8,128)(2,1)S(1)}, bf16[288,1152]{1,0:T(8,128)(2,1)S(1)}, u32[]{:S(2)}, u32[]{:S(2)}) collective-permute-start(bf16[288,1152]{1,0:T(8,128)(2,1)S(1)} %add_convert_fusion.16), channel_id=1, source_target_pairs={{8,16},{16,8},{9,17},{17,9},{10,18},{18,10},{11,19},{19,11},{12,20... | collective-permute-start | bytes 1990664 | tf_op jit(solution)/shard_map/ppermute | solution.py:659
  207.9 19.5 %collective-permute-start.51 = (bf16[288,1152]{1,0:T(8,128)(2,1)S(1)}, bf16[288,1152]{1,0:T(8,128)(2,1)S(1)}, u32[]{:S(2)}, u32[]{:S(2)}) collective-permute-start(bf16[288,1152]{1,0:T(8,128)(2,1)S(1)} %broadcast_select_fusion.14), channel_id=1, source_target_pairs={{0,8},{8,0},{16,24},{24,16},{1,9},{9,1},{17,25},{25,17},{2,10},{10... | collective-permute-start | bytes 1990664 | tf_op jit(solution)/shard_map/ppermute | solution.py:652
  212.0 15.4 %collective-permute-start.52 = (bf16[288,1152]{1,0:T(8,128)(2,1)S(1)}, bf16[288,1152]{1,0:T(8,128)(2,1)S(1)}, u32[]{:S(2)}, u32[]{:S(2)}) collective-permute-start(bf16[288,1152]{1,0:T(8,128)(2,1)S(1)} %add_convert_fusion.13), channel_id=1, source_target_pairs={{8,16},{16,8},{9,17},{17,9},{10,18},{18,10},{11,19},{19,11},{12,20... | collective-permute-start | bytes 1990664 | tf_op jit(solution)/shard_map/ppermute | solution.py:659
  213.4 14.0 %collective-permute-start.54 = (bf16[256,512]{1,0:T(8,128)(2,1)S(1)}, bf16[256,512]{1,0:T(8,128)(2,1)S(1)}, u32[]{:S(2)}, u32[]{:S(2)}) collective-permute-start(bf16[256,512]{1,0:T(8,128)(2,1)S(1)} %get-tuple-element.728), channel_id=1, source_target_pairs={{0,2},{1,3},{2,0},{3,1},{4,6},{5,7},{6,4},{7,5},{8,10},{9,11},{10,... | collective-permute-start | bytes 786440 | tf_op jit(solution)/shard_map/ppermute | solution.py:517
  214.4 13.0 %collective-permute-start.55 = (bf16[256,512]{1,0:T(8,128)(2,1)S(1)}, bf16[256,512]{1,0:T(8,128)(2,1)S(1)}, u32[]{:S(2)}, u32[]{:S(2)}) collective-permute-start(bf16[256,512]{1,0:T(8,128)(2,1)S(1)} %get-tuple-element.727), channel_id=1, source_target_pairs={{0,4},{1,5},{2,6},{3,7},{4,0},{5,1},{6,2},{7,3},{8,12},{9,13},{10,... | collective-permute-start | bytes 786440 | tf_op jit(solution)/shard_map/ppermute | solution.py:517
  230.6 18.3 %collective-permute-start.56 = (bf16[288,1152]{1,0:T(8,128)(2,1)S(1)}, bf16[288,1152]{1,0:T(8,128)(2,1)S(1)}, u32[]{:S(2)}, u32[]{:S(2)}) collective-permute-start(bf16[288,1152]{1,0:T(8,128)(2,1)S(1)} %broadcast_select_fusion.13), channel_id=1, source_target_pairs={{0,8},{8,0},{16,24},{24,16},{1,9},{9,1},{17,25},{25,17},{2,10},{10... | collective-permute-start | bytes 1990664 | tf_op jit(solution)/shard_map/ppermute | solution.py:652
  234.4 14.5 %collective-permute-start.57 = (bf16[288,1152]{1,0:T(8,128)(2,1)S(1)}, bf16[288,1152]{1,0:T(8,128)(2,1)S(1)}, u32[]{:S(2)}, u32[]{:S(2)}) collective-permute-start(bf16[288,1152]{1,0:T(8,128)(2,1)S(1)} %add_convert_fusion.11), channel_id=1, source_target_pairs={{8,16},{16,8},{9,17},{17,9},{10,18},{18,10},{11,19},{19,11},{12,20... | collective-permute-start | bytes 1990664 | tf_op jit(solution)/shard_map/ppermute | solution.py:659
  249.6 17.4 %collective-permute-start.60 = (bf16[288,1152]{1,0:T(8,128)(2,1)S(1)}, bf16[288,1152]{1,0:T(8,128)(2,1)S(1)}, u32[]{:S(2)}, u32[]{:S(2)}) collective-permute-start(bf16[288,1152]{1,0:T(8,128)(2,1)S(1)} %broadcast_select_fusion.12), channel_id=1, source_target_pairs={{0,8},{8,0},{16,24},{24,16},{1,9},{9,1},{17,25},{25,17},{2,10},{10... | collective-permute-start | bytes 1990664 | tf_op jit(solution)/shard_map/ppermute | solution.py:652
  253.4 13.6 %collective-permute-start.61 = (bf16[288,1152]{1,0:T(8,128)(2,1)S(1)}, bf16[288,1152]{1,0:T(8,128)(2,1)S(1)}, u32[]{:S(2)}, u32[]{:S(2)}) collective-permute-start(bf16[288,1152]{1,0:T(8,128)(2,1)S(1)} %add_convert_fusion.10), channel_id=1, source_target_pairs={{8,16},{16,8},{9,17},{17,9},{10,18},{18,10},{11,19},{19,11},{12,20... | collective-permute-start | bytes 1990664 | tf_op jit(solution)/shard_map/ppermute | solution.py:659
  267.3 16.4 %collective-permute-start.64 = (bf16[288,1152]{1,0:T(8,128)(2,1)S(1)}, bf16[288,1152]{1,0:T(8,128)(2,1)S(1)}, u32[]{:S(2)}, u32[]{:S(2)}) collective-permute-start(bf16[288,1152]{1,0:T(8,128)(2,1)S(1)} %broadcast_select_fusion.11), channel_id=1, source_target_pairs={{0,8},{8,0},{16,24},{24,16},{1,9},{9,1},{17,25},{25,17},{2,10},{10... | collective-permute-start | bytes 1990664 | tf_op jit(solution)/shard_map/ppermute | solution.py:652
  271.2 12.5 %collective-permute-start.65 = (bf16[288,1152]{1,0:T(8,128)(2,1)S(1)}, bf16[288,1152]{1,0:T(8,128)(2,1)S(1)}, u32[]{:S(2)}, u32[]{:S(2)}) collective-permute-start(bf16[288,1152]{1,0:T(8,128)(2,1)S(1)} %add_convert_fusion.7), channel_id=1, source_target_pairs={{8,16},{16,8},{9,17},{17,9},{10,18},{18,10},{11,19},{19,11},{12,20... | collective-permute-start | bytes 1990664 | tf_op jit(solution)/shard_map/ppermute | solution.py:659
  283.9 21.7 %collective-permute-start.68 = (bf16[288,1152]{1,0:T(8,128)(2,1)S(1)}, bf16[288,1152]{1,0:T(8,128)(2,1)S(1)}, u32[]{:S(2)}, u32[]{:S(2)}) collective-permute-start(bf16[288,1152]{1,0:T(8,128)(2,1)S(1)} %broadcast_select_fusion.10), channel_id=1, source_target_pairs={{0,8},{8,0},{16,24},{24,16},{1,9},{9,1},{17,25},{25,17},{2,10},{10... | collective-permute-start | bytes 1990664 | tf_op jit(solution)/shard_map/ppermute | solution.py:652
  291.0 14.6 %collective-permute-start.69 = (bf16[288,1152]{1,0:T(8,128)(2,1)S(1)}, bf16[288,1152]{1,0:T(8,128)(2,1)S(1)}, u32[]{:S(2)}, u32[]{:S(2)}) collective-permute-start(bf16[288,1152]{1,0:T(8,128)(2,1)S(1)} %add_convert_fusion.5), channel_id=1, source_target_pairs={{8,16},{16,8},{9,17},{17,9},{10,18},{18,10},{11,19},{19,11},{12,20... | collective-permute-start | bytes 1990664 | tf_op jit(solution)/shard_map/ppermute | solution.py:659
  291.9 12.6 %collective-permute-start.70 = (bf16[160,1536]{1,0:T(8,128)(2,1)S(1)}, bf16[160,1536]{1,0:T(8,128)(2,1)S(1)}, u32[]{:S(2)}, u32[]{:S(2)}) collective-permute-start(bf16[160,1536]{1,0:T(8,128)(2,1)S(1)} %get-tuple-element.665), channel_id=1, source_target_pairs={{0,2},{1,3},{2,0},{3,1},{4,6},{5,7},{6,4},{7,5},{8,10},{9,11},{10,... | collective-permute-start | bytes 1474568 | tf_op jit(solution)/shard_map/ppermute | solution.py:517
  305.8 17.8 %collective-permute-start.72 = (bf16[288,1152]{1,0:T(8,128)(2,1)S(1)}, bf16[288,1152]{1,0:T(8,128)(2,1)S(1)}, u32[]{:S(2)}, u32[]{:S(2)}) collective-permute-start(bf16[288,1152]{1,0:T(8,128)(2,1)S(1)} %broadcast_select_fusion.9), channel_id=1, source_target_pairs={{0,8},{8,0},{16,24},{24,16},{1,9},{9,1},{17,25},{25,17},{2,10},{10... | collective-permute-start | bytes 1990664 | tf_op jit(solution)/shard_map/ppermute | solution.py:652
  309.9 13.7 %collective-permute-start.73 = (bf16[288,1152]{1,0:T(8,128)(2,1)S(1)}, bf16[288,1152]{1,0:T(8,128)(2,1)S(1)}, u32[]{:S(2)}, u32[]{:S(2)}) collective-permute-start(bf16[288,1152]{1,0:T(8,128)(2,1)S(1)} %add_convert_fusion.3), channel_id=1, source_target_pairs={{8,16},{16,8},{9,17},{17,9},{10,18},{18,10},{11,19},{19,11},{12,20... | collective-permute-start | bytes 1990664 | tf_op jit(solution)/shard_map/ppermute | solution.py:659
  310.6 12.6 %collective-permute-start.74 = (bf16[160,1536]{1,0:T(8,128)(2,1)S(1)}, bf16[160,1536]{1,0:T(8,128)(2,1)S(1)}, u32[]{:S(2)}, u32[]{:S(2)}) collective-permute-start(bf16[160,1536]{1,0:T(8,128)(2,1)S(1)} %get-tuple-element.673), channel_id=1, source_target_pairs={{0,6},{1,7},{2,4},{3,5},{4,2},{5,3},{6,0},{7,1},{8,14},{9,15},{10,... | collective-permute-start | bytes 1474568 | tf_op jit(solution)/shard_map/ppermute | solution.py:517
  323.8 19.4 %collective-permute-start.76 = (bf16[288,1152]{1,0:T(8,128)(2,1)S(1)}, bf16[288,1152]{1,0:T(8,128)(2,1)S(1)}, u32[]{:S(2)}, u32[]{:S(2)}) collective-permute-start(bf16[288,1152]{1,0:T(8,128)(2,1)S(1)} %add_convert_fusion.2), channel_id=1, source_target_pairs={{8,16},{16,8},{9,17},{17,9},{10,18},{18,10},{11,19},{19,11},{12,20... | collective-permute-start | bytes 1990664 | tf_op jit(solution)/shard_map/ppermute | solution.py:659
  324.7 20.8 %collective-permute-start.77 = (bf16[288,1152]{1,0:T(8,128)(2,1)S(1)}, bf16[288,1152]{1,0:T(8,128)(2,1)S(1)}, u32[]{:S(2)}, u32[]{:S(2)}) collective-permute-start(bf16[288,1152]{1,0:T(8,128)(2,1)S(1)} %add_convert_fusion.1), channel_id=1, source_target_pairs={{8,0},{16,24},{9,1},{17,25},{10,2},{18,26},{11,3},{19,27},{12,4},{... | collective-permute-start | bytes 1990664 | tf_op jit(solution)/shard_map/ppermute | solution.py:655
  326.3 17.0 %collective-permute-start.75 = (bf16[160,1536]{1,0:T(8,128)(2,1)S(1)}, bf16[160,1536]{1,0:T(8,128)(2,1)S(1)}, u32[]{:S(2)}, u32[]{:S(2)}) collective-permute-start(bf16[160,1536]{1,0:T(8,128)(2,1)S(1)} %add_convert_fusion.21), channel_id=1, source_target_pairs={{0,8},{24,16},{1,9},{25,17},{2,10},{26,18},{3,11},{27,19},{4,12},{... | collective-permute-start | bytes 1474568 | tf_op jit(solution)/shard_map/ppermute | solution.py:657
  347.8 15.1 %collective-permute-start.80 = (bf16[288,1152]{1,0:T(8,128)(2,1)S(1)}, bf16[288,1152]{1,0:T(8,128)(2,1)S(1)}, u32[]{:S(2)}, u32[]{:S(2)}) collective-permute-start(bf16[288,1152]{1,0:T(8,128)(2,1)S(1)} %add_convert_fusion), channel_id=1, source_target_pairs={{8,0},{16,24},{9,1},{17,25},{10,2},{18,26},{11,3},{19,27},{12,4},{... | collective-permute-start | bytes 1990664 | tf_op jit(solution)/shard_map/ppermute | solution.py:655
  (78 other events, 486.4 us)

commit v5 on v4

--- a/solution.py
+++ b/solution.py
@@ -463,9 +463,14 @@
     def far(self, near):
         return ()
 
+    def spread(self, shard):
+        return tuple(jnp.split(self.joined(shard, (), ())[0], self.n, axis=0))
+
+    def first(self, shard, near):
+        return (near[0],)
+
     def tokens(self, shard, near, far):
-        whole = lax.all_gather(shard, "seq", axis=0, tiled=True)
-        return [(part,) for part in jnp.split(whole, self.n, axis=0)]
+        return [(part,) for part in near]
 
     def early(self, x, y):
         return ()
@@ -538,6 +543,12 @@
     def far(self, near):
         half = near[0].shape[0] // 2
         return (self.hop(near[1][:half], 2), self.hop(near[0][half:], 4))
+
+    def spread(self, shard):
+        return self.near(shard)
+
+    def first(self, shard, near):
+        return (shard,)
 
     def tokens(self, shard, near, far):
         return [(shard,), *[(v,) for v in near], tuple(far)]
@@ -652,7 +663,7 @@
             got["in"] = lax.ppermute(both, "dp", [(0, 1), (1, 0), (2, 3), (3, 2)])
         else:
             if back is not None:
-                got["out"] = lax.ppermute(back, "dp", [(1, 0), (2, 3)])
+                got["out"] = self.outwards(back)
             if mine is not None:
                 got["in"] = lax.ppermute(mine, "dp", [(0, 1), (3, 2)])
         if half is not None:
@@ -673,10 +684,18 @@
 
     def finish(self, early):
         count = len(self.chunks)
-        while self.at < count + 1:
+        while self.at < count:
             self.step(lambda values: values)
-        made = self.step(lambda _: early(self.out[count - 2].astype(f32)))
+        back, half = self.totals[count - 2], self.halves[count - 1]
+        back_moved = self.outwards(back)
+        total = add(half, lax.ppermute(half, "dp", [(1, 2), (2, 1)])).astype(bf16)
+        self.out[count - 2] = jnp.where(self.inner, back, back_moved)
+        self.out[count - 1] = jnp.where(self.inner, total, self.outwards(total))
+        made = early(self.out[count - 2].astype(f32))
         return [self.out[i].astype(f32) for i in range(count)], made
+
+    def outwards(self, value):
+        return lax.ppermute(value, "dp", [(1, 0), (2, 3)])
 
 
 def all_of(values):
@@ -771,8 +790,8 @@
     b_low, query_blocks, keyval_blocks = fence((b_low, query_blocks, keyval_blocks))
     weights = [w[i] for i in range(groups) for w in (gate_w, up_w, down_w)]
 
-    near = comm.near(b_low)
-    kept = [feed((b_low,), weights, f32)]
+    near = comm.spread(b_low)
+    kept = [feed(comm.first(b_low, near), weights, f32)]
     query_whole = comm.ordered(query_blocks)
     kept, near, query_whole, keyval_blocks = fence((kept, near, query_whole, keyval_blocks))
     far = comm.far(near)
@@ -801,9 +820,9 @@
     def other_half(lefts, rights):
         return weight_grad(1, [ff], lefts, rights) if groups > 1 else ()
 
-    near = comm.near(d_ffn)
+    near = comm.spread(d_ffn)
     gain_post_ffn = jnp.sum(g * ffn_normed, axis=0)
-    kept = [back((d_ffn,), 0)]
+    kept = [back(comm.first(d_ffn, near), 0)]
     keyval_whole = comm.ordered(keyval_blocks)
     kept, near, gain_post_ffn, keyval_whole = fence((kept, near, gain_post_ffn, keyval_whole))
     far = comm.far(near)

time: 392 us -> 388 us (0.990)
  waiting for transfers between devices: 165 us -> 157 us
  starting transfers between devices: 106 us -> 110 us
    ppermute x58, waiting for transfers between devices: 96.9 us -> 92.9 us  [hop(): return lax.ppermute(value, 'seq', [(i, i ^ bit) for i in range(8)])]
    ppermute x4 -> x5, waiting for transfers between devices: 24.6 us -> 21.4 us  [the longest x4 21.4 us: outwards(): return lax.ppermute(value, 'dp', [(1, 0), (2, 3)])]
    ppermute x11 -> x10, starting transfers between devices: 8.31 us -> 7.63 us  [step(): got['middle'] = lax.ppermute(half, 'dp', [(1, 2), (2, 1)])]
where the time goes in v5:
time: 388 us; the launch traced here: 382 us
  waiting for transfers between devices  157 us (40%)
  starting transfers between devices  110 us (28%)
  Pallas kernels  58.7 us (15%)
  other arithmetic  24.7 us (6%)
  matrix products  18.7 us (5%)
  local copies, waits for them, and re-layouts  9.94 us (3%)
    ppermute x58, waiting for transfers between devices, hop(): return lax.ppermute(value, 'seq', [(i, i ^ bit) for i in range(8)])  92.9 us
    ppermute x58, starting transfers between devices, hop(): return lax.ppermute(value, 'seq', [(i, i ^ bit) for i in range(8)])  48.9 us
    ppermute x7, waiting for transfers between devices, step(): got['in'] = lax.ppermute(both, 'dp', [(0, 1), (1, 0), (2, 3), (3, 2)])  31.7 us
    ppermute x7, starting transfers between devices, step(): got['in'] = lax.ppermute(both, 'dp', [(0, 1), (1, 0), (2, 3), (3, 2)])  30.5 us
    ppermute x4, waiting for transfers between devices, outwards(): return lax.ppermute(value, 'dp', [(1, 0), (2, 3)])  21.4 us
    pallas_call x4, Pallas kernels, feed(): pl.pallas_call(functools.partial(feed_kernel, groups, len(b)), out_shape=...  18.1 us
    pallas_call x4, Pallas kernels, feed_back(): pl.pallas_call(functools.partial(feed_back_kernel, groups, len(d)), out_s...  17.7 us
    ppermute x4, starting transfers between devices, step(): got['in'] = lax.ppermute(mine, 'dp', [(0, 1), (3, 2)])  17.1 us
  transfers between devices with their start and end apart: 84, of which 51 were waited for; matrix products, arithmetic and copies ran while one was open for 11% of the time, Pallas kernels for 14%

profile of v5, /device:TPU:0, one launch (start us, length us, event | category | flops | bytes accessed | tf_op | source)
XLA Modules:
  0.0 382.3 jit_solution(14692051067075980883)
XLA Ops:
  35.2 4.6 %collective-permute-done.10 = bf16[256,512]{1,0:T(8,128)(2,1)S(1)} collective-permute-done((bf16[256,512]{1,0:T(8,128)(2,1)S(1)}, bf16[256,512]{1,0:T(8,128)(2,1)S(1)}, u32[]{:S(2)}, u32[]{:S(2)}) %collective-permute-start.10) | collective-permute-done | bytes 262176 | tf_op jit(solution)/shard_map/ppermute | solution.py:522
  48.0 5.2 %collective-permute-done.17 = bf16[64,1152]{1,0:T(8,128)(2,1)S(1)} collective-permute-done((bf16[64,1152]{1,0:T(8,128)(2,1)S(1)}, bf16[64,1152]{1,0:T(8,128)(2,1)S(1)}, u32[]{:S(2)}, u32[]{:S(2)}) %collective-permute-start.17) | collective-permute-done | bytes 147488 | tf_op jit(solution)/shard_map/ppermute | solution.py:522
  64.2 4.6 %convolution_convert_fusion = bf16[1152,1024]{1,0:T(8,128)(2,1)} fusion(bf16[576,1024]{1,0:T(8,128)(2,1)S(1)} %collective-permute-done.9, bf16[576,1024]{1,0:T(8,128)(2,1)S(1)} %constant_dynamic-update-slice_fusion.5, s32[]{:T(128)S(6)} %axis_index.22, s32[1152]{0:T(1024)S(1)} %get-tuple-element.727, s32[1152]{0:T(1024)S(1)} %get-tuple-element.728, ...), kind=kOutput, calls=%fused_computation.58 | convolution fusion | flops 2771582976 | bytes 4739332 | tf_op jit(solution)/shard_map/dot_general | solution.py:49
  69.6 4.5 %feed.4 = (f32[128,1152]{1,0:T(8,128)S(1)}, f32[128,1152]{1,0:T(8,128)S(1)}, bf16[2,256,864]{2,1,0:T(8,128)(2,1)S(1)}, bf16[2,256,864]{2,1,0:T(8,128)(2,1)S(1)}, bf16[2,256,864]{2,1,0:T(8,128)(2,1)S(1)}) custom-call(bf16[256,1152]{1,0:T(8,128)(2,1)S(1)} %multiply_convert_fusion.1.refs_0_.refs_4_, bf16[864,1152]{1,0:T(8,128)(2,1)S(1)} %bitcast.54, ...), custom_call_target="tpu_custom_call" | custom-call | flops 1 | bytes 1 | tf_op jit(solution)/shard_map/feed/pallas_call | solution.py:306
  79.8 4.7 %feed.5 = (bf16[128,1152]{1,0:T(8,128)(2,1)S(1)}, bf16[128,1152]{1,0:T(8,128)(2,1)S(1)}, bf16[2,256,864]{2,1,0:T(8,128)(2,1)S(1)}, bf16[2,256,864]{2,1,0:T(8,128)(2,1)S(1)}, bf16[2,256,864]{2,1,0:T(8,128)(2,1)S(1)}) custom-call(bf16[256,1152]{1,0:T(8,128)(2,1)S(1)} %collective-permute-done.23.refs_0_.refs_5_, bf16[864,1152]{1,0:T(8,128)(2,1)S(1)} %bitcast.55, ...), custom_call_target="tpu_custom_call" | custom-call | flops 1 | bytes 1 | tf_op jit(solution)/shard_map/feed/pallas_call | solution.py:306
  84.5 4.5 %feed.6 = (bf16[128,1152]{1,0:T(8,128)(2,1)S(1)}, bf16[128,1152]{1,0:T(8,128)(2,1)S(1)}, bf16[2,256,864]{2,1,0:T(8,128)(2,1)S(1)}, bf16[2,256,864]{2,1,0:T(8,128)(2,1)S(1)}, bf16[2,256,864]{2,1,0:T(8,128)(2,1)S(1)}) custom-call(bf16[256,1152]{1,0:T(8,128)(2,1)S(1)} %collective-permute-done.24.refs_0_.refs_6_, bf16[864,1152]{1,0:T(8,128)(2,1)S(1)} %bitcast.56, ...), custom_call_target="tpu_custom_call" | custom-call | flops 1 | bytes 1 | tf_op jit(solution)/shard_map/feed/pallas_call | solution.py:306
  91.6 4.5 %feed.7 = (bf16[128,1152]{1,0:T(8,128)(2,1)S(1)}, bf16[128,1152]{1,0:T(8,128)(2,1)S(1)}, bf16[2,256,864]{2,1,0:T(8,128)(2,1)S(1)}, bf16[2,256,864]{2,1,0:T(8,128)(2,1)S(1)}, bf16[2,256,864]{2,1,0:T(8,128)(2,1)S(1)}) custom-call(bf16[128,1152]{1,0:T(8,128)(2,1)S(1)} %collective-permute-done.25.refs_0_.refs_7_, ...), custom_call_target="tpu_custom_call" | custom-call | flops 1 | bytes 1 | tf_op jit(solution)/shard_map/feed/pallas_call | solution.py:306
  99.3 5.8 %collective-permute-done.31 = bf16[128,1152]{1,0:T(8,128)(2,1)S(1)} collective-permute-done((bf16[128,1152]{1,0:T(8,128)(2,1)S(1)}, bf16[128,1152]{1,0:T(8,128)(2,1)S(1)}, u32[]{:S(2)}, u32[]{:S(2)}) %collective-permute-start.31) | collective-permute-done | bytes 294944 | tf_op jit(solution)/shard_map/ppermute | solution.py:522
  120.6 4.5 %feed_back.4 = (f32[128,1152]{1,0:T(8,128)S(1)}, f32[128,1152]{1,0:T(8,128)S(1)}, bf16[2,256,864]{2,1,0:T(8,128)(2,1)S(1)}, bf16[2,256,864]{2,1,0:T(8,128)(2,1)S(1)}) custom-call(bf16[2,256,864]{2,1,0:T(8,128)(2,1)S(1)} %get-tuple-element.459.act_ref, bf16[2,256,864]{2,1,0:T(8,128)(2,1)S(1)} %get-tuple-element.460.slope_ref, ...), custom_call_target="tpu_custom_call" | custom-call | flops 1 | bytes 1 | tf_op jit(solution)/shard_map/feed_back/pallas_call | solution.py:337
  131.4 4.3 %feed_back.5 = (bf16[128,1152]{1,0:T(8,128)(2,1)S(1)}, bf16[128,1152]{1,0:T(8,128)(2,1)S(1)}, bf16[2,256,864]{2,1,0:T(8,128)(2,1)S(1)}, bf16[2,256,864]{2,1,0:T(8,128)(2,1)S(1)}) custom-call(bf16[2,256,864]{2,1,0:T(8,128)(2,1)S(1)} %get-tuple-element.474.act_ref, bf16[2,256,864]{2,1,0:T(8,128)(2,1)S(1)} %get-tuple-element.475.slope_ref, ...), custom_call_target="tpu_custom_call" | custom-call | flops 1 | bytes 1 | tf_op jit(solution)/shard_map/feed_back/pallas_call | solution.py:337
  135.7 4.3 %feed_back.6 = (bf16[128,1152]{1,0:T(8,128)(2,1)S(1)}, bf16[128,1152]{1,0:T(8,128)(2,1)S(1)}, bf16[2,256,864]{2,1,0:T(8,128)(2,1)S(1)}, bf16[2,256,864]{2,1,0:T(8,128)(2,1)S(1)}) custom-call(bf16[2,256,864]{2,1,0:T(8,128)(2,1)S(1)} %get-tuple-element.480.act_ref, bf16[2,256,864]{2,1,0:T(8,128)(2,1)S(1)} %get-tuple-element.481.slope_ref, ...), custom_call_target="tpu_custom_call" | custom-call | flops 1 | bytes 1 | tf_op jit(solution)/shard_map/feed_back/pallas_call | solution.py:337
  142.6 4.7 %feed_back.7 = (bf16[128,1152]{1,0:T(8,128)(2,1)S(1)}, bf16[128,1152]{1,0:T(8,128)(2,1)S(1)}, bf16[2,256,864]{2,1,0:T(8,128)(2,1)S(1)}, bf16[2,256,864]{2,1,0:T(8,128)(2,1)S(1)}) custom-call(bf16[2,256,864]{2,1,0:T(8,128)(2,1)S(1)} %get-tuple-element.500.act_ref, bf16[2,256,864]{2,1,0:T(8,128)(2,1)S(1)} %get-tuple-element.501.slope_ref, ...), custom_call_target="tpu_custom_call" | custom-call | flops 1 | bytes 1 | tf_op jit(solution)/shard_map/feed_back/pallas_call | solution.py:337
  149.8 3.9 %collective-permute-start.38 = (bf16[288,1152]{1,0:T(8,128)(2,1)S(1)}, bf16[288,1152]{1,0:T(8,128)(2,1)S(1)}, u32[]{:S(2)}, u32[]{:S(2)}) collective-permute-start(bf16[288,1152]{1,0:T(8,128)(2,1)S(1)} %get-tuple-element.526), channel_id=1, source_target_pairs={{0,8},{24,16},{1,9},{25,17},{2,10},{26,18},{3,11},{27,19},{4,12},{... | collective-permute-start | bytes 1990664 | tf_op jit(solution)/shard_map/ppermute | solution.py:668
  164.5 4.6 %collective-permute-done.41 = bf16[128,1152]{1,0:T(8,128)(2,1)S(1)} collective-permute-done((bf16[128,1152]{1,0:T(8,128)(2,1)S(1)}, bf16[128,1152]{1,0:T(8,128)(2,1)S(1)}, u32[]{:S(2)}, u32[]{:S(2)}) %collective-permute-start.41) | collective-permute-done | bytes 294944 | tf_op jit(solution)/shard_map/ppermute | solution.py:522
  187.9 4.5 %collective-permute-start.48 = (bf16[288,1152]{1,0:T(8,128)(2,1)S(1)}, bf16[288,1152]{1,0:T(8,128)(2,1)S(1)}, u32[]{:S(2)}, u32[]{:S(2)}) collective-permute-start(bf16[288,1152]{1,0:T(8,128)(2,1)S(1)} %broadcast_select_fusion.15), channel_id=1, source_target_pairs={{0,8},{8,0},{16,24},{24,16},{1,9},{9,1},{17,25},{25,17},{2,10},{10... | collective-permute-start | bytes 1990664 | tf_op jit(solution)/shard_map/ppermute | solution.py:663
  197.8 10.2 %collective-permute-done.48 = bf16[288,1152]{1,0:T(8,128)(2,1)S(1)} collective-permute-done((bf16[288,1152]{1,0:T(8,128)(2,1)S(1)}, bf16[288,1152]{1,0:T(8,128)(2,1)S(1)}, u32[]{:S(2)}, u32[]{:S(2)}) %collective-permute-start.48) | collective-permute-done | bytes 663584 | tf_op jit(solution)/shard_map/ppermute | solution.py:663
  208.3 3.9 %collective-permute-start.51 = (bf16[288,1152]{1,0:T(8,128)(2,1)S(1)}, bf16[288,1152]{1,0:T(8,128)(2,1)S(1)}, u32[]{:S(2)}, u32[]{:S(2)}) collective-permute-start(bf16[288,1152]{1,0:T(8,128)(2,1)S(1)} %broadcast_select_fusion.14), channel_id=1, source_target_pairs={{0,8},{8,0},{16,24},{24,16},{1,9},{9,1},{17,25},{25,17},{2,10},{10... | collective-permute-start | bytes 1990664 | tf_op jit(solution)/shard_map/ppermute | solution.py:663
  219.1 8.7 %collective-permute-done.51 = bf16[288,1152]{1,0:T(8,128)(2,1)S(1)} collective-permute-done((bf16[288,1152]{1,0:T(8,128)(2,1)S(1)}, bf16[288,1152]{1,0:T(8,128)(2,1)S(1)}, u32[]{:S(2)}, u32[]{:S(2)}) %collective-permute-start.51) | collective-permute-done | bytes 663584 | tf_op jit(solution)/shard_map/ppermute | solution.py:663
  230.4 3.8 collective-permute-start.56
  241.2 7.6 %collective-permute-done.56 = bf16[288,1152]{1,0:T(8,128)(2,1)S(1)} collective-permute-done((bf16[288,1152]{1,0:T(8,128)(2,1)S(1)}, bf16[288,1152]{1,0:T(8,128)(2,1)S(1)}, u32[]{:S(2)}, u32[]{:S(2)}) %collective-permute-start.56) | collective-permute-done | bytes 663584 | tf_op jit(solution)/shard_map/ppermute | solution.py:663
  249.4 3.8 %collective-permute-start.60 = (bf16[288,1152]{1,0:T(8,128)(2,1)S(1)}, bf16[288,1152]{1,0:T(8,128)(2,1)S(1)}, u32[]{:S(2)}, u32[]{:S(2)}) collective-permute-start(bf16[288,1152]{1,0:T(8,128)(2,1)S(1)} %broadcast_select_fusion.12), channel_id=1, source_target_pairs={{0,8},{8,0},{16,24},{24,16},{1,9},{9,1},{17,25},{25,17},{2,10},{10... | collective-permute-start | bytes 1990664 | tf_op jit(solution)/shard_map/ppermute | solution.py:663
  262.3 4.6 %collective-permute-done.60 = bf16[288,1152]{1,0:T(8,128)(2,1)S(1)} collective-permute-done((bf16[288,1152]{1,0:T(8,128)(2,1)S(1)}, bf16[288,1152]{1,0:T(8,128)(2,1)S(1)}, u32[]{:S(2)}, u32[]{:S(2)}) %collective-permute-start.60) | collective-permute-done | bytes 663584 | tf_op jit(solution)/shard_map/ppermute | solution.py:663
  267.1 3.7 collective-permute-start.64
  274.8 7.6 %collective-permute-done.67 = bf16[128,1152]{1,0:T(8,128)(2,1)S(1)} collective-permute-done((bf16[128,1152]{1,0:T(8,128)(2,1)S(1)}, bf16[128,1152]{1,0:T(8,128)(2,1)S(1)}, u32[]{:S(2)}, u32[]{:S(2)}) %collective-permute-start.67) | collective-permute-done | bytes 294944 | tf_op jit(solution)/shard_map/ppermute | solution.py:522
  283.8 6.9 %collective-permute-start.68 = (bf16[288,1152]{1,0:T(8,128)(2,1)S(1)}, bf16[288,1152]{1,0:T(8,128)(2,1)S(1)}, u32[]{:S(2)}, u32[]{:S(2)}) collective-permute-start(bf16[288,1152]{1,0:T(8,128)(2,1)S(1)} %broadcast_select_fusion.10), channel_id=1, source_target_pairs={{0,8},{8,0},{16,24},{24,16},{1,9},{9,1},{17,25},{25,17},{2,10},{10... | collective-permute-start | bytes 1990664 | tf_op jit(solution)/shard_map/ppermute | solution.py:663
  293.8 10.6 %collective-permute-done.70 = bf16[160,1536]{1,0:T(8,128)(2,1)S(1)} collective-permute-done((bf16[160,1536]{1,0:T(8,128)(2,1)S(1)}, bf16[160,1536]{1,0:T(8,128)(2,1)S(1)}, u32[]{:S(2)}, u32[]{:S(2)}) %collective-permute-start.70) | collective-permute-done | bytes 491552 | tf_op jit(solution)/shard_map/ppermute | solution.py:522
  305.7 3.9 %collective-permute-start.72 = (bf16[288,1152]{1,0:T(8,128)(2,1)S(1)}, bf16[288,1152]{1,0:T(8,128)(2,1)S(1)}, u32[]{:S(2)}, u32[]{:S(2)}) collective-permute-start(bf16[288,1152]{1,0:T(8,128)(2,1)S(1)} %broadcast_select_fusion.9), channel_id=1, source_target_pairs={{0,8},{8,0},{16,24},{24,16},{1,9},{9,1},{17,25},{25,17},{2,10},{10... | collective-permute-start | bytes 1990664 | tf_op jit(solution)/shard_map/ppermute | solution.py:663
  314.1 9.0 %collective-permute-done.74 = bf16[160,1536]{1,0:T(8,128)(2,1)S(1)} collective-permute-done((bf16[160,1536]{1,0:T(8,128)(2,1)S(1)}, bf16[160,1536]{1,0:T(8,128)(2,1)S(1)}, u32[]{:S(2)}, u32[]{:S(2)}) %collective-permute-start.74) | collective-permute-done | bytes 491552 | tf_op jit(solution)/shard_map/ppermute | solution.py:522
  326.1 8.2 %collective-permute-start.75 = (bf16[160,1536]{1,0:T(8,128)(2,1)S(1)}, bf16[160,1536]{1,0:T(8,128)(2,1)S(1)}, u32[]{:S(2)}, u32[]{:S(2)}) collective-permute-start(bf16[160,1536]{1,0:T(8,128)(2,1)S(1)} %add_convert_fusion.21), channel_id=1, source_target_pairs={{0,8},{24,16},{1,9},{25,17},{2,10},{26,18},{3,11},{27,19},{4,12},{... | collective-permute-start | bytes 1474568 | tf_op jit(solution)/shard_map/ppermute | solution.py:668
  334.6 8.0 %collective-permute-done.75 = bf16[160,1536]{1,0:T(8,128)(2,1)S(1)} collective-permute-done((bf16[160,1536]{1,0:T(8,128)(2,1)S(1)}, bf16[160,1536]{1,0:T(8,128)(2,1)S(1)}, u32[]{:S(2)}, u32[]{:S(2)}) %collective-permute-start.75) | collective-permute-done | bytes 491552 | tf_op jit(solution)/shard_map/ppermute | solution.py:668
  351.2 11.1 %collective-permute-done.80 = bf16[288,1152]{1,0:T(8,128)(2,1)S(1)} collective-permute-done((bf16[288,1152]{1,0:T(8,128)(2,1)S(1)}, bf16[288,1152]{1,0:T(8,128)(2,1)S(1)}, u32[]{:S(2)}, u32[]{:S(2)}) %collective-permute-start.80) | collective-permute-done | bytes 663584 | tf_op jit(solution)/shard_map/ppermute | solution.py:698
  368.1 6.7 %collective-permute-done.81 = bf16[160,1536]{1,0:T(8,128)(2,1)S(1)} collective-permute-done((bf16[160,1536]{1,0:T(8,128)(2,1)S(1)}, bf16[160,1536]{1,0:T(8,128)(2,1)S(1)}, u32[]{:S(2)}, u32[]{:S(2)}) %collective-permute-start.81) | collective-permute-done | bytes 491552 | tf_op jit(solution)/shard_map/ppermute | solution.py:698
  (370 shorter events, 191.7 us)
Async XLA Ops:
  61.0 15.7 %collective-permute-start.23 = (bf16[256,1152]{1,0:T(8,128)(2,1)S(1)}, bf16[256,1152]{1,0:T(8,128)(2,1)S(1)}, u32[]{:S(2)}, u32[]{:S(2)}) collective-permute-start(bf16[256,1152]{1,0:T(8,128)(2,1)S(1)} %multiply_convert_fusion.1.refs_0_.refs_4_), channel_id=1, source_target_pairs={{0,2},{1,3},{2,0},{3,1},{4,6},{5,7},{6,4},{7,5},{8,10},{9,11},{10,... | collective-permute-start | bytes 1769480 | tf_op jit(solution)/shard_map/ppermute | solution.py:522
  63.1 15.0 %collective-permute-start.24 = (bf16[256,1152]{1,0:T(8,128)(2,1)S(1)}, bf16[256,1152]{1,0:T(8,128)(2,1)S(1)}, u32[]{:S(2)}, u32[]{:S(2)}) collective-permute-start(bf16[256,1152]{1,0:T(8,128)(2,1)S(1)} %multiply_convert_fusion.1.refs_0_.refs_4_), channel_id=1, source_target_pairs={{0,4},{1,5},{2,6},{3,7},{4,0},{5,1},{6,2},{7,3},{8,12},{9,13},{10,... | collective-permute-start | bytes 1769480 | tf_op jit(solution)/shard_map/ppermute | solution.py:522
  116.5 13.0 %collective-permute-start.34 = (bf16[256,1152]{1,0:T(8,128)(2,1)S(1)}, bf16[256,1152]{1,0:T(8,128)(2,1)S(1)}, u32[]{:S(2)}, u32[]{:S(2)}) collective-permute-start(bf16[256,1152]{1,0:T(8,128)(2,1)S(1)} %get-tuple-element.458.refs_0_.refs_4_), channel_id=1, source_target_pairs={{0,4},{1,5},{2,6},{3,7},{4,0},{5,1},{6,2},{7,3},{8,12},{9,13},{10,... | collective-permute-start | bytes 1769480 | tf_op jit(solution)/shard_map/ppermute | solution.py:522
  149.8 20.3 %collective-permute-start.38 = (bf16[288,1152]{1,0:T(8,128)(2,1)S(1)}, bf16[288,1152]{1,0:T(8,128)(2,1)S(1)}, u32[]{:S(2)}, u32[]{:S(2)}) collective-permute-start(bf16[288,1152]{1,0:T(8,128)(2,1)S(1)} %get-tuple-element.526), channel_id=1, source_target_pairs={{0,8},{24,16},{1,9},{25,17},{2,10},{26,18},{3,11},{27,19},{4,12},{... | collective-permute-start | bytes 1990664 | tf_op jit(solution)/shard_map/ppermute | solution.py:668
  156.6 12.5 %collective-permute-start.41 = (bf16[128,1152]{1,0:T(8,128)(2,1)S(1)}, bf16[128,1152]{1,0:T(8,128)(2,1)S(1)}, u32[]{:S(2)}, u32[]{:S(2)}) collective-permute-start(bf16[128,1152]{1,0:T(8,128)(2,1)S(1)} %get-tuple-element.529), channel_id=1, source_target_pairs={{0,2},{1,3},{2,0},{3,1},{4,6},{5,7},{6,4},{7,5},{8,10},{9,11},{10,... | collective-permute-start | bytes 884744 | tf_op jit(solution)/shard_map/ppermute | solution.py:522
  157.7 12.4 %collective-permute-start.42 = (bf16[128,1152]{1,0:T(8,128)(2,1)S(1)}, bf16[128,1152]{1,0:T(8,128)(2,1)S(1)}, u32[]{:S(2)}, u32[]{:S(2)}) collective-permute-start(bf16[128,1152]{1,0:T(8,128)(2,1)S(1)} %get-tuple-element.530), channel_id=1, source_target_pairs={{0,4},{1,5},{2,6},{3,7},{4,0},{5,1},{6,2},{7,3},{8,12},{9,13},{10,... | collective-permute-start | bytes 884744 | tf_op jit(solution)/shard_map/ppermute | solution.py:522
  170.1 17.5 %collective-permute-start.43 = (bf16[288,1152]{1,0:T(8,128)(2,1)S(1)}, bf16[288,1152]{1,0:T(8,128)(2,1)S(1)}, u32[]{:S(2)}, u32[]{:S(2)}) collective-permute-start(bf16[288,1152]{1,0:T(8,128)(2,1)S(1)} %get-tuple-element.545), channel_id=1, source_target_pairs={{0,8},{24,16},{1,9},{25,17},{2,10},{26,18},{3,11},{27,19},{4,12},{... | collective-permute-start | bytes 1990664 | tf_op jit(solution)/shard_map/ppermute | solution.py:668
  173.1 14.6 %collective-permute-start.44 = (bf16[288,1152]{1,0:T(8,128)(2,1)S(1)}, bf16[288,1152]{1,0:T(8,128)(2,1)S(1)}, u32[]{:S(2)}, u32[]{:S(2)}) collective-permute-start(bf16[288,1152]{1,0:T(8,128)(2,1)S(1)} %add_convert_fusion.17), channel_id=1, source_target_pairs={{8,16},{16,8},{9,17},{17,9},{10,18},{18,10},{11,19},{19,11},{12,20... | collective-permute-start | bytes 1990664 | tf_op jit(solution)/shard_map/ppermute | solution.py:670
  187.7 20.4 %collective-permute-start.50 = (bf16[864,1152]{1,0:T(8,128)(2,1)S(1)}, bf16[864,1152]{1,0:T(8,128)(2,1)S(1)}, u32[]{:S(2)}, u32[]{:S(2)}) collective-permute-start(bf16[864,1152]{1,0:T(8,128)(2,1)S(1)} %weight_grad.9), channel_id=1, source_target_pairs={{0,1},{1,0},{2,3},{3,2},{4,5},{5,4},{6,7},{7,6},{8,9},{9,8},{10,11... | collective-permute-start | bytes 5971976 | tf_op jit(solution)/shard_map/ppermute | solution.py:522
  187.9 20.1 %collective-permute-start.48 = (bf16[288,1152]{1,0:T(8,128)(2,1)S(1)}, bf16[288,1152]{1,0:T(8,128)(2,1)S(1)}, u32[]{:S(2)}, u32[]{:S(2)}) collective-permute-start(bf16[288,1152]{1,0:T(8,128)(2,1)S(1)} %broadcast_select_fusion.15), channel_id=1, source_target_pairs={{0,8},{8,0},{16,24},{24,16},{1,9},{9,1},{17,25},{25,17},{2,10},{10... | collective-permute-start | bytes 1990664 | tf_op jit(solution)/shard_map/ppermute | solution.py:663
  192.7 15.4 %collective-permute-start.49 = (bf16[288,1152]{1,0:T(8,128)(2,1)S(1)}, bf16[288,1152]{1,0:T(8,128)(2,1)S(1)}, u32[]{:S(2)}, u32[]{:S(2)}) collective-permute-start(bf16[288,1152]{1,0:T(8,128)(2,1)S(1)} %add_convert_fusion.16), channel_id=1, source_target_pairs={{8,16},{16,8},{9,17},{17,9},{10,18},{18,10},{11,19},{19,11},{12,20... | collective-permute-start | bytes 1990664 | tf_op jit(solution)/shard_map/ppermute | solution.py:670
  208.3 19.5 %collective-permute-start.51 = (bf16[288,1152]{1,0:T(8,128)(2,1)S(1)}, bf16[288,1152]{1,0:T(8,128)(2,1)S(1)}, u32[]{:S(2)}, u32[]{:S(2)}) collective-permute-start(bf16[288,1152]{1,0:T(8,128)(2,1)S(1)} %broadcast_select_fusion.14), channel_id=1, source_target_pairs={{0,8},{8,0},{16,24},{24,16},{1,9},{9,1},{17,25},{25,17},{2,10},{10... | collective-permute-start | bytes 1990664 | tf_op jit(solution)/shard_map/ppermute | solution.py:663
  212.4 15.4 %collective-permute-start.52 = (bf16[288,1152]{1,0:T(8,128)(2,1)S(1)}, bf16[288,1152]{1,0:T(8,128)(2,1)S(1)}, u32[]{:S(2)}, u32[]{:S(2)}) collective-permute-start(bf16[288,1152]{1,0:T(8,128)(2,1)S(1)} %add_convert_fusion.13), channel_id=1, source_target_pairs={{8,16},{16,8},{9,17},{17,9},{10,18},{18,10},{11,19},{19,11},{12,20... | collective-permute-start | bytes 1990664 | tf_op jit(solution)/shard_map/ppermute | solution.py:670
  213.8 14.0 %collective-permute-start.54 = (bf16[256,512]{1,0:T(8,128)(2,1)S(1)}, bf16[256,512]{1,0:T(8,128)(2,1)S(1)}, u32[]{:S(2)}, u32[]{:S(2)}) collective-permute-start(bf16[256,512]{1,0:T(8,128)(2,1)S(1)} %get-tuple-element.706), channel_id=1, source_target_pairs={{0,2},{1,3},{2,0},{3,1},{4,6},{5,7},{6,4},{7,5},{8,10},{9,11},{10,... | collective-permute-start | bytes 786440 | tf_op jit(solution)/shard_map/ppermute | solution.py:522
  230.4 18.3 %collective-permute-start.56 = (bf16[288,1152]{1,0:T(8,128)(2,1)S(1)}, bf16[288,1152]{1,0:T(8,128)(2,1)S(1)}, u32[]{:S(2)}, u32[]{:S(2)}) collective-permute-start(bf16[288,1152]{1,0:T(8,128)(2,1)S(1)} %broadcast_select_fusion.13), channel_id=1, source_target_pairs={{0,8},{8,0},{16,24},{24,16},{1,9},{9,1},{17,25},{25,17},{2,10},{10... | collective-permute-start | bytes 1990664 | tf_op jit(solution)/shard_map/ppermute | solution.py:663
  234.2 14.5 %collective-permute-start.57 = (bf16[288,1152]{1,0:T(8,128)(2,1)S(1)}, bf16[288,1152]{1,0:T(8,128)(2,1)S(1)}, u32[]{:S(2)}, u32[]{:S(2)}) collective-permute-start(bf16[288,1152]{1,0:T(8,128)(2,1)S(1)} %add_convert_fusion.11), channel_id=1, source_target_pairs={{8,16},{16,8},{9,17},{17,9},{10,18},{18,10},{11,19},{19,11},{12,20... | collective-permute-start | bytes 1990664 | tf_op jit(solution)/shard_map/ppermute | solution.py:670
  249.4 17.4 %collective-permute-start.60 = (bf16[288,1152]{1,0:T(8,128)(2,1)S(1)}, bf16[288,1152]{1,0:T(8,128)(2,1)S(1)}, u32[]{:S(2)}, u32[]{:S(2)}) collective-permute-start(bf16[288,1152]{1,0:T(8,128)(2,1)S(1)} %broadcast_select_fusion.12), channel_id=1, source_target_pairs={{0,8},{8,0},{16,24},{24,16},{1,9},{9,1},{17,25},{25,17},{2,10},{10... | collective-permute-start | bytes 1990664 | tf_op jit(solution)/shard_map/ppermute | solution.py:663
  253.3 13.6 %collective-permute-start.61 = (bf16[288,1152]{1,0:T(8,128)(2,1)S(1)}, bf16[288,1152]{1,0:T(8,128)(2,1)S(1)}, u32[]{:S(2)}, u32[]{:S(2)}) collective-permute-start(bf16[288,1152]{1,0:T(8,128)(2,1)S(1)} %add_convert_fusion.10), channel_id=1, source_target_pairs={{8,16},{16,8},{9,17},{17,9},{10,18},{18,10},{11,19},{19,11},{12,20... | collective-permute-start | bytes 1990664 | tf_op jit(solution)/shard_map/ppermute | solution.py:670
  267.1 16.4 %collective-permute-start.64 = (bf16[288,1152]{1,0:T(8,128)(2,1)S(1)}, bf16[288,1152]{1,0:T(8,128)(2,1)S(1)}, u32[]{:S(2)}, u32[]{:S(2)}) collective-permute-start(bf16[288,1152]{1,0:T(8,128)(2,1)S(1)} %broadcast_select_fusion.11), channel_id=1, source_target_pairs={{0,8},{8,0},{16,24},{24,16},{1,9},{9,1},{17,25},{25,17},{2,10},{10... | collective-permute-start | bytes 1990664 | tf_op jit(solution)/shard_map/ppermute | solution.py:663
  271.0 12.5 %collective-permute-start.65 = (bf16[288,1152]{1,0:T(8,128)(2,1)S(1)}, bf16[288,1152]{1,0:T(8,128)(2,1)S(1)}, u32[]{:S(2)}, u32[]{:S(2)}) collective-permute-start(bf16[288,1152]{1,0:T(8,128)(2,1)S(1)} %add_convert_fusion.7), channel_id=1, source_target_pairs={{8,16},{16,8},{9,17},{17,9},{10,18},{18,10},{11,19},{19,11},{12,20... | collective-permute-start | bytes 1990664 | tf_op jit(solution)/shard_map/ppermute | solution.py:670
  283.8 21.7 %collective-permute-start.68 = (bf16[288,1152]{1,0:T(8,128)(2,1)S(1)}, bf16[288,1152]{1,0:T(8,128)(2,1)S(1)}, u32[]{:S(2)}, u32[]{:S(2)}) collective-permute-start(bf16[288,1152]{1,0:T(8,128)(2,1)S(1)} %broadcast_select_fusion.10), channel_id=1, source_target_pairs={{0,8},{8,0},{16,24},{24,16},{1,9},{9,1},{17,25},{25,17},{2,10},{10... | collective-permute-start | bytes 1990664 | tf_op jit(solution)/shard_map/ppermute | solution.py:663
  290.9 14.6 %collective-permute-start.69 = (bf16[288,1152]{1,0:T(8,128)(2,1)S(1)}, bf16[288,1152]{1,0:T(8,128)(2,1)S(1)}, u32[]{:S(2)}, u32[]{:S(2)}) collective-permute-start(bf16[288,1152]{1,0:T(8,128)(2,1)S(1)} %add_convert_fusion.5), channel_id=1, source_target_pairs={{8,16},{16,8},{9,17},{17,9},{10,18},{18,10},{11,19},{19,11},{12,20... | collective-permute-start | bytes 1990664 | tf_op jit(solution)/shard_map/ppermute | solution.py:670
  291.8 12.6 %collective-permute-start.70 = (bf16[160,1536]{1,0:T(8,128)(2,1)S(1)}, bf16[160,1536]{1,0:T(8,128)(2,1)S(1)}, u32[]{:S(2)}, u32[]{:S(2)}) collective-permute-start(bf16[160,1536]{1,0:T(8,128)(2,1)S(1)} %get-tuple-element.654), channel_id=1, source_target_pairs={{0,2},{1,3},{2,0},{3,1},{4,6},{5,7},{6,4},{7,5},{8,10},{9,11},{10,... | collective-permute-start | bytes 1474568 | tf_op jit(solution)/shard_map/ppermute | solution.py:522
  305.7 17.8 %collective-permute-start.72 = (bf16[288,1152]{1,0:T(8,128)(2,1)S(1)}, bf16[288,1152]{1,0:T(8,128)(2,1)S(1)}, u32[]{:S(2)}, u32[]{:S(2)}) collective-permute-start(bf16[288,1152]{1,0:T(8,128)(2,1)S(1)} %broadcast_select_fusion.9), channel_id=1, source_target_pairs={{0,8},{8,0},{16,24},{24,16},{1,9},{9,1},{17,25},{25,17},{2,10},{10... | collective-permute-start | bytes 1990664 | tf_op jit(solution)/shard_map/ppermute | solution.py:663
  309.8 13.7 %collective-permute-start.73 = (bf16[288,1152]{1,0:T(8,128)(2,1)S(1)}, bf16[288,1152]{1,0:T(8,128)(2,1)S(1)}, u32[]{:S(2)}, u32[]{:S(2)}) collective-permute-start(bf16[288,1152]{1,0:T(8,128)(2,1)S(1)} %add_convert_fusion.3), channel_id=1, source_target_pairs={{8,16},{16,8},{9,17},{17,9},{10,18},{18,10},{11,19},{19,11},{12,20... | collective-permute-start | bytes 1990664 | tf_op jit(solution)/shard_map/ppermute | solution.py:670
  310.5 12.6 %collective-permute-start.74 = (bf16[160,1536]{1,0:T(8,128)(2,1)S(1)}, bf16[160,1536]{1,0:T(8,128)(2,1)S(1)}, u32[]{:S(2)}, u32[]{:S(2)}) collective-permute-start(bf16[160,1536]{1,0:T(8,128)(2,1)S(1)} %get-tuple-element.662), channel_id=1, source_target_pairs={{0,6},{1,7},{2,4},{3,5},{4,2},{5,3},{6,0},{7,1},{8,14},{9,15},{10,... | collective-permute-start | bytes 1474568 | tf_op jit(solution)/shard_map/ppermute | solution.py:522
  323.7 18.9 %collective-permute-start.76 = (bf16[288,1152]{1,0:T(8,128)(2,1)S(1)}, bf16[288,1152]{1,0:T(8,128)(2,1)S(1)}, u32[]{:S(2)}, u32[]{:S(2)}) collective-permute-start(bf16[288,1152]{1,0:T(8,128)(2,1)S(1)} %add_convert_fusion.2), channel_id=1, source_target_pairs={{8,16},{16,8},{9,17},{17,9},{10,18},{18,10},{11,19},{19,11},{12,20... | collective-permute-start | bytes 1990664 | tf_op jit(solution)/shard_map/ppermute | solution.py:670
  324.6 20.2 %collective-permute-start.77 = (bf16[288,1152]{1,0:T(8,128)(2,1)S(1)}, bf16[288,1152]{1,0:T(8,128)(2,1)S(1)}, u32[]{:S(2)}, u32[]{:S(2)}) collective-permute-start(bf16[288,1152]{1,0:T(8,128)(2,1)S(1)} %add_convert_fusion.1), channel_id=1, source_target_pairs={{8,0},{16,24},{9,1},{17,25},{10,2},{18,26},{11,3},{19,27},{12,4},{... | collective-permute-start | bytes 1990664 | tf_op jit(solution)/shard_map/ppermute | solution.py:698
  326.1 16.5 %collective-permute-start.75 = (bf16[160,1536]{1,0:T(8,128)(2,1)S(1)}, bf16[160,1536]{1,0:T(8,128)(2,1)S(1)}, u32[]{:S(2)}, u32[]{:S(2)}) collective-permute-start(bf16[160,1536]{1,0:T(8,128)(2,1)S(1)} %add_convert_fusion.21), channel_id=1, source_target_pairs={{0,8},{24,16},{1,9},{25,17},{2,10},{26,18},{3,11},{27,19},{4,12},{... | collective-permute-start | bytes 1474568 | tf_op jit(solution)/shard_map/ppermute | solution.py:668
  347.2 15.1 %collective-permute-start.80 = (bf16[288,1152]{1,0:T(8,128)(2,1)S(1)}, bf16[288,1152]{1,0:T(8,128)(2,1)S(1)}, u32[]{:S(2)}, u32[]{:S(2)}) collective-permute-start(bf16[288,1152]{1,0:T(8,128)(2,1)S(1)} %add_convert_fusion), channel_id=1, source_target_pairs={{8,0},{16,24},{9,1},{17,25},{10,2},{18,26},{11,3},{19,27},{12,4},{... | collective-permute-start | bytes 1990664 | tf_op jit(solution)/shard_map/ppermute | solution.py:698
  362.4 12.4 %collective-permute-start.81 = (bf16[160,1536]{1,0:T(8,128)(2,1)S(1)}, bf16[160,1536]{1,0:T(8,128)(2,1)S(1)}, u32[]{:S(2)}, u32[]{:S(2)}) collective-permute-start(bf16[160,1536]{1,0:T(8,128)(2,1)S(1)} %add_convert_fusion.19), channel_id=1, source_target_pairs={{8,0},{16,24},{9,1},{17,25},{10,2},{18,26},{11,3},{19,27},{12,4},{... | collective-permute-start | bytes 1474568 | tf_op jit(solution)/shard_map/ppermute | solution.py:698
  366.8 14.3 %collective-permute-start.83 = (bf16[128,1152]{1,0:T(8,128)(2,1)S(1)}, bf16[128,1152]{1,0:T(8,128)(2,1)S(1)}, u32[]{:S(2)}, u32[]{:S(2)}) collective-permute-start(bf16[128,1152]{1,0:T(8,128)(2,1)S(1)} %add_convert_fusion.22), channel_id=1, source_target_pairs={{8,0},{16,24},{9,1},{17,25},{10,2},{18,26},{11,3},{19,27},{12,4},{... | collective-permute-start | bytes 884744 | tf_op jit(solution)/shard_map/ppermute | solution.py:698
  (78 other events, 495.4 us)

commit v6 on v5

--- a/solution.py
+++ b/solution.py
@@ -637,7 +637,7 @@
         source, start, size = self.chunks[at]
         return self.wholes[source][start : start + size]
 
-    def step(self, beside):
+    def step(self, beside, sum_first=False):
         return fence(beside(()))
 
     def finish(self, early):
@@ -652,7 +652,7 @@
         self.halves, self.totals, self.out = {}, {}, {}
         self.at = 0
 
-    def step(self, beside):
+    def step(self, beside, sum_first=False):
         tick = self.at
         self.at += 1
         mine = self.chunk(tick) if tick < len(self.chunks) else None
@@ -667,7 +667,8 @@
             if mine is not None:
                 got["in"] = lax.ppermute(mine, "dp", [(0, 1), (3, 2)])
         if half is not None:
-            got["middle"] = lax.ppermute(half, "dp", [(1, 2), (2, 1)])
+            across = lax.ppermute(half, "dp", [(1, 2), (2, 1)])
+            got["middle"] = add(half, across).astype(bf16) if sum_first else across
         values = beside(())
         later = [c for c in self.chunks[tick + 1 :] if len(c) == 1]
         got, values, later, self.wholes = fence((got, values, later, self.wholes))
@@ -677,7 +678,8 @@
         if mine is not None:
             self.halves[tick] = add(mine, got["in"]).astype(bf16)
         if half is not None:
-            self.totals[tick - 1] = add(half, got["middle"]).astype(bf16)
+            middle = got["middle"]
+            self.totals[tick - 1] = middle if sum_first else add(half, middle).astype(bf16)
         if back is not None:
             self.out[tick - 2] = jnp.where(self.inner, back, got["out"] if "out" in got else got["in"])
         return values
@@ -904,7 +906,7 @@
         grad_qkv = comm.projection(a_late, d_qkv, gains)
         return out_group, out_near, grad_qkv, d_a
 
-    out_group, out_near, grad_qkv, d_a = line.step(beside)
+    out_group, out_near, grad_qkv, d_a = line.step(beside, True)
 
     def beside(_):
         qkv_moved = comm.across(grad_qkv[-1].astype(bf16))
@@ -913,17 +915,17 @@
         total_out = comm.group_sum(out_group, out_near, out_far).astype(bf16)
         return comm.group(grad_qkv, qkv_moved), total_out, d_input
 
-    group, total_out, d_input = line.step(beside)
+    group, total_out, d_input = line.step(beside, True)
 
     def beside(_):
         return group, comm.group_near(group), total_out
 
-    group, near, total_out = line.step(beside)
+    group, near, total_out = line.step(beside, True)
 
     def beside(_):
         return comm.group_far(group), near, total_out
 
-    far, near, total_out = line.step(beside)
+    far, near, total_out = line.step(beside, True)
     line.chunks += [(comm.group_sum(group, near, far).astype(bf16),), (total_out,)]
     def owned(tail):
         def mine(row, start, size):

time: 388 us -> 384 us (0.990)
  waiting for transfers between devices: 157 us -> 147 us
  starting transfers between devices: 110 us -> 117 us
    ppermute x58, waiting for transfers between devices: 92.9 us -> 81.5 us  [hop(): return lax.ppermute(value, 'seq', [(i, i ^ bit) for i in range(8)])]
    ppermute x58, starting transfers between devices: 48.9 us -> 56.9 us  [hop(): return lax.ppermute(value, 'seq', [(i, i ^ bit) for i in range(8)])]
  transfers between devices with their start and end apart: 84 -> 84, of which waited for: 51 -> 50; matrix products, arithmetic and copies ran while one was open for 11% -> 11% of each run, Pallas kernels for 14% -> 14%
where the time goes in v6:
time: 384 us; the launch traced here: 379 us
  waiting for transfers between devices  147 us (38%)
  starting transfers between devices  117 us (30%)
  Pallas kernels  58.7 us (15%)
  other arithmetic  24.2 us (6%)
  matrix products  18.7 us (5%)
  local copies, waits for them, and re-layouts  9.94 us (3%)
    ppermute x58, waiting for transfers between devices, hop(): return lax.ppermute(value, 'seq', [(i, i ^ bit) for i in range(8)])  81.5 us
    ppermute x58, starting transfers between devices, hop(): return lax.ppermute(value, 'seq', [(i, i ^ bit) for i in range(8)])  56.9 us
    ppermute x7, waiting for transfers between devices, step(): got['in'] = lax.ppermute(both, 'dp', [(0, 1), (1, 0), (2, 3), (3, 2)])  32.5 us
    ppermute x7, starting transfers between devices, step(): got['in'] = lax.ppermute(both, 'dp', [(0, 1), (1, 0), (2, 3), (3, 2)])  31.9 us
    ppermute x4, waiting for transfers between devices, outwards(): return lax.ppermute(value, 'dp', [(1, 0), (2, 3)])  21.9 us
    pallas_call x4, Pallas kernels, feed(): pl.pallas_call(functools.partial(feed_kernel, groups, len(b)), out_shape=...  18.1 us
    pallas_call x4, Pallas kernels, feed_back(): pl.pallas_call(functools.partial(feed_back_kernel, groups, len(d)), out_s...  17.7 us
    pallas_call x6, Pallas kernels, weight_grad(): pl.pallas_call(functools.partial(weight_grad_kernel, index, sizes, len(le...  15 us
  transfers between devices with their start and end apart: 84, of which 50 were waited for; matrix products, arithmetic and copies ran while one was open for 11% of the time, Pallas kernels for 14%

profile of v6, /device:TPU:0, one launch (start us, length us, event | category | flops | bytes accessed | tf_op | source)
XLA Modules:
  0.0 378.6 jit_solution(8793086508670959240)
XLA Ops:
  35.2 4.6 %collective-permute-done.10 = bf16[256,512]{1,0:T(8,128)(2,1)S(1)} collective-permute-done((bf16[256,512]{1,0:T(8,128)(2,1)S(1)}, bf16[256,512]{1,0:T(8,128)(2,1)S(1)}, u32[]{:S(2)}, u32[]{:S(2)}) %collective-permute-start.10) | collective-permute-done | bytes 262176 | tf_op jit(solution)/shard_map/ppermute | solution.py:522
  48.0 5.2 %collective-permute-done.17 = bf16[64,1152]{1,0:T(8,128)(2,1)S(1)} collective-permute-done((bf16[64,1152]{1,0:T(8,128)(2,1)S(1)}, bf16[64,1152]{1,0:T(8,128)(2,1)S(1)}, u32[]{:S(2)}, u32[]{:S(2)}) %collective-permute-start.17) | collective-permute-done | bytes 147488 | tf_op jit(solution)/shard_map/ppermute | solution.py:522
  64.4 4.6 %convolution_convert_fusion = bf16[1152,1024]{1,0:T(8,128)(2,1)} fusion(bf16[576,1024]{1,0:T(8,128)(2,1)S(1)} %collective-permute-done.9, bf16[576,1024]{1,0:T(8,128)(2,1)S(1)} %constant_dynamic-update-slice_fusion.5, s32[]{:T(128)S(6)} %axis_index.22, s32[1152]{0:T(1024)S(1)} %get-tuple-element.727, s32[1152]{0:T(1024)S(1)} %get-tuple-element.728, ...), kind=kOutput, calls=%fused_computation.58 | convolution fusion | flops 2771582976 | bytes 4739332 | tf_op jit(solution)/shard_map/dot_general | solution.py:49
  69.6 4.5 %feed.4 = (f32[128,1152]{1,0:T(8,128)S(1)}, f32[128,1152]{1,0:T(8,128)S(1)}, bf16[2,256,864]{2,1,0:T(8,128)(2,1)S(1)}, bf16[2,256,864]{2,1,0:T(8,128)(2,1)S(1)}, bf16[2,256,864]{2,1,0:T(8,128)(2,1)S(1)}) custom-call(bf16[256,1152]{1,0:T(8,128)(2,1)S(1)} %multiply_convert_fusion.1.refs_0_.refs_4_, bf16[864,1152]{1,0:T(8,128)(2,1)S(1)} %bitcast.54, ...), custom_call_target="tpu_custom_call" | custom-call | flops 1 | bytes 1 | tf_op jit(solution)/shard_map/feed/pallas_call | solution.py:306
  80.3 4.7 %feed.5 = (bf16[128,1152]{1,0:T(8,128)(2,1)S(1)}, bf16[128,1152]{1,0:T(8,128)(2,1)S(1)}, bf16[2,256,864]{2,1,0:T(8,128)(2,1)S(1)}, bf16[2,256,864]{2,1,0:T(8,128)(2,1)S(1)}, bf16[2,256,864]{2,1,0:T(8,128)(2,1)S(1)}) custom-call(bf16[256,1152]{1,0:T(8,128)(2,1)S(1)} %collective-permute-done.23.refs_0_.refs_5_, bf16[864,1152]{1,0:T(8,128)(2,1)S(1)} %bitcast.55, ...), custom_call_target="tpu_custom_call" | custom-call | flops 1 | bytes 1 | tf_op jit(solution)/shard_map/feed/pallas_call | solution.py:306
  85.0 4.5 %feed.6 = (bf16[128,1152]{1,0:T(8,128)(2,1)S(1)}, bf16[128,1152]{1,0:T(8,128)(2,1)S(1)}, bf16[2,256,864]{2,1,0:T(8,128)(2,1)S(1)}, bf16[2,256,864]{2,1,0:T(8,128)(2,1)S(1)}, bf16[2,256,864]{2,1,0:T(8,128)(2,1)S(1)}) custom-call(bf16[256,1152]{1,0:T(8,128)(2,1)S(1)} %collective-permute-done.24.refs_0_.refs_6_, bf16[864,1152]{1,0:T(8,128)(2,1)S(1)} %bitcast.56, ...), custom_call_target="tpu_custom_call" | custom-call | flops 1 | bytes 1 | tf_op jit(solution)/shard_map/feed/pallas_call | solution.py:306
  91.5 4.5 %feed.7 = (bf16[128,1152]{1,0:T(8,128)(2,1)S(1)}, bf16[128,1152]{1,0:T(8,128)(2,1)S(1)}, bf16[2,256,864]{2,1,0:T(8,128)(2,1)S(1)}, bf16[2,256,864]{2,1,0:T(8,128)(2,1)S(1)}, bf16[2,256,864]{2,1,0:T(8,128)(2,1)S(1)}) custom-call(bf16[128,1152]{1,0:T(8,128)(2,1)S(1)} %collective-permute-done.25.refs_0_.refs_7_, ...), custom_call_target="tpu_custom_call" | custom-call | flops 1 | bytes 1 | tf_op jit(solution)/shard_map/feed/pallas_call | solution.py:306
  99.5 5.9 %collective-permute-done.31 = bf16[128,1152]{1,0:T(8,128)(2,1)S(1)} collective-permute-done((bf16[128,1152]{1,0:T(8,128)(2,1)S(1)}, bf16[128,1152]{1,0:T(8,128)(2,1)S(1)}, u32[]{:S(2)}, u32[]{:S(2)}) %collective-permute-start.31) | collective-permute-done | bytes 294944 | tf_op jit(solution)/shard_map/ppermute | solution.py:522
  121.8 4.5 %feed_back.4 = (f32[128,1152]{1,0:T(8,128)S(1)}, f32[128,1152]{1,0:T(8,128)S(1)}, bf16[2,256,864]{2,1,0:T(8,128)(2,1)S(1)}, bf16[2,256,864]{2,1,0:T(8,128)(2,1)S(1)}) custom-call(bf16[2,256,864]{2,1,0:T(8,128)(2,1)S(1)} %get-tuple-element.459.act_ref, bf16[2,256,864]{2,1,0:T(8,128)(2,1)S(1)} %get-tuple-element.460.slope_ref, ...), custom_call_target="tpu_custom_call" | custom-call | flops 1 | bytes 1 | tf_op jit(solution)/shard_map/feed_back/pallas_call | solution.py:337
  133.6 4.3 %feed_back.5 = (bf16[128,1152]{1,0:T(8,128)(2,1)S(1)}, bf16[128,1152]{1,0:T(8,128)(2,1)S(1)}, bf16[2,256,864]{2,1,0:T(8,128)(2,1)S(1)}, bf16[2,256,864]{2,1,0:T(8,128)(2,1)S(1)}) custom-call(bf16[2,256,864]{2,1,0:T(8,128)(2,1)S(1)} %get-tuple-element.474.act_ref, bf16[2,256,864]{2,1,0:T(8,128)(2,1)S(1)} %get-tuple-element.475.slope_ref, ...), custom_call_target="tpu_custom_call" | custom-call | flops 1 | bytes 1 | tf_op jit(solution)/shard_map/feed_back/pallas_call | solution.py:337
  137.9 4.3 %feed_back.6 = (bf16[128,1152]{1,0:T(8,128)(2,1)S(1)}, bf16[128,1152]{1,0:T(8,128)(2,1)S(1)}, bf16[2,256,864]{2,1,0:T(8,128)(2,1)S(1)}, bf16[2,256,864]{2,1,0:T(8,128)(2,1)S(1)}) custom-call(bf16[2,256,864]{2,1,0:T(8,128)(2,1)S(1)} %get-tuple-element.480.act_ref, bf16[2,256,864]{2,1,0:T(8,128)(2,1)S(1)} %get-tuple-element.481.slope_ref, ...), custom_call_target="tpu_custom_call" | custom-call | flops 1 | bytes 1 | tf_op jit(solution)/shard_map/feed_back/pallas_call | solution.py:337
  144.8 4.7 %feed_back.7 = (bf16[128,1152]{1,0:T(8,128)(2,1)S(1)}, bf16[128,1152]{1,0:T(8,128)(2,1)S(1)}, bf16[2,256,864]{2,1,0:T(8,128)(2,1)S(1)}, bf16[2,256,864]{2,1,0:T(8,128)(2,1)S(1)}) custom-call(bf16[2,256,864]{2,1,0:T(8,128)(2,1)S(1)} %get-tuple-element.500.act_ref, bf16[2,256,864]{2,1,0:T(8,128)(2,1)S(1)} %get-tuple-element.501.slope_ref, ...), custom_call_target="tpu_custom_call" | custom-call | flops 1 | bytes 1 | tf_op jit(solution)/shard_map/feed_back/pallas_call | solution.py:337
  164.5 4.6 %collective-permute-done.41 = bf16[128,1152]{1,0:T(8,128)(2,1)S(1)} collective-permute-done((bf16[128,1152]{1,0:T(8,128)(2,1)S(1)}, bf16[128,1152]{1,0:T(8,128)(2,1)S(1)}, u32[]{:S(2)}, u32[]{:S(2)}) %collective-permute-start.41) | collective-permute-done | bytes 294944 | tf_op jit(solution)/shard_map/ppermute | solution.py:522
  187.9 5.2 %collective-permute-start.48 = (bf16[288,1152]{1,0:T(8,128)(2,1)S(1)}, bf16[288,1152]{1,0:T(8,128)(2,1)S(1)}, u32[]{:S(2)}, u32[]{:S(2)}) collective-permute-start(bf16[288,1152]{1,0:T(8,128)(2,1)S(1)} %broadcast_select_fusion.15), channel_id=1, source_target_pairs={{0,8},{8,0},{16,24},{24,16},{1,9},{9,1},{17,25},{25,17},{2,10},{10... | collective-permute-start | bytes 1990664 | tf_op jit(solution)/shard_map/ppermute | solution.py:663
  198.5 10.2 %collective-permute-done.48 = bf16[288,1152]{1,0:T(8,128)(2,1)S(1)} collective-permute-done((bf16[288,1152]{1,0:T(8,128)(2,1)S(1)}, bf16[288,1152]{1,0:T(8,128)(2,1)S(1)}, u32[]{:S(2)}, u32[]{:S(2)}) %collective-permute-start.48) | collective-permute-done | bytes 663584 | tf_op jit(solution)/shard_map/ppermute | solution.py:663
  209.0 3.9 %collective-permute-start.51 = (bf16[288,1152]{1,0:T(8,128)(2,1)S(1)}, bf16[288,1152]{1,0:T(8,128)(2,1)S(1)}, u32[]{:S(2)}, u32[]{:S(2)}) collective-permute-start(bf16[288,1152]{1,0:T(8,128)(2,1)S(1)} %broadcast_select_fusion.14), channel_id=1, source_target_pairs={{0,8},{8,0},{16,24},{24,16},{1,9},{9,1},{17,25},{25,17},{2,10},{10... | collective-permute-start | bytes 1990664 | tf_op jit(solution)/shard_map/ppermute | solution.py:663
  219.0 9.4 %collective-permute-done.51 = bf16[288,1152]{1,0:T(8,128)(2,1)S(1)} collective-permute-done((bf16[288,1152]{1,0:T(8,128)(2,1)S(1)}, bf16[288,1152]{1,0:T(8,128)(2,1)S(1)}, u32[]{:S(2)}, u32[]{:S(2)}) %collective-permute-start.51) | collective-permute-done | bytes 663584 | tf_op jit(solution)/shard_map/ppermute | solution.py:663
  230.4 3.8 %collective-permute-start.56 = (bf16[288,1152]{1,0:T(8,128)(2,1)S(1)}, bf16[288,1152]{1,0:T(8,128)(2,1)S(1)}, u32[]{:S(2)}, u32[]{:S(2)}) collective-permute-start(bf16[288,1152]{1,0:T(8,128)(2,1)S(1)} %broadcast_select_fusion.13), channel_id=1, source_target_pairs={{0,8},{8,0},{16,24},{24,16},{1,9},{9,1},{17,25},{25,17},{2,10},{10... | collective-permute-start | bytes 1990664 | tf_op jit(solution)/shard_map/ppermute | solution.py:663
  241.8 6.9 %collective-permute-done.56 = bf16[288,1152]{1,0:T(8,128)(2,1)S(1)} collective-permute-done((bf16[288,1152]{1,0:T(8,128)(2,1)S(1)}, bf16[288,1152]{1,0:T(8,128)(2,1)S(1)}, u32[]{:S(2)}, u32[]{:S(2)}) %collective-permute-start.56) | collective-permute-done | bytes 663584 | tf_op jit(solution)/shard_map/ppermute | solution.py:663
  249.5 3.8 %collective-permute-start.60 = (bf16[288,1152]{1,0:T(8,128)(2,1)S(1)}, bf16[288,1152]{1,0:T(8,128)(2,1)S(1)}, u32[]{:S(2)}, u32[]{:S(2)}) collective-permute-start(bf16[288,1152]{1,0:T(8,128)(2,1)S(1)} %broadcast_select_fusion.12), channel_id=1, source_target_pairs={{0,8},{8,0},{16,24},{24,16},{1,9},{9,1},{17,25},{25,17},{2,10},{10... | collective-permute-start | bytes 1990664 | tf_op jit(solution)/shard_map/ppermute | solution.py:663
  263.1 3.8 collective-permute-done.60
  267.5 3.9 %collective-permute-start.64 = (bf16[288,1152]{1,0:T(8,128)(2,1)S(1)}, bf16[288,1152]{1,0:T(8,128)(2,1)S(1)}, u32[]{:S(2)}, u32[]{:S(2)}) collective-permute-start(bf16[288,1152]{1,0:T(8,128)(2,1)S(1)} %broadcast_select_fusion.11), channel_id=1, source_target_pairs={{0,8},{8,0},{16,24},{24,16},{1,9},{9,1},{17,25},{25,17},{2,10},{10... | collective-permute-start | bytes 1990664 | tf_op jit(solution)/shard_map/ppermute | solution.py:663
  275.9 6.8 %collective-permute-done.67 = bf16[128,1152]{1,0:T(8,128)(2,1)S(1)} collective-permute-done((bf16[128,1152]{1,0:T(8,128)(2,1)S(1)}, bf16[128,1152]{1,0:T(8,128)(2,1)S(1)}, u32[]{:S(2)}, u32[]{:S(2)}) %collective-permute-start.67) | collective-permute-done | bytes 294944 | tf_op jit(solution)/shard_map/ppermute | solution.py:522
  285.0 7.1 %collective-permute-start.68 = (bf16[288,1152]{1,0:T(8,128)(2,1)S(1)}, bf16[288,1152]{1,0:T(8,128)(2,1)S(1)}, u32[]{:S(2)}, u32[]{:S(2)}) collective-permute-start(bf16[288,1152]{1,0:T(8,128)(2,1)S(1)} %broadcast_select_fusion.10), channel_id=1, source_target_pairs={{0,8},{8,0},{16,24},{24,16},{1,9},{9,1},{17,25},{25,17},{2,10},{10... | collective-permute-start | bytes 1990664 | tf_op jit(solution)/shard_map/ppermute | solution.py:663
  295.5 6.5 %collective-permute-done.70 = bf16[160,1536]{1,0:T(8,128)(2,1)S(1)} collective-permute-done((bf16[160,1536]{1,0:T(8,128)(2,1)S(1)}, bf16[160,1536]{1,0:T(8,128)(2,1)S(1)}, u32[]{:S(2)}, u32[]{:S(2)}) %collective-permute-start.70) | collective-permute-done | bytes 491552 | tf_op jit(solution)/shard_map/ppermute | solution.py:522
  305.1 4.1 %collective-permute-start.72 = (bf16[288,1152]{1,0:T(8,128)(2,1)S(1)}, bf16[288,1152]{1,0:T(8,128)(2,1)S(1)}, u32[]{:S(2)}, u32[]{:S(2)}) collective-permute-start(bf16[288,1152]{1,0:T(8,128)(2,1)S(1)} %broadcast_select_fusion.9), channel_id=1, source_target_pairs={{0,8},{8,0},{16,24},{24,16},{1,9},{9,1},{17,25},{25,17},{2,10},{10... | collective-permute-start | bytes 1990664 | tf_op jit(solution)/shard_map/ppermute | solution.py:663
  313.9 5.1 %collective-permute-done.74 = bf16[160,1536]{1,0:T(8,128)(2,1)S(1)} collective-permute-done((bf16[160,1536]{1,0:T(8,128)(2,1)S(1)}, bf16[160,1536]{1,0:T(8,128)(2,1)S(1)}, u32[]{:S(2)}, u32[]{:S(2)}) %collective-permute-start.74) | collective-permute-done | bytes 491552 | tf_op jit(solution)/shard_map/ppermute | solution.py:522
  322.4 5.7 %collective-permute-start.75 = (bf16[160,1536]{1,0:T(8,128)(2,1)S(1)}, bf16[160,1536]{1,0:T(8,128)(2,1)S(1)}, u32[]{:S(2)}, u32[]{:S(2)}) collective-permute-start(bf16[160,1536]{1,0:T(8,128)(2,1)S(1)} %add_convert_fusion.21), channel_id=1, source_target_pairs={{0,8},{24,16},{1,9},{25,17},{2,10},{26,18},{3,11},{27,19},{4,12},{... | collective-permute-start | bytes 1474568 | tf_op jit(solution)/shard_map/ppermute | solution.py:668
  328.2 8.1 %collective-permute-done.75 = bf16[160,1536]{1,0:T(8,128)(2,1)S(1)} collective-permute-done((bf16[160,1536]{1,0:T(8,128)(2,1)S(1)}, bf16[160,1536]{1,0:T(8,128)(2,1)S(1)}, u32[]{:S(2)}, u32[]{:S(2)}) %collective-permute-start.75) | collective-permute-done | bytes 491552 | tf_op jit(solution)/shard_map/ppermute | solution.py:668
  336.3 4.4 %collective-permute-start.78 = (bf16[128,1152]{1,0:T(8,128)(2,1)S(1)}, bf16[128,1152]{1,0:T(8,128)(2,1)S(1)}, u32[]{:S(2)}, u32[]{:S(2)}) collective-permute-start(bf16[128,1152]{1,0:T(8,128)(2,1)S(1)} %add_convert_fusion.24), channel_id=1, source_target_pairs={{0,8},{24,16},{1,9},{25,17},{2,10},{26,18},{3,11},{27,19},{4,12},{... | collective-permute-start | bytes 884744 | tf_op jit(solution)/shard_map/ppermute | solution.py:668
  345.0 13.7 %collective-permute-done.80 = bf16[288,1152]{1,0:T(8,128)(2,1)S(1)} collective-permute-done((bf16[288,1152]{1,0:T(8,128)(2,1)S(1)}, bf16[288,1152]{1,0:T(8,128)(2,1)S(1)}, u32[]{:S(2)}, u32[]{:S(2)}) %collective-permute-start.80) | collective-permute-done | bytes 663584 | tf_op jit(solution)/shard_map/ppermute | solution.py:700
  364.5 5.0 %collective-permute-done.81 = bf16[160,1536]{1,0:T(8,128)(2,1)S(1)} collective-permute-done((bf16[160,1536]{1,0:T(8,128)(2,1)S(1)}, bf16[160,1536]{1,0:T(8,128)(2,1)S(1)}, u32[]{:S(2)}, u32[]{:S(2)}) %collective-permute-start.81) | collective-permute-done | bytes 491552 | tf_op jit(solution)/shard_map/ppermute | solution.py:700
  (373 shorter events, 197.3 us)
Async XLA Ops:
  0.6 11.0 %collective-permute-start = (bf16[144,512]{1,0:T(8,128)(2,1)}, bf16[144,512]{1,0:T(8,128)(2,1)S(1)}, u32[]{:S(2)}, u32[]{:S(2)}) collective-permute-start(bf16[144,512]{1,0:T(8,128)(2,1)} %param.21), channel_id=1, source_target_pairs={{0,2},{1,3},{2,0},{3,1},{4,6},{5,7},{6,4},{7,5},{8,10},{9,11},{10,... | collective-permute-start | bytes 442376 | tf_op jit(solution)/shard_map/ppermute | solution.py:522
  61.0 15.4 %collective-permute-start.23 = (bf16[256,1152]{1,0:T(8,128)(2,1)S(1)}, bf16[256,1152]{1,0:T(8,128)(2,1)S(1)}, u32[]{:S(2)}, u32[]{:S(2)}) collective-permute-start(bf16[256,1152]{1,0:T(8,128)(2,1)S(1)} %multiply_convert_fusion.1.refs_0_.refs_4_), channel_id=1, source_target_pairs={{0,2},{1,3},{2,0},{3,1},{4,6},{5,7},{6,4},{7,5},{8,10},{9,11},{10,... | collective-permute-start | bytes 1769480 | tf_op jit(solution)/shard_map/ppermute | solution.py:522
  62.5 15.5 %collective-permute-start.24 = (bf16[256,1152]{1,0:T(8,128)(2,1)S(1)}, bf16[256,1152]{1,0:T(8,128)(2,1)S(1)}, u32[]{:S(2)}, u32[]{:S(2)}) collective-permute-start(bf16[256,1152]{1,0:T(8,128)(2,1)S(1)} %multiply_convert_fusion.1.refs_0_.refs_4_), channel_id=1, source_target_pairs={{0,4},{1,5},{2,6},{3,7},{4,0},{5,1},{6,2},{7,3},{8,12},{9,13},{10,... | collective-permute-start | bytes 1769480 | tf_op jit(solution)/shard_map/ppermute | solution.py:522
  78.1 11.4 %collective-permute-start.25 = (bf16[128,1152]{1,0:T(8,128)(2,1)S(1)}, bf16[128,1152]{1,0:T(8,128)(2,1)S(1)}, u32[]{:S(2)}, u32[]{:S(2)}) collective-permute-start(bf16[128,1152]{1,0:T(8,128)(2,1)S(1)} %slice.131), channel_id=1, source_target_pairs={{0,2},{1,3},{2,0},{3,1},{4,6},{5,7},{6,4},{7,5},{8,10},{9,11},{10,... | collective-permute-start | bytes 884744 | tf_op jit(solution)/shard_map/ppermute | solution.py:522
  116.4 11.4 %collective-permute-start.33 = (bf16[256,1152]{1,0:T(8,128)(2,1)S(1)}, bf16[256,1152]{1,0:T(8,128)(2,1)S(1)}, u32[]{:S(2)}, u32[]{:S(2)}) collective-permute-start(bf16[256,1152]{1,0:T(8,128)(2,1)S(1)} %get-tuple-element.458.refs_0_.refs_4_), channel_id=1, source_target_pairs={{0,2},{1,3},{2,0},{3,1},{4,6},{5,7},{6,4},{7,5},{8,10},{9,11},{10,... | collective-permute-start | bytes 1769480 | tf_op jit(solution)/shard_map/ppermute | solution.py:522
  117.0 12.2 %collective-permute-start.34 = (bf16[256,1152]{1,0:T(8,128)(2,1)S(1)}, bf16[256,1152]{1,0:T(8,128)(2,1)S(1)}, u32[]{:S(2)}, u32[]{:S(2)}) collective-permute-start(bf16[256,1152]{1,0:T(8,128)(2,1)S(1)} %get-tuple-element.458.refs_0_.refs_4_), channel_id=1, source_target_pairs={{0,4},{1,5},{2,6},{3,7},{4,0},{5,1},{6,2},{7,3},{8,12},{9,13},{10,... | collective-permute-start | bytes 1769480 | tf_op jit(solution)/shard_map/ppermute | solution.py:522
  129.2 12.9 %collective-permute-start.35 = (bf16[128,1152]{1,0:T(8,128)(2,1)S(1)}, bf16[128,1152]{1,0:T(8,128)(2,1)S(1)}, u32[]{:S(2)}, u32[]{:S(2)}) collective-permute-start(bf16[128,1152]{1,0:T(8,128)(2,1)S(1)} %slice.133), channel_id=1, source_target_pairs={{0,2},{1,3},{2,0},{3,1},{4,6},{5,7},{6,4},{7,5},{8,10},{9,11},{10,... | collective-permute-start | bytes 884744 | tf_op jit(solution)/shard_map/ppermute | solution.py:522
  152.0 18.1 %collective-permute-start.38 = (bf16[288,1152]{1,0:T(8,128)(2,1)S(1)}, bf16[288,1152]{1,0:T(8,128)(2,1)S(1)}, u32[]{:S(2)}, u32[]{:S(2)}) collective-permute-start(bf16[288,1152]{1,0:T(8,128)(2,1)S(1)} %get-tuple-element.526), channel_id=1, source_target_pairs={{0,8},{24,16},{1,9},{25,17},{2,10},{26,18},{3,11},{27,19},{4,12},{... | collective-permute-start | bytes 1990664 | tf_op jit(solution)/shard_map/ppermute | solution.py:668
  156.6 12.5 %collective-permute-start.41 = (bf16[128,1152]{1,0:T(8,128)(2,1)S(1)}, bf16[128,1152]{1,0:T(8,128)(2,1)S(1)}, u32[]{:S(2)}, u32[]{:S(2)}) collective-permute-start(bf16[128,1152]{1,0:T(8,128)(2,1)S(1)} %get-tuple-element.529), channel_id=1, source_target_pairs={{0,2},{1,3},{2,0},{3,1},{4,6},{5,7},{6,4},{7,5},{8,10},{9,11},{10,... | collective-permute-start | bytes 884744 | tf_op jit(solution)/shard_map/ppermute | solution.py:522
  157.7 12.4 %collective-permute-start.42 = (bf16[128,1152]{1,0:T(8,128)(2,1)S(1)}, bf16[128,1152]{1,0:T(8,128)(2,1)S(1)}, u32[]{:S(2)}, u32[]{:S(2)}) collective-permute-start(bf16[128,1152]{1,0:T(8,128)(2,1)S(1)} %get-tuple-element.530), channel_id=1, source_target_pairs={{0,4},{1,5},{2,6},{3,7},{4,0},{5,1},{6,2},{7,3},{8,12},{9,13},{10,... | collective-permute-start | bytes 884744 | tf_op jit(solution)/shard_map/ppermute | solution.py:522
  170.1 17.5 %collective-permute-start.43 = (bf16[288,1152]{1,0:T(8,128)(2,1)S(1)}, bf16[288,1152]{1,0:T(8,128)(2,1)S(1)}, u32[]{:S(2)}, u32[]{:S(2)}) collective-permute-start(bf16[288,1152]{1,0:T(8,128)(2,1)S(1)} %get-tuple-element.546), channel_id=1, source_target_pairs={{0,8},{24,16},{1,9},{25,17},{2,10},{26,18},{3,11},{27,19},{4,12},{... | collective-permute-start | bytes 1990664 | tf_op jit(solution)/shard_map/ppermute | solution.py:668
  173.1 14.6 %collective-permute-start.44 = (bf16[288,1152]{1,0:T(8,128)(2,1)S(1)}, bf16[288,1152]{1,0:T(8,128)(2,1)S(1)}, u32[]{:S(2)}, u32[]{:S(2)}) collective-permute-start(bf16[288,1152]{1,0:T(8,128)(2,1)S(1)} %add_convert_fusion.17), channel_id=1, source_target_pairs={{8,16},{16,8},{9,17},{17,9},{10,18},{18,10},{11,19},{19,11},{12,20... | collective-permute-start | bytes 1990664 | tf_op jit(solution)/shard_map/ppermute | solution.py:670
  187.7 21.1 %collective-permute-start.50 = (bf16[864,1152]{1,0:T(8,128)(2,1)S(1)}, bf16[864,1152]{1,0:T(8,128)(2,1)S(1)}, u32[]{:S(2)}, u32[]{:S(2)}) collective-permute-start(bf16[864,1152]{1,0:T(8,128)(2,1)S(1)} %weight_grad.9), channel_id=1, source_target_pairs={{0,1},{1,0},{2,3},{3,2},{4,5},{5,4},{6,7},{7,6},{8,9},{9,8},{10,11... | collective-permute-start | bytes 5971976 | tf_op jit(solution)/shard_map/ppermute | solution.py:522
  187.9 20.8 %collective-permute-start.48 = (bf16[288,1152]{1,0:T(8,128)(2,1)S(1)}, bf16[288,1152]{1,0:T(8,128)(2,1)S(1)}, u32[]{:S(2)}, u32[]{:S(2)}) collective-permute-start(bf16[288,1152]{1,0:T(8,128)(2,1)S(1)} %broadcast_select_fusion.15), channel_id=1, source_target_pairs={{0,8},{8,0},{16,24},{24,16},{1,9},{9,1},{17,25},{25,17},{2,10},{10... | collective-permute-start | bytes 1990664 | tf_op jit(solution)/shard_map/ppermute | solution.py:663
  193.3 15.4 %collective-permute-start.49 = (bf16[288,1152]{1,0:T(8,128)(2,1)S(1)}, bf16[288,1152]{1,0:T(8,128)(2,1)S(1)}, u32[]{:S(2)}, u32[]{:S(2)}) collective-permute-start(bf16[288,1152]{1,0:T(8,128)(2,1)S(1)} %add_convert_fusion.15), channel_id=1, source_target_pairs={{8,16},{16,8},{9,17},{17,9},{10,18},{18,10},{11,19},{19,11},{12,20... | collective-permute-start | bytes 1990664 | tf_op jit(solution)/shard_map/ppermute | solution.py:670
  209.0 19.5 %collective-permute-start.51 = (bf16[288,1152]{1,0:T(8,128)(2,1)S(1)}, bf16[288,1152]{1,0:T(8,128)(2,1)S(1)}, u32[]{:S(2)}, u32[]{:S(2)}) collective-permute-start(bf16[288,1152]{1,0:T(8,128)(2,1)S(1)} %broadcast_select_fusion.14), channel_id=1, source_target_pairs={{0,8},{8,0},{16,24},{24,16},{1,9},{9,1},{17,25},{25,17},{2,10},{10... | collective-permute-start | bytes 1990664 | tf_op jit(solution)/shard_map/ppermute | solution.py:663
  213.0 15.4 %collective-permute-start.52 = (bf16[288,1152]{1,0:T(8,128)(2,1)S(1)}, bf16[288,1152]{1,0:T(8,128)(2,1)S(1)}, u32[]{:S(2)}, u32[]{:S(2)}) collective-permute-start(bf16[288,1152]{1,0:T(8,128)(2,1)S(1)} %add_convert_fusion.13), channel_id=1, source_target_pairs={{8,16},{16,8},{9,17},{17,9},{10,18},{18,10},{11,19},{19,11},{12,20... | collective-permute-start | bytes 1990664 | tf_op jit(solution)/shard_map/ppermute | solution.py:670
  214.4 14.0 %collective-permute-start.54 = (bf16[256,512]{1,0:T(8,128)(2,1)S(1)}, bf16[256,512]{1,0:T(8,128)(2,1)S(1)}, u32[]{:S(2)}, u32[]{:S(2)}) collective-permute-start(bf16[256,512]{1,0:T(8,128)(2,1)S(1)} %get-tuple-element.706), channel_id=1, source_target_pairs={{0,2},{1,3},{2,0},{3,1},{4,6},{5,7},{6,4},{7,5},{8,10},{9,11},{10,... | collective-permute-start | bytes 786440 | tf_op jit(solution)/shard_map/ppermute | solution.py:522
  215.6 12.9 %collective-permute-start.55 = (bf16[256,512]{1,0:T(8,128)(2,1)S(1)}, bf16[256,512]{1,0:T(8,128)(2,1)S(1)}, u32[]{:S(2)}, u32[]{:S(2)}) collective-permute-start(bf16[256,512]{1,0:T(8,128)(2,1)S(1)} %get-tuple-element.705), channel_id=1, source_target_pairs={{0,4},{1,5},{2,6},{3,7},{4,0},{5,1},{6,2},{7,3},{8,12},{9,13},{10,... | collective-permute-start | bytes 786440 | tf_op jit(solution)/shard_map/ppermute | solution.py:522
  230.4 18.3 %collective-permute-start.56 = (bf16[288,1152]{1,0:T(8,128)(2,1)S(1)}, bf16[288,1152]{1,0:T(8,128)(2,1)S(1)}, u32[]{:S(2)}, u32[]{:S(2)}) collective-permute-start(bf16[288,1152]{1,0:T(8,128)(2,1)S(1)} %broadcast_select_fusion.13), channel_id=1, source_target_pairs={{0,8},{8,0},{16,24},{24,16},{1,9},{9,1},{17,25},{25,17},{2,10},{10... | collective-permute-start | bytes 1990664 | tf_op jit(solution)/shard_map/ppermute | solution.py:663
  234.2 14.5 %collective-permute-start.57 = (bf16[288,1152]{1,0:T(8,128)(2,1)S(1)}, bf16[288,1152]{1,0:T(8,128)(2,1)S(1)}, u32[]{:S(2)}, u32[]{:S(2)}) collective-permute-start(bf16[288,1152]{1,0:T(8,128)(2,1)S(1)} %add_convert_fusion.12), channel_id=1, source_target_pairs={{8,16},{16,8},{9,17},{17,9},{10,18},{18,10},{11,19},{19,11},{12,20... | collective-permute-start | bytes 1990664 | tf_op jit(solution)/shard_map/ppermute | solution.py:670
  249.5 17.4 %collective-permute-start.60 = (bf16[288,1152]{1,0:T(8,128)(2,1)S(1)}, bf16[288,1152]{1,0:T(8,128)(2,1)S(1)}, u32[]{:S(2)}, u32[]{:S(2)}) collective-permute-start(bf16[288,1152]{1,0:T(8,128)(2,1)S(1)} %broadcast_select_fusion.12), channel_id=1, source_target_pairs={{0,8},{8,0},{16,24},{24,16},{1,9},{9,1},{17,25},{25,17},{2,10},{10... | collective-permute-start | bytes 1990664 | tf_op jit(solution)/shard_map/ppermute | solution.py:663
  267.5 16.6 %collective-permute-start.64 = (bf16[288,1152]{1,0:T(8,128)(2,1)S(1)}, bf16[288,1152]{1,0:T(8,128)(2,1)S(1)}, u32[]{:S(2)}, u32[]{:S(2)}) collective-permute-start(bf16[288,1152]{1,0:T(8,128)(2,1)S(1)} %broadcast_select_fusion.11), channel_id=1, source_target_pairs={{0,8},{8,0},{16,24},{24,16},{1,9},{9,1},{17,25},{25,17},{2,10},{10... | collective-permute-start | bytes 1990664 | tf_op jit(solution)/shard_map/ppermute | solution.py:663
  271.4 11.5 %collective-permute-start.65 = (bf16[288,1152]{1,0:T(8,128)(2,1)S(1)}, bf16[288,1152]{1,0:T(8,128)(2,1)S(1)}, u32[]{:S(2)}, u32[]{:S(2)}) collective-permute-start(bf16[288,1152]{1,0:T(8,128)(2,1)S(1)} %add_convert_fusion.7), channel_id=1, source_target_pairs={{8,16},{16,8},{9,17},{17,9},{10,18},{18,10},{11,19},{19,11},{12,20... | collective-permute-start | bytes 1990664 | tf_op jit(solution)/shard_map/ppermute | solution.py:670
  284.2 11.1 %collective-permute-start.69 = (bf16[288,1152]{1,0:T(8,128)(2,1)S(1)}, bf16[288,1152]{1,0:T(8,128)(2,1)S(1)}, u32[]{:S(2)}, u32[]{:S(2)}) collective-permute-start(bf16[288,1152]{1,0:T(8,128)(2,1)S(1)} %add_convert_fusion.5), channel_id=1, source_target_pairs={{8,16},{16,8},{9,17},{17,9},{10,18},{18,10},{11,19},{19,11},{12,20... | collective-permute-start | bytes 1990664 | tf_op jit(solution)/shard_map/ppermute | solution.py:670
  285.0 19.0 %collective-permute-start.68 = (bf16[288,1152]{1,0:T(8,128)(2,1)S(1)}, bf16[288,1152]{1,0:T(8,128)(2,1)S(1)}, u32[]{:S(2)}, u32[]{:S(2)}) collective-permute-start(bf16[288,1152]{1,0:T(8,128)(2,1)S(1)} %broadcast_select_fusion.10), channel_id=1, source_target_pairs={{0,8},{8,0},{16,24},{24,16},{1,9},{9,1},{17,25},{25,17},{2,10},{10... | collective-permute-start | bytes 1990664 | tf_op jit(solution)/shard_map/ppermute | solution.py:663
  305.1 14.9 %collective-permute-start.72 = (bf16[288,1152]{1,0:T(8,128)(2,1)S(1)}, bf16[288,1152]{1,0:T(8,128)(2,1)S(1)}, u32[]{:S(2)}, u32[]{:S(2)}) collective-permute-start(bf16[288,1152]{1,0:T(8,128)(2,1)S(1)} %broadcast_select_fusion.9), channel_id=1, source_target_pairs={{0,8},{8,0},{16,24},{24,16},{1,9},{9,1},{17,25},{25,17},{2,10},{10... | collective-permute-start | bytes 1990664 | tf_op jit(solution)/shard_map/ppermute | solution.py:663
  320.1 16.3 %collective-permute-start.76 = (bf16[288,1152]{1,0:T(8,128)(2,1)S(1)}, bf16[288,1152]{1,0:T(8,128)(2,1)S(1)}, u32[]{:S(2)}, u32[]{:S(2)}) collective-permute-start(bf16[288,1152]{1,0:T(8,128)(2,1)S(1)} %add_convert_fusion.1), channel_id=1, source_target_pairs={{8,16},{16,8},{9,17},{17,9},{10,18},{18,10},{11,19},{19,11},{12,20... | collective-permute-start | bytes 1990664 | tf_op jit(solution)/shard_map/ppermute | solution.py:670
  320.8 15.5 %collective-permute-start.77 = (bf16[288,1152]{1,0:T(8,128)(2,1)S(1)}, bf16[288,1152]{1,0:T(8,128)(2,1)S(1)}, u32[]{:S(2)}, u32[]{:S(2)}) collective-permute-start(bf16[288,1152]{1,0:T(8,128)(2,1)S(1)} %add_convert_fusion.2), channel_id=1, source_target_pairs={{8,0},{16,24},{9,1},{17,25},{10,2},{18,26},{11,3},{19,27},{12,4},{... | collective-permute-start | bytes 1990664 | tf_op jit(solution)/shard_map/ppermute | solution.py:700
  322.4 14.0 %collective-permute-start.75 = (bf16[160,1536]{1,0:T(8,128)(2,1)S(1)}, bf16[160,1536]{1,0:T(8,128)(2,1)S(1)}, u32[]{:S(2)}, u32[]{:S(2)}) collective-permute-start(bf16[160,1536]{1,0:T(8,128)(2,1)S(1)} %add_convert_fusion.21), channel_id=1, source_target_pairs={{0,8},{24,16},{1,9},{25,17},{2,10},{26,18},{3,11},{27,19},{4,12},{... | collective-permute-start | bytes 1474568 | tf_op jit(solution)/shard_map/ppermute | solution.py:668
  340.9 17.8 %collective-permute-start.80 = (bf16[288,1152]{1,0:T(8,128)(2,1)S(1)}, bf16[288,1152]{1,0:T(8,128)(2,1)S(1)}, u32[]{:S(2)}, u32[]{:S(2)}) collective-permute-start(bf16[288,1152]{1,0:T(8,128)(2,1)S(1)} %add_convert_fusion), channel_id=1, source_target_pairs={{8,0},{16,24},{9,1},{17,25},{10,2},{18,26},{11,3},{19,27},{12,4},{... | collective-permute-start | bytes 1990664 | tf_op jit(solution)/shard_map/ppermute | solution.py:700
  363.2 14.3 %collective-permute-start.83 = (bf16[128,1152]{1,0:T(8,128)(2,1)S(1)}, bf16[128,1152]{1,0:T(8,128)(2,1)S(1)}, u32[]{:S(2)}, u32[]{:S(2)}) collective-permute-start(bf16[128,1152]{1,0:T(8,128)(2,1)S(1)} %add_convert_fusion.22), channel_id=1, source_target_pairs={{8,0},{16,24},{9,1},{17,25},{10,2},{18,26},{11,3},{19,27},{12,4},{... | collective-permute-start | bytes 884744 | tf_op jit(solution)/shard_map/ppermute | solution.py:700
  (78 other events, 494.8 us)

commit v7 on v6

--- a/solution.py
+++ b/solution.py
@@ -869,7 +869,7 @@
         grad_out = [dot_cols(v, d_attn) for v in att_columns]
         return heads, d_up, grad_out, [comm.hop(v, 1) for v in other_up]
 
-    heads, d_up, grad_out, other_up = line.step(beside)
+    heads, d_up, grad_out, other_up = line.step(beside, True)
     d_q_pre, *d_kv_blocks, gain_query = heads
 
     def beside(_):

time: 384 us -> 383 us (level)
  starting transfers between devices: 117 us -> 106 us
  waiting for transfers between devices: 147 us -> 156 us
    ppermute x58, waiting for transfers between devices: 81.5 us -> 91.8 us  [hop(): return lax.ppermute(value, 'seq', [(i, i ^ bit) for i in range(8)])]
    ppermute x58, starting transfers between devices: 56.9 us -> 47.3 us  [hop(): return lax.ppermute(value, 'seq', [(i, i ^ bit) for i in range(8)])]
  transfers between devices with their start and end apart: 84 -> 84, of which waited for: 50 -> 51; matrix products, arithmetic and copies ran while one was open for 11% -> 11% of each run, Pallas kernels for 14% -> 14%
where the time goes in v7:
time: 383 us; the launch traced here: 377 us
  waiting for transfers between devices  156 us (41%)
  starting transfers between devices  106 us (28%)
  Pallas kernels  58.6 us (15%)
  other arithmetic  24 us (6%)
  matrix products  18.7 us (5%)
  local copies, waits for them, and re-layouts  9.93 us (3%)
    ppermute x58, waiting for transfers between devices, hop(): return lax.ppermute(value, 'seq', [(i, i ^ bit) for i in range(8)])  91.8 us
    ppermute x58, starting transfers between devices, hop(): return lax.ppermute(value, 'seq', [(i, i ^ bit) for i in range(8)])  47.3 us
    ppermute x7, waiting for transfers between devices, step(): got['in'] = lax.ppermute(both, 'dp', [(0, 1), (1, 0), (2, 3), (3, 2)])  33.8 us
    ppermute x7, starting transfers between devices, step(): got['in'] = lax.ppermute(both, 'dp', [(0, 1), (1, 0), (2, 3), (3, 2)])  30 us
    ppermute x4, waiting for transfers between devices, outwards(): return lax.ppermute(value, 'dp', [(1, 0), (2, 3)])  20.8 us
    pallas_call x4, Pallas kernels, feed(): pl.pallas_call(functools.partial(feed_kernel, groups, len(b)), out_shape=...  18.1 us
    pallas_call x4, Pallas kernels, feed_back(): pl.pallas_call(functools.partial(feed_back_kernel, groups, len(d)), out_s...  17.7 us
    ppermute x4, starting transfers between devices, step(): got['in'] = lax.ppermute(mine, 'dp', [(0, 1), (3, 2)])  15.5 us
  transfers between devices with their start and end apart: 84, of which 51 were waited for; matrix products, arithmetic and copies ran while one was open for 11% of the time, Pallas kernels for 14%

profile of v7, /device:TPU:0, one launch (start us, length us, event | category | flops | bytes accessed | tf_op | source)
XLA Modules:
  0.0 376.9 jit_solution(9276341603888551815)
XLA Ops:
  35.2 4.6 %collective-permute-done.10 = bf16[256,512]{1,0:T(8,128)(2,1)S(1)} collective-permute-done((bf16[256,512]{1,0:T(8,128)(2,1)S(1)}, bf16[256,512]{1,0:T(8,128)(2,1)S(1)}, u32[]{:S(2)}, u32[]{:S(2)}) %collective-permute-start.10) | collective-permute-done | bytes 262176 | tf_op jit(solution)/shard_map/ppermute | solution.py:522
  48.0 5.2 %collective-permute-done.17 = bf16[64,1152]{1,0:T(8,128)(2,1)S(1)} collective-permute-done((bf16[64,1152]{1,0:T(8,128)(2,1)S(1)}, bf16[64,1152]{1,0:T(8,128)(2,1)S(1)}, u32[]{:S(2)}, u32[]{:S(2)}) %collective-permute-start.17) | collective-permute-done | bytes 147488 | tf_op jit(solution)/shard_map/ppermute | solution.py:522
  64.2 4.6 %convolution_convert_fusion = bf16[1152,1024]{1,0:T(8,128)(2,1)} fusion(bf16[576,1024]{1,0:T(8,128)(2,1)S(1)} %collective-permute-done.9, bf16[576,1024]{1,0:T(8,128)(2,1)S(1)} %constant_dynamic-update-slice_fusion.5, s32[]{:T(128)S(6)} %axis_index.22, s32[1152]{0:T(1024)S(1)} %get-tuple-element.727, s32[1152]{0:T(1024)S(1)} %get-tuple-element.728, ...), kind=kOutput, calls=%fused_computation.58 | convolution fusion | flops 2771582976 | bytes 4739332 | tf_op jit(solution)/shard_map/dot_general | solution.py:49
  69.6 4.5 %feed.4 = (f32[128,1152]{1,0:T(8,128)S(1)}, f32[128,1152]{1,0:T(8,128)S(1)}, bf16[2,256,864]{2,1,0:T(8,128)(2,1)S(1)}, bf16[2,256,864]{2,1,0:T(8,128)(2,1)S(1)}, bf16[2,256,864]{2,1,0:T(8,128)(2,1)S(1)}) custom-call(bf16[256,1152]{1,0:T(8,128)(2,1)S(1)} %multiply_convert_fusion.1.refs_0_.refs_4_, bf16[864,1152]{1,0:T(8,128)(2,1)S(1)} %bitcast.54, ...), custom_call_target="tpu_custom_call" | custom-call | flops 1 | bytes 1 | tf_op jit(solution)/shard_map/feed/pallas_call | solution.py:306
  79.8 4.7 %feed.5 = (bf16[128,1152]{1,0:T(8,128)(2,1)S(1)}, bf16[128,1152]{1,0:T(8,128)(2,1)S(1)}, bf16[2,256,864]{2,1,0:T(8,128)(2,1)S(1)}, bf16[2,256,864]{2,1,0:T(8,128)(2,1)S(1)}, bf16[2,256,864]{2,1,0:T(8,128)(2,1)S(1)}) custom-call(bf16[256,1152]{1,0:T(8,128)(2,1)S(1)} %collective-permute-done.23.refs_0_.refs_5_, bf16[864,1152]{1,0:T(8,128)(2,1)S(1)} %bitcast.55, ...), custom_call_target="tpu_custom_call" | custom-call | flops 1 | bytes 1 | tf_op jit(solution)/shard_map/feed/pallas_call | solution.py:306
  84.5 4.5 %feed.6 = (bf16[128,1152]{1,0:T(8,128)(2,1)S(1)}, bf16[128,1152]{1,0:T(8,128)(2,1)S(1)}, bf16[2,256,864]{2,1,0:T(8,128)(2,1)S(1)}, bf16[2,256,864]{2,1,0:T(8,128)(2,1)S(1)}, bf16[2,256,864]{2,1,0:T(8,128)(2,1)S(1)}) custom-call(bf16[256,1152]{1,0:T(8,128)(2,1)S(1)} %collective-permute-done.24.refs_0_.refs_6_, bf16[864,1152]{1,0:T(8,128)(2,1)S(1)} %bitcast.56, ...), custom_call_target="tpu_custom_call" | custom-call | flops 1 | bytes 1 | tf_op jit(solution)/shard_map/feed/pallas_call | solution.py:306
  91.6 4.5 %feed.7 = (bf16[128,1152]{1,0:T(8,128)(2,1)S(1)}, bf16[128,1152]{1,0:T(8,128)(2,1)S(1)}, bf16[2,256,864]{2,1,0:T(8,128)(2,1)S(1)}, bf16[2,256,864]{2,1,0:T(8,128)(2,1)S(1)}, bf16[2,256,864]{2,1,0:T(8,128)(2,1)S(1)}) custom-call(bf16[128,1152]{1,0:T(8,128)(2,1)S(1)} %collective-permute-done.25.refs_0_.refs_7_, ...), custom_call_target="tpu_custom_call" | custom-call | flops 1 | bytes 1 | tf_op jit(solution)/shard_map/feed/pallas_call | solution.py:306
  99.3 5.8 %collective-permute-done.31 = bf16[128,1152]{1,0:T(8,128)(2,1)S(1)} collective-permute-done((bf16[128,1152]{1,0:T(8,128)(2,1)S(1)}, bf16[128,1152]{1,0:T(8,128)(2,1)S(1)}, u32[]{:S(2)}, u32[]{:S(2)}) %collective-permute-start.31) | collective-permute-done | bytes 294944 | tf_op jit(solution)/shard_map/ppermute | solution.py:522
  120.6 4.5 %feed_back.4 = (f32[128,1152]{1,0:T(8,128)S(1)}, f32[128,1152]{1,0:T(8,128)S(1)}, bf16[2,256,864]{2,1,0:T(8,128)(2,1)S(1)}, bf16[2,256,864]{2,1,0:T(8,128)(2,1)S(1)}) custom-call(bf16[2,256,864]{2,1,0:T(8,128)(2,1)S(1)} %get-tuple-element.459.act_ref, bf16[2,256,864]{2,1,0:T(8,128)(2,1)S(1)} %get-tuple-element.460.slope_ref, ...), custom_call_target="tpu_custom_call" | custom-call | flops 1 | bytes 1 | tf_op jit(solution)/shard_map/feed_back/pallas_call | solution.py:337
  131.4 4.3 %feed_back.5 = (bf16[128,1152]{1,0:T(8,128)(2,1)S(1)}, bf16[128,1152]{1,0:T(8,128)(2,1)S(1)}, bf16[2,256,864]{2,1,0:T(8,128)(2,1)S(1)}, bf16[2,256,864]{2,1,0:T(8,128)(2,1)S(1)}) custom-call(bf16[2,256,864]{2,1,0:T(8,128)(2,1)S(1)} %get-tuple-element.474.act_ref, bf16[2,256,864]{2,1,0:T(8,128)(2,1)S(1)} %get-tuple-element.475.slope_ref, ...), custom_call_target="tpu_custom_call" | custom-call | flops 1 | bytes 1 | tf_op jit(solution)/shard_map/feed_back/pallas_call | solution.py:337
  135.7 4.3 %feed_back.6 = (bf16[128,1152]{1,0:T(8,128)(2,1)S(1)}, bf16[128,1152]{1,0:T(8,128)(2,1)S(1)}, bf16[2,256,864]{2,1,0:T(8,128)(2,1)S(1)}, bf16[2,256,864]{2,1,0:T(8,128)(2,1)S(1)}) custom-call(bf16[2,256,864]{2,1,0:T(8,128)(2,1)S(1)} %get-tuple-element.480.act_ref, bf16[2,256,864]{2,1,0:T(8,128)(2,1)S(1)} %get-tuple-element.481.slope_ref, ...), custom_call_target="tpu_custom_call" | custom-call | flops 1 | bytes 1 | tf_op jit(solution)/shard_map/feed_back/pallas_call | solution.py:337
  142.6 4.7 %feed_back.7 = (bf16[128,1152]{1,0:T(8,128)(2,1)S(1)}, bf16[128,1152]{1,0:T(8,128)(2,1)S(1)}, bf16[2,256,864]{2,1,0:T(8,128)(2,1)S(1)}, bf16[2,256,864]{2,1,0:T(8,128)(2,1)S(1)}) custom-call(bf16[2,256,864]{2,1,0:T(8,128)(2,1)S(1)} %get-tuple-element.500.act_ref, bf16[2,256,864]{2,1,0:T(8,128)(2,1)S(1)} %get-tuple-element.501.slope_ref, ...), custom_call_target="tpu_custom_call" | custom-call | flops 1 | bytes 1 | tf_op jit(solution)/shard_map/feed_back/pallas_call | solution.py:337
  149.8 3.5 collective-permute-start.38
  165.0 3.9 %collective-permute-done.41 = bf16[128,1152]{1,0:T(8,128)(2,1)S(1)} collective-permute-done((bf16[128,1152]{1,0:T(8,128)(2,1)S(1)}, bf16[128,1152]{1,0:T(8,128)(2,1)S(1)}, u32[]{:S(2)}, u32[]{:S(2)}) %collective-permute-start.41) | collective-permute-done | bytes 294944 | tf_op jit(solution)/shard_map/ppermute | solution.py:522
  178.9 4.0 %collective-permute-done.45.refs_5_ = bf16[128,1152]{1,0:T(8,128)(2,1)S(1)} collective-permute-done((bf16[128,1152]{1,0:T(8,128)(2,1)S(1)}, bf16[128,1152]{1,0:T(8,128)(2,1)S(1)}, u32[]{:S(2)}, u32[]{:S(2)}) %collective-permute-start.45) | collective-permute-done | bytes 294944 | tf_op jit(solution)/shard_map/ppermute | solution.py:522
  188.5 7.2 %collective-permute-start.48 = (bf16[288,1152]{1,0:T(8,128)(2,1)S(1)}, bf16[288,1152]{1,0:T(8,128)(2,1)S(1)}, u32[]{:S(2)}, u32[]{:S(2)}) collective-permute-start(bf16[288,1152]{1,0:T(8,128)(2,1)S(1)} %broadcast_select_fusion.15), channel_id=1, source_target_pairs={{0,8},{8,0},{16,24},{24,16},{1,9},{9,1},{17,25},{25,17},{2,10},{10... | collective-permute-start | bytes 1990664 | tf_op jit(solution)/shard_map/ppermute | solution.py:663
  196.7 3.3 attend_back.1
  200.2 10.7 %collective-permute-done.48 = bf16[288,1152]{1,0:T(8,128)(2,1)S(1)} collective-permute-done((bf16[288,1152]{1,0:T(8,128)(2,1)S(1)}, bf16[288,1152]{1,0:T(8,128)(2,1)S(1)}, u32[]{:S(2)}, u32[]{:S(2)}) %collective-permute-start.48) | collective-permute-done | bytes 663584 | tf_op jit(solution)/shard_map/ppermute | solution.py:663
  220.2 8.2 %collective-permute-done.51 = bf16[288,1152]{1,0:T(8,128)(2,1)S(1)} collective-permute-done((bf16[288,1152]{1,0:T(8,128)(2,1)S(1)}, bf16[288,1152]{1,0:T(8,128)(2,1)S(1)}, u32[]{:S(2)}, u32[]{:S(2)}) %collective-permute-start.51) | collective-permute-done | bytes 663584 | tf_op jit(solution)/shard_map/ppermute | solution.py:663
  231.4 3.9 %collective-permute-start.56 = (bf16[288,1152]{1,0:T(8,128)(2,1)S(1)}, bf16[288,1152]{1,0:T(8,128)(2,1)S(1)}, u32[]{:S(2)}, u32[]{:S(2)}) collective-permute-start(bf16[288,1152]{1,0:T(8,128)(2,1)S(1)} %broadcast_select_fusion.13), channel_id=1, source_target_pairs={{0,8},{8,0},{16,24},{24,16},{1,9},{9,1},{17,25},{25,17},{2,10},{10... | collective-permute-start | bytes 1990664 | tf_op jit(solution)/shard_map/ppermute | solution.py:663
  241.7 7.8 %collective-permute-done.56 = bf16[288,1152]{1,0:T(8,128)(2,1)S(1)} collective-permute-done((bf16[288,1152]{1,0:T(8,128)(2,1)S(1)}, bf16[288,1152]{1,0:T(8,128)(2,1)S(1)}, u32[]{:S(2)}, u32[]{:S(2)}) %collective-permute-start.56) | collective-permute-done | bytes 663584 | tf_op jit(solution)/shard_map/ppermute | solution.py:663
  250.2 3.8 %collective-permute-start.60 = (bf16[288,1152]{1,0:T(8,128)(2,1)S(1)}, bf16[288,1152]{1,0:T(8,128)(2,1)S(1)}, u32[]{:S(2)}, u32[]{:S(2)}) collective-permute-start(bf16[288,1152]{1,0:T(8,128)(2,1)S(1)} %broadcast_select_fusion.12), channel_id=1, source_target_pairs={{0,8},{8,0},{16,24},{24,16},{1,9},{9,1},{17,25},{25,17},{2,10},{10... | collective-permute-start | bytes 1990664 | tf_op jit(solution)/shard_map/ppermute | solution.py:663
  262.7 4.6 %collective-permute-done.60 = bf16[288,1152]{1,0:T(8,128)(2,1)S(1)} collective-permute-done((bf16[288,1152]{1,0:T(8,128)(2,1)S(1)}, bf16[288,1152]{1,0:T(8,128)(2,1)S(1)}, u32[]{:S(2)}, u32[]{:S(2)}) %collective-permute-start.60) | collective-permute-done | bytes 663584 | tf_op jit(solution)/shard_map/ppermute | solution.py:663
  267.8 3.9 %collective-permute-start.64 = (bf16[288,1152]{1,0:T(8,128)(2,1)S(1)}, bf16[288,1152]{1,0:T(8,128)(2,1)S(1)}, u32[]{:S(2)}, u32[]{:S(2)}) collective-permute-start(bf16[288,1152]{1,0:T(8,128)(2,1)S(1)} %broadcast_select_fusion.11), channel_id=1, source_target_pairs={{0,8},{8,0},{16,24},{24,16},{1,9},{9,1},{17,25},{25,17},{2,10},{10... | collective-permute-start | bytes 1990664 | tf_op jit(solution)/shard_map/ppermute | solution.py:663
  275.1 8.0 %collective-permute-done.67 = bf16[128,1152]{1,0:T(8,128)(2,1)S(1)} collective-permute-done((bf16[128,1152]{1,0:T(8,128)(2,1)S(1)}, bf16[128,1152]{1,0:T(8,128)(2,1)S(1)}, u32[]{:S(2)}, u32[]{:S(2)}) %collective-permute-start.67) | collective-permute-done | bytes 294944 | tf_op jit(solution)/shard_map/ppermute | solution.py:522
  285.4 6.1 %collective-permute-start.68 = (bf16[288,1152]{1,0:T(8,128)(2,1)S(1)}, bf16[288,1152]{1,0:T(8,128)(2,1)S(1)}, u32[]{:S(2)}, u32[]{:S(2)}) collective-permute-start(bf16[288,1152]{1,0:T(8,128)(2,1)S(1)} %broadcast_select_fusion.10), channel_id=1, source_target_pairs={{0,8},{8,0},{16,24},{24,16},{1,9},{9,1},{17,25},{25,17},{2,10},{10... | collective-permute-start | bytes 1990664 | tf_op jit(solution)/shard_map/ppermute | solution.py:663
  292.9 9.4 %collective-permute-done.70 = bf16[160,1536]{1,0:T(8,128)(2,1)S(1)} collective-permute-done((bf16[160,1536]{1,0:T(8,128)(2,1)S(1)}, bf16[160,1536]{1,0:T(8,128)(2,1)S(1)}, u32[]{:S(2)}, u32[]{:S(2)}) %collective-permute-start.70) | collective-permute-done | bytes 491552 | tf_op jit(solution)/shard_map/ppermute | solution.py:522
  311.7 7.7 %collective-permute-done.74 = bf16[160,1536]{1,0:T(8,128)(2,1)S(1)} collective-permute-done((bf16[160,1536]{1,0:T(8,128)(2,1)S(1)}, bf16[160,1536]{1,0:T(8,128)(2,1)S(1)}, u32[]{:S(2)}, u32[]{:S(2)}) %collective-permute-start.74) | collective-permute-done | bytes 491552 | tf_op jit(solution)/shard_map/ppermute | solution.py:522
  323.2 6.3 %collective-permute-start.75 = (bf16[160,1536]{1,0:T(8,128)(2,1)S(1)}, bf16[160,1536]{1,0:T(8,128)(2,1)S(1)}, u32[]{:S(2)}, u32[]{:S(2)}) collective-permute-start(bf16[160,1536]{1,0:T(8,128)(2,1)S(1)} %add_convert_fusion.21), channel_id=1, source_target_pairs={{0,8},{24,16},{1,9},{25,17},{2,10},{26,18},{3,11},{27,19},{4,12},{... | collective-permute-start | bytes 1474568 | tf_op jit(solution)/shard_map/ppermute | solution.py:668
  329.6 7.1 %collective-permute-done.75 = bf16[160,1536]{1,0:T(8,128)(2,1)S(1)} collective-permute-done((bf16[160,1536]{1,0:T(8,128)(2,1)S(1)}, bf16[160,1536]{1,0:T(8,128)(2,1)S(1)}, u32[]{:S(2)}, u32[]{:S(2)}) %collective-permute-start.75) | collective-permute-done | bytes 491552 | tf_op jit(solution)/shard_map/ppermute | solution.py:668
  345.3 11.6 %collective-permute-done.80 = bf16[288,1152]{1,0:T(8,128)(2,1)S(1)} collective-permute-done((bf16[288,1152]{1,0:T(8,128)(2,1)S(1)}, bf16[288,1152]{1,0:T(8,128)(2,1)S(1)}, u32[]{:S(2)}, u32[]{:S(2)}) %collective-permute-start.80) | collective-permute-done | bytes 663584 | tf_op jit(solution)/shard_map/ppermute | solution.py:700
  362.7 7.0 %collective-permute-done.81 = bf16[160,1536]{1,0:T(8,128)(2,1)S(1)} collective-permute-done((bf16[160,1536]{1,0:T(8,128)(2,1)S(1)}, bf16[160,1536]{1,0:T(8,128)(2,1)S(1)}, u32[]{:S(2)}, u32[]{:S(2)}) %collective-permute-start.81) | collective-permute-done | bytes 491552 | tf_op jit(solution)/shard_map/ppermute | solution.py:700
  (374 shorter events, 189.7 us)
Async XLA Ops:
  0.6 11.0 %collective-permute-start = (bf16[144,512]{1,0:T(8,128)(2,1)}, bf16[144,512]{1,0:T(8,128)(2,1)S(1)}, u32[]{:S(2)}, u32[]{:S(2)}) collective-permute-start(bf16[144,512]{1,0:T(8,128)(2,1)} %param.21), channel_id=1, source_target_pairs={{0,2},{1,3},{2,0},{3,1},{4,6},{5,7},{6,4},{7,5},{8,10},{9,11},{10,... | collective-permute-start | bytes 442376 | tf_op jit(solution)/shard_map/ppermute | solution.py:522
  29.0 10.9 %collective-permute-start.10 = (bf16[256,512]{1,0:T(8,128)(2,1)S(1)}, bf16[256,512]{1,0:T(8,128)(2,1)S(1)}, u32[]{:S(2)}, u32[]{:S(2)}) collective-permute-start(bf16[256,512]{1,0:T(8,128)(2,1)S(1)} %pad_maximum_fusion.6), channel_id=1, source_target_pairs={{0,2},{1,3},{2,0},{3,1},{4,6},{5,7},{6,4},{7,5},{8,10},{9,11},{10,... | collective-permute-start | bytes 786440 | tf_op jit(solution)/shard_map/ppermute | solution.py:522
  61.0 15.7 %collective-permute-start.23 = (bf16[256,1152]{1,0:T(8,128)(2,1)S(1)}, bf16[256,1152]{1,0:T(8,128)(2,1)S(1)}, u32[]{:S(2)}, u32[]{:S(2)}) collective-permute-start(bf16[256,1152]{1,0:T(8,128)(2,1)S(1)} %multiply_convert_fusion.1.refs_0_.refs_4_), channel_id=1, source_target_pairs={{0,2},{1,3},{2,0},{3,1},{4,6},{5,7},{6,4},{7,5},{8,10},{9,11},{10,... | collective-permute-start | bytes 1769480 | tf_op jit(solution)/shard_map/ppermute | solution.py:522
  63.1 15.0 %collective-permute-start.24 = (bf16[256,1152]{1,0:T(8,128)(2,1)S(1)}, bf16[256,1152]{1,0:T(8,128)(2,1)S(1)}, u32[]{:S(2)}, u32[]{:S(2)}) collective-permute-start(bf16[256,1152]{1,0:T(8,128)(2,1)S(1)} %multiply_convert_fusion.1.refs_0_.refs_4_), channel_id=1, source_target_pairs={{0,4},{1,5},{2,6},{3,7},{4,0},{5,1},{6,2},{7,3},{8,12},{9,13},{10,... | collective-permute-start | bytes 1769480 | tf_op jit(solution)/shard_map/ppermute | solution.py:522
  78.2 10.8 %collective-permute-start.25 = (bf16[128,1152]{1,0:T(8,128)(2,1)S(1)}, bf16[128,1152]{1,0:T(8,128)(2,1)S(1)}, u32[]{:S(2)}, u32[]{:S(2)}) collective-permute-start(bf16[128,1152]{1,0:T(8,128)(2,1)S(1)} %slice.131), channel_id=1, source_target_pairs={{0,2},{1,3},{2,0},{3,1},{4,6},{5,7},{6,4},{7,5},{8,10},{9,11},{10,... | collective-permute-start | bytes 884744 | tf_op jit(solution)/shard_map/ppermute | solution.py:522
  116.3 12.0 %collective-permute-start.33 = (bf16[256,1152]{1,0:T(8,128)(2,1)S(1)}, bf16[256,1152]{1,0:T(8,128)(2,1)S(1)}, u32[]{:S(2)}, u32[]{:S(2)}) collective-permute-start(bf16[256,1152]{1,0:T(8,128)(2,1)S(1)} %get-tuple-element.458.refs_0_.refs_4_), channel_id=1, source_target_pairs={{0,2},{1,3},{2,0},{3,1},{4,6},{5,7},{6,4},{7,5},{8,10},{9,11},{10,... | collective-permute-start | bytes 1769480 | tf_op jit(solution)/shard_map/ppermute | solution.py:522
  116.5 13.0 %collective-permute-start.34 = (bf16[256,1152]{1,0:T(8,128)(2,1)S(1)}, bf16[256,1152]{1,0:T(8,128)(2,1)S(1)}, u32[]{:S(2)}, u32[]{:S(2)}) collective-permute-start(bf16[256,1152]{1,0:T(8,128)(2,1)S(1)} %get-tuple-element.458.refs_0_.refs_4_), channel_id=1, source_target_pairs={{0,4},{1,5},{2,6},{3,7},{4,0},{5,1},{6,2},{7,3},{8,12},{9,13},{10,... | collective-permute-start | bytes 1769480 | tf_op jit(solution)/shard_map/ppermute | solution.py:522
  149.8 20.5 %collective-permute-start.38 = (bf16[288,1152]{1,0:T(8,128)(2,1)S(1)}, bf16[288,1152]{1,0:T(8,128)(2,1)S(1)}, u32[]{:S(2)}, u32[]{:S(2)}) collective-permute-start(bf16[288,1152]{1,0:T(8,128)(2,1)S(1)} %get-tuple-element.526), channel_id=1, source_target_pairs={{0,8},{24,16},{1,9},{25,17},{2,10},{26,18},{3,11},{27,19},{4,12},{... | collective-permute-start | bytes 1990664 | tf_op jit(solution)/shard_map/ppermute | solution.py:668
  155.8 13.1 %collective-permute-start.41 = (bf16[128,1152]{1,0:T(8,128)(2,1)S(1)}, bf16[128,1152]{1,0:T(8,128)(2,1)S(1)}, u32[]{:S(2)}, u32[]{:S(2)}) collective-permute-start(bf16[128,1152]{1,0:T(8,128)(2,1)S(1)} %get-tuple-element.529), channel_id=1, source_target_pairs={{0,2},{1,3},{2,0},{3,1},{4,6},{5,7},{6,4},{7,5},{8,10},{9,11},{10,... | collective-permute-start | bytes 884744 | tf_op jit(solution)/shard_map/ppermute | solution.py:522
  156.2 14.0 %collective-permute-start.42 = (bf16[128,1152]{1,0:T(8,128)(2,1)S(1)}, bf16[128,1152]{1,0:T(8,128)(2,1)S(1)}, u32[]{:S(2)}, u32[]{:S(2)}) collective-permute-start(bf16[128,1152]{1,0:T(8,128)(2,1)S(1)} %get-tuple-element.530), channel_id=1, source_target_pairs={{0,4},{1,5},{2,6},{3,7},{4,0},{5,1},{6,2},{7,3},{8,12},{9,13},{10,... | collective-permute-start | bytes 884744 | tf_op jit(solution)/shard_map/ppermute | solution.py:522
  170.3 17.0 %collective-permute-start.43 = (bf16[288,1152]{1,0:T(8,128)(2,1)S(1)}, bf16[288,1152]{1,0:T(8,128)(2,1)S(1)}, u32[]{:S(2)}, u32[]{:S(2)}) collective-permute-start(bf16[288,1152]{1,0:T(8,128)(2,1)S(1)} %get-tuple-element.546), channel_id=1, source_target_pairs={{0,8},{24,16},{1,9},{25,17},{2,10},{26,18},{3,11},{27,19},{4,12},{... | collective-permute-start | bytes 1990664 | tf_op jit(solution)/shard_map/ppermute | solution.py:668
  172.7 14.6 %collective-permute-start.44 = (bf16[288,1152]{1,0:T(8,128)(2,1)S(1)}, bf16[288,1152]{1,0:T(8,128)(2,1)S(1)}, u32[]{:S(2)}, u32[]{:S(2)}) collective-permute-start(bf16[288,1152]{1,0:T(8,128)(2,1)S(1)} %add_convert_fusion.17), channel_id=1, source_target_pairs={{8,16},{16,8},{9,17},{17,9},{10,18},{18,10},{11,19},{19,11},{12,20... | collective-permute-start | bytes 1990664 | tf_op jit(solution)/shard_map/ppermute | solution.py:670
  187.3 23.6 %collective-permute-start.50 = (bf16[864,1152]{1,0:T(8,128)(2,1)S(1)}, bf16[864,1152]{1,0:T(8,128)(2,1)S(1)}, u32[]{:S(2)}, u32[]{:S(2)}) collective-permute-start(bf16[864,1152]{1,0:T(8,128)(2,1)S(1)} %weight_grad.9), channel_id=1, source_target_pairs={{0,1},{1,0},{2,3},{3,2},{4,5},{5,4},{6,7},{7,6},{8,9},{9,8},{10,11... | collective-permute-start | bytes 5971976 | tf_op jit(solution)/shard_map/ppermute | solution.py:522
  187.5 12.5 %collective-permute-start.49 = (bf16[288,1152]{1,0:T(8,128)(2,1)S(1)}, bf16[288,1152]{1,0:T(8,128)(2,1)S(1)}, u32[]{:S(2)}, u32[]{:S(2)}) collective-permute-start(bf16[288,1152]{1,0:T(8,128)(2,1)S(1)} %add_convert_fusion.15), channel_id=1, source_target_pairs={{8,16},{16,8},{9,17},{17,9},{10,18},{18,10},{11,19},{19,11},{12,20... | collective-permute-start | bytes 1990664 | tf_op jit(solution)/shard_map/ppermute | solution.py:670
  188.5 22.5 %collective-permute-start.48 = (bf16[288,1152]{1,0:T(8,128)(2,1)S(1)}, bf16[288,1152]{1,0:T(8,128)(2,1)S(1)}, u32[]{:S(2)}, u32[]{:S(2)}) collective-permute-start(bf16[288,1152]{1,0:T(8,128)(2,1)S(1)} %broadcast_select_fusion.15), channel_id=1, source_target_pairs={{0,8},{8,0},{16,24},{24,16},{1,9},{9,1},{17,25},{25,17},{2,10},{10... | collective-permute-start | bytes 1990664 | tf_op jit(solution)/shard_map/ppermute | solution.py:663
  211.0 17.4 %collective-permute-start.51 = (bf16[288,1152]{1,0:T(8,128)(2,1)S(1)}, bf16[288,1152]{1,0:T(8,128)(2,1)S(1)}, u32[]{:S(2)}, u32[]{:S(2)}) collective-permute-start(bf16[288,1152]{1,0:T(8,128)(2,1)S(1)} %broadcast_select_fusion.14), channel_id=1, source_target_pairs={{0,8},{8,0},{16,24},{24,16},{1,9},{9,1},{17,25},{25,17},{2,10},{10... | collective-permute-start | bytes 1990664 | tf_op jit(solution)/shard_map/ppermute | solution.py:663
  213.0 15.4 %collective-permute-start.52 = (bf16[288,1152]{1,0:T(8,128)(2,1)S(1)}, bf16[288,1152]{1,0:T(8,128)(2,1)S(1)}, u32[]{:S(2)}, u32[]{:S(2)}) collective-permute-start(bf16[288,1152]{1,0:T(8,128)(2,1)S(1)} %add_convert_fusion.13), channel_id=1, source_target_pairs={{8,16},{16,8},{9,17},{17,9},{10,18},{18,10},{11,19},{19,11},{12,20... | collective-permute-start | bytes 1990664 | tf_op jit(solution)/shard_map/ppermute | solution.py:670
  214.4 14.0 %collective-permute-start.54 = (bf16[256,512]{1,0:T(8,128)(2,1)S(1)}, bf16[256,512]{1,0:T(8,128)(2,1)S(1)}, u32[]{:S(2)}, u32[]{:S(2)}) collective-permute-start(bf16[256,512]{1,0:T(8,128)(2,1)S(1)} %get-tuple-element.706), channel_id=1, source_target_pairs={{0,2},{1,3},{2,0},{3,1},{4,6},{5,7},{6,4},{7,5},{8,10},{9,11},{10,... | collective-permute-start | bytes 786440 | tf_op jit(solution)/shard_map/ppermute | solution.py:522
  216.1 12.3 %collective-permute-start.55 = (bf16[256,512]{1,0:T(8,128)(2,1)S(1)}, bf16[256,512]{1,0:T(8,128)(2,1)S(1)}, u32[]{:S(2)}, u32[]{:S(2)}) collective-permute-start(bf16[256,512]{1,0:T(8,128)(2,1)S(1)} %get-tuple-element.705), channel_id=1, source_target_pairs={{0,4},{1,5},{2,6},{3,7},{4,0},{5,1},{6,2},{7,3},{8,12},{9,13},{10,... | collective-permute-start | bytes 786440 | tf_op jit(solution)/shard_map/ppermute | solution.py:522
  231.4 18.1 %collective-permute-start.56 = (bf16[288,1152]{1,0:T(8,128)(2,1)S(1)}, bf16[288,1152]{1,0:T(8,128)(2,1)S(1)}, u32[]{:S(2)}, u32[]{:S(2)}) collective-permute-start(bf16[288,1152]{1,0:T(8,128)(2,1)S(1)} %broadcast_select_fusion.13), channel_id=1, source_target_pairs={{0,8},{8,0},{16,24},{24,16},{1,9},{9,1},{17,25},{25,17},{2,10},{10... | collective-permute-start | bytes 1990664 | tf_op jit(solution)/shard_map/ppermute | solution.py:663
  235.3 14.2 %collective-permute-start.57 = (bf16[288,1152]{1,0:T(8,128)(2,1)S(1)}, bf16[288,1152]{1,0:T(8,128)(2,1)S(1)}, u32[]{:S(2)}, u32[]{:S(2)}) collective-permute-start(bf16[288,1152]{1,0:T(8,128)(2,1)S(1)} %add_convert_fusion.12), channel_id=1, source_target_pairs={{8,16},{16,8},{9,17},{17,9},{10,18},{18,10},{11,19},{19,11},{12,20... | collective-permute-start | bytes 1990664 | tf_op jit(solution)/shard_map/ppermute | solution.py:670
  250.2 17.1 %collective-permute-start.60 = (bf16[288,1152]{1,0:T(8,128)(2,1)S(1)}, bf16[288,1152]{1,0:T(8,128)(2,1)S(1)}, u32[]{:S(2)}, u32[]{:S(2)}) collective-permute-start(bf16[288,1152]{1,0:T(8,128)(2,1)S(1)} %broadcast_select_fusion.12), channel_id=1, source_target_pairs={{0,8},{8,0},{16,24},{24,16},{1,9},{9,1},{17,25},{25,17},{2,10},{10... | collective-permute-start | bytes 1990664 | tf_op jit(solution)/shard_map/ppermute | solution.py:663
  267.8 16.6 %collective-permute-start.64 = (bf16[288,1152]{1,0:T(8,128)(2,1)S(1)}, bf16[288,1152]{1,0:T(8,128)(2,1)S(1)}, u32[]{:S(2)}, u32[]{:S(2)}) collective-permute-start(bf16[288,1152]{1,0:T(8,128)(2,1)S(1)} %broadcast_select_fusion.11), channel_id=1, source_target_pairs={{0,8},{8,0},{16,24},{24,16},{1,9},{9,1},{17,25},{25,17},{2,10},{10... | collective-permute-start | bytes 1990664 | tf_op jit(solution)/shard_map/ppermute | solution.py:663
  271.8 11.5 %collective-permute-start.65 = (bf16[288,1152]{1,0:T(8,128)(2,1)S(1)}, bf16[288,1152]{1,0:T(8,128)(2,1)S(1)}, u32[]{:S(2)}, u32[]{:S(2)}) collective-permute-start(bf16[288,1152]{1,0:T(8,128)(2,1)S(1)} %add_convert_fusion.7), channel_id=1, source_target_pairs={{8,16},{16,8},{9,17},{17,9},{10,18},{18,10},{11,19},{19,11},{12,20... | collective-permute-start | bytes 1990664 | tf_op jit(solution)/shard_map/ppermute | solution.py:670
  285.4 19.0 %collective-permute-start.68 = (bf16[288,1152]{1,0:T(8,128)(2,1)S(1)}, bf16[288,1152]{1,0:T(8,128)(2,1)S(1)}, u32[]{:S(2)}, u32[]{:S(2)}) collective-permute-start(bf16[288,1152]{1,0:T(8,128)(2,1)S(1)} %broadcast_select_fusion.10), channel_id=1, source_target_pairs={{0,8},{8,0},{16,24},{24,16},{1,9},{9,1},{17,25},{25,17},{2,10},{10... | collective-permute-start | bytes 1990664 | tf_op jit(solution)/shard_map/ppermute | solution.py:663
  305.4 15.3 %collective-permute-start.72 = (bf16[288,1152]{1,0:T(8,128)(2,1)S(1)}, bf16[288,1152]{1,0:T(8,128)(2,1)S(1)}, u32[]{:S(2)}, u32[]{:S(2)}) collective-permute-start(bf16[288,1152]{1,0:T(8,128)(2,1)S(1)} %broadcast_select_fusion.9), channel_id=1, source_target_pairs={{0,8},{8,0},{16,24},{24,16},{1,9},{9,1},{17,25},{25,17},{2,10},{10... | collective-permute-start | bytes 1990664 | tf_op jit(solution)/shard_map/ppermute | solution.py:663
  320.9 15.8 %collective-permute-start.76 = (bf16[288,1152]{1,0:T(8,128)(2,1)S(1)}, bf16[288,1152]{1,0:T(8,128)(2,1)S(1)}, u32[]{:S(2)}, u32[]{:S(2)}) collective-permute-start(bf16[288,1152]{1,0:T(8,128)(2,1)S(1)} %add_convert_fusion.1), channel_id=1, source_target_pairs={{8,16},{16,8},{9,17},{17,9},{10,18},{18,10},{11,19},{19,11},{12,20... | collective-permute-start | bytes 1990664 | tf_op jit(solution)/shard_map/ppermute | solution.py:670
  321.6 16.1 %collective-permute-start.77 = (bf16[288,1152]{1,0:T(8,128)(2,1)S(1)}, bf16[288,1152]{1,0:T(8,128)(2,1)S(1)}, u32[]{:S(2)}, u32[]{:S(2)}) collective-permute-start(bf16[288,1152]{1,0:T(8,128)(2,1)S(1)} %add_convert_fusion.2), channel_id=1, source_target_pairs={{8,0},{16,24},{9,1},{17,25},{10,2},{18,26},{11,3},{19,27},{12,4},{... | collective-permute-start | bytes 1990664 | tf_op jit(solution)/shard_map/ppermute | solution.py:700
  323.2 13.5 %collective-permute-start.75 = (bf16[160,1536]{1,0:T(8,128)(2,1)S(1)}, bf16[160,1536]{1,0:T(8,128)(2,1)S(1)}, u32[]{:S(2)}, u32[]{:S(2)}) collective-permute-start(bf16[160,1536]{1,0:T(8,128)(2,1)S(1)} %add_convert_fusion.21), channel_id=1, source_target_pairs={{0,8},{24,16},{1,9},{25,17},{2,10},{26,18},{3,11},{27,19},{4,12},{... | collective-permute-start | bytes 1474568 | tf_op jit(solution)/shard_map/ppermute | solution.py:668
  341.3 15.6 %collective-permute-start.80 = (bf16[288,1152]{1,0:T(8,128)(2,1)S(1)}, bf16[288,1152]{1,0:T(8,128)(2,1)S(1)}, u32[]{:S(2)}, u32[]{:S(2)}) collective-permute-start(bf16[288,1152]{1,0:T(8,128)(2,1)S(1)} %add_convert_fusion), channel_id=1, source_target_pairs={{8,0},{16,24},{9,1},{17,25},{10,2},{18,26},{11,3},{19,27},{12,4},{... | collective-permute-start | bytes 1990664 | tf_op jit(solution)/shard_map/ppermute | solution.py:700
  357.0 12.7 %collective-permute-start.81 = (bf16[160,1536]{1,0:T(8,128)(2,1)S(1)}, bf16[160,1536]{1,0:T(8,128)(2,1)S(1)}, u32[]{:S(2)}, u32[]{:S(2)}) collective-permute-start(bf16[160,1536]{1,0:T(8,128)(2,1)S(1)} %add_convert_fusion.19), channel_id=1, source_target_pairs={{8,0},{16,24},{9,1},{17,25},{10,2},{18,26},{11,3},{19,27},{12,4},{... | collective-permute-start | bytes 1474568 | tf_op jit(solution)/shard_map/ppermute | solution.py:700
  361.4 14.3 %collective-permute-start.83 = (bf16[128,1152]{1,0:T(8,128)(2,1)S(1)}, bf16[128,1152]{1,0:T(8,128)(2,1)S(1)}, u32[]{:S(2)}, u32[]{:S(2)}) collective-permute-start(bf16[128,1152]{1,0:T(8,128)(2,1)S(1)} %add_convert_fusion.22), channel_id=1, source_target_pairs={{8,0},{16,24},{9,1},{17,25},{10,2},{18,26},{11,3},{19,27},{12,4},{... | collective-permute-start | bytes 884744 | tf_op jit(solution)/shard_map/ppermute | solution.py:700
  (78 other events, 475.8 us)
